TPU v7x, 32 devices: a whole 2x2x4 slice. The times are simulated.
32 devices in a mesh: row: 8 (over z, y), col: 4 (over x, core).
Axes of the slice: x: 2, y: 2, z: 4, core: 2. Of those that a mesh axis runs over, the one named last changes fastest.
Arguments:
- tokens: bfloat16 [16384, 1024], P('row', 'col'), may hold values from -6 to 6
- segments: int32 [16, 1024], P('row'), may hold values from 0 to 7, never falling along the last dimension, each value on 1 to 256 neighbouring positions
- wqkv: bfloat16 [1024, 3072], P('row', 'col'), may hold values from -0.1875 to 0.1875
- bias_qv: bfloat16 [2048], P('col'), may hold values from -3 to 3
- wo: bfloat16 [1024, 1024], P('col', 'row'), may hold values from -1.5 to 1.5
- bias_o: bfloat16 [1024], P('col'), may hold values from -3 to 3
- gain_a: bfloat16 [1024], P('col'), may hold values from 0.099609375 to 1.8984375
- shift_a: bfloat16 [1024], P('col'), may hold values from -3 to 3
- w_in: bfloat16 [1024, 4096], P('row', 'col'), may hold values from -0.1875 to 0.1875
- bias_in: bfloat16 [4096], P('col'), may hold values from -3 to 3
- w_out: bfloat16 [4096, 1024], P('col', 'row'), may hold values from -0.1875 to 0.1875
- bias_out: bfloat16 [1024], P('col'), may hold values from -3 to 3
- gain_b: bfloat16 [1024], P('col'), may hold values from 0.099609375 to 1.8984375
- shift_b: bfloat16 [1024], P('col'), may hold values from -3 to 3
- cotangent: bfloat16 [16384, 1024], P('row', 'col'), may hold values from -6 to 6
Outputs:
- output: bfloat16 [16384, 1024], P('row', 'col')
- grad_tokens: float32 [16384, 1024], P('row', 'col')
- grad_wqkv: float32 [1024, 3072], P('row', 'col')
- grad_bias_qv: float32 [2048], P('col')
- grad_wo: float32 [1024, 1024], P('col', 'row')
- grad_bias_o: float32 [1024], P('col')
- grad_gain_a: float32 [1024], P('col')
- grad_shift_a: float32 [1024], P('col')
- grad_w_in: float32 [1024, 4096], P('row', 'col')
- grad_bias_in: float32 [4096], P('col')
- grad_w_out: float32 [4096, 1024], P('col', 'row')
- grad_bias_out: float32 [1024], P('col')
- grad_gain_b: float32 [1024], P('col')
- grad_shift_b: float32 [1024], P('col')
Inputs may be any that keep to these rules, and one draw needn't show every extreme that they name: `segments`: within each sequence the document numbers never fall and each of the 8 documents has 1 to 256 tokens; each sequence has one document of exactly 256 tokens.
All inputs are finite; a program needn't handle non-finite values.
Results may differ from a plain program's by a relative error of at most 0.017.
Values may be sent and summed in bfloat16 or wider, within the bound.
No kernel may reach another device: no remote copies, remote signals or barrier semaphores. Data moves between devices by JAX's collectives and lax.ppermute only.
A program may use at most 128 MiB of HBM per device.

v0:
```python
import math

import jax
import jax.numpy as jnp
from jax import lax
from jax.sharding import PartitionSpec as P

D = 1024
DH = 64


NORM_EPS = 1e-06
MASKED = -1000000000.0
block_limit = 512


def cross_rows(left, right):
    return lax.dot_general(
        left, right, (((0,), (0,)), ((), ())), preferred_element_type=jnp.float32
    )


def times_back(left, right):
    return lax.dot_general(
        left, right, (((1,), (1,)), ((), ())), preferred_element_type=jnp.float32
    )


def features(local_rows):
    return lax.all_gather(local_rows, "col", axis=1, tiled=True)


def fold_cols(partial_terms):
    return lax.psum_scatter(partial_terms, "col", scatter_dimension=1, tiled=True)


def row_totals(first, second):
    return lax.psum((jnp.sum(first, axis=1), jnp.sum(second, axis=1)), "col")


def norm_forward(hidden, gain, shift):
    row_total, row_square = row_totals(hidden, hidden * hidden)
    row_mean = row_total / D
    inv_std = lax.rsqrt(row_square / D - row_mean * row_mean + NORM_EPS)
    centred = (hidden - row_mean[:, None]) * inv_std[:, None]
    return (centred * gain + shift, centred, inv_std)


def norm_backward(incoming, centred, inv_std, gain):
    scaled = incoming * gain
    row_total, row_cross = row_totals(scaled, scaled * centred)
    return inv_std[:, None] * (scaled - row_total[:, None] / D - centred * (row_cross[:, None] / D))


def project_in(whole_rows, weight):
    return jnp.dot(
        whole_rows,
        lax.all_gather(weight, "row", axis=0, tiled=True),
        preferred_element_type=jnp.float32,
    )


def project_out(local_rows, weight):
    return jnp.dot(
        local_rows,
        lax.all_gather(weight, "row", axis=1, tiled=True),
        preferred_element_type=jnp.float32,
    )


def back_in(grad_rows, weight):
    return times_back(grad_rows, lax.all_gather(weight, "row", axis=0, tiled=True))


def back_out(grad_whole, weight):
    return times_back(grad_whole, lax.all_gather(weight, "row", axis=1, tiled=True))


def attend(queries, key_rows, value_rows, labels):
    length = queries.shape[0]
    block_rows = min(block_limit, length)
    score_scale = 1.0 / math.sqrt(queries.shape[1])

    def one_block(first_row):
        query_block = lax.dynamic_slice_in_dim(queries, first_row, block_rows, 0)
        label_block = lax.dynamic_slice_in_dim(labels, first_row, block_rows, 0)
        scores = (
            jnp.einsum("qd,kd->qk", query_block, key_rows, preferred_element_type=jnp.float32)
            * score_scale
        )
        scores = jnp.where(label_block[:, None] == labels[None, :], scores, MASKED)
        row_max = jnp.max(scores, axis=1, keepdims=True)
        shifted = jnp.exp(scores - row_max)
        row_total = jnp.sum(shifted, axis=1, keepdims=True)
        probabilities = (shifted / row_total).astype(jnp.bfloat16)
        context = jnp.dot(probabilities, value_rows, preferred_element_type=jnp.float32)
        return (context, (row_max + jnp.log(row_total))[:, 0])

    starts = jnp.arange(length // block_rows, dtype=jnp.int32) * block_rows
    context, log_total = lax.map(one_block, starts)
    return (context.reshape(length, -1), log_total.reshape(length))


def attend_back(queries, key_rows, value_rows, labels, log_total, grad_context):
    length = queries.shape[0]
    block_rows = min(block_limit, length)
    score_scale = 1.0 / math.sqrt(queries.shape[1])

    def one_block(state_pair, first_row):
        grad_keys, grad_values = state_pair
        query_block = lax.dynamic_slice_in_dim(queries, first_row, block_rows, 0)
        label_block = lax.dynamic_slice_in_dim(labels, first_row, block_rows, 0)
        total_block = lax.dynamic_slice_in_dim(log_total, first_row, block_rows, 0)
        grad_block = lax.dynamic_slice_in_dim(grad_context, first_row, block_rows, 0)
        scores = (
            jnp.einsum("qd,kd->qk", query_block, key_rows, preferred_element_type=jnp.float32)
            * score_scale
        )
        scores = jnp.where(label_block[:, None] == labels[None, :], scores, MASKED)
        probabilities = jnp.exp(scores - total_block[:, None])
        grad_prob = jnp.einsum(
            "qd,kd->qk", grad_block, value_rows, preferred_element_type=jnp.float32
        )
        row_dot = jnp.sum(probabilities * grad_prob, axis=1, keepdims=True)
        dscore = (probabilities * (grad_prob - row_dot)).astype(jnp.bfloat16)
        grad_query = jnp.dot(dscore, key_rows, preferred_element_type=jnp.float32) * score_scale
        grad_keys = (
            grad_keys
            + jnp.einsum("qk,qd->kd", dscore, query_block, preferred_element_type=jnp.float32)
            * score_scale
        )
        grad_values = grad_values + jnp.einsum(
            "qk,qd->kd",
            probabilities.astype(jnp.bfloat16),
            grad_block,
            preferred_element_type=jnp.float32,
        )
        return ((grad_keys, grad_values), grad_query)

    starts = jnp.arange(length // block_rows, dtype=jnp.int32) * block_rows
    zero_rows = jnp.zeros(key_rows.shape, jnp.float32)
    (grad_keys, grad_values), grad_query = lax.scan(one_block, (zero_rows, zero_rows), starts)
    return (grad_query.reshape(queries.shape), grad_keys, grad_values)


def body(
    tokens,
    segments,
    wqkv,
    bias_qv,
    wo,
    bias_o,
    gain_a,
    shift_a,
    w_in,
    bias_in,
    w_out,
    bias_out,
    gain_b,
    shift_b,
    cotangent,
):
    local_width = tokens.shape[1]
    local_heads = wqkv.shape[1] // (3 * DH)
    micro_count = segments.shape[0]
    gain_a32 = gain_a.astype(jnp.float32)
    gain_b32 = gain_b.astype(jnp.float32)
    shift_a32 = shift_a.astype(jnp.float32)
    shift_b32 = shift_b.astype(jnp.float32)
    bias_o32 = bias_o.astype(jnp.float32)
    attend_all = jax.vmap(
        jax.vmap(attend, in_axes=(1, 1, 1, None), out_axes=1), in_axes=(0, 0, 0, 0)
    )
    attend_all_back = jax.vmap(
        jax.vmap(attend_back, in_axes=(1, 1, 1, None, 1, 1), out_axes=1), in_axes=(0, 0, 0, 0, 0, 0)
    )

    def one_micro(carry, sliced):
        big_acc, small_acc = carry
        tokens_m, labels_m, cot_m = sliced
        row_count = tokens_m.shape[0]
        labels = labels_m[None]
        whole_x = features(tokens_m)
        projected = project_in(whole_x, wqkv).reshape(row_count, local_heads, 3, DH)
        biases = bias_qv.astype(jnp.float32).reshape(local_heads, 2, DH)
        queries = (
            (projected[:, :, 0] + biases[:, 0])
            .astype(jnp.bfloat16)
            .reshape(1, row_count, local_heads, DH)
        )
        key_rows = projected[:, :, 1].astype(jnp.bfloat16).reshape(1, row_count, local_heads, DH)
        value_rows = (
            (projected[:, :, 2] + biases[:, 1])
            .astype(jnp.bfloat16)
            .reshape(1, row_count, local_heads, DH)
        )
        context_grid, log_total = attend_all(queries, key_rows, value_rows, labels)
        context = context_grid.reshape(row_count, local_heads * DH).astype(jnp.bfloat16)
        residual = tokens_m.astype(jnp.float32) + bias_o32
        partial_a = project_out(context, wo)
        hidden_a = fold_cols(partial_a) + residual
        normed_a, centred_a, inv_std_a = norm_forward(hidden_a, gain_a32, shift_a32)
        whole_y = features(normed_a.astype(jnp.bfloat16))
        inner = project_in(whole_y, w_in) + bias_in.astype(jnp.float32)
        active = jax.nn.gelu(inner, approximate=False).astype(jnp.bfloat16)
        partial_b = project_out(active, w_out)
        hidden_b = fold_cols(partial_b) + bias_out.astype(jnp.float32) + normed_a
        output, centred_b, inv_std_b = norm_forward(hidden_b, gain_b32, shift_b32)
        grad_out = cot_m.astype(jnp.float32)
        grad_b = norm_backward(grad_out, centred_b, inv_std_b, gain_b32)
        whole_gb = features(grad_b.astype(jnp.bfloat16))
        grad_w_out = cross_rows(active, whole_gb)
        grad_active = back_out(whole_gb, w_out)
        grad_inner = jax.vjp(lambda value_in: jax.nn.gelu(value_in, approximate=False), inner)[1](
            grad_active
        )[0]
        grad_inner_low = grad_inner.astype(jnp.bfloat16)
        grad_w_in = cross_rows(whole_y, grad_inner_low)
        grad_normed = fold_cols(back_in(grad_inner_low, w_in)) + grad_b
        grad_a = norm_backward(grad_normed, centred_a, inv_std_a, gain_a32)
        whole_ga = features(grad_a.astype(jnp.bfloat16))
        grad_wo = cross_rows(context, whole_ga)
        grad_context = (
            back_out(whole_ga, wo).astype(jnp.bfloat16).reshape(1, row_count, local_heads, DH)
        )
        grad_queries, grad_keys, grad_values = attend_all_back(
            queries, key_rows, value_rows, labels, log_total, grad_context
        )
        grad_bias_qv = jnp.stack(
            (jnp.sum(grad_queries, axis=(0, 1)), jnp.sum(grad_values, axis=(0, 1))), axis=1
        ).reshape(-1)
        grad_projected = (
            jnp.stack((grad_queries, grad_keys, grad_values), axis=3)
            .reshape(row_count, local_heads * 3 * DH)
            .astype(jnp.bfloat16)
        )
        grad_wqkv = cross_rows(whole_x, grad_projected)
        grad_tokens = fold_cols(back_in(grad_projected, wqkv)) + grad_a
        small_terms = (
            grad_bias_qv,
            jnp.sum(grad_a, axis=0),
            jnp.sum(grad_normed * centred_a, axis=0),
            jnp.sum(grad_normed, axis=0),
            jnp.sum(grad_inner, axis=0),
            jnp.sum(grad_b, axis=0),
            jnp.sum(grad_out * centred_b, axis=0),
            jnp.sum(grad_out, axis=0),
        )
        big_terms = (grad_wqkv, grad_wo, grad_w_in, grad_w_out)
        big_next = tuple((total + term for total, term in zip(big_acc, big_terms)))
        small_next = tuple((total + term for total, term in zip(small_acc, small_terms)))
        return ((big_next, small_next), (output.astype(jnp.bfloat16), grad_tokens))

    big_init = (
        jnp.zeros((D, wqkv.shape[1]), jnp.float32),
        jnp.zeros((wo.shape[0], D), jnp.float32),
        jnp.zeros((D, w_in.shape[1]), jnp.float32),
        jnp.zeros((w_out.shape[0], D), jnp.float32),
    )
    width_zero = jnp.zeros((local_width,), jnp.float32)
    small_init = (
        jnp.zeros(bias_qv.shape, jnp.float32),
        width_zero,
        width_zero,
        width_zero,
        jnp.zeros(bias_in.shape, jnp.float32),
        width_zero,
        width_zero,
        width_zero,
    )
    sliced_in = (
        tokens.reshape(micro_count, -1, local_width),
        segments,
        cotangent.reshape(micro_count, -1, local_width),
    )
    (big_acc, small_acc), (outputs, grad_rows) = lax.scan(
        one_micro, (big_init, small_init), sliced_in
    )
    small_sums = lax.psum(
        (
            small_acc[0],
            small_acc[1],
            small_acc[2],
            small_acc[3],
            small_acc[4],
            small_acc[5],
            small_acc[6],
            small_acc[7],
        ),
        "row",
    )
    big_sums = (
        lax.psum_scatter(
            big_acc[0].astype(jnp.bfloat16), "row", scatter_dimension=0, tiled=True
        ).astype(jnp.float32),
        lax.psum_scatter(
            big_acc[1].astype(jnp.bfloat16), "row", scatter_dimension=1, tiled=True
        ).astype(jnp.float32),
        lax.psum_scatter(
            big_acc[2].astype(jnp.bfloat16), "row", scatter_dimension=0, tiled=True
        ).astype(jnp.float32),
        lax.psum_scatter(
            big_acc[3].astype(jnp.bfloat16), "row", scatter_dimension=1, tiled=True
        ).astype(jnp.float32),
    )
    return (
        outputs.reshape(-1, local_width),
        grad_rows.reshape(-1, local_width),
        big_sums[0],
        small_sums[0],
        big_sums[1],
        small_sums[1],
        small_sums[2],
        small_sums[3],
        big_sums[2],
        small_sums[4],
        big_sums[3],
        small_sums[5],
        small_sums[6],
        small_sums[7],
    )


def solution(mesh):
    in_specs = (
        P("row", "col"),
        P("row", None),
        P("row", "col"),
        P("col"),
        P("col", "row"),
        P("col"),
        P("col"),
        P("col"),
        P("row", "col"),
        P("col"),
        P("col", "row"),
        P("col"),
        P("col"),
        P("col"),
        P("row", "col"),
    )
    out_specs = (
        P("row", "col"),
        P("row", "col"),
        P("row", "col"),
        P("col"),
        P("col", "row"),
        P("col"),
        P("col"),
        P("col"),
        P("row", "col"),
        P("col"),
        P("col", "row"),
        P("col"),
        P("col"),
        P("col"),
    )
    return jax.shard_map(body, mesh=mesh, in_specs=in_specs, out_specs=out_specs, check_vma=False)
```

profile of v0, /device:TPU:0, one launch (start us, length us, event | category | flops | bytes accessed | tf_op | source)
XLA Modules:
  0.0 1406.3 jit_solution(3819591589664098520)
XLA Ops:
  13.1 1106.8 %while.79 = (s32[]{:T(128)}, f32[1024,768]{1,0:T(8,128)}, f32[256,1024]{1,0:T(8,128)}, f32[1024,1024]{1,0:T(8,128)}, f32[1024,1024]{1,0:T(8,128)}, /*index=5*/f3...) while((s32[]{:T(128)}, f32[1024,768]{1,0:T(8,128)}, ...), condition=%wide.region_37.38_spmd.clone.clone, body=%wide.region_0.37_spmd.clone.sunk.clone | while | flops 21379561472 | bytes 533671712 | solution.py:276
  17.4 31.3 %all_gather.50 = bf16[256,1024]{1,0:T(8,128)(2,1)S(1)} all-gather(bf16[256,128]{1,0:T(8,128)(2,1)} %get-tuple-element.1446), channel_id=1, replica_groups=mesh['row'=8,'col'=4] {'row'}, dimensions={1}, use_global_device_ids=true | all-gather | bytes 589824 | tf_op jit(solution)/shard_map/while/body/eval_jaxpr/all_gather | solution.py:66
  48.7 16.5 %all-gather.13.cloned.1.call-done = bf16[1024,768]{1,0:T(8,128)(2,1)} async-done(((bf16[128,768]{1,0:T(8,128)(2,1)}), bf16[1024,768]{1,0:T(8,128)(2,1)}) %all-gather.13.cloned.1.call-update) | async-done | bytes 1572880 | tf_op jit(solution)/shard_map/while/body/eval_jaxpr/all_gather | solution.py:58
  65.2 23.3 %all-gather.15.cloned.1.call-done = bf16[1,1024,1024]{2,1,0:T(8,128)(2,1)} async-done(((bf16[1,1024,256]{2,1,0:T(8,128)(2,1)}), bf16[1,1024,1024]{2,1,0:T(8,128)(2,1)}) %all-gather.15.cloned.1.call-update) | async-done | bytes 2097168 | tf_op jit(solution)/shard_map/while/body/eval_jaxpr/all_gather | solution.py:30
  93.0 20.9 %while.77 = (s32[]{:T(128)}, bf16[2,1,4,512,64]{3,4,2,1,0:T(8,128)(2,1)S(1)}, f32[2,1,4,512]{3,2,1,0:T(4,128)S(1)}, s32[2]{0:T(128)S(1)}, s32[1,1024]{1,0:T(1,12...) while((s32[]{:T(128)}, ...), condition=%wide.region_4.4_spmd, body=%wide.region_1.3_spmd.sunk | while | flops 562558976 | bytes 29174480 | solution.py:100
  118.1 43.9 %reduce-scatter.21.cloned.1.call-done = f32[1024,256]{1,0:T(8,128)} async-done(((f32[1024,1024]{1,0:T(8,128)}), f32[1024,256]{1,0:T(8,128)}) %reduce-scatter.21.cloned.1.call-update) | async-done | bytes 1048592 | tf_op jit(solution)/shard_map/while/body/eval_jaxpr/reduce_scatter | solution.py:34
  163.8 5.9 all-reduce.13
  172.7 40.4 %all-gather.17.cloned.1.call-done = bf16[1024,1024]{1,0:T(8,128)(2,1)} async-done(((bf16[128,1024]{1,0:T(8,128)(2,1)}), bf16[1024,1024]{1,0:T(8,128)(2,1)}) %all-gather.17.cloned.1.call-update) | async-done | bytes 2097168 | tf_op jit(solution)/shard_map/while/body/eval_jaxpr/all_gather | solution.py:58
  213.1 23.3 %all-gather.19.cloned.1.call-done = bf16[1024,1024]{1,0:T(8,128)(2,1)} async-done(((bf16[1024,256]{1,0:T(8,128)(2,1)}), bf16[1024,1024]{1,0:T(8,128)(2,1)}) %all-gather.19.cloned.1.call-update) | async-done | bytes 2097168 | tf_op jit(solution)/shard_map/while/body/eval_jaxpr/all_gather | solution.py:30
  236.5 15.0 %multiply_convert_fusion.6 = (bf16[1024,1024]{1,0:T(8,128)(2,1)}, f32[1024,1024]{1,0:T(8,128)}, f32[1024,1024]{1,0:T(8,128)}) fusion(f32[1024]{0:T(1024)S(1)} %convert_element_type.282, bf16[1024,1024]{1,0:T(8,128)(2,1)} %all-gather.19.cloned.1.call-done, bf16[1024,1024]{1,0:T(8,128)(2,1)} %all-gather.17.cloned.1.call-done), kind=kOutput, calls=%fused_computation.62.clone.1.clone | convolution fusion | flops 2216689664 | bytes 14684160 | tf_op jit(solution)/shard_map/while/body/eval_jaxpr/dot_general | solution.py:56
  251.4 37.3 %all-gather.21.cloned.1.call-done = bf16[1024,1024]{1,0:T(8,128)(2,1)} async-done(((bf16[1024,128]{1,0:T(8,128)(2,1)}), bf16[1024,1024]{1,0:T(8,128)(2,1)}) %all-gather.21.cloned.1.call-update) | async-done | bytes 2097168 | tf_op jit(solution)/shard_map/while/body/eval_jaxpr/all_gather | solution.py:66
  288.8 6.5 fusion.270
  295.9 42.1 %reduce-scatter.23.cloned.1.call-done = f32[1024,256]{1,0:T(8,128)} async-done(((f32[1024,1024]{1,0:T(8,128)}), f32[1024,256]{1,0:T(8,128)}) %reduce-scatter.23.cloned.1.call-update) | async-done | bytes 1048592 | tf_op jit(solution)/shard_map/while/body/eval_jaxpr/reduce_scatter | solution.py:34
  340.7 5.8 all-reduce.14
  358.3 23.5 %all-gather.23.cloned.1.call-done = bf16[1024,1024]{1,0:T(8,128)(2,1)} async-done(((bf16[1024,256]{1,0:T(8,128)(2,1)}), bf16[1024,1024]{1,0:T(8,128)(2,1)}) %all-gather.23.cloned.1.call-update) | async-done | bytes 2097168 | tf_op jit(solution)/shard_map/while/body/eval_jaxpr/all_gather | solution.py:30
  381.9 8.5 fusion.273
  396.0 44.5 %reduce-scatter.25.cloned.1.call-done = f32[1024,256]{1,0:T(8,128)} async-done(((f32[1024,1024]{1,0:T(8,128)}), f32[1024,256]{1,0:T(8,128)}) %reduce-scatter.25.cloned.1.call-update) | async-done | bytes 1048592 | tf_op jit(solution)/shard_map/while/body/eval_jaxpr/reduce_scatter | solution.py:34
  443.4 5.8 all-reduce.16
  453.3 23.3 %all-gather.25.cloned.1.call-done = bf16[1024,1024]{1,0:T(8,128)(2,1)} async-done(((bf16[1024,256]{1,0:T(8,128)(2,1)}), bf16[1024,1024]{1,0:T(8,128)(2,1)}) %all-gather.25.cloned.1.call-update) | async-done | bytes 2097168 | tf_op jit(solution)/shard_map/while/body/eval_jaxpr/all_gather | solution.py:30
  479.0 33.4 %while.78 = (s32[]{:T(128)}, f32[1,4,1024,64]{2,3,1,0:T(8,128)S(1)}, f32[1,4,1024,64]{2,3,1,0:T(8,128)}, f32[2,1,4,512,64]{3,4,2,1,0:T(8,128)}, s32[2]{0:T(128)S...) while((s32[]{:T(128)}, ...), condition=%wide.region_26.26_spmd.clone, body=%wide.region_24.25_spmd.clone.sunk | while | flops 1375598592 | bytes 89198944 | solution.py:142
  522.6 7.1 select_add_fusion.33
  542.0 22.6 %reduce-scatter.27.cloned.1.call-done = f32[1024,256]{1,0:T(8,128)} async-done(((f32[1024,1024]{1,0:T(8,128)}), f32[1024,256]{1,0:T(8,128)}) %reduce-scatter.27.cloned.1.call-update) | async-done | bytes 1048592 | tf_op jit(solution)/shard_map/while/body/eval_jaxpr/reduce_scatter | solution.py:34
  571.1 29.4 %all_gather.50 = bf16[256,1024]{1,0:T(8,128)(2,1)S(1)} all-gather(bf16[256,128]{1,0:T(8,128)(2,1)} %get-tuple-element.1446), channel_id=1, replica_groups=mesh['row'=8,'col'=4] {'row'}, dimensions={1}, use_global_device_ids=true | all-gather | bytes 589824 | tf_op jit(solution)/shard_map/while/body/eval_jaxpr/all_gather | solution.py:66
  600.5 15.6 %all-gather.13.cloned.1.call-done = bf16[1024,768]{1,0:T(8,128)(2,1)} async-done(((bf16[128,768]{1,0:T(8,128)(2,1)}), bf16[1024,768]{1,0:T(8,128)(2,1)}) %all-gather.13.cloned.1.call-update) | async-done | bytes 1572880 | tf_op jit(solution)/shard_map/while/body/eval_jaxpr/all_gather | solution.py:58
  616.0 23.3 %all-gather.15.cloned.1.call-done = bf16[1,1024,1024]{2,1,0:T(8,128)(2,1)} async-done(((bf16[1,1024,256]{2,1,0:T(8,128)(2,1)}), bf16[1,1024,1024]{2,1,0:T(8,128)(2,1)}) %all-gather.15.cloned.1.call-update) | async-done | bytes 2097168 | tf_op jit(solution)/shard_map/while/body/eval_jaxpr/all_gather | solution.py:30
  643.8 20.9 %while.77 = (s32[]{:T(128)}, bf16[2,1,4,512,64]{3,4,2,1,0:T(8,128)(2,1)S(1)}, f32[2,1,4,512]{3,2,1,0:T(4,128)S(1)}, s32[2]{0:T(128)S(1)}, s32[1,1024]{1,0:T(1,12...) while((s32[]{:T(128)}, ...), condition=%wide.region_4.4_spmd, body=%wide.region_1.3_spmd.sunk | while | flops 562558976 | bytes 29174480 | solution.py:100
  668.9 43.9 %reduce-scatter.21.cloned.1.call-done = f32[1024,256]{1,0:T(8,128)} async-done(((f32[1024,1024]{1,0:T(8,128)}), f32[1024,256]{1,0:T(8,128)}) %reduce-scatter.21.cloned.1.call-update) | async-done | bytes 1048592 | tf_op jit(solution)/shard_map/while/body/eval_jaxpr/reduce_scatter | solution.py:34
  714.6 5.9 all-reduce.13
  723.2 40.7 %all-gather.17.cloned.1.call-done = bf16[1024,1024]{1,0:T(8,128)(2,1)} async-done(((bf16[128,1024]{1,0:T(8,128)(2,1)}), bf16[1024,1024]{1,0:T(8,128)(2,1)}) %all-gather.17.cloned.1.call-update) | async-done | bytes 2097168 | tf_op jit(solution)/shard_map/while/body/eval_jaxpr/all_gather | solution.py:58
  763.9 23.4 %all-gather.19.cloned.1.call-done = bf16[1024,1024]{1,0:T(8,128)(2,1)} async-done(((bf16[1024,256]{1,0:T(8,128)(2,1)}), bf16[1024,1024]{1,0:T(8,128)(2,1)}) %all-gather.19.cloned.1.call-update) | async-done | bytes 2097168 | tf_op jit(solution)/shard_map/while/body/eval_jaxpr/all_gather | solution.py:30
  787.3 15.0 %multiply_convert_fusion.6 = (bf16[1024,1024]{1,0:T(8,128)(2,1)}, f32[1024,1024]{1,0:T(8,128)}, f32[1024,1024]{1,0:T(8,128)}) fusion(f32[1024]{0:T(1024)S(1)} %convert_element_type.282, bf16[1024,1024]{1,0:T(8,128)(2,1)} %all-gather.19.cloned.1.call-done, bf16[1024,1024]{1,0:T(8,128)(2,1)} %all-gather.17.cloned.1.call-done), kind=kOutput, calls=%fused_computation.62.clone.1.clone | convolution fusion | flops 2216689664 | bytes 14684160 | tf_op jit(solution)/shard_map/while/body/eval_jaxpr/dot_general | solution.py:56
  802.3 37.3 %all-gather.21.cloned.1.call-done = bf16[1024,1024]{1,0:T(8,128)(2,1)} async-done(((bf16[1024,128]{1,0:T(8,128)(2,1)}), bf16[1024,1024]{1,0:T(8,128)(2,1)}) %all-gather.21.cloned.1.call-update) | async-done | bytes 2097168 | tf_op jit(solution)/shard_map/while/body/eval_jaxpr/all_gather | solution.py:66
  839.6 6.5 fusion.270
  846.7 42.1 %reduce-scatter.23.cloned.1.call-done = f32[1024,256]{1,0:T(8,128)} async-done(((f32[1024,1024]{1,0:T(8,128)}), f32[1024,256]{1,0:T(8,128)}) %reduce-scatter.23.cloned.1.call-update) | async-done | bytes 1048592 | tf_op jit(solution)/shard_map/while/body/eval_jaxpr/reduce_scatter | solution.py:34
  891.5 5.8 all-reduce.14
  909.2 23.5 %all-gather.23.cloned.1.call-done = bf16[1024,1024]{1,0:T(8,128)(2,1)} async-done(((bf16[1024,256]{1,0:T(8,128)(2,1)}), bf16[1024,1024]{1,0:T(8,128)(2,1)}) %all-gather.23.cloned.1.call-update) | async-done | bytes 2097168 | tf_op jit(solution)/shard_map/while/body/eval_jaxpr/all_gather | solution.py:30
  932.7 8.5 fusion.273
  946.8 44.5 %reduce-scatter.25.cloned.1.call-done = f32[1024,256]{1,0:T(8,128)} async-done(((f32[1024,1024]{1,0:T(8,128)}), f32[1024,256]{1,0:T(8,128)}) %reduce-scatter.25.cloned.1.call-update) | async-done | bytes 1048592 | tf_op jit(solution)/shard_map/while/body/eval_jaxpr/reduce_scatter | solution.py:34
  994.2 5.8 all-reduce.16
  1004.4 23.1 %all-gather.25.cloned.1.call-done = bf16[1024,1024]{1,0:T(8,128)(2,1)} async-done(((bf16[1024,256]{1,0:T(8,128)(2,1)}), bf16[1024,1024]{1,0:T(8,128)(2,1)}) %all-gather.25.cloned.1.call-update) | async-done | bytes 2097168 | tf_op jit(solution)/shard_map/while/body/eval_jaxpr/all_gather | solution.py:30
  1029.9 33.2 %while.78 = (s32[]{:T(128)}, f32[1,4,1024,64]{2,3,1,0:T(8,128)S(1)}, f32[1,4,1024,64]{2,3,1,0:T(8,128)}, f32[2,1,4,512,64]{3,4,2,1,0:T(8,128)}, s32[2]{0:T(128)S...) while((s32[]{:T(128)}, ...), condition=%wide.region_26.26_spmd.clone, body=%wide.region_24.25_spmd.clone.sunk | while | flops 1375598592 | bytes 89198944 | solution.py:142
  1073.2 8.6 select_add_fusion.33
  1096.4 18.7 %reduce-scatter.27.cloned.1.call-done = f32[1024,256]{1,0:T(8,128)} async-done(((f32[1024,1024]{1,0:T(8,128)}), f32[1024,256]{1,0:T(8,128)}) %reduce-scatter.27.cloned.1.call-update) | async-done | bytes 1048592 | tf_op jit(solution)/shard_map/while/body/eval_jaxpr/reduce_scatter | solution.py:34
  1137.6 37.1 %all-reduce.4 = (f32[512]{0:T(512)}, f32[256]{0:T(256)}, f32[256]{0:T(256)}, f32[256]{0:T(256)}, f32[1024]{0:T(1024)}, /*index=5*/f32[256]{0:T(256)}, f32[256]{0:T(256)}, f32[256]{0:T(256)}) all-reduce(f32[512]{0:T(512)S(1)} %copy-done.25, f32[256]{0:T(256)S(1)} %copy-done.38, ...), channel_id=1, replica_groups=mesh['row'=8,'col'=4] {'row'}, use_global_device_ids=true, to_apply=%region_39.40 | all-reduce | flops 3072 | bytes 24576 | tf_op jit(solution)/shard_map/psum | solution.py:279
  1174.7 12.3 reduce-scatter.17.cloned.1.call-done
  1188.7 66.4 %reduce-scatter.13.cloned.1.call-done = bf16[128,768]{1,0:T(8,128)(2,1)} async-done(((bf16[1024,768]{1,0:T(8,128)(2,1)}), bf16[128,768]{1,0:T(8,128)(2,1)}) %reduce-scatter.13.cloned.1.call-update) | async-done | bytes 196624 | tf_op jit(solution)/shard_map/reduce_scatter | solution.py:293
  1256.7 69.0 %reduce-scatter.19.cloned.1.call-done = bf16[128,1024]{1,0:T(8,128)(2,1)} async-done(((bf16[1024,1024]{1,0:T(8,128)(2,1)}), bf16[128,1024]{1,0:T(8,128)(2,1)}) %reduce-scatter.19.cloned.1.call-update) | async-done | bytes 262160
  1327.7 69.0 %reduce-scatter.15.cloned.1.call-done = bf16[128,1024]{1,0:T(8,128)(2,1)} async-done(((bf16[1024,1024]{1,0:T(8,128)(2,1)}), bf16[128,1024]{1,0:T(8,128)(2,1)}) %reduce-scatter.15.cloned.1.call-update) | async-done | bytes 262160 | tf_op jit(solution)/shard_map/reduce_scatter | solution.py:299
  (491 shorter events, 267.0 us)
Async XLA Ops:
  13.1 52.1 %all-gather.13.cloned.1.call-start = ((), (), s32[]{:S(2)}) async-start(), calls=%async_computation.12 | async-start | bytes 1769472 | tf_op jit(solution)/shard_map/while/body/eval_jaxpr/all_gather | solution.py:58
  13.9 74.7 %all-gather.15.cloned.1.call-start = ((), (), s32[]{:S(2)}) async-start(), calls=%async_computation.13 | async-start | bytes 2621440 | tf_op jit(solution)/shard_map/while/body/eval_jaxpr/all_gather | solution.py:30
  15.8 146.2 %reduce-scatter.21.cloned.1.call-start = ((), (), s32[]{:S(2)}) async-start(), calls=%async_computation.14 | async-start | bytes 5242880 | tf_op jit(solution)/shard_map/while/body/eval_jaxpr/reduce_scatter | solution.py:34
  48.7 65.2 %copy-start.13 = (bf16[256,1024]{1,0:T(8,128)(2,1)}, bf16[256,1024]{1,0:T(8,128)(2,1)S(1)}, u32[]{:S(2)}) copy-start(bf16[256,1024]{1,0:T(8,128)(2,1)S(1)} %all_gather.50) | copy-start | bytes 1572868 | tf_op jit(solution)/shard_map/while
  117.4 55.3 %copy-start.26 = (bf16[1024]{0:T(1024)(128)(2,1)S(1)}, bf16[1024]{0:T(1024)(128)(2,1)}, u32[]{:S(2)}) copy-start(bf16[1024]{0:T(1024)(128)(2,1)} %get-tuple-element.1451) | copy-start | bytes 6148 | tf_op jit(solution)/shard_map/while
  117.5 95.7 %all-gather.17.cloned.1.call-start = ((), (), s32[]{:S(2)}) async-start(), calls=%async_computation.15 | async-start | bytes 2359296 | tf_op jit(solution)/shard_map/while/body/eval_jaxpr/all_gather | solution.py:58
  118.0 118.4 %all-gather.19.cloned.1.call-start = ((), (), s32[]{:S(2)}) async-start(), calls=%async_computation.16 | async-start | bytes 2621440 | tf_op jit(solution)/shard_map/while/body/eval_jaxpr/all_gather | solution.py:30
  171.5 117.3 %all-gather.21.cloned.1.call-start = ((), (), s32[]{:S(2)}) async-start(), calls=%async_computation.17 | async-start | bytes 2359296 | tf_op jit(solution)/shard_map/while/body/eval_jaxpr/all_gather | solution.py:66
  172.1 166.0 %reduce-scatter.23.cloned.1.call-start = ((), (), s32[]{:S(2)}) async-start(), calls=%async_computation.18 | async-start | bytes 5242880 | tf_op jit(solution)/shard_map/while/body/eval_jaxpr/reduce_scatter | solution.py:34
  295.3 86.5 %all-gather.23.cloned.1.call-start = ((), (), s32[]{:S(2)}) async-start(), calls=%async_computation.19 | async-start | bytes 2621440 | tf_op jit(solution)/shard_map/while/body/eval_jaxpr/all_gather | solution.py:30
  358.1 82.4 %reduce-scatter.25.cloned.1.call-start = ((), (), s32[]{:S(2)}) async-start(), calls=%async_computation.20 | async-start | bytes 5242880 | tf_op jit(solution)/shard_map/while/body/eval_jaxpr/reduce_scatter | solution.py:34
  381.9 9.8 copy-start.48
  396.0 80.6 %all-gather.25.cloned.1.call-start = ((), (), s32[]{:S(2)}) async-start(), calls=%async_computation.21 | async-start | bytes 2621440 | tf_op jit(solution)/shard_map/while/body/eval_jaxpr/all_gather | solution.py:30
  453.0 111.5 %reduce-scatter.27.cloned.1.call-start = ((), (), s32[]{:S(2)}) async-start(), calls=%async_computation.22 | async-start | bytes 5242880 | tf_op jit(solution)/shard_map/while/body/eval_jaxpr/reduce_scatter | solution.py:34
  532.9 9.1 copy-start.37
  532.9 9.0 copy-start.40
  533.0 9.0 copy-start.43
  538.4 26.2 %copy-start.5 = (f32[1024,256]{1,0:T(8,128)S(1)}, f32[1024,256]{1,0:T(8,128)}, u32[]{:S(2)}) copy-start(f32[1024,256]{1,0:T(8,128)} %copy-done.4) | copy-start | bytes 3145732 | tf_op jit(solution)/shard_map/while
  567.0 49.0 %all-gather.13.cloned.1.call-start = ((), (), s32[]{:S(2)}) async-start(), calls=%async_computation.12 | async-start | bytes 1769472 | tf_op jit(solution)/shard_map/while/body/eval_jaxpr/all_gather | solution.py:58
  567.6 71.8 %all-gather.15.cloned.1.call-start = ((), (), s32[]{:S(2)}) async-start(), calls=%async_computation.13 | async-start | bytes 2621440 | tf_op jit(solution)/shard_map/while/body/eval_jaxpr/all_gather | solution.py:30
  569.5 143.3 %reduce-scatter.21.cloned.1.call-start = ((), (), s32[]{:S(2)}) async-start(), calls=%async_computation.14 | async-start | bytes 5242880 | tf_op jit(solution)/shard_map/while/body/eval_jaxpr/reduce_scatter | solution.py:34
  600.5 64.3 %copy-start.13 = (bf16[256,1024]{1,0:T(8,128)(2,1)}, bf16[256,1024]{1,0:T(8,128)(2,1)S(1)}, u32[]{:S(2)}) copy-start(bf16[256,1024]{1,0:T(8,128)(2,1)S(1)} %all_gather.50) | copy-start | bytes 1572868 | tf_op jit(solution)/shard_map/while
  668.2 54.9 %copy-start.26 = (bf16[1024]{0:T(1024)(128)(2,1)S(1)}, bf16[1024]{0:T(1024)(128)(2,1)}, u32[]{:S(2)}) copy-start(bf16[1024]{0:T(1024)(128)(2,1)} %get-tuple-element.1451) | copy-start | bytes 6148 | tf_op jit(solution)/shard_map/while
  668.3 95.7 %all-gather.17.cloned.1.call-start = ((), (), s32[]{:S(2)}) async-start(), calls=%async_computation.15 | async-start | bytes 2359296 | tf_op jit(solution)/shard_map/while/body/eval_jaxpr/all_gather | solution.py:58
  668.9 118.4 %all-gather.19.cloned.1.call-start = ((), (), s32[]{:S(2)}) async-start(), calls=%async_computation.16 | async-start | bytes 2621440 | tf_op jit(solution)/shard_map/while/body/eval_jaxpr/all_gather | solution.py:30
  722.3 117.3 %all-gather.21.cloned.1.call-start = ((), (), s32[]{:S(2)}) async-start(), calls=%async_computation.17 | async-start | bytes 2359296 | tf_op jit(solution)/shard_map/while/body/eval_jaxpr/all_gather | solution.py:66
  722.9 165.9 %reduce-scatter.23.cloned.1.call-start = ((), (), s32[]{:S(2)}) async-start(), calls=%async_computation.18 | async-start | bytes 5242880 | tf_op jit(solution)/shard_map/while/body/eval_jaxpr/reduce_scatter | solution.py:34
  846.1 86.6 %all-gather.23.cloned.1.call-start = ((), (), s32[]{:S(2)}) async-start(), calls=%async_computation.19 | async-start | bytes 2621440 | tf_op jit(solution)/shard_map/while/body/eval_jaxpr/all_gather | solution.py:30
  908.9 82.4 %reduce-scatter.25.cloned.1.call-start = ((), (), s32[]{:S(2)}) async-start(), calls=%async_computation.20 | async-start | bytes 5242880 | tf_op jit(solution)/shard_map/while/body/eval_jaxpr/reduce_scatter | solution.py:34
  932.7 9.8 copy-start.48
  946.8 80.6 %all-gather.25.cloned.1.call-start = ((), (), s32[]{:S(2)}) async-start(), calls=%async_computation.21 | async-start | bytes 2621440 | tf_op jit(solution)/shard_map/while/body/eval_jaxpr/all_gather | solution.py:30
  1003.8 111.3 %reduce-scatter.27.cloned.1.call-start = ((), (), s32[]{:S(2)}) async-start(), calls=%async_computation.22 | async-start | bytes 5242880 | tf_op jit(solution)/shard_map/while/body/eval_jaxpr/reduce_scatter | solution.py:34
  1071.8 10.0 copy-start.28
  1071.9 10.0 copy-start.31
  1071.9 9.9 copy-start.34
  1073.2 8.7 copy-start.21
  1073.2 8.7 copy-start.18
  1073.2 8.7 copy-start.47
  1073.2 8.7 copy-start.52
  1085.0 11.4 copy-start.37
  1085.1 11.3 copy-start.40
  1085.1 11.3 copy-start.43
  1087.1 9.3 copy-start.24
  1090.8 24.3 %copy-start.5 = (f32[1024,256]{1,0:T(8,128)S(1)}, f32[1024,256]{1,0:T(8,128)}, u32[]{:S(2)}) copy-start(f32[1024,256]{1,0:T(8,128)} %copy-done.4) | copy-start | bytes 3145732 | tf_op jit(solution)/shard_map/while
  1119.9 67.1 %reduce-scatter.17.cloned.1.call-start = ((), (), s32[]{:S(2)}) async-start(), calls=%async_computation.10 | async-start | bytes 589824
  1122.3 132.7 %reduce-scatter.13.cloned.1.call-start = ((), (), s32[]{:S(2)}) async-start(), calls=%async_computation.8 | async-start | bytes 1769472 | tf_op jit(solution)/shard_map/reduce_scatter | solution.py:293
  1125.6 200.1 %reduce-scatter.19.cloned.1.call-start = ((), (), s32[]{:S(2)}) async-start(), calls=%async_computation.11 | async-start | bytes 2359296
  1133.5 263.2 %reduce-scatter.15.cloned.1.call-start = ((), (), s32[]{:S(2)}) async-start(), calls=%async_computation.9 | async-start | bytes 2359296 | tf_op jit(solution)/shard_map/reduce_scatter | solution.py:299
  (84 other events, 238.6 us)
Sparse Core Ops, SparseCore 0:
  16.1 49.0 all-gather.12
  67.4 21.1 all-gather.14
  117.6 44.3 reduce-scatter.20
  164.0 49.0 all-gather.16
  215.1 21.3 all-gather.18
  238.4 50.3 all-gather.20
  295.4 42.5 reduce-scatter.22
  358.2 23.5 all-gather.22
  396.1 44.3 reduce-scatter.24
  453.1 23.4 all-gather.24
  520.0 44.4 reduce-scatter.26
  569.7 46.2 all-gather.12
  618.2 21.1 all-gather.14
  668.4 44.4 reduce-scatter.20
  714.8 49.0 all-gather.16
  765.9 21.3 all-gather.18
  789.2 50.3 all-gather.20
  846.2 42.5 reduce-scatter.22
  909.0 23.5 all-gather.22
  946.9 44.3 reduce-scatter.24
  1003.9 23.4 all-gather.24
  1070.6 44.4 reduce-scatter.26
Sparse Core Ops, SparseCore 1:
  1124.3 62.6 reduce-scatter.16
  1190.3 64.6 reduce-scatter.12
  1258.4 67.3 reduce-scatter.18
  1329.3 67.3 reduce-scatter.14
where the time goes:
time: 1410 us
  waiting for transfers between devices  897 us (64%)
  matrix products  191 us (14%)
  blocking collectives  144 us (10%)
  other arithmetic  87 us (6%)
  local copies, waits for them, and re-layouts  45.9 us (3%)
  loops' own time  21 us (1%)
  between operations  16.2 us (1%)
    reduce_scatter x8, waiting for transfers between devices, fold_cols(): lax.psum_scatter(partial_terms, 'col', scatter_dimension=1, tiled=True)  302 us
    all_gather x8, waiting for transfers between devices, features(): return lax.all_gather(local_rows, 'col', axis=1, tiled=True)  187 us
    all_gather x4, waiting for transfers between devices, project_in(): lax.all_gather(weight, 'row', axis=0, tiled=True)  113 us
    unnamed x6, waiting for transfers between devices  81.4 us
    all_gather x2, waiting for transfers between devices, project_out(): lax.all_gather(weight, 'row', axis=1, tiled=True)  74.7 us
    reduce_scatter x1, waiting for transfers between devices, body(): lax.psum_scatter(big_acc[2].astype(jnp.bfloat16), 'row', scatter_dimensio...  69 us
    reduce_scatter x1, waiting for transfers between devices, body(): lax.psum_scatter(big_acc[0].astype(jnp.bfloat16), 'row', scatter_dimensio...  66.4 us
    all_gather x2, blocking collectives, project_out(): lax.all_gather(weight, 'row', axis=1, tiled=True)  60.7 us
  transfers between devices with their start and end apart: 26, of which 26 were waited for; matrix products, arithmetic and copies ran while one was open for 7% of the time, Pallas kernels for 0%

commit v1 on v0

v1 whole, which is shorter than its diff:
```python
import math

import jax
import jax.numpy as jnp
from jax import lax
from jax.sharding import PartitionSpec as P

DH = 64
NORM_EPS = 1e-06
MASKED = -1000000000.0
block_limit = 512
F32 = jnp.float32
BF16 = jnp.bfloat16


def nn(left, right):
    return lax.dot_general(left, right, (((1,), (0,)), ((), ())), preferred_element_type=F32)


def nt(left, right):
    return lax.dot_general(left, right, (((1,), (1,)), ((), ())), preferred_element_type=F32)


def tn(left, right):
    return lax.dot_general(left, right, (((0,), (0,)), ((), ())), preferred_element_type=F32)


def trade(block, axis, count, mask):
    return lax.ppermute(block, axis, [(i, i ^ mask) for i in range(count)])


def pick(block, bit, dim):
    return lax.dynamic_slice_in_dim(block, bit, 1, dim)


class Stage:
    def __init__(self, axis, count, mask, index, dim):
        self.axis, self.count, self.mask, self.dim = axis, count, mask, dim
        self.bit = (index // mask) % 2

    def trade(self, block):
        return trade(block, self.axis, self.count, self.mask)

    def join(self, mine, other, dim):
        low = self.bit == 0
        return jnp.concatenate(
            (jnp.where(low, mine, other), jnp.where(low, other, mine)), axis=dim
        )

    def gather(self, block):
        return self.join(block, self.trade(block), self.dim)

    def reduce(self, block):
        keep = pick(block, self.bit, self.dim)
        sent = pick(block, 1 - self.bit, self.dim)
        got = self.trade(sent)
        return (keep.astype(F32) + got.astype(F32)).astype(block.dtype)

    def swap(self, block, split, dim):
        keep = pick(block, self.bit, split)
        sent = pick(block, 1 - self.bit, split)
        return self.join(keep, self.trade(sent), dim)


def bits_of(count):
    return [1 << b for b in reversed(range(count.bit_length() - 1))]


def attend(queries, key_rows, value_rows, labels):
    length = queries.shape[0]
    block_rows = min(block_limit, length)
    score_scale = 1.0 / math.sqrt(queries.shape[1])

    def one_block(first_row):
        query_block = lax.dynamic_slice_in_dim(queries, first_row, block_rows, 0)
        label_block = lax.dynamic_slice_in_dim(labels, first_row, block_rows, 0)
        scores = nt(query_block, key_rows) * score_scale
        scores = jnp.where(label_block[:, None] == labels[None, :], scores, MASKED)
        row_max = jnp.max(scores, axis=1, keepdims=True)
        shifted = jnp.exp(scores - row_max)
        row_total = jnp.sum(shifted, axis=1, keepdims=True)
        probabilities = (shifted / row_total).astype(BF16)
        context = nn(probabilities, value_rows)
        return (context, (row_max + jnp.log(row_total))[:, 0])

    starts = jnp.arange(length // block_rows, dtype=jnp.int32) * block_rows
    context, log_total = lax.map(one_block, starts)
    return (context.reshape(length, -1), log_total.reshape(length))


def attend_back(queries, key_rows, value_rows, labels, log_total, grad_context):
    length = queries.shape[0]
    block_rows = min(block_limit, length)
    score_scale = 1.0 / math.sqrt(queries.shape[1])

    def one_block(state_pair, first_row):
        grad_keys, grad_values = state_pair
        query_block = lax.dynamic_slice_in_dim(queries, first_row, block_rows, 0)
        label_block = lax.dynamic_slice_in_dim(labels, first_row, block_rows, 0)
        total_block = lax.dynamic_slice_in_dim(log_total, first_row, block_rows, 0)
        grad_block = lax.dynamic_slice_in_dim(grad_context, first_row, block_rows, 0)
        scores = nt(query_block, key_rows) * score_scale
        scores = jnp.where(label_block[:, None] == labels[None, :], scores, MASKED)
        probabilities = jnp.exp(scores - total_block[:, None])
        grad_prob = nt(grad_block, value_rows)
        row_dot = jnp.sum(probabilities * grad_prob, axis=1, keepdims=True)
        dscore = (probabilities * (grad_prob - row_dot)).astype(BF16)
        grad_query = nn(dscore, key_rows) * score_scale
        grad_keys = grad_keys + tn(dscore, query_block) * score_scale
        grad_values = grad_values + tn(probabilities.astype(BF16), grad_block)
        return ((grad_keys, grad_values), grad_query)

    starts = jnp.arange(length // block_rows, dtype=jnp.int32) * block_rows
    zero_rows = jnp.zeros(key_rows.shape, F32)
    (grad_keys, grad_values), grad_query = lax.scan(one_block, (zero_rows, zero_rows), starts)
    return (grad_query.reshape(queries.shape), grad_keys, grad_values)


attend_heads = jax.vmap(attend, in_axes=(1, 1, 1, None), out_axes=1)
attend_heads_back = jax.vmap(attend_back, in_axes=(1, 1, 1, None, 1, 1), out_axes=1)


def body(
    rows,
    cols,
    tokens,
    segments,
    wqkv,
    bias_qv,
    wo,
    bias_o,
    gain_a,
    shift_a,
    w_in,
    bias_in,
    w_out,
    bias_out,
    gain_b,
    shift_b,
    cotangent,
):
    seqs, length = segments.shape
    ways = cols // seqs
    width = tokens.shape[1]
    model = width * cols
    heads = wqkv.shape[1] // (3 * DH)
    hid = w_in.shape[1]
    part = length // ways
    own_rows = wqkv.shape[0]
    row, col = lax.axis_index("row"), lax.axis_index("col")
    seq, way = col // ways, col % ways
    row_masks, seq_masks, way_masks = bits_of(rows), bits_of(seqs), bits_of(ways)
    ns, nw, nr = len(seq_masks), len(way_masks), len(row_masks)
    by_seq = [Stage("col", cols, mask * ways, col, i) for i, mask in enumerate(seq_masks)]
    by_way = [Stage("col", cols, mask, col, i) for i, mask in enumerate(way_masks)]
    by_row = [Stage("row", rows, mask, row, ns + i) for i, mask in enumerate(row_masks)]
    order_a = by_row + by_seq
    order_b = by_row[:-1] + by_seq + by_row[-1:]

    def gather_weight(shard):
        half = shard.shape[1] // 2
        parts = []
        for order, piece in ((order_a, shard[:, :half]), (order_b, shard[:, half:])):
            block = piece.reshape((1,) * (ns + nr) + piece.shape)
            for stage in order:
                block = stage.gather(block)
            parts.append(block.reshape(seqs, rows * own_rows, half))
        return jnp.concatenate(parts, axis=2)

    def scatter_weight(grads):
        whole = jnp.stack(grads, axis=0)
        half = whole.shape[2] // 2
        parts = []
        for order, piece in ((order_a, whole[:, :, :half]), (order_b, whole[:, :, half:])):
            block = piece.reshape((2,) * (ns + nr) + (own_rows, half))
            for stage in reversed(order):
                block = stage.reduce(block)
            parts.append(block.reshape(own_rows, half))
        return jnp.concatenate(parts, axis=1).astype(F32)

    def gather_ways(block):
        block = block.reshape((1,) * nw + block.shape)
        for stage in by_way:
            block = stage.gather(block)
        return block.reshape(length, model)

    def scatter_ways(partial_terms):
        block = partial_terms.reshape((2,) * nw + (part, model))
        for stage in by_way:
            keep = pick(block, stage.bit, stage.dim)
            sent = pick(block, 1 - stage.bit, stage.dim)
            got = stage.trade(sent.astype(BF16))
            block = keep + got.astype(F32)
        return block.reshape(part, model)

    small = jnp.concatenate(
        [v.reshape(-1, width) for v in (bias_o, gain_a, shift_a, bias_out, gain_b, shift_b, bias_qv, bias_in)]
    )
    small = small.reshape((1,) * (ns + nw) + small.shape)
    for stage in by_seq:
        small = stage.gather(small)
    for i, stage in enumerate(by_way):
        small = stage.join(small, stage.trade(small), ns + i)
    small = small.reshape(cols, -1, width).astype(F32)
    full = [small[:, i].reshape(1, model) for i in range(6)]
    bias_o32, gain_a32, shift_a32, bias_out32, gain_b32, shift_b32 = full
    mine = small.reshape(seqs, ways, -1, width)
    mine = lax.dynamic_slice_in_dim(mine, way, 1, 1)[:, 0]
    nq = bias_qv.shape[0] // width
    bias_qv_all = mine[:, 6 : 6 + nq].reshape(seqs, heads, 2, DH)
    bias_in_all = mine[:, 6 + nq :].reshape(seqs, 1, hid)

    def own_sequence(array):
        block = array.reshape((2,) * ns + (1,) * ns + (length, width))
        for i, stage in enumerate(by_seq):
            block = stage.swap(block, i, ns + i)
        return block.reshape((seqs, length, width))

    def own_part(array):
        block = own_sequence(array)
        block = block.reshape((seqs,) + (1,) * nw + (2,) * nw + (part, width))
        for i, stage in enumerate(by_way):
            block = stage.swap(block, 1 + nw + i, 1 + i)
        block = block.reshape(cols, part, width)
        return jnp.transpose(block, (1, 0, 2)).reshape(part, model)

    def back_to_features(array):
        block = array.reshape((part, seqs) + (2,) * nw + (width,))
        block = jnp.moveaxis(block, 0, -2).reshape((seqs,) + (2,) * nw + (1,) * nw + (part, width))
        for i, stage in enumerate(by_way):
            block = stage.swap(block, 1 + i, 1 + nw + i)
        block = block.reshape((2,) * ns + (1,) * ns + (length, width))
        for i, stage in enumerate(by_seq):
            block = stage.swap(block, i, ns + i)
        return block.reshape(seqs * length, width)

    labels = lax.dynamic_slice_in_dim(segments, seq, 1, 0)[0]

    tokens_x = own_sequence(tokens)
    block = tokens_x.reshape((seqs,) + (1,) * nw + (length, width))
    for i, stage in enumerate(by_way):
        block = stage.join(block, stage.trade(block), 1 + i)
    block = block.reshape(cols, length, width)
    whole_x = jnp.transpose(block, (1, 0, 2)).reshape(length, model)
    cot = own_part(cotangent).astype(F32)

    def by_kind(weight):
        n = weight.shape[0]
        return weight.reshape(n, heads, 3, DH).transpose(0, 2, 1, 3).reshape(n, -1)

    def by_head(weight):
        n = weight.shape[0]
        return weight.reshape(n, 3, heads, DH).transpose(0, 2, 1, 3).reshape(n, -1)

    qkv_all = gather_weight(by_kind(wqkv))
    wo_all = gather_weight(wo.T)
    in_all = gather_weight(w_in)
    out_all = gather_weight(w_out.T)

    queries, key_rows, value_rows = [], [], []
    for j in range(seqs):
        projected = nn(whole_x, qkv_all[j]).reshape(length, 3, heads, DH)
        queries.append((projected[:, 0] + bias_qv_all[j][:, 0]).astype(BF16))
        key_rows.append(projected[:, 1].astype(BF16))
        value_rows.append((projected[:, 2] + bias_qv_all[j][:, 1]).astype(BF16))
    queries = jnp.concatenate(queries, axis=1)
    key_rows = jnp.concatenate(key_rows, axis=1)
    value_rows = jnp.concatenate(value_rows, axis=1)
    context, log_total = attend_heads(queries, key_rows, value_rows, labels)
    context = context.astype(BF16).reshape(length, seqs, heads * DH)
    partial_a = sum(nt(context[:, j], wo_all[j]) for j in range(seqs))
    own_x = lax.dynamic_slice_in_dim(whole_x, way * part, part, 0)
    hidden_a = scatter_ways(partial_a) + own_x.astype(F32) + bias_o32

    def norm(hidden):
        mean = jnp.mean(hidden, axis=1, keepdims=True)
        square = jnp.mean(hidden * hidden, axis=1, keepdims=True)
        inv_std = lax.rsqrt(square - mean * mean + NORM_EPS)
        return (hidden - mean) * inv_std, inv_std

    def norm_back(incoming, centred, inv_std, gain):
        scaled = incoming * gain
        first = jnp.mean(scaled, axis=1, keepdims=True)
        second = jnp.mean(scaled * centred, axis=1, keepdims=True)
        return inv_std * (scaled - first - centred * second)

    centred_a, inv_std_a = norm(hidden_a)
    normed_a = centred_a * gain_a32 + shift_a32
    whole_y = gather_ways(normed_a.astype(BF16))
    gelu = lambda v: jax.nn.gelu(v, approximate=False)
    inner = [nn(whole_y, in_all[j]) + bias_in_all[j] for j in range(seqs)]
    active = [gelu(v).astype(BF16) for v in inner]
    partial_b = sum(nt(active[j], out_all[j]) for j in range(seqs))
    hidden_b = scatter_ways(partial_b) + bias_out32 + normed_a
    centred_b, inv_std_b = norm(hidden_b)
    output = back_to_features((centred_b * gain_b32 + shift_b32).astype(BF16))

    grad_b = norm_back(cot, centred_b, inv_std_b, gain_b32)
    whole_gb = gather_ways(grad_b.astype(BF16))
    grad_inner = [jax.vjp(gelu, inner[j])[1](nn(whole_gb, out_all[j]))[0] for j in range(seqs)]
    grad_inner_low = [v.astype(BF16) for v in grad_inner]
    partial_n = sum(nt(grad_inner_low[j], in_all[j]) for j in range(seqs))
    grad_w_out = scatter_weight([tn(whole_gb, active[j]).astype(BF16) for j in range(seqs)])
    grad_w_in = scatter_weight([tn(whole_y, grad_inner_low[j]).astype(BF16) for j in range(seqs)])
    grad_normed = scatter_ways(partial_n) + grad_b
    grad_a = norm_back(grad_normed, centred_a, inv_std_a, gain_a32)
    whole_ga = gather_ways(grad_a.astype(BF16))
    grad_context = [nn(whole_ga, wo_all[j]).astype(BF16) for j in range(seqs)]
    grad_wo = scatter_weight([tn(whole_ga, context[:, j]).astype(BF16) for j in range(seqs)])
    grad_context = jnp.concatenate(grad_context, axis=1).reshape(length, seqs * heads, DH)
    grad_q, grad_k, grad_v = attend_heads_back(
        queries, key_rows, value_rows, labels, log_total, grad_context
    )
    split = lambda v: v.reshape(length, seqs, heads * DH)
    grad_q, grad_k, grad_v = split(grad_q), split(grad_k), split(grad_v)
    grad_projected = [
        jnp.concatenate((grad_q[:, j], grad_k[:, j], grad_v[:, j]), axis=1).astype(BF16)
        for j in range(seqs)
    ]
    partial_x = sum(nt(grad_projected[j], qkv_all[j]) for j in range(seqs))
    grad_wqkv = scatter_weight([tn(whole_x, grad_projected[j]).astype(BF16) for j in range(seqs)])
    grad_tokens = back_to_features((scatter_ways(partial_x) + grad_a).astype(BF16)).astype(F32)

    per_hidden = jnp.stack(
        [
            jnp.concatenate(
                (
                    jnp.stack(
                        (
                            jnp.sum(grad_q[:, j], axis=0).reshape(heads, DH),
                            jnp.sum(grad_v[:, j], axis=0).reshape(heads, DH),
                        ),
                        axis=1,
                    ).reshape(-1),
                    jnp.sum(grad_inner[j], axis=0),
                )
            )
            for j in range(seqs)
        ]
    )
    per_feature = jnp.stack(
        [
            jnp.sum(v, axis=0)
            for v in (
                grad_a,
                grad_normed * centred_a,
                grad_normed,
                grad_b,
                cot * centred_b,
                cot,
            )
        ]
    )
    block = per_feature.reshape((6, seqs) + (2,) * nw + (width,))
    for i, stage in enumerate(by_way):
        keep = pick(block, stage.bit, 2 + i)
        sent = pick(block, 1 - stage.bit, 2 + i)
        block = keep + stage.trade(sent)
    block = block.reshape(6, seqs, width).transpose(1, 0, 2).reshape(seqs, 6 * width)
    block = jnp.concatenate((per_hidden, block), axis=1).reshape((2,) * ns + (-1,))
    for stage in by_seq:
        block = stage.reduce(block)
    sums = lax.psum(block.reshape(-1), "row")
    nqv = bias_qv.shape[0]
    sum_qv, sum_in = sums[:nqv], sums[nqv : nqv + hid]
    rest = sums[nqv + hid :].reshape(6, width)
    return (
        output,
        grad_tokens,
        by_head(grad_wqkv),
        sum_qv,
        grad_wo.T,
        rest[0],
        rest[1],
        rest[2],
        grad_w_in,
        sum_in,
        grad_w_out.T,
        rest[3],
        rest[4],
        rest[5],
    )


def solution(mesh):
    tile, across, down, flat = P("row", "col"), P("row", None), P("col", "row"), P("col")
    in_specs = (tile, across, tile, flat, down, flat, flat, flat, tile, flat, down, flat, flat, flat, tile)
    out_specs = (tile, tile, tile, flat, down, flat, flat, flat, tile, flat, down, flat, flat, flat)
    rows, cols = mesh.shape["row"], mesh.shape["col"]

    def layer(*args):
        return body(rows, cols, *args)

    return jax.shard_map(layer, mesh=mesh, in_specs=in_specs, out_specs=out_specs, check_vma=False)
```

time: 1410 us -> 740 us (0.52)
  waiting for transfers between devices: 897 us -> 217 us
  blocking collectives: 144 us -> 34.5 us
  starting transfers between devices: 2.97 us -> 78.8 us
  local copies, waits for them, and re-layouts: 45.9 us -> 95.7 us
  other arithmetic: 87 us -> 110 us
    reduce_scatter x10 -> x0, waiting for transfers between devices: 438 us -> none  [the longest x8 302 us: fold_cols(): lax.psum_scatter(partial_terms, 'col', scatter_dimension=1, tiled=True)]
    all_gather x14 -> x0, waiting for transfers between devices: 375 us -> none  [the longest x8 187 us: features(): return lax.all_gather(local_rows, 'col', axis=1, tiled=True)]
    ppermute x0 -> x83, waiting for transfers between devices: none -> 217 us  [trade(): return lax.ppermute(block, axis, [(i, i ^ mask) for i in range(count)])]
    unnamed x6 -> x0, waiting for transfers between devices: 81.4 us -> none
    ppermute x0 -> x83, starting transfers between devices: none -> 78.8 us  [trade(): return lax.ppermute(block, axis, [(i, i ^ mask) for i in range(count)])]
    all_gather x2 -> x0, blocking collectives: 60.7 us -> none  [project_out(): lax.all_gather(weight, 'row', axis=1, tiled=True)]
    psum x9 -> x1, blocking collectives: 83.7 us -> 34.5 us  [body(): sums = lax.psum(block.reshape(-1), 'row')]
    unnamed x20 -> x240, local copies, waits for them, and re-layouts: 7.07 us -> 35 us
  transfers between devices with their start and end apart: 26 -> 83, of which waited for: 26 -> 40; matrix products, arithmetic and copies ran while one was open for 7% -> 27% of each run, Pallas kernels for 0% -> 0%
where the time goes in v1:
time: 740 us; the launch traced here: 732 us
  waiting for transfers between devices  217 us (29%)
  matrix products  184 us (25%)
  other arithmetic  110 us (15%)
  local copies, waits for them, and re-layouts  95.7 us (13%)
  starting transfers between devices  78.8 us (11%)
  blocking collectives  34.5 us (5%)
  loops' own time  9.01 us (1%)
    ppermute x83, waiting for transfers between devices, trade(): return lax.ppermute(block, axis, [(i, i ^ mask) for i in range(count)])  217 us
    ppermute x83, starting transfers between devices, trade(): return lax.ppermute(block, axis, [(i, i ^ mask) for i in range(count)])  78.8 us
    dot_general x14, matrix products, nt(): lax.dot_general(left, right, (((1,), (1,)), ((), ())), preferred_element_...  78.2 us
    dot_general x12, matrix products, nn(): lax.dot_general(left, right, (((1,), (0,)), ((), ())), preferred_element_...  66.9 us
    dot_general x12, matrix products, tn(): lax.dot_general(left, right, (((0,), (0,)), ((), ())), preferred_element_...  38.7 us
    unnamed x240, local copies, waits for them, and re-layouts  35 us
    psum x1, blocking collectives, body(): sums = lax.psum(block.reshape(-1), 'row')  34.5 us
    convert_element_type x2, other arithmetic, one_block(): dscore = (probabilities * (grad_prob - row_dot)).astype(BF16)  23 us
  transfers between devices with their start and end apart: 83, of which 40 were waited for; matrix products, arithmetic and copies ran while one was open for 27% of the time, Pallas kernels for 0%

profile of v1, /device:TPU:0, one launch (start us, length us, event | category | flops | bytes accessed | tf_op | source)
XLA Modules:
  0.0 732.2 jit_solution(3615620399226448178)
XLA Ops:
  42.4 5.9 collective-permute-done.34
  52.6 12.4 %collective-permute-done.18 = bf16[1,2,2,1,128,128]{5,4,3,2,1,0:T(8,128)(2,1)S(1)} collective-permute-done((bf16[1,2,2,1,128,128]{5,4,3,2,1,0:T(8,128)(2,1)S(1)}, bf16[1,2,2,1,128,128]{5,4,3,2,1,0:T(8,128)(2,1)S(1)}, u32[]{:S(2)}, u32[]{:S(2)}) %collective-permute-start.18) | collective-permute-done | bytes 131104 | tf_op jit(solution)/shard_map/ppermute | solution.py:29
  68.7 4.1 collective-permute-done.7
  74.3 4.2 collective-permute-done.27
  79.8 8.7 %collective-permute-done.31 = bf16[1,2,1,1,128,512]{5,4,3,2,1,0:T(8,128)(2,1)S(1)} collective-permute-done((bf16[1,2,1,1,128,512]{5,4,3,2,1,0:T(8,128)(2,1)S(1)}, bf16[1,2,1,1,128,512]{5,4,3,2,1,0:T(8,128)(2,1)S(1)}, u32[]{:S(2)}, u32[]{:S(2)}) %collective-permute-start.31) | collective-permute-done | bytes 262176 | tf_op jit(solution)/shard_map/ppermute | solution.py:29
  93.0 4.6 collective-permute-done.15
  112.4 8.4 %collective-permute-done.28 = bf16[1,2,2,1,128,512]{5,4,3,2,1,0:T(8,128)(2,1)S(1)} collective-permute-done((bf16[1,2,2,1,128,512]{5,4,3,2,1,0:T(8,128)(2,1)S(1)}, bf16[1,2,2,1,128,512]{5,4,3,2,1,0:T(8,128)(2,1)S(1)}, u32[]{:S(2)}, u32[]{:S(2)}) %collective-permute-start.28) | collective-permute-done | bytes 524320 | tf_op jit(solution)/shard_map/ppermute | solution.py:29
  121.1 10.9 %collective-permute-done.36 = bf16[1,2,2,1,128,512]{5,4,3,2,1,0:T(8,128)(2,1)S(1)} collective-permute-done((bf16[1,2,2,1,128,512]{5,4,3,2,1,0:T(8,128)(2,1)S(1)}, bf16[1,2,2,1,128,512]{5,4,3,2,1,0:T(8,128)(2,1)S(1)}, u32[]{:S(2)}, u32[]{:S(2)}) %collective-permute-start.36) | collective-permute-done | bytes 524320 | tf_op jit(solution)/shard_map/ppermute | solution.py:29
  137.3 4.7 collective-permute-done.5
  143.9 4.1 collective-permute-done.9
  164.8 4.0 fusion.49
  175.0 39.2 %while.33 = (s32[]{:T(128)}, bf16[2,8,512,64]{2,3,1,0:T(8,128)(2,1)S(1)}, f32[2,8,512]{2,1,0:T(8,128)}, s32[2]{0:T(128)S(1)}, s32[1024]{0:T(1024)S(1)}, /*index=...) while((s32[]{:T(128)}, ...), condition=%wide.region_3.4_spmd.clone, body=%wide.region_0.3_spmd.sunk.clone | while | flops 1124593664 | bytes 56240312 | solution.py:87
  178.6 5.1 fusion.210
  183.7 4.4 fusion.211
  188.0 6.2 fusion.212
  197.9 5.0 fusion.210
  203.0 4.4 fusion.211
  207.4 6.2 fusion.212
  226.8 17.9 %collective-permute-done.25 = bf16[1,2,2,2,128,512]{5,4,3,2,1,0:T(8,128)(2,1)S(1)} collective-permute-done((bf16[1,2,2,2,128,512]{5,4,3,2,1,0:T(8,128)(2,1)S(1)}, bf16[1,2,2,2,128,512]{5,4,3,2,1,0:T(8,128)(2,1)S(1)}, u32[]{:S(2)}, u32[]{:S(2)}) %collective-permute-start.25) | collective-permute-done | bytes 1048608 | tf_op jit(solution)/shard_map/ppermute | solution.py:29
  244.8 21.1 %collective-permute-done.33 = bf16[1,2,2,2,128,512]{5,4,3,2,1,0:T(8,128)(2,1)S(1)} collective-permute-done((bf16[1,2,2,2,128,512]{5,4,3,2,1,0:T(8,128)(2,1)S(1)}, bf16[1,2,2,2,128,512]{5,4,3,2,1,0:T(8,128)(2,1)S(1)}, u32[]{:S(2)}, u32[]{:S(2)}) %collective-permute-start.33) | collective-permute-done | bytes 1048608 | tf_op jit(solution)/shard_map/ppermute | solution.py:29
  268.0 12.8 %multiply_convert_fusion.1 = (bf16[1024,1024]{1,0:T(8,128)(2,1)S(1)}, f32[1024,1024]{1,0:T(8,128)}, f32[1024,1024]{1,0:T(8,128)}) fusion(f32[1024]{0:T(1024)S(1)} %bitcast.636, bf16[1024,1024]{1,0:T(8,128)(2,1)S(1)} %bitcast.571, bf16[2,1024,512]{2,1,0:T(8,128)(2,1)S(1)} %bitcast.555, bf16[2,1024,512]{2,1,0:T(8,128)(2,1)S(1)} %bitcast.563), kind=kOutput, calls=%fused_computation.52 | convolution fusion | flops 2220883968 | bytes 16781312 | tf_op jit(solution)/shard_map/dot_general | solution.py:17
  280.8 12.8 %multiply_convert_fusion.2 = (bf16[1024,1024]{1,0:T(8,128)(2,1)S(1)}, f32[1024,1024]{1,0:T(8,128)}, f32[1024,1024]{1,0:T(8,128)}) fusion(f32[1024]{0:T(1024)S(1)} %bitcast.634, bf16[1024,1024]{1,0:T(8,128)(2,1)S(1)} %bitcast.572, bf16[2,1024,512]{2,1,0:T(8,128)(2,1)S(1)} %bitcast.564, bf16[2,1024,512]{2,1,0:T(8,128)(2,1)S(1)} %bitcast.556), kind=kOutput, calls=%fused_computation.65 | convolution fusion | flops 2220883968 | bytes 16781312 | tf_op jit(solution)/shard_map/dot_general | solution.py:17
  314.5 13.5 %collective-permute-done.40 = bf16[1,1,1024,256]{3,2,1,0:T(8,128)(2,1)} collective-permute-done((bf16[1,1,1024,256]{3,2,1,0:T(8,128)(2,1)}, bf16[1,1,1024,256]{3,2,1,0:T(8,128)(2,1)}, u32[]{:S(2)}, u32[]{:S(2)}) %collective-permute-start.40) | collective-permute-done | bytes 524320 | tf_op jit(solution)/shard_map/ppermute | solution.py:29
  341.0 4.7 fusion.143
  349.5 4.3 fusion.73
  368.5 9.0 %fusion.144 = (f32[1024]{0:T(1024)}, bf16[1024,1024]{1,0:T(8,128)(2,1)S(1)}) fusion(f32[1024,1024]{1,0:T(8,128)} %get-tuple-element.321, bf16[1024,1024]{1,0:T(8,128)(2,1)} %bitcast.578, bf16[2,1024,512]{2,1,0:T(8,128)(2,1)} %bitcast.569, bf16[2,1024,512]{2,1,0:T(8,128)(2,1)} %bitcast.561, f32[1024,1024]{1,0:T(8,128)} %get-tuple-element.495, ...), kind=kOutput, calls=%fused_computation.506 | convolution fusion | flops 2168454144 | bytes 16785408 | tf_op jit(solution)/shard_map/dot_general | solution.py:17
  386.9 7.1 collective-permute-done.79
  397.2 19.2 %collective-permute-done.67 = bf16[1,2,2,2,128,512]{5,4,3,2,1,0:T(8,128)(2,1)S(1)} collective-permute-done((bf16[1,2,2,2,128,512]{5,4,3,2,1,0:T(8,128)(2,1)S(1)}, bf16[1,2,2,2,128,512]{5,4,3,2,1,0:T(8,128)(2,1)S(1)}, u32[]{:S(2)}, u32[]{:S(2)}) %collective-permute-start.67) | collective-permute-done | bytes 1048608 | tf_op jit(solution)/shard_map/ppermute | solution.py:29
  445.1 5.2 collective-permute-done.77
  452.4 6.3 collective-permute-done.69
  465.4 8.8 %collective-permute-done.70 = bf16[1,1,1,1,128,512]{5,4,3,2,1,0:T(8,128)(2,1)S(1)} collective-permute-done((bf16[1,1,1,1,128,512]{5,4,3,2,1,0:T(8,128)(2,1)S(1)}, bf16[1,1,1,1,128,512]{5,4,3,2,1,0:T(8,128)(2,1)S(1)}, u32[]{:S(2)}, u32[]{:S(2)}) %collective-permute-start.70) | collective-permute-done | bytes 131104 | tf_op jit(solution)/shard_map/ppermute | solution.py:29
  484.8 112.6 %while.34 = (s32[]{:T(128)}, f32[8,1024,64]{1,2,0:T(8,128)}, f32[8,1024,64]{1,2,0:T(8,128)}, f32[2,8,512,64]{2,3,1,0:T(8,128)}, s32[2]{0:T(128)S(1)}, /*index=5*...) while((s32[]{:T(128)}, f32[8,1024,64]{1,2,0:T(8,128)}, ...), condition=%wide.region_14.15_spmd.clone.clone, body=%wide.region_12.14_spmd.clone.sunk.clone | while | flops 2725507072 | bytes 225536304 | solution.py:115
  488.1 9.7 %fusion.222 = f32[8,512,1024]{2,1,0:T(8,128)} fusion(bf16[8,1024,64]{1,2,0:T(8,128)(2,1)} %get-tuple-element.775, bf16[8,1024,64]{1,2,0:T(8,128)(2,1)} %get-tuple-element.774, s32[]{:T(128)S(1)} %bitcast.608), kind=kOutput, calls=%fused_computation.27.clone.1.clone | convolution fusion | flops 536870912 | bytes 18350084 | tf_op jit(solution)/shard_map/vmap()/while/body/eval_jaxpr/dot_general | solution.py:21
  497.8 13.4 %multiply_reduce_fusion.10 = (f32[8,512]{1,0:T(8,128)S(1)}, f32[8,512,1024]{2,1,0:T(8,128)}) fusion(f32[8,512,1024]{2,1,0:T(8,128)} %fusion.222, f32[8,512]{1,0:T(8,128)S(1)} %constant_dynamic-slice_fusion.55, bf16[8,1024,64]{1,2,0:T(8,128)(2,1)} %get-tuple-element.772, bf16[8,1024,64]{1,2,0:T(8,128)(2,1)} %get-tuple-element.771, ...), kind=kOutput, calls=%fused_computation.17.clone.1.clone | convolution fusion | flops 557838336 | bytes 35684356 | tf_op jit(solution)/shard_map/vmap()/while/body/eval_jaxpr/dot_general | solution.py:21
  511.2 11.5 %multiply_convert_fusion.5 = bf16[8,512,1024]{2,1,0:T(8,128)(2,1)S(1)} fusion(f32[8,512,1024]{2,1,0:T(8,128)} %get-tuple-element.689, f32[8,512,1024]{2,1,0:T(8,128)} %fusion.222, f32[8,512]{1,0:T(8,128)S(1)} %get-tuple-element.690), kind=kLoop, calls=%fused_computation.16.clone.1.clone | loop fusion | flops 12582912 | bytes 41959424 | tf_op jit(solution)/shard_map/vmap()/while/body/eval_jaxpr/convert_element_type | solution.py:107
  522.7 3.9 copy-done.2
  526.6 4.1 select_add_fusion.7
  530.7 4.3 select_add_fusion.6
  543.4 9.7 %fusion.222 = f32[8,512,1024]{2,1,0:T(8,128)} fusion(bf16[8,1024,64]{1,2,0:T(8,128)(2,1)} %get-tuple-element.775, bf16[8,1024,64]{1,2,0:T(8,128)(2,1)} %get-tuple-element.774, s32[]{:T(128)S(1)} %bitcast.608), kind=kOutput, calls=%fused_computation.27.clone.1.clone | convolution fusion | flops 536870912 | bytes 18350084 | tf_op jit(solution)/shard_map/vmap()/while/body/eval_jaxpr/dot_general | solution.py:21
  553.1 13.4 %multiply_reduce_fusion.10 = (f32[8,512]{1,0:T(8,128)S(1)}, f32[8,512,1024]{2,1,0:T(8,128)}) fusion(f32[8,512,1024]{2,1,0:T(8,128)} %fusion.222, f32[8,512]{1,0:T(8,128)S(1)} %constant_dynamic-slice_fusion.55, bf16[8,1024,64]{1,2,0:T(8,128)(2,1)} %get-tuple-element.772, bf16[8,1024,64]{1,2,0:T(8,128)(2,1)} %get-tuple-element.771, ...), kind=kOutput, calls=%fused_computation.17.clone.1.clone | convolution fusion | flops 557838336 | bytes 35684356 | tf_op jit(solution)/shard_map/vmap()/while/body/eval_jaxpr/dot_general | solution.py:21
  566.5 11.5 %multiply_convert_fusion.5 = bf16[8,512,1024]{2,1,0:T(8,128)(2,1)S(1)} fusion(f32[8,512,1024]{2,1,0:T(8,128)} %get-tuple-element.689, f32[8,512,1024]{2,1,0:T(8,128)} %fusion.222, f32[8,512]{1,0:T(8,128)S(1)} %get-tuple-element.690), kind=kLoop, calls=%fused_computation.16.clone.1.clone | loop fusion | flops 12582912 | bytes 41959424 | tf_op jit(solution)/shard_map/vmap()/while/body/eval_jaxpr/convert_element_type | solution.py:107
  578.0 3.9 copy-done.2
  581.9 4.8 select_add_fusion.7
  586.7 5.0 select_add_fusion.6
  628.7 5.1 convolution_add_fusion.1
  637.0 34.5 %psum.7 = f32[3072]{0:T(1024)S(1)} all-reduce(f32[3072]{0:T(1024)S(1)} %bitcast.623), channel_id=1, replica_groups=mesh['row'=8,'col'=4] {'row'}, use_global_device_ids=true, to_apply=%region_27.28 | all-reduce | flops 3072 | bytes 24576 | tf_op jit(solution)/shard_map/psum | solution.py:363
  715.9 4.3 collective-permute-done.56
  723.0 7.2 collective-permute-done.48
  (704 shorter events, 327.4 us)
Async XLA Ops:
  6.1 15.6 %collective-permute-start.10 = (bf16[1,1,12,256]{3,2,1,0:T(8,128)(2,1)S(1)}, bf16[1,1,12,256]{3,2,1,0:T(8,128)(2,1)S(1)}, u32[]{:S(2)}, u32[]{:S(2)}) collective-permute-start(bf16[1,1,12,256]{3,2,1,0:T(8,128)(2,1)S(1)} %bitcast.624), channel_id=1, source_target_pairs={{0,2},{1,3},{2,0},{3,1},{4,6},{5,7},{6,4},{7,5},{8,10},{9,11},{10,... | collective-permute-start | bytes 18440 | tf_op jit(solution)/shard_map/ppermute | solution.py:29
  10.7 16.4 %collective-permute-start.16 = (bf16[1,1,1,1,128,128]{5,4,3,2,1,0:T(8,128)(2,1)}, bf16[1,1,1,1,128,128]{5,4,3,2,1,0:T(8,128)(2,1)}, u32[]{:S(2)}, u32[]{:S(2)}) collective-permute-start(bf16[1,1,1,1,128,128]{5,4,3,2,1,0:T(8,128)(2,1)} %get-tuple-element.470), channel_id=1, source_target_pairs={{0,16},{4,20},{8,24},{12,28},{16,0},{20,4},{24,8},{28,12},{1,17},{... | collective-permute-start | bytes 98312 | tf_op jit(solution)/shard_map/ppermute | solution.py:29
  14.9 22.1 %collective-permute-start.6 = (bf16[1,1,1,1,128,384]{5,4,3,2,1,0:T(8,128)(2,1)S(1)}, bf16[1,1,1,1,128,384]{5,4,3,2,1,0:T(8,128)(2,1)}, u32[]{:S(2)}, u32[]{:S(2)}) collective-permute-start(bf16[1,1,1,1,128,384]{5,4,3,2,1,0:T(8,128)(2,1)S(1)} %bitcast.604), channel_id=1, source_target_pairs={{0,16},{4,20},{8,24},{12,28},{16,0},{20,4},{24,8},{28,12},{1,17},{... | collective-permute-start | bytes 294920 | tf_op jit(solution)/shard_map/ppermute | solution.py:29
  17.7 21.5 %collective-permute-start.2 = (bf16[1,1,1,1,128,384]{5,4,3,2,1,0:T(8,128)(2,1)S(1)}, bf16[1,1,1,1,128,384]{5,4,3,2,1,0:T(8,128)(2,1)}, u32[]{:S(2)}, u32[]{:S(2)}) collective-permute-start(bf16[1,1,1,1,128,384]{5,4,3,2,1,0:T(8,128)(2,1)S(1)} %bitcast.605), channel_id=1, source_target_pairs={{0,16},{4,20},{8,24},{12,28},{16,0},{20,4},{24,8},{28,12},{1,17},{... | collective-permute-start | bytes 294920 | tf_op jit(solution)/shard_map/ppermute | solution.py:29
  23.0 17.8 %collective-permute-start.30 = (bf16[1,1,1,1,128,512]{5,4,3,2,1,0:T(8,128)(2,1)}, bf16[1,1,1,1,128,512]{5,4,3,2,1,0:T(8,128)(2,1)}, u32[]{:S(2)}, u32[]{:S(2)}) collective-permute-start(bf16[1,1,1,1,128,512]{5,4,3,2,1,0:T(8,128)(2,1)} %get-tuple-element.438), channel_id=1, source_target_pairs={{0,16},{4,20},{8,24},{12,28},{16,0},{20,4},{24,8},{28,12},{1,17},{... | collective-permute-start | bytes 393224 | tf_op jit(solution)/shard_map/ppermute | solution.py:29
  37.0 15.5 %collective-permute-start.26 = (bf16[1,1,1,1,128,512]{5,4,3,2,1,0:T(8,128)(2,1)S(1)}, bf16[1,1,1,1,128,512]{5,4,3,2,1,0:T(8,128)(2,1)S(1)}, u32[]{:S(2)}, u32[]{:S(2)}) collective-permute-start(bf16[1,1,1,1,128,512]{5,4,3,2,1,0:T(8,128)(2,1)S(1)} %get-tuple-element.443), channel_id=1, source_target_pairs={{0,16},{4,20},{8,24},{12,28},{16,0},{20,4},{24,8},{28,12},{1,17},{... | collective-permute-start | bytes 393224 | tf_op jit(solution)/shard_map/ppermute | solution.py:29
  39.2 62.9 %collective-permute-start.41 = (bf16[1,1,1024,256]{3,2,1,0:T(8,128)(2,1)}, bf16[1,1,1024,256]{3,2,1,0:T(8,128)(2,1)S(1)}, u32[]{:S(2)}, u32[]{:S(2)}) collective-permute-start(bf16[1,1,1024,256]{3,2,1,0:T(8,128)(2,1)} %constant_dynamic-slice_fusion.46), channel_id=1, source_target_pairs={{0,2},{1,3},{2,0},{3,1},{4,6},{5,7},{6,4},{7,5},{8,10},{9,11},{10,... | collective-permute-start | bytes 1572872 | tf_op jit(solution)/shard_map/ppermute | solution.py:29
  40.8 63.2 %collective-permute-start = (bf16[1,1,1024,256]{3,2,1,0:T(8,128)(2,1)}, bf16[1,1,1024,256]{3,2,1,0:T(8,128)(2,1)S(1)}, u32[]{:S(2)}, u32[]{:S(2)}) collective-permute-start(bf16[1,1,1024,256]{3,2,1,0:T(8,128)(2,1)} %constant_dynamic-slice_fusion.51), channel_id=1, source_target_pairs={{0,2},{1,3},{2,0},{3,1},{4,6},{5,7},{6,4},{7,5},{8,10},{9,11},{10,... | collective-permute-start | bytes 1572872 | tf_op jit(solution)/shard_map/ppermute | solution.py:29
  48.3 18.1 %collective-permute-start.14 = (bf16[1,2,2,1,128,128]{5,4,3,2,1,0:T(8,128)(2,1)S(1)}, bf16[1,2,2,1,128,128]{5,4,3,2,1,0:T(8,128)(2,1)S(1)}, u32[]{:S(2)}, u32[]{:S(2)}) collective-permute-start(bf16[1,2,2,1,128,128]{5,4,3,2,1,0:T(8,128)(2,1)S(1)} %pad_maximum_fusion.53), channel_id=1, source_target_pairs={{0,4},{4,0},{8,12},{12,8},{16,20},{20,16},{24,28},{28,24},{1,5},{5... | collective-permute-start | bytes 393224 | tf_op jit(solution)/shard_map/ppermute | solution.py:29
  67.3 22.4 %collective-permute-start.23 = (bf16[1,2,1,1,128,512]{5,4,3,2,1,0:T(8,128)(2,1)S(1)}, bf16[1,2,1,1,128,512]{5,4,3,2,1,0:T(8,128)(2,1)S(1)}, u32[]{:S(2)}, u32[]{:S(2)}) collective-permute-start(bf16[1,2,1,1,128,512]{5,4,3,2,1,0:T(8,128)(2,1)S(1)} %pad_maximum_fusion.46), channel_id=1, source_target_pairs={{0,8},{4,12},{8,0},{12,4},{16,24},{20,28},{24,16},{28,20},{1,9},{5... | collective-permute-start | bytes 786440 | tf_op jit(solution)/shard_map/ppermute | solution.py:29
  72.8 15.6 %collective-permute-start.31 = (bf16[1,2,1,1,128,512]{5,4,3,2,1,0:T(8,128)(2,1)S(1)}, bf16[1,2,1,1,128,512]{5,4,3,2,1,0:T(8,128)(2,1)S(1)}, u32[]{:S(2)}, u32[]{:S(2)}) collective-permute-start(bf16[1,2,1,1,128,512]{5,4,3,2,1,0:T(8,128)(2,1)S(1)} %pad_maximum_fusion.48), channel_id=1, source_target_pairs={{0,8},{4,12},{8,0},{12,4},{16,24},{20,28},{24,16},{28,20},{1,9},{5... | collective-permute-start | bytes 786440 | tf_op jit(solution)/shard_map/ppermute | solution.py:29
  91.5 20.7 %collective-permute-start.4 = (bf16[1,2,2,1,128,384]{5,4,3,2,1,0:T(8,128)(2,1)S(1)}, bf16[1,2,2,1,128,384]{5,4,3,2,1,0:T(8,128)(2,1)S(1)}, u32[]{:S(2)}, u32[]{:S(2)}) collective-permute-start(bf16[1,2,2,1,128,384]{5,4,3,2,1,0:T(8,128)(2,1)S(1)} %pad_maximum_fusion.42), channel_id=1, source_target_pairs={{0,4},{4,0},{8,12},{12,8},{16,20},{20,16},{24,28},{28,24},{1,5},{5... | collective-permute-start | bytes 1179656 | tf_op jit(solution)/shard_map/ppermute | solution.py:29
  98.9 21.9 %collective-permute-start.28 = (bf16[1,2,2,1,128,512]{5,4,3,2,1,0:T(8,128)(2,1)S(1)}, bf16[1,2,2,1,128,512]{5,4,3,2,1,0:T(8,128)(2,1)S(1)}, u32[]{:S(2)}, u32[]{:S(2)}) collective-permute-start(bf16[1,2,2,1,128,512]{5,4,3,2,1,0:T(8,128)(2,1)S(1)} %pad_maximum_fusion.39), channel_id=1, source_target_pairs={{0,2},{1,3},{2,0},{3,1},{4,6},{5,7},{6,4},{7,5},{8,10},{9,11},{10,... | collective-permute-start | bytes 1572872 | tf_op jit(solution)/shard_map/ppermute | solution.py:29
  102.0 34.0 %collective-permute-start.24 = (bf16[1,2,2,1,128,512]{5,4,3,2,1,0:T(8,128)(2,1)S(1)}, bf16[1,2,2,1,128,512]{5,4,3,2,1,0:T(8,128)(2,1)S(1)}, u32[]{:S(2)}, u32[]{:S(2)}) collective-permute-start(bf16[1,2,2,1,128,512]{5,4,3,2,1,0:T(8,128)(2,1)S(1)} %pad_maximum_fusion.38), channel_id=1, source_target_pairs={{0,4},{4,0},{8,12},{12,8},{16,20},{20,16},{24,28},{28,24},{1,5},{5... | collective-permute-start | bytes 1572872 | tf_op jit(solution)/shard_map/ppermute | solution.py:29
  104.0 28.1 %collective-permute-start.36 = (bf16[1,2,2,1,128,512]{5,4,3,2,1,0:T(8,128)(2,1)S(1)}, bf16[1,2,2,1,128,512]{5,4,3,2,1,0:T(8,128)(2,1)S(1)}, u32[]{:S(2)}, u32[]{:S(2)}) collective-permute-start(bf16[1,2,2,1,128,512]{5,4,3,2,1,0:T(8,128)(2,1)S(1)} %pad_maximum_fusion.41), channel_id=1, source_target_pairs={{0,2},{1,3},{2,0},{3,1},{4,6},{5,7},{6,4},{7,5},{8,10},{9,11},{10,... | collective-permute-start | bytes 1572872 | tf_op jit(solution)/shard_map/ppermute | solution.py:29
  109.6 109.1 %collective-permute-start.32 = (bf16[1,2,2,1,128,512]{5,4,3,2,1,0:T(8,128)(2,1)}, bf16[1,2,2,1,128,512]{5,4,3,2,1,0:T(8,128)(2,1)}, u32[]{:S(2)}, u32[]{:S(2)}) collective-permute-start(bf16[1,2,2,1,128,512]{5,4,3,2,1,0:T(8,128)(2,1)} %pad_maximum_fusion.40), channel_id=1, source_target_pairs={{0,4},{4,0},{8,12},{12,8},{16,20},{20,16},{24,28},{28,24},{1,5},{5... | collective-permute-start | bytes 1572872 | tf_op jit(solution)/shard_map/ppermute | solution.py:29
  112.2 186.9 %collective-permute-start.42 = (bf16[2,1,1,512,256]{4,3,2,0,1:T(8,128)(2,1)}, bf16[2,1,1,512,256]{4,3,2,0,1:T(8,128)(2,1)}, u32[]{:S(2)}, u32[]{:S(2)}) collective-permute-start(bf16[2,1,1,512,256]{4,3,2,0,1:T(8,128)(2,1)} %constant_dynamic-slice_fusion.45), channel_id=1, source_target_pairs={{0,1},{1,0},{2,3},{3,2},{4,5},{5,4},{6,7},{7,6},{8,9},{9,8},{10,11... | collective-permute-start | bytes 1572872 | tf_op jit(solution)/shard_map/ppermute | solution.py:29
  120.8 21.2 %collective-permute-start.5 = (bf16[1,2,2,2,128,384]{5,4,3,2,1,0:T(8,128)(2,1)S(1)}, bf16[1,2,2,2,128,384]{5,4,3,2,1,0:T(8,128)(2,1)S(1)}, u32[]{:S(2)}, u32[]{:S(2)}) collective-permute-start(bf16[1,2,2,2,128,384]{5,4,3,2,1,0:T(8,128)(2,1)S(1)} %pad_maximum_fusion.28), channel_id=1, source_target_pairs={{0,2},{1,3},{2,0},{3,1},{4,6},{5,7},{6,4},{7,5},{8,10},{9,11},{10,... | collective-permute-start | bytes 2359304 | tf_op jit(solution)/shard_map/ppermute | solution.py:29
  132.1 16.0 %collective-permute-start.9 = (bf16[2,2,2,1,128,384]{5,4,3,2,1,0:T(8,128)(2,1)}, bf16[2,2,2,1,128,384]{5,4,3,2,1,0:T(8,128)(2,1)}, u32[]{:S(2)}, u32[]{:S(2)}) collective-permute-start(bf16[2,2,2,1,128,384]{5,4,3,2,1,0:T(8,128)(2,1)} %pad_maximum_fusion.29), channel_id=1, source_target_pairs={{0,4},{4,0},{8,12},{12,8},{16,20},{20,16},{24,28},{28,24},{1,5},{5... | collective-permute-start | bytes 2359304 | tf_op jit(solution)/shard_map/ppermute | solution.py:29
  136.1 21.3 %collective-permute-start.1 = (bf16[2,1,1024,256]{3,2,1,0:T(8,128)(2,1)}, bf16[2,1,1024,256]{3,2,1,0:T(8,128)(2,1)}, u32[]{:S(2)}, u32[]{:S(2)}) collective-permute-start(bf16[2,1,1024,256]{3,2,1,0:T(8,128)(2,1)} %maximum_bitcast_fusion), channel_id=1, source_target_pairs={{0,1},{1,0},{2,3},{3,2},{4,5},{5,4},{6,7},{7,6},{8,9},{9,8},{10,11... | collective-permute-start | bytes 3145736 | tf_op jit(solution)/shard_map/ppermute | solution.py:29
  142.0 79.1 %collective-permute-start.29 = (bf16[2,2,2,1,128,512]{5,4,3,2,1,0:T(8,128)(2,1)}, bf16[2,2,2,1,128,512]{5,4,3,2,1,0:T(8,128)(2,1)}, u32[]{:S(2)}, u32[]{:S(2)}) collective-permute-start(bf16[2,2,2,1,128,512]{5,4,3,2,1,0:T(8,128)(2,1)} %pad_maximum_fusion.19), channel_id=1, source_target_pairs={{0,4},{4,0},{8,12},{12,8},{16,20},{20,16},{24,28},{28,24},{1,5},{5... | collective-permute-start | bytes 3145736 | tf_op jit(solution)/shard_map/ppermute | solution.py:29
  148.1 75.7 %collective-permute-start.37 = (bf16[2,2,2,1,128,512]{5,4,3,2,1,0:T(8,128)(2,1)}, bf16[2,2,2,1,128,512]{5,4,3,2,1,0:T(8,128)(2,1)}, u32[]{:S(2)}, u32[]{:S(2)}) collective-permute-start(bf16[2,2,2,1,128,512]{5,4,3,2,1,0:T(8,128)(2,1)} %pad_maximum_fusion.21), channel_id=1, source_target_pairs={{0,4},{4,0},{8,12},{12,8},{16,20},{20,16},{24,28},{28,24},{1,5},{5... | collective-permute-start | bytes 3145736 | tf_op jit(solution)/shard_map/ppermute | solution.py:29
  218.7 26.1 %collective-permute-start.25 = (bf16[1,2,2,2,128,512]{5,4,3,2,1,0:T(8,128)(2,1)S(1)}, bf16[1,2,2,2,128,512]{5,4,3,2,1,0:T(8,128)(2,1)S(1)}, u32[]{:S(2)}, u32[]{:S(2)}) collective-permute-start(bf16[1,2,2,2,128,512]{5,4,3,2,1,0:T(8,128)(2,1)S(1)} %pad_maximum_fusion.18), channel_id=1, source_target_pairs={{0,2},{1,3},{2,0},{3,1},{4,6},{5,7},{6,4},{7,5},{8,10},{9,11},{10,... | collective-permute-start | bytes 3145736 | tf_op jit(solution)/shard_map/ppermute | solution.py:29
  221.1 44.8 %collective-permute-start.33 = (bf16[1,2,2,2,128,512]{5,4,3,2,1,0:T(8,128)(2,1)S(1)}, bf16[1,2,2,2,128,512]{5,4,3,2,1,0:T(8,128)(2,1)S(1)}, u32[]{:S(2)}, u32[]{:S(2)}) collective-permute-start(bf16[1,2,2,2,128,512]{5,4,3,2,1,0:T(8,128)(2,1)S(1)} %pad_maximum_fusion.20), channel_id=1, source_target_pairs={{0,2},{1,3},{2,0},{3,1},{4,6},{5,7},{6,4},{7,5},{8,10},{9,11},{10,... | collective-permute-start | bytes 3145736 | tf_op jit(solution)/shard_map/ppermute | solution.py:29
  226.3 40.2 %collective-permute-start.21 = (bf16[1,512,1024]{2,1,0:T(8,128)(2,1)S(1)}, bf16[1,512,1024]{2,1,0:T(8,128)(2,1)S(1)}, u32[]{:S(2)}, u32[]{:S(2)}) collective-permute-start(bf16[1,512,1024]{2,1,0:T(8,128)(2,1)S(1)} %fusion.63), channel_id=1, source_target_pairs={{0,1},{1,0},{2,3},{3,2},{4,5},{5,4},{6,7},{7,6},{8,9},{9,8},{10,11... | collective-permute-start | bytes 3145736 | tf_op jit(solution)/shard_map/ppermute | solution.py:29
  311.9 18.3 %collective-permute-start.43 = (bf16[1,512,1024]{2,1,0:T(8,128)(2,1)}, bf16[1,512,1024]{2,1,0:T(8,128)(2,1)}, u32[]{:S(2)}, u32[]{:S(2)}) collective-permute-start(bf16[1,512,1024]{2,1,0:T(8,128)(2,1)} %convert_bitcast_fusion.5), channel_id=1, source_target_pairs={{0,1},{1,0},{2,3},{3,2},{4,5},{5,4},{6,7},{7,6},{8,9},{9,8},{10,11... | collective-permute-start | bytes 3145736 | tf_op jit(solution)/shard_map/ppermute | solution.py:29
  367.7 26.2 %collective-permute-start.79 = (bf16[2,2,2,1,128,512]{4,5,3,2,1,0:T(8,128)(2,1)}, bf16[2,2,2,1,128,512]{4,5,3,2,1,0:T(8,128)(2,1)S(1)}, u32[]{:S(2)}, u32[]{:S(2)}) collective-permute-start(bf16[2,2,2,1,128,512]{4,5,3,2,1,0:T(8,128)(2,1)} %copy.179), channel_id=1, source_target_pairs={{0,4},{4,0},{8,12},{12,8},{16,20},{20,16},{24,28},{28,24},{1,5},{5... | collective-permute-start | bytes 3145736 | tf_op jit(solution)/shard_map/ppermute | solution.py:29
  367.7 28.1 %collective-permute-start.75 = (bf16[1,2,2,2,128,512]{4,5,3,2,1,0:T(8,128)(2,1)}, bf16[1,2,2,2,128,512]{4,5,3,2,1,0:T(8,128)(2,1)S(1)}, u32[]{:S(2)}, u32[]{:S(2)}) collective-permute-start(bf16[1,2,2,2,128,512]{4,5,3,2,1,0:T(8,128)(2,1)} %copy.177), channel_id=1, source_target_pairs={{0,2},{1,3},{2,0},{3,1},{4,6},{5,7},{6,4},{7,5},{8,10},{9,11},{10,... | collective-permute-start | bytes 3145736 | tf_op jit(solution)/shard_map/ppermute | solution.py:29
  380.7 35.7 %collective-permute-start.67 = (bf16[1,2,2,2,128,512]{5,4,3,2,1,0:T(8,128)(2,1)S(1)}, bf16[1,2,2,2,128,512]{5,4,3,2,1,0:T(8,128)(2,1)S(1)}, u32[]{:S(2)}, u32[]{:S(2)}) collective-permute-start(bf16[1,2,2,2,128,512]{5,4,3,2,1,0:T(8,128)(2,1)S(1)} %constant_dynamic-slice_fusion.17), channel_id=1, source_target_pairs={{0,2},{1,3},{2,0},{3,1},{4,6},{5,7},{6,4},{7,5},{8,10},{9,11},{10,... | collective-permute-start | bytes 3145736 | tf_op jit(solution)/shard_map/ppermute | solution.py:29
  382.1 37.6 %collective-permute-start.71 = (bf16[2,2,2,1,128,512]{5,4,3,2,1,0:T(8,128)(2,1)S(1)}, bf16[2,2,2,1,128,512]{5,4,3,2,1,0:T(8,128)(2,1)S(1)}, u32[]{:S(2)}, u32[]{:S(2)}) collective-permute-start(bf16[2,2,2,1,128,512]{5,4,3,2,1,0:T(8,128)(2,1)S(1)} %constant_dynamic-slice_fusion.13), channel_id=1, source_target_pairs={{0,4},{4,0},{8,12},{12,8},{16,20},{20,16},{24,28},{28,24},{1,5},{5... | collective-permute-start | bytes 3145736 | tf_op jit(solution)/shard_map/ppermute | solution.py:29
  386.8 35.3 %collective-permute-start.44 = (bf16[1,512,1024]{2,1,0:T(8,128)(2,1)S(1)}, bf16[1,512,1024]{2,1,0:T(8,128)(2,1)S(1)}, u32[]{:S(2)}, u32[]{:S(2)}) collective-permute-start(bf16[1,512,1024]{2,1,0:T(8,128)(2,1)S(1)} %dynamic-slice_convert_fusion.1), channel_id=1, source_target_pairs={{0,1},{1,0},{2,3},{3,2},{4,5},{5,4},{6,7},{7,6},{8,9},{9,8},{10,11... | collective-permute-start | bytes 3145736 | tf_op jit(solution)/shard_map/ppermute | solution.py:29
  395.1 36.2 %collective-permute-start.80 = (bf16[1,2,2,1,128,512]{4,5,3,2,1,0:T(8,128)(2,1)}, bf16[1,2,2,1,128,512]{4,5,3,2,1,0:T(8,128)(2,1)}, u32[]{:S(2)}, u32[]{:S(2)}) collective-permute-start(bf16[1,2,2,1,128,512]{4,5,3,2,1,0:T(8,128)(2,1)} %constant_dynamic-slice_fusion.2), channel_id=1, source_target_pairs={{0,2},{1,3},{2,0},{3,1},{4,6},{5,7},{6,4},{7,5},{8,10},{9,11},{10,... | collective-permute-start | bytes 1572872 | tf_op jit(solution)/shard_map/ppermute | solution.py:29
  397.1 35.6 %collective-permute-start.76 = (bf16[1,2,2,1,128,512]{4,5,3,2,1,0:T(8,128)(2,1)}, bf16[1,2,2,1,128,512]{4,5,3,2,1,0:T(8,128)(2,1)}, u32[]{:S(2)}, u32[]{:S(2)}) collective-permute-start(bf16[1,2,2,1,128,512]{4,5,3,2,1,0:T(8,128)(2,1)} %constant_dynamic-slice_fusion.7), channel_id=1, source_target_pairs={{0,4},{4,0},{8,12},{12,8},{16,20},{20,16},{24,28},{28,24},{1,5},{5... | collective-permute-start | bytes 1572872 | tf_op jit(solution)/shard_map/ppermute | solution.py:29
  417.7 19.7 %collective-permute-start.68 = (bf16[1,2,2,1,128,512]{5,4,3,2,1,0:T(8,128)(2,1)}, bf16[1,2,2,1,128,512]{5,4,3,2,1,0:T(8,128)(2,1)}, u32[]{:S(2)}, u32[]{:S(2)}) collective-permute-start(bf16[1,2,2,1,128,512]{5,4,3,2,1,0:T(8,128)(2,1)} %constant_dynamic-slice_fusion.16), channel_id=1, source_target_pairs={{0,4},{4,0},{8,12},{12,8},{16,20},{20,16},{24,28},{28,24},{1,5},{5... | collective-permute-start | bytes 1572872 | tf_op jit(solution)/shard_map/ppermute | solution.py:29
  421.3 17.3 %collective-permute-start.72 = (bf16[1,2,2,1,128,512]{5,4,3,2,1,0:T(8,128)(2,1)}, bf16[1,2,2,1,128,512]{5,4,3,2,1,0:T(8,128)(2,1)}, u32[]{:S(2)}, u32[]{:S(2)}) collective-permute-start(bf16[1,2,2,1,128,512]{5,4,3,2,1,0:T(8,128)(2,1)} %constant_dynamic-slice_fusion.12), channel_id=1, source_target_pairs={{0,2},{1,3},{2,0},{3,1},{4,6},{5,7},{6,4},{7,5},{8,10},{9,11},{10,... | collective-permute-start | bytes 1572872 | tf_op jit(solution)/shard_map/ppermute | solution.py:29
  430.1 47.5 %collective-permute-start.45 = (bf16[1,512,1024]{2,1,0:T(8,128)(2,1)S(1)}, bf16[1,512,1024]{2,1,0:T(8,128)(2,1)S(1)}, u32[]{:S(2)}, u32[]{:S(2)}) collective-permute-start(bf16[1,512,1024]{2,1,0:T(8,128)(2,1)S(1)} %convert_bitcast_fusion.4), channel_id=1, source_target_pairs={{0,1},{1,0},{2,3},{3,2},{4,5},{5,4},{6,7},{7,6},{8,9},{9,8},{10,11... | collective-permute-start | bytes 3145736 | tf_op jit(solution)/shard_map/ppermute | solution.py:29
  434.0 16.3 %collective-permute-start.77 = (bf16[1,2,1,1,128,512]{4,5,3,2,1,0:T(8,128)(2,1)S(1)}, bf16[1,2,1,1,128,512]{4,5,3,2,1,0:T(8,128)(2,1)S(1)}, u32[]{:S(2)}, u32[]{:S(2)}) collective-permute-start(bf16[1,2,1,1,128,512]{4,5,3,2,1,0:T(8,128)(2,1)S(1)} %constant_dynamic-slice_fusion.6), channel_id=1, source_target_pairs={{0,8},{4,12},{8,0},{12,4},{16,24},{20,28},{24,16},{28,20},{1,9},{5... | collective-permute-start | bytes 786440 | tf_op jit(solution)/shard_map/ppermute | solution.py:29
  438.5 20.2 %collective-permute-start.69 = (bf16[1,2,1,1,128,512]{5,4,3,2,1,0:T(8,128)(2,1)S(1)}, bf16[1,2,1,1,128,512]{5,4,3,2,1,0:T(8,128)(2,1)S(1)}, u32[]{:S(2)}, u32[]{:S(2)}) collective-permute-start(bf16[1,2,1,1,128,512]{5,4,3,2,1,0:T(8,128)(2,1)S(1)} %constant_dynamic-slice_fusion.15), channel_id=1, source_target_pairs={{0,8},{4,12},{8,0},{12,4},{16,24},{20,28},{24,16},{28,20},{1,9},{5... | collective-permute-start | bytes 786440 | tf_op jit(solution)/shard_map/ppermute | solution.py:29
  439.9 23.8 %collective-permute-start.73 = (bf16[1,2,1,1,128,512]{5,4,3,2,1,0:T(8,128)(2,1)S(1)}, bf16[1,2,1,1,128,512]{5,4,3,2,1,0:T(8,128)(2,1)S(1)}, u32[]{:S(2)}, u32[]{:S(2)}) collective-permute-start(bf16[1,2,1,1,128,512]{5,4,3,2,1,0:T(8,128)(2,1)S(1)} %constant_dynamic-slice_fusion.11), channel_id=1, source_target_pairs={{0,8},{4,12},{8,0},{12,4},{16,24},{20,28},{24,16},{28,20},{1,9},{5... | collective-permute-start | bytes 786440 | tf_op jit(solution)/shard_map/ppermute | solution.py:29
  442.0 23.3 %collective-permute-start.82 = (bf16[1,1,1,1,128,512]{4,5,3,2,1,0:T(8,128)(2,1)S(1)}, bf16[1,1,1,1,128,512]{4,5,3,2,1,0:T(8,128)(2,1)S(1)}, u32[]{:S(2)}, u32[]{:S(2)}) collective-permute-start(bf16[1,1,1,1,128,512]{4,5,3,2,1,0:T(8,128)(2,1)S(1)} %constant_dynamic-slice_fusion.50), channel_id=1, source_target_pairs={{0,16},{4,20},{8,24},{12,28},{16,0},{20,4},{24,8},{28,12},{1,17},{... | collective-permute-start | bytes 393224 | tf_op jit(solution)/shard_map/ppermute | solution.py:29
  458.8 15.3 %collective-permute-start.70 = (bf16[1,1,1,1,128,512]{5,4,3,2,1,0:T(8,128)(2,1)S(1)}, bf16[1,1,1,1,128,512]{5,4,3,2,1,0:T(8,128)(2,1)S(1)}, u32[]{:S(2)}, u32[]{:S(2)}) collective-permute-start(bf16[1,1,1,1,128,512]{5,4,3,2,1,0:T(8,128)(2,1)S(1)} %constant_dynamic-slice_fusion.14), channel_id=1, source_target_pairs={{0,16},{4,20},{8,24},{12,28},{16,0},{20,4},{24,8},{28,12},{1,17},{... | collective-permute-start | bytes 393224 | tf_op jit(solution)/shard_map/ppermute | solution.py:29
  616.1 57.2 %collective-permute-start.63 = (bf16[2,2,2,1,128,128]{4,5,3,2,1,0:T(8,128)(2,1)}, bf16[2,2,2,1,128,128]{4,5,3,2,1,0:T(8,128)(2,1)}, u32[]{:S(2)}, u32[]{:S(2)}) collective-permute-start(bf16[2,2,2,1,128,128]{4,5,3,2,1,0:T(8,128)(2,1)} %copy.175), channel_id=1, source_target_pairs={{0,4},{4,0},{8,12},{12,8},{16,20},{20,16},{24,28},{28,24},{1,5},{5... | collective-permute-start | bytes 786440 | tf_op jit(solution)/shard_map/ppermute | solution.py:29
  616.1 59.8 %collective-permute-start.59 = (bf16[1,2,2,2,128,128]{4,5,3,2,1,0:T(8,128)(2,1)}, bf16[1,2,2,2,128,128]{4,5,3,2,1,0:T(8,128)(2,1)}, u32[]{:S(2)}, u32[]{:S(2)}) collective-permute-start(bf16[1,2,2,2,128,128]{4,5,3,2,1,0:T(8,128)(2,1)} %copy.173), channel_id=1, source_target_pairs={{0,2},{1,3},{2,0},{3,1},{4,6},{5,7},{6,4},{7,5},{8,10},{9,11},{10,... | collective-permute-start | bytes 786440 | tf_op jit(solution)/shard_map/ppermute | solution.py:29
  618.1 18.8 %collective-permute-start.58 = (f32[1,3072]{1,0:T(1,128)S(1)}, f32[1,3072]{1,0:T(1,128)S(1)}, u32[]{:S(2)}, u32[]{:S(2)}) collective-permute-start(f32[1,3072]{1,0:T(1,128)S(1)} %constant_dynamic-slice_fusion.28), channel_id=1, source_target_pairs={{0,2},{1,3},{2,0},{3,1},{4,6},{5,7},{6,4},{7,5},{8,10},{9,11},{10,... | collective-permute-start | bytes 36872 | tf_op jit(solution)/shard_map/ppermute | solution.py:29
  625.3 66.7 %collective-permute-start.53 = (bf16[2,2,2,1,128,384]{4,5,3,2,1,0:T(8,128)(2,1)}, bf16[2,2,2,1,128,384]{4,5,3,2,1,0:T(8,128)(2,1)}, u32[]{:S(2)}, u32[]{:S(2)}) collective-permute-start(bf16[2,2,2,1,128,384]{4,5,3,2,1,0:T(8,128)(2,1)} %copy.171), channel_id=1, source_target_pairs={{0,4},{4,0},{8,12},{12,8},{16,20},{20,16},{24,28},{28,24},{1,5},{5... | collective-permute-start | bytes 2359304 | tf_op jit(solution)/shard_map/ppermute | solution.py:29
  627.4 67.8 %collective-permute-start.49 = (bf16[1,2,2,2,128,384]{4,5,3,2,1,0:T(8,128)(2,1)}, bf16[1,2,2,2,128,384]{4,5,3,2,1,0:T(8,128)(2,1)}, u32[]{:S(2)}, u32[]{:S(2)}) collective-permute-start(bf16[1,2,2,2,128,384]{4,5,3,2,1,0:T(8,128)(2,1)} %copy.169), channel_id=1, source_target_pairs={{0,2},{1,3},{2,0},{3,1},{4,6},{5,7},{6,4},{7,5},{8,10},{9,11},{10,... | collective-permute-start | bytes 2359304 | tf_op jit(solution)/shard_map/ppermute | solution.py:29
  636.9 60.4 %collective-permute-start.46 = (bf16[1,512,1024]{2,1,0:T(8,128)(2,1)}, bf16[1,512,1024]{2,1,0:T(8,128)(2,1)}, u32[]{:S(2)}, u32[]{:S(2)}) collective-permute-start(bf16[1,512,1024]{2,1,0:T(8,128)(2,1)} %dynamic-slice_convert_fusion), channel_id=1, source_target_pairs={{0,1},{1,0},{2,3},{3,2},{4,5},{5,4},{6,7},{7,6},{8,9},{9,8},{10,11... | collective-permute-start | bytes 3145736 | tf_op jit(solution)/shard_map/ppermute | solution.py:29
  702.3 17.9 %collective-permute-start.47 = (bf16[2,1,1,512,256]{4,3,2,0,1:T(8,128)(2,1)S(1)}, bf16[2,1,1,512,256]{4,3,2,0,1:T(8,128)(2,1)S(1)}, u32[]{:S(2)}, u32[]{:S(2)}) collective-permute-start(bf16[2,1,1,512,256]{4,3,2,0,1:T(8,128)(2,1)S(1)} %bitcast.602), channel_id=1, source_target_pairs={{0,1},{1,0},{2,3},{3,2},{4,5},{5,4},{6,7},{7,6},{8,9},{9,8},{10,11... | collective-permute-start | bytes 1572872 | tf_op jit(solution)/shard_map/ppermute | solution.py:29
  (147 other events, 980.0 us)

commit v2 on v1

v2 whole, which is shorter than its diff:
```python
import functools
import math

import jax
import jax.numpy as jnp
from jax import lax
from jax.experimental import pallas as pl
from jax.experimental.pallas import tpu as pltpu
from jax.sharding import PartitionSpec as P

DH = 64
NORM_EPS = 1e-06
MASKED = -1000000000.0
LONGEST = 256
F32 = jnp.float32
BF16 = jnp.bfloat16


def nn(left, right):
    return lax.dot_general(left, right, (((1,), (0,)), ((), ())), preferred_element_type=F32)


def nt(left, right):
    return lax.dot_general(left, right, (((1,), (1,)), ((), ())), preferred_element_type=F32)


def tn(left, right):
    return lax.dot_general(left, right, (((0,), (0,)), ((), ())), preferred_element_type=F32)


def after(block, *others):
    return lax.optimization_barrier((block,) + others)[0]


def pick(block, bit, dim):
    return lax.dynamic_slice_in_dim(block, bit, 1, dim)


def bits_of(count):
    return [1 << b for b in reversed(range(count.bit_length() - 1))]


class Stage:
    def __init__(self, axis, count, mask, index):
        self.axis, self.pairs = axis, [(i, i ^ mask) for i in range(count)]
        self.bit = (index // mask) % 2

    def trade(self, block):
        return lax.ppermute(block, self.axis, self.pairs)

    def join(self, mine, other, dim):
        low = self.bit == 0
        return jnp.concatenate(
            (jnp.where(low, mine, other), jnp.where(low, other, mine)), axis=dim
        )

    def gather(self, block, dim):
        return self.join(block, self.trade(block), dim)

    def swap(self, block, split, dim):
        keep = pick(block, self.bit, split)
        return self.join(keep, self.trade(pick(block, 1 - self.bit, split)), dim)

    def reduce(self, block, dim):
        got = self.trade(pick(block, 1 - self.bit, dim))
        return add(pick(block, self.bit, dim), got)


def add(mine, other):
    return (mine.astype(F32) + other.astype(F32)).astype(mine.dtype)


def tiles_of(length):
    return min(256, length), min(128, length)


def key_windows(labels):
    rows, step = tiles_of(labels.shape[0])
    first, last = labels[::rows], labels[rows - 1 :: rows]
    start = jnp.sum(labels[None, :] < first[:, None], axis=1)
    stop = jnp.sum(labels[None, :] <= last[:, None], axis=1)
    block = start // step
    return jnp.stack((block, (stop - 1) // step + 1 - block)).astype(jnp.int32)


def for_each_block(windows, length, run):
    rows, step = tiles_of(length)
    reach = -(-(LONGEST - 1) // step)
    most = min(length // step, rows // step + 2 * reach)

    def one(i, carry):
        q0 = pl.multiple_of(i * rows, rows)
        k0 = pl.multiple_of(windows[0, i] * step, step)
        for n in range(1, most + 1):
            pl.when(windows[1, i] == n)(functools.partial(run, q0, k0, rows, n * step))
        return carry

    lax.fori_loop(0, length // rows, one, 0)


def attend_kernel(
    windows, x_ref, w_ref, b_ref, lab_col, lab_row, q_ref, k_ref, v_ref, ctx_ref, lse_ref
):
    length, lanes = q_ref.shape
    rows, _ = tiles_of(length)

    def project(i, carry):
        here = pl.ds(pl.multiple_of(i * rows, rows), rows)
        projected = nn(x_ref[here, :], w_ref[...]) + b_ref[...]
        scale = 1.0 / math.sqrt(DH)
        q_ref[here, :] = (projected[:, :lanes].astype(BF16).astype(F32) * scale).astype(BF16)
        k_ref[here, :] = projected[:, lanes : 2 * lanes].astype(BF16)
        v_ref[here, :] = projected[:, 2 * lanes :].astype(BF16)
        return carry

    lax.fori_loop(0, length // rows, project, 0)

    def run(q0, k0, rows, span):
        q = q_ref[pl.ds(q0, rows), :]
        k = k_ref[pl.ds(k0, span), :]
        v_t = v_ref[pl.ds(k0, span), :].T
        same = lab_col[pl.ds(k0, span), :] == lab_row[:, pl.ds(q0, rows)]
        head = lax.broadcasted_iota(jnp.int32, (span, lanes), 1) // DH
        outs = []
        for h in range(lanes // DH):
            scores = nt(jnp.where(head == h, k, jnp.zeros_like(k)), q)
            scores = jnp.where(same, scores, MASKED)
            top = jnp.max(scores, axis=0, keepdims=True)
            shifted = jnp.exp(scores - top)
            total = jnp.sum(shifted, axis=0, keepdims=True)
            outs.append(nn(v_t[h * DH : (h + 1) * DH, :], shifted.astype(BF16)) / total)
            lse_ref[h : h + 1, pl.ds(q0, rows)] = top + jnp.log(total)
        ctx_ref[pl.ds(q0, rows), :] = jnp.concatenate(outs, axis=0).T.astype(BF16)

    for_each_block(windows, length, run)


def attend_back_kernel(
    windows, ga_ref, wo_ref, q_ref, k_ref, v_ref, lse_ref, lab_col, lab_row, gp_ref, sum_ref,
    do_ref, dk_acc, dv_acc,
):
    length, lanes = q_ref.shape
    tile_rows, _ = tiles_of(length)
    scale = 1.0 / math.sqrt(DH)
    dk_acc[...] = jnp.zeros_like(dk_acc)
    dv_acc[...] = jnp.zeros_like(dv_acc)
    sum_ref[...] = jnp.zeros_like(sum_ref)

    def project(i, carry):
        here = pl.ds(pl.multiple_of(i * tile_rows, tile_rows), tile_rows)
        do_ref[here, :] = nn(ga_ref[here, :], wo_ref[...]).astype(BF16)
        return carry

    lax.fori_loop(0, length // tile_rows, project, 0)

    def run(q0, k0, rows, span):
        q = q_ref[pl.ds(q0, rows), :]
        do = do_ref[pl.ds(q0, rows), :]
        k = k_ref[pl.ds(k0, span), :]
        v = v_ref[pl.ds(k0, span), :]
        k_t = k.T
        same = lab_col[pl.ds(k0, span), :] == lab_row[:, pl.ds(q0, rows)]
        head = lax.broadcasted_iota(jnp.int32, (span, lanes), 1) // DH
        head_q = lax.broadcasted_iota(jnp.int32, (rows, lanes), 1) // DH
        dqs = []
        dk = dv = None
        for h in range(lanes // DH):
            only = lambda a, own: jnp.where(own == h, a, jnp.zeros_like(a))
            scores = jnp.where(same, nt(only(k, head), q), MASKED)
            prob = jnp.exp(scores - lse_ref[h : h + 1, pl.ds(q0, rows)])
            weighted = prob * nt(only(v, head), do)
            row_dot = jnp.sum(weighted, axis=0, keepdims=True)
            dscore = (weighted - prob * row_dot).astype(BF16)
            dv_h = nn(prob.astype(BF16), only(do, head_q))
            dk_h = nn(dscore, only(q, head_q))
            dv = dv_h if dv is None else dv + dv_h
            dk = dk_h if dk is None else dk + dk_h
            dqs.append(nn(k_t[h * DH : (h + 1) * DH, :], dscore))
        dq = jnp.concatenate(dqs, axis=0).T * scale
        gp_ref[pl.ds(q0, rows), :lanes] = dq.astype(BF16)
        sum_ref[0:1, :] += jnp.sum(dq, axis=0, keepdims=True)
        dk_acc[pl.ds(k0, span), :] += dk
        dv_acc[pl.ds(k0, span), :] += dv

    for_each_block(windows, length, run)
    gp_ref[:, lanes : 2 * lanes] = dk_acc[...].astype(BF16)
    gp_ref[:, 2 * lanes :] = dv_acc[...].astype(BF16)
    sum_ref[1:2, :] = jnp.sum(dv_acc[...], axis=0, keepdims=True)


def whole_call(kernel, scalars, operands, outs, scratch, flops, name):
    full = lambda a: pl.BlockSpec(a.shape, lambda i, *_: (0,) * len(a.shape))
    moved = sum(math.prod(a.shape) * a.dtype.itemsize for a in list(operands) + list(outs))
    return pl.pallas_call(
        kernel,
        grid_spec=pltpu.PrefetchScalarGridSpec(
            num_scalar_prefetch=len(scalars),
            grid=(1,),
            in_specs=[full(a) for a in operands],
            out_specs=[full(a) for a in outs],
            scratch_shapes=scratch,
        ),
        out_shape=outs,
        cost_estimate=pl.CostEstimate(flops=flops, transcendentals=0, bytes_accessed=moved),
        name=name,
    )(*scalars, *operands)


def attend(windows, x, weight, bias, lab_col, lab_row):
    length, model = x.shape
    lanes = weight.shape[1] // 3
    rows = jax.ShapeDtypeStruct((length, lanes), BF16)
    outs = [rows, rows, rows, rows, jax.ShapeDtypeStruct((lanes // DH, length), F32)]
    return whole_call(
        attend_kernel, [windows], [x, weight, bias, lab_col, lab_row], outs, [],
        6 * length * model * lanes + 20 * length * 640 * lanes, "attend",
    )


def attend_back(windows, ga, wo, q, k, v, lse, lab_col, lab_row):
    length, lanes = q.shape
    outs = [
        jax.ShapeDtypeStruct((length, 3 * lanes), BF16),
        jax.ShapeDtypeStruct((2, lanes), F32),
    ]
    scratch = [pltpu.VMEM((length, lanes), BF16)] + [pltpu.VMEM((length, lanes), F32)] * 2
    return whole_call(
        attend_back_kernel, [windows], [ga, wo, q, k, v, lse, lab_col, lab_row], outs, scratch,
        2 * length * ga.shape[1] * lanes + 40 * length * 640 * lanes, "attend_back",
    )


def ffn_in_kernel(y_ref, w_ref, b_ref, act_ref, slope_ref):
    inner = nn(y_ref[...], w_ref[...]) + b_ref[...]
    share = 0.5 + 0.5 * lax.erf(inner * math.sqrt(0.5))
    density = jnp.exp(-0.5 * inner * inner) * (1.0 / math.sqrt(2.0 * math.pi))
    act_ref[...] = (inner * share).astype(BF16)
    slope_ref[...] = (share + inner * density).astype(BF16)


def ffn_back_kernel(gb_ref, w_ref, slope_ref, gi_ref, sum_ref):
    grad = nn(gb_ref[...], w_ref[...]) * slope_ref[...].astype(F32)
    gi_ref[...] = grad.astype(BF16)
    sum_ref[...] = jnp.sum(grad, axis=0, keepdims=True)


def by_columns(kernel, rows, weight, extra, outs, flops, name):
    length, model = rows.shape
    wide = weight.shape[1]
    tile = min(256, wide)
    column = lambda a: pl.BlockSpec((a.shape[0], tile), lambda i: (0, i))
    moved = sum(math.prod(a.shape) * a.dtype.itemsize for a in [rows, weight, extra] + list(outs))
    return pl.pallas_call(
        kernel,
        grid=(wide // tile,),
        in_specs=[pl.BlockSpec((length, model), lambda i: (0, 0)), column(weight), column(extra)],
        out_specs=[column(a) for a in outs],
        out_shape=outs,
        cost_estimate=pl.CostEstimate(flops=flops, transcendentals=0, bytes_accessed=moved),
        name=name,
    )(rows, weight, extra)


def ffn_in(y, weight, bias):
    out = jax.ShapeDtypeStruct((y.shape[0], weight.shape[1]), BF16)
    flops = 2 * math.prod(y.shape) * weight.shape[1] * 3
    return by_columns(ffn_in_kernel, y, weight, bias, [out, out], flops, "ffn_in")


def ffn_back(gb, weight, slope):
    outs = [
        jax.ShapeDtypeStruct(slope.shape, BF16),
        jax.ShapeDtypeStruct((1, slope.shape[1]), F32),
    ]
    flops = 2 * math.prod(gb.shape) * weight.shape[1]
    return by_columns(ffn_back_kernel, gb, weight, slope, outs, flops, "ffn_back")


def body(
    rows,
    cols,
    tokens,
    segments,
    wqkv,
    bias_qv,
    wo,
    bias_o,
    gain_a,
    shift_a,
    w_in,
    bias_in,
    w_out,
    bias_out,
    gain_b,
    shift_b,
    cotangent,
):
    seqs, length = segments.shape
    ways = cols // seqs
    width = tokens.shape[1]
    model = width * cols
    heads = wqkv.shape[1] // (3 * DH)
    hid = w_in.shape[1]
    part = length // ways
    own_rows = wqkv.shape[0]
    row, col = lax.axis_index("row"), lax.axis_index("col")
    seq, way = col // ways, col % ways
    by_seq = [Stage("col", cols, mask * ways, col) for mask in bits_of(seqs)]
    by_way = [Stage("col", cols, mask, col) for mask in bits_of(ways)]
    by_row = [Stage("row", rows, mask, row) for mask in bits_of(rows)]
    ns, nw, nr = len(by_seq), len(by_way), len(by_row)
    far, near = by_row[:-1], by_row[-1]

    def gather_far(shard):
        block = shard.reshape((1,) * nr + shard.shape)
        for i, stage in enumerate(far):
            block = stage.gather(block, i)
        return block

    def gather_near_first(block):
        mine = near.gather(block, nr - 1).reshape(model, -1)
        return [mine]

    def gather_seq_last(blocks):
        for stage in by_seq:
            blocks = blocks + [stage.trade(b) for b in blocks]
        return blocks

    def gather_seq_first(block):
        block = block[None]
        for stage in by_seq:
            block = jnp.concatenate((block, stage.trade(block)), axis=0)
        return block

    def gather_near_last(block):
        block = near.gather(block, nr)
        return [block[j].reshape(model, -1) for j in range(seqs)]

    shards = []
    halves = lambda w: w.reshape(own_rows, 2, heads // 2, 3, DH)
    shards.append(halves(wqkv).transpose(0, 1, 3, 2, 4).reshape(own_rows, -1))
    shards.append(wo.T)
    shards.append(w_in)
    shards.append(w_out.T)

    labels = lax.dynamic_slice_in_dim(segments, seq, 1, 0)[0]
    windows = key_windows(labels)
    lab_col, lab_row = labels[:, None], labels[None, :]

    vectors = jnp.concatenate(
        [v.reshape(-1, width) for v in (bias_o, gain_a, shift_a, bias_out, gain_b, shift_b, bias_qv, bias_in)]
    )

    def own_sequence(array):
        block = array.reshape((2,) * ns + (1,) * ns + (length, width))
        for i, stage in enumerate(by_seq):
            block = stage.swap(block, i, ns + i)
        return block.reshape((seqs, length, width))

    tokens_x = own_sequence(tokens)
    block = tokens_x.reshape((seqs,) + (1,) * nw + (length, width))
    for i, stage in enumerate(by_way):
        block = stage.gather(block, 1 + i)
    block = block.reshape(cols, length, width)
    whole_x = jnp.transpose(block, (1, 0, 2)).reshape(length, model)

    pairs = [vectors]
    for stage in by_seq:
        pairs = pairs + [stage.trade(v) for v in pairs]
    block = vectors.reshape((1,) * (ns + nw) + vectors.shape)[..., :6, :]
    for i, stage in enumerate(by_seq):
        block = stage.join(block, pairs[1 << i].reshape((1,) * (ns + nw) + vectors.shape)[..., :6, :], i)
    for i, stage in enumerate(by_way):
        block = stage.gather(block, ns + i)
    full = block.reshape(cols, 6, width).transpose(1, 0, 2).reshape(6, 1, model).astype(F32)
    bias_o32, gain_a32, shift_a32, bias_out32, gain_b32, shift_b32 = (full[i] for i in range(6))
    nq = bias_qv.shape[0] // width

    def qkv_bias(j, half):
        both = pairs[j][6 : 6 + nq].astype(F32).reshape(2, heads // 2, 2, DH)[half]
        q, v = both[:, 0].reshape(1, -1), both[:, 1].reshape(1, -1)
        return jnp.concatenate((q, jnp.zeros_like(q), v), axis=1)

    def in_bias(j, half):
        return pairs[j][6 + nq :].astype(F32).reshape(2, 1, hid // 2)[half]

    gathered = []
    held_far = held_first = None
    for shard in shards:
        if held_far is not None:
            shard = after(shard, held_far)
        block = gather_far(shard)
        held_far = block
        half = block.shape[-1] // 2
        one, two = block[..., :half], block[..., half:]
        if held_first is not None:
            one, two = after(one, *held_first), after(two, *held_first)
        one, two = gather_near_first(one), gather_seq_first(two)
        held_first = (one[0], two)
        one, two = gather_seq_last(one), gather_near_last(two)
        gathered.append([(one[j], two[j]) for j in range(seqs)])
    flat = [[blk for pair in weight for blk in pair] for weight in gathered]
    qkv_all, wo_all, in_all, out_all = flat
    places = [(j, half) for j in range(seqs) for half in range(2)]

    def own_part(array):
        block = own_sequence(array)
        block = block.reshape((seqs,) + (1,) * nw + (2,) * nw + (part, width))
        for i, stage in enumerate(by_way):
            block = stage.swap(block, 1 + nw + i, 1 + i)
        block = block.reshape(cols, part, width)
        return jnp.transpose(block, (1, 0, 2)).reshape(part, model)

    def back_to_features(array):
        block = array.reshape((part, seqs) + (2,) * nw + (width,))
        block = jnp.moveaxis(block, 0, -2).reshape((seqs,) + (2,) * nw + (1,) * nw + (part, width))
        for i, stage in enumerate(by_way):
            block = stage.swap(block, 1 + i, 1 + nw + i)
        block = block.reshape((2,) * ns + (1,) * ns + (length, width))
        for i, stage in enumerate(by_seq):
            block = stage.swap(block, i, ns + i)
        return block.reshape(seqs * length, width)

    def gather_ways(block):
        block = block.reshape((1,) * nw + block.shape)
        for i, stage in enumerate(by_way):
            block = stage.gather(block, i)
        return block.reshape(length, model)

    def scatter_ways(partial_terms):
        block = partial_terms.reshape((2,) * nw + (part, model))
        for i, stage in enumerate(by_way):
            got = stage.trade(pick(block, 1 - stage.bit, i).astype(BF16))
            block = pick(block, stage.bit, i) + got.astype(F32)
        return block.reshape(part, model)

    def scatter_weight(blocks):
        ones, twos = blocks[0::2], blocks[1::2]
        for stage in reversed(by_seq):
            count = len(ones) // 2
            ones = [add(ones[j], stage.trade(ones[count + j])) for j in range(count)]
        one = near.reduce(ones[0].reshape((2,) * nr + (own_rows, -1)), nr - 1)
        two = jnp.stack([b.reshape((2,) * nr + (own_rows, -1)) for b in twos])
        two = near.reduce(two, nr)
        for stage in reversed(by_seq):
            count = two.shape[0] // 2
            two = add(two[:count], stage.trade(two[count:]))
        block = jnp.concatenate((one, two[0]), axis=-1)
        for i, stage in reversed(list(enumerate(far))):
            block = stage.reduce(block, i)
        return block.reshape(own_rows, -1).astype(F32)

    cot = own_part(after(cotangent, held_first[0])).astype(F32)

    kept = [
        attend(windows, whole_x, qkv_all[i], qkv_bias(*places[i]), lab_col, lab_row)
        for i in range(2 * seqs)
    ]
    context = jnp.concatenate([k[3] for k in kept], axis=1)
    partial_a = nt(context, jnp.concatenate(wo_all, axis=1))
    own_x = lax.dynamic_slice_in_dim(whole_x, way * part, part, 0)
    hidden_a = scatter_ways(partial_a) + own_x.astype(F32) + bias_o32

    def norm(hidden):
        mean = jnp.mean(hidden, axis=1, keepdims=True)
        square = jnp.mean(hidden * hidden, axis=1, keepdims=True)
        inv_std = lax.rsqrt(square - mean * mean + NORM_EPS)
        return (hidden - mean) * inv_std, inv_std

    def norm_back(incoming, centred, inv_std, gain):
        scaled = incoming * gain
        first = jnp.mean(scaled, axis=1, keepdims=True)
        second = jnp.mean(scaled * centred, axis=1, keepdims=True)
        return inv_std * (scaled - first - centred * second)

    centred_a, inv_std_a = norm(hidden_a)
    normed_a = centred_a * gain_a32 + shift_a32
    whole_y = gather_ways(normed_a.astype(BF16))
    active, slope = zip(
        *[ffn_in(whole_y, in_all[i], in_bias(*places[i])) for i in range(2 * seqs)]
    )
    partial_b = sum(nt(active[i], out_all[i]) for i in range(2 * seqs))
    hidden_b = scatter_ways(partial_b) + bias_out32 + normed_a
    centred_b, inv_std_b = norm(hidden_b)
    output = back_to_features((centred_b * gain_b32 + shift_b32).astype(BF16))

    grad_b = norm_back(cot, centred_b, inv_std_b, gain_b32)
    whole_gb = gather_ways(grad_b.astype(BF16))
    grad_w_out = scatter_weight([tn(whole_gb, a).astype(BF16) for a in active])
    grad_inner, sum_inner = zip(
        *[ffn_back(whole_gb, out_all[i], slope[i]) for i in range(2 * seqs)]
    )
    partial_n = sum(nt(grad_inner[i], in_all[i]) for i in range(2 * seqs))
    grad_w_in = scatter_weight([tn(whole_y, g).astype(BF16) for g in grad_inner])
    grad_normed = scatter_ways(partial_n) + grad_b
    grad_a = norm_back(grad_normed, centred_a, inv_std_a, gain_a32)
    whole_ga = gather_ways(grad_a.astype(BF16))
    grad_wo = scatter_weight([tn(whole_ga, k[3]).astype(BF16) for k in kept])
    grad_projected, sum_projected = zip(
        *[
            attend_back(windows, whole_ga, wo_all[i], *kept[i][:3], kept[i][4], lab_col, lab_row)
            for i in range(2 * seqs)
        ]
    )
    grad_wqkv = scatter_weight([tn(whole_x, g).astype(BF16) for g in grad_projected])
    partial_x = sum(nt(grad_projected[i], qkv_all[i]) for i in range(2 * seqs))
    grad_tokens = back_to_features((scatter_ways(partial_x) + grad_a).astype(BF16)).astype(F32)

    per_hidden = []
    for j in range(seqs):
        two = [sum_projected[2 * j + h].reshape(2, heads // 2, DH).transpose(1, 0, 2) for h in range(2)]
        sums = [s.reshape(-1) for s in two] + [sum_inner[2 * j + h].reshape(-1) for h in range(2)]
        per_hidden.append(jnp.concatenate(sums))
    per_feature = jnp.stack(
        [
            jnp.sum(v, axis=0)
            for v in (
                grad_a,
                grad_normed * centred_a,
                grad_normed,
                grad_b,
                cot * centred_b,
                cot,
            )
        ]
    )
    block = per_feature.reshape((6, seqs) + (2,) * nw + (width,))
    for i, stage in enumerate(by_way):
        block = stage.reduce(block, 2 + i)
    block = block.reshape((6,) + (2,) * ns + (width,))
    for i, stage in enumerate(by_seq):
        block = stage.reduce(block, 1 + i)
    for stage in reversed(by_seq):
        count = len(per_hidden) // 2
        per_hidden = [per_hidden[j] + stage.trade(per_hidden[count + j]) for j in range(count)]
    sums = jnp.concatenate((per_hidden[0], block.reshape(-1)))
    for stage in by_row:
        sums = sums + stage.trade(sums)
    nqv = bias_qv.shape[0]
    sum_qv, sum_in = sums[:nqv], sums[nqv : nqv + hid]
    rest = sums[nqv + hid :].reshape(6, width)
    by_kind = grad_wqkv.reshape(own_rows, 2, 3, heads // 2, DH)
    return (
        output,
        grad_tokens,
        by_kind.transpose(0, 1, 3, 2, 4).reshape(own_rows, -1),
        sum_qv,
        grad_wo.T,
        rest[0],
        rest[1],
        rest[2],
        grad_w_in,
        sum_in,
        grad_w_out.T,
        rest[3],
        rest[4],
        rest[5],
    )


def solution(mesh):
    tile, across, down, flat = P("row", "col"), P("row", None), P("col", "row"), P("col")
    in_specs = (tile, across, tile, flat, down, flat, flat, flat, tile, flat, down, flat, flat, flat, tile)
    out_specs = (tile, tile, tile, flat, down, flat, flat, flat, tile, flat, down, flat, flat, flat)
    rows, cols = mesh.shape["row"], mesh.shape["col"]

    def layer(*args):
        return body(rows, cols, *args)

    return jax.shard_map(layer, mesh=mesh, in_specs=in_specs, out_specs=out_specs, check_vma=False)
```

time: 740 us -> 640 us (0.86)
  Pallas kernels: 0 us -> 118 us
  matrix products: 184 us -> 93.3 us
  blocking collectives: 34.5 us -> 0 us
  waiting for transfers between devices: 217 us -> 184 us
  local copies, waits for them, and re-layouts: 95.7 us -> 76.2 us
  other arithmetic: 110 us -> 93.8 us
  starting transfers between devices: 78.8 us -> 64.8 us
  loops' own time: 9.01 us -> 0 us
    pallas_call x0 -> x16, Pallas kernels: none -> 118 us  [the longest x8 80.4 us: whole_call(): pl.pallas_call(kernel, grid_spec=pltpu.PrefetchScalarGridSpec(num_scalar_...]
    dot_general x12 -> x0, matrix products: 66.9 us -> none  [nn(): lax.dot_general(left, right, (((1,), (0,)), ((), ())), preferred_element_...]
    psum x1 -> x0, blocking collectives: 34.5 us -> none  [body(): sums = lax.psum(block.reshape(-1), 'row')]
    ppermute x83 -> x71, waiting for transfers between devices: 217 us -> 184 us  [trade(): return lax.ppermute(block, self.axis, self.pairs)]
    dot_general x14 -> x13, matrix products: 78.2 us -> 51.1 us  [nt(): lax.dot_general(left, right, (((1,), (1,)), ((), ())), preferred_element_...]
    convert_element_type x31 -> x23, other arithmetic: 37.2 us -> 18.4 us  [the longest x16 16.4 us: add(): return (mine.astype(F32) + other.astype(F32)).astype(mine.dtype)]
    unnamed x240 -> x231, local copies, waits for them, and re-layouts: 35 us -> 16.2 us
    slice x7 -> x19, local copies, waits for them, and re-layouts: 2.07 us -> 18.1 us  [the longest x8 14.3 us: gather_near_last(): return [block[j].reshape(model, -1) for j in range(seqs)]]
  transfers between devices with their start and end apart: 83 -> 71, of which waited for: 40 -> 23; matrix products, arithmetic and copies ran while one was open for 27% -> 34% of each run, Pallas kernels for 0% -> 17%
where the time goes in v2:
time: 640 us; the launch traced here: 633 us
  waiting for transfers between devices  184 us (29%)
  Pallas kernels  118 us (18%)
  other arithmetic  93.8 us (15%)
  matrix products  93.3 us (15%)
  local copies, waits for them, and re-layouts  76.2 us (12%)
  starting transfers between devices  64.8 us (10%)
    ppermute x71, waiting for transfers between devices, trade(): return lax.ppermute(block, self.axis, self.pairs)  184 us
    pallas_call x8, Pallas kernels, whole_call(): pl.pallas_call(kernel, grid_spec=pltpu.PrefetchScalarGridSpec(num_scalar_...  80.4 us
    ppermute x71, starting transfers between devices, trade(): return lax.ppermute(block, self.axis, self.pairs)  64.8 us
    dot_general x13, matrix products, nt(): lax.dot_general(left, right, (((1,), (1,)), ((), ())), preferred_element_...  51.1 us
    dot_general x16, matrix products, tn(): lax.dot_general(left, right, (((0,), (0,)), ((), ())), preferred_element_...  42.2 us
    pallas_call x8, Pallas kernels, by_columns(): pl.pallas_call(kernel, grid=(wide // tile,), in_specs=[pl.BlockSpec((leng...  37.6 us
    select_n x26, other arithmetic, join(): jnp.where(low, mine, other)  19.6 us
    convert_element_type x16, other arithmetic, add(): return (mine.astype(F32) + other.astype(F32)).astype(mine.dtype)  16.4 us
  transfers between devices with their start and end apart: 71, of which 23 were waited for; matrix products, arithmetic and copies ran while one was open for 34% of the time, Pallas kernels for 17%

profile of v2, /device:TPU:0, one launch (start us, length us, event | category | flops | bytes accessed | tf_op | source)
XLA Modules:
  0.0 633.3 jit_solution(2487516851248197248)
XLA Ops:
  2.0 4.1 collective-permute-start.2
  17.4 7.0 %collective-permute-done.8 = bf16[12,256]{1,0:T(8,128)(2,1)S(1)} collective-permute-done((bf16[12,256]{1,0:T(8,128)(2,1)S(1)}, bf16[12,256]{1,0:T(8,128)(2,1)S(1)}, u32[]{:S(2)}, u32[]{:S(2)}) %collective-permute-start.8) | collective-permute-done | bytes 6176 | tf_op jit(solution)/shard_map/ppermute | solution.py:49
  29.5 6.7 %collective-permute-done.10 = bf16[2,1,1,128,256]{3,4,2,1,0:T(8,128)(2,1)S(1)} collective-permute-done((bf16[2,1,1,128,256]{3,4,2,1,0:T(8,128)(2,1)S(1)}, bf16[2,1,1,128,256]{3,4,2,1,0:T(8,128)(2,1)S(1)}, u32[]{:S(2)}, u32[]{:S(2)}) %collective-permute-start.10) | collective-permute-done | bytes 131104 | tf_op jit(solution)/shard_map/ppermute | solution.py:49
  44.6 5.9 collective-permute-done.3
  53.8 8.0 %collective-permute-done.19 = bf16[2,1,1,128,1024]{3,4,1,0,2:T(8,128)(2,1)S(1)} collective-permute-done((bf16[2,1,1,128,1024]{3,4,1,0,2:T(8,128)(2,1)S(1)}, bf16[2,1,1,128,1024]{3,4,1,0,2:T(8,128)(2,1)S(1)}, u32[]{:S(2)}, u32[]{:S(2)}) %collective-permute-start.19) | collective-permute-done | bytes 524320 | tf_op jit(solution)/shard_map/ppermute | solution.py:49
  61.9 11.1 %collective-permute-done.22 = bf16[2,1,1,128,1024]{3,4,1,0,2:T(8,128)(2,1)S(1)} collective-permute-done((bf16[2,1,1,128,1024]{3,4,1,0,2:T(8,128)(2,1)S(1)}, bf16[2,1,1,128,1024]{3,4,1,0,2:T(8,128)(2,1)S(1)}, u32[]{:S(2)}, u32[]{:S(2)}) %collective-permute-start.22) | collective-permute-done | bytes 524320 | tf_op jit(solution)/shard_map/ppermute | solution.py:49
  90.6 18.1 %collective-permute-done.13 = bf16[2,2,2,1,128,128]{4,5,2,1,3,0:T(8,128)(2,1)} collective-permute-done((bf16[2,2,2,1,128,128]{4,5,2,1,3,0:T(8,128)(2,1)}, bf16[2,2,2,1,128,128]{4,5,2,1,3,0:T(8,128)(2,1)}, u32[]{:S(2)}, u32[]{:S(2)}) %collective-permute-start.13) | collective-permute-done | bytes 262176 | tf_op jit(solution)/shard_map/ppermute | solution.py:49
  119.6 9.9 %attend.4 = (bf16[1024,128]{1,0:T(8,128)(2,1)}, bf16[1024,128]{1,0:T(8,128)(2,1)}, bf16[1024,128]{1,0:T(8,128)(2,1)}, bf16[1024,128]{1,0:T(8,128)(2,1)}, f32[2,1024]{1,0:T(2,128)}) custom-call(s32[2,4]{1,0:T(2,128)} %pad_add_fusion.windows, bf16[1024,1024]{1,0:T(8,128)(2,1)} %bitcast.380, bf16[1024,384]{1,0:T(8,128)(2,1)} %bitcast.10.w_ref, ...), custom_call_target="tpu_custom_call" | custom-call | flops 2483027968 | bytes 3950080 | tf_op jit(solution)/shard_map/attend/pallas_call | solution.py:194
  140.6 9.7 %attend.5 = (bf16[1024,128]{1,0:T(8,128)(2,1)}, bf16[1024,128]{1,0:T(8,128)(2,1)}, bf16[1024,128]{1,0:T(8,128)(2,1)}, bf16[1024,128]{1,0:T(8,128)(2,1)}, f32[2,1024]{1,0:T(2,128)}) custom-call(s32[2,4]{1,0:T(2,128)} %pad_add_fusion.windows, bf16[1024,1024]{1,0:T(8,128)(2,1)} %bitcast.381, bf16[1024,384]{1,0:T(8,128)(2,1)} %bitcast.414, ...), custom_call_target="tpu_custom_call" | custom-call | flops 2483027968 | bytes 3950080 | tf_op jit(solution)/shard_map/attend/pallas_call | solution.py:194
  150.4 10.1 %attend.7 = (bf16[1024,128]{1,0:T(8,128)(2,1)}, bf16[1024,128]{1,0:T(8,128)(2,1)}, bf16[1024,128]{1,0:T(8,128)(2,1)}, bf16[1024,128]{1,0:T(8,128)(2,1)}, f32[2,1024]{1,0:T(2,128)}) custom-call(s32[2,4]{1,0:T(2,128)} %pad_add_fusion.windows, bf16[1024,1024]{1,0:T(8,128)(2,1)} %bitcast.382, bf16[1024,384]{1,0:T(8,128)(2,1)} %bitcast.412, ...), custom_call_target="tpu_custom_call" | custom-call | flops 2483027968 | bytes 3950080 | tf_op jit(solution)/shard_map/attend/pallas_call | solution.py:194
  160.5 9.9 %attend.6 = (bf16[1024,128]{1,0:T(8,128)(2,1)}, bf16[1024,128]{1,0:T(8,128)(2,1)}, bf16[1024,128]{1,0:T(8,128)(2,1)}, bf16[1024,128]{1,0:T(8,128)(2,1)}, f32[2,1024]{1,0:T(2,128)}) custom-call(s32[2,4]{1,0:T(2,128)} %pad_add_fusion.windows, bf16[1024,1024]{1,0:T(8,128)(2,1)} %bitcast.383, bf16[1024,384]{1,0:T(8,128)(2,1)} %collective-permute-done.7.w_ref, ...), custom_call_target="tpu_custom_call" | custom-call | flops 2483027968 | bytes 3950080 | tf_op jit(solution)/shard_map/attend/pallas_call | solution.py:194
  195.2 38.8 %collective-permute-done.33 = bf16[1,1,1024,256]{3,2,1,0:T(8,128)(2,1)} collective-permute-done((bf16[1,1,1024,256]{3,2,1,0:T(8,128)(2,1)S(1)}, bf16[1,1,1024,256]{3,2,1,0:T(8,128)(2,1)}, u32[]{:S(2)}, u32[]{:S(2)}) %collective-permute-start.33) | collective-permute-done | bytes 524320 | tf_op jit(solution)/shard_map/ppermute | solution.py:49
  246.3 4.9 ffn_in.4
  251.2 5.0 ffn_in.5
  256.2 5.1 ffn_in.7
  261.3 4.5 fusion.77
  265.8 5.0 ffn_in.6
  294.0 14.1 %collective-permute-done.32 = bf16[1,1,1024,256]{3,2,1,0:T(8,128)(2,1)} collective-permute-done((bf16[1,1,1024,256]{3,2,1,0:T(8,128)(2,1)}, bf16[1,1,1024,256]{3,2,1,0:T(8,128)(2,1)}, u32[]{:S(2)}, u32[]{:S(2)}) %collective-permute-start.32) | collective-permute-done | bytes 524320 | tf_op jit(solution)/shard_map/ppermute | solution.py:49
  322.4 4.4 ffn_back.5
  326.8 4.4 convolution_convert_fusion.5
  331.2 3.3 fusion.81
  334.5 4.5 ffn_back.7
  339.0 4.3 convolution_convert_fusion.4
  343.3 3.3 fusion.82
  356.3 4.4 ffn_back.4
  360.6 4.9 fusion.80
  365.5 4.4 ffn_back.6
  369.9 6.7 %add_add_fusion.1 = f32[1024,1024]{1,0:T(8,128)S(1)} fusion(f32[1024,1024]{1,0:T(8,128)} %fusion.82, f32[1024,1024]{1,0:T(8,128)} %fusion.80, f32[1024,1024]{1,0:T(8,128)} %fusion.81, bf16[1024,512]{1,0:T(8,128)(2,1)} %get-tuple-element.91, bf16[1024,512]{1,0:T(8,128)(2,1)} %collective-permute-done.28.w_ref), kind=kOutput, calls=%fused_computation.1 | convolution fusion | flops 1076887552 | bytes 18874368 | tf_op jit(solution)/shard_map/dot_general | solution.py:24
  394.0 7.7 %collective-permute-done.61 = bf16[2,2,2,1,128,512]{5,4,2,1,3,0:T(8,128)(2,1)} collective-permute-done((bf16[2,2,2,1,128,512]{5,4,2,1,3,0:T(8,128)(2,1)}, bf16[2,2,2,1,128,512]{5,4,2,1,3,0:T(8,128)(2,1)}, u32[]{:S(2)}, u32[]{:S(2)}) %collective-permute-start.61) | collective-permute-done | bytes 1048608 | tf_op jit(solution)/shard_map/ppermute | solution.py:49
  404.5 3.2 multiply_reduce_fusion.1
  417.5 13.2 %collective-permute-done.49 = f32[6,1,256]{2,1,0:T(1,128)S(1)} collective-permute-done((f32[6,1,256]{2,1,0:T(1,128)S(1)}, f32[6,1,256]{2,1,0:T(1,128)S(1)}, u32[]{:S(2)}, u32[]{:S(2)}) %collective-permute-start.49) | collective-permute-done | bytes 6176 | tf_op jit(solution)/shard_map/ppermute | solution.py:49
  447.0 10.2 %attend_back.5 = (bf16[1024,384]{1,0:T(8,128)(2,1)}, f32[2,128]{1,0:T(2,128)}) custom-call(s32[2,4]{1,0:T(2,128)} %pad_add_fusion.windows, bf16[1024,1024]{1,0:T(8,128)(2,1)} %bitcast.354, bf16[1024,128]{1,0:T(8,128)(2,1)} %bitcast.455, bf16[1024,128]{1,0:T(8,128)(2,1)} %get-tuple-element.99.q_ref, bf16[1024,128]{1,0:T(8,128)(2,1)} %get-tuple-element.100.k_ref, ...), custom_call_target="tpu_custom_call" | custom-call | flops 3623878656 | bytes 3949568 | tf_op jit(solution)/shard_map/attend_back/pallas_call | solution.py:194
  457.2 3.5 convolution_convert_fusion.9
  460.7 3.3 fusion.84
  463.9 10.3 %attend_back.4 = (bf16[1024,384]{1,0:T(8,128)(2,1)}, f32[2,128]{1,0:T(2,128)}) custom-call(s32[2,4]{1,0:T(2,128)} %pad_add_fusion.windows, bf16[1024,1024]{1,0:T(8,128)(2,1)} %bitcast.355, bf16[1024,128]{1,0:T(8,128)(2,1)} %bitcast.17.wo_ref, bf16[1024,128]{1,0:T(8,128)(2,1)} %get-tuple-element.94.q_ref, bf16[1024,128]{1,0:T(8,128)(2,1)} %get-tuple-element.95.k_ref, ...), custom_call_target="tpu_custom_call" | custom-call | flops 3623878656 | bytes 3949568 | tf_op jit(solution)/shard_map/attend_back/pallas_call | solution.py:194
  474.2 3.4 convolution_convert_fusion.11
  477.6 4.5 fusion.83
  482.1 10.0 %attend_back.7 = (bf16[1024,384]{1,0:T(8,128)(2,1)}, f32[2,128]{1,0:T(2,128)}) custom-call(s32[2,4]{1,0:T(2,128)} %pad_add_fusion.windows, bf16[1024,1024]{1,0:T(8,128)(2,1)} %bitcast.356, bf16[1024,128]{1,0:T(8,128)(2,1)} %bitcast.453, bf16[1024,128]{1,0:T(8,128)(2,1)} %get-tuple-element.109.q_ref, bf16[1024,128]{1,0:T(8,128)(2,1)} %get-tuple-element.110.k_ref, ...), custom_call_target="tpu_custom_call" | custom-call | flops 3623878656 | bytes 3949568 | tf_op jit(solution)/shard_map/attend_back/pallas_call | solution.py:194
  492.1 3.4 convolution_convert_fusion.8
  495.6 3.3 fusion.85
  501.8 10.2 %attend_back.6 = (bf16[1024,384]{1,0:T(8,128)(2,1)}, f32[2,128]{1,0:T(2,128)}) custom-call(s32[2,4]{1,0:T(2,128)} %pad_add_fusion.windows, bf16[1024,1024]{1,0:T(8,128)(2,1)} %bitcast.357, bf16[1024,128]{1,0:T(8,128)(2,1)} %collective-permute-done.14.wo_ref, bf16[1024,128]{1,0:T(8,128)(2,1)} %get-tuple-element.104.q_ref, ...), custom_call_target="tpu_custom_call" | custom-call | flops 3623878656 | bytes 3949568 | tf_op jit(solution)/shard_map/attend_back/pallas_call | solution.py:194
  515.7 8.5 %add_add_fusion = f32[1024,1024]{1,0:T(8,128)} fusion(f32[1024,1024]{1,0:T(8,128)} %fusion.85, f32[1024,1024]{1,0:T(8,128)} %fusion.83, f32[1024,1024]{1,0:T(8,128)} %fusion.84, bf16[1024,384]{1,0:T(8,128)(2,1)} %get-tuple-element.108, bf16[1024,384]{1,0:T(8,128)(2,1)} %collective-permute-done.7.w_ref), kind=kOutput, calls=%fused_computation | convolution fusion | flops 808452096 | bytes 18350080 | tf_op jit(solution)/shard_map/dot_general | solution.py:24
  528.4 3.4 convolution_convert_fusion.10
  545.6 5.2 collective-permute-done.52
  559.4 14.8 %collective-permute-done.70 = bf16[1,1,1,128,1024]{3,4,2,1,0:T(8,128)(2,1)} collective-permute-done((bf16[1,1,1,128,1024]{3,4,2,1,0:T(8,128)(2,1)}, bf16[1,1,1,128,1024]{3,4,2,1,0:T(8,128)(2,1)}, u32[]{:S(2)}, u32[]{:S(2)}) %collective-permute-start.70) | collective-permute-done | bytes 262176 | tf_op jit(solution)/shard_map/ppermute | solution.py:49
  586.3 3.0 collective-permute-done.57
  609.9 8.4 %collective-permute-done.45 = bf16[2,1,1,128,768]{3,4,2,1,0:T(8,128)(2,1)S(1)} collective-permute-done((bf16[2,1,1,128,768]{3,4,2,1,0:T(8,128)(2,1)S(1)}, bf16[2,1,1,128,768]{3,4,2,1,0:T(8,128)(2,1)S(1)}, u32[]{:S(2)}, u32[]{:S(2)}) %collective-permute-start.45) | collective-permute-done | bytes 393248 | tf_op jit(solution)/shard_map/ppermute | solution.py:49
  621.6 8.6 %collective-permute-done.46 = bf16[1,1,1,128,768]{3,4,2,1,0:T(8,128)(2,1)S(1)} collective-permute-done((bf16[1,1,1,128,768]{3,4,2,1,0:T(8,128)(2,1)S(1)}, bf16[1,1,1,128,768]{3,4,2,1,0:T(8,128)(2,1)S(1)}, u32[]{:S(2)}, u32[]{:S(2)}) %collective-permute-start.46) | collective-permute-done | bytes 196640 | tf_op jit(solution)/shard_map/ppermute | solution.py:49
  (611 shorter events, 270.0 us)
Async XLA Ops:
  2.0 35.0 %collective-permute-start.2 = (bf16[1,1,1,128,768]{3,4,2,1,0:T(8,128)(2,1)S(1)}, bf16[1,1,1,128,768]{3,4,2,1,0:T(8,128)(2,1)S(1)}, u32[]{:S(2)}, u32[]{:S(2)}) collective-permute-start(bf16[1,1,1,128,768]{3,4,2,1,0:T(8,128)(2,1)S(1)} %bitcast.449), channel_id=1, source_target_pairs={{0,16},{4,20},{8,24},{12,28},{16,0},{20,4},{24,8},{28,12},{1,17},{... | collective-permute-start | bytes 589832 | tf_op jit(solution)/shard_map/ppermute | solution.py:49
  6.1 21.1 %collective-permute-start.9 = (bf16[1,1,1,128,256]{3,4,2,1,0:T(8,128)(2,1)}, bf16[1,1,1,128,256]{3,4,2,1,0:T(8,128)(2,1)S(1)}, u32[]{:S(2)}, u32[]{:S(2)}) collective-permute-start(bf16[1,1,1,128,256]{3,4,2,1,0:T(8,128)(2,1)} %bitcast.466), channel_id=1, source_target_pairs={{0,16},{4,20},{8,24},{12,28},{16,0},{20,4},{24,8},{28,12},{1,17},{... | collective-permute-start | bytes 196616 | tf_op jit(solution)/shard_map/ppermute | solution.py:49
  7.3 32.4 %collective-permute-start.18 = (bf16[1,1,1,128,1024]{3,4,1,0,2:T(8,128)(2,1)S(1)}, bf16[1,1,1,128,1024]{3,4,1,0,2:T(8,128)(2,1)S(1)}, u32[]{:S(2)}, u32[]{:S(2)}) collective-permute-start(bf16[1,1,1,128,1024]{3,4,1,0,2:T(8,128)(2,1)S(1)} %bitcast.438), channel_id=1, source_target_pairs={{0,16},{4,20},{8,24},{12,28},{16,0},{20,4},{24,8},{28,12},{1,17},{... | collective-permute-start | bytes 786440 | tf_op jit(solution)/shard_map/ppermute | solution.py:49
  11.3 31.1 %collective-permute-start = (bf16[1,1,1024,256]{3,2,1,0:T(8,128)(2,1)S(1)}, bf16[1,1,1024,256]{3,2,1,0:T(8,128)(2,1)}, u32[]{:S(2)}, u32[]{:S(2)}) collective-permute-start(bf16[1,1,1024,256]{3,2,1,0:T(8,128)(2,1)S(1)} %constant_dynamic-slice_fusion.23), channel_id=1, source_target_pairs={{0,2},{1,3},{2,0},{3,1},{4,6},{5,7},{6,4},{7,5},{8,10},{9,11},{10,... | collective-permute-start | bytes 1572872 | tf_op jit(solution)/shard_map/ppermute | solution.py:49
  26.8 15.4 %collective-permute-start.21 = (bf16[1,1,1,128,1024]{3,4,1,0,2:T(8,128)(2,1)S(1)}, bf16[1,1,1,128,1024]{3,4,1,0,2:T(8,128)(2,1)S(1)}, u32[]{:S(2)}, u32[]{:S(2)}) collective-permute-start(bf16[1,1,1,128,1024]{3,4,1,0,2:T(8,128)(2,1)S(1)} %bitcast.443), channel_id=1, source_target_pairs={{0,16},{4,20},{8,24},{12,28},{16,0},{20,4},{24,8},{28,12},{1,17},{... | collective-permute-start | bytes 786440 | tf_op jit(solution)/shard_map/ppermute | solution.py:49
  39.8 22.0 %collective-permute-start.19 = (bf16[2,1,1,128,1024]{3,4,1,0,2:T(8,128)(2,1)S(1)}, bf16[2,1,1,128,1024]{3,4,1,0,2:T(8,128)(2,1)S(1)}, u32[]{:S(2)}, u32[]{:S(2)}) collective-permute-start(bf16[2,1,1,128,1024]{3,4,1,0,2:T(8,128)(2,1)S(1)} %pad_maximum_fusion.21), channel_id=1, source_target_pairs={{0,8},{4,12},{8,0},{12,4},{16,24},{20,28},{24,16},{28,20},{1,9},{5... | collective-permute-start | bytes 1572872 | tf_op jit(solution)/shard_map/ppermute | solution.py:49
  42.3 30.7 %collective-permute-start.22 = (bf16[2,1,1,128,1024]{3,4,1,0,2:T(8,128)(2,1)S(1)}, bf16[2,1,1,128,1024]{3,4,1,0,2:T(8,128)(2,1)S(1)}, u32[]{:S(2)}, u32[]{:S(2)}) collective-permute-start(bf16[2,1,1,128,1024]{3,4,1,0,2:T(8,128)(2,1)S(1)} %fusion.51), channel_id=1, source_target_pairs={{0,8},{4,12},{8,0},{12,4},{16,24},{20,28},{24,16},{28,20},{1,9},{5... | collective-permute-start | bytes 1572872 | tf_op jit(solution)/shard_map/ppermute | solution.py:49
  44.6 70.1 %collective-permute-start.1 = (bf16[2,1,1024,256]{3,2,1,0:T(8,128)(2,1)}, bf16[2,1,1024,256]{3,2,1,0:T(8,128)(2,1)}, u32[]{:S(2)}, u32[]{:S(2)}) collective-permute-start(bf16[2,1,1024,256]{3,2,1,0:T(8,128)(2,1)} %maximum_bitcast_fusion), channel_id=1, source_target_pairs={{0,1},{1,0},{2,3},{3,2},{4,5},{5,4},{6,7},{7,6},{8,9},{9,8},{10,11... | collective-permute-start | bytes 3145736 | tf_op jit(solution)/shard_map/ppermute | solution.py:49
  50.7 26.6 %collective-permute-start.5 = (bf16[1,2,2,1,128,384]{4,5,2,1,3,0:T(8,128)(2,1)S(1)}, bf16[1,2,2,1,128,384]{4,5,2,1,3,0:T(8,128)(2,1)}, u32[]{:S(2)}, u32[]{:S(2)}) collective-permute-start(bf16[1,2,2,1,128,384]{4,5,2,1,3,0:T(8,128)(2,1)S(1)} %get-tuple-element.265), channel_id=1, source_target_pairs={{0,2},{1,3},{2,0},{3,1},{4,6},{5,7},{6,4},{7,5},{8,10},{9,11},{10,... | collective-permute-start | bytes 1179656 | tf_op jit(solution)/shard_map/ppermute | solution.py:49
  52.3 21.7 %collective-permute-start.4 = (bf16[2,2,1,128,384]{3,4,2,1,0:T(8,128)(2,1)S(1)}, bf16[2,2,1,128,384]{3,4,2,1,0:T(8,128)(2,1)S(1)}, u32[]{:S(2)}, u32[]{:S(2)}) collective-permute-start(bf16[2,2,1,128,384]{3,4,2,1,0:T(8,128)(2,1)S(1)} %get-tuple-element.264), channel_id=1, source_target_pairs={{0,4},{4,0},{8,12},{12,8},{16,20},{20,16},{24,28},{28,24},{1,5},{5... | collective-permute-start | bytes 1179656 | tf_op jit(solution)/shard_map/ppermute | solution.py:49
  83.4 51.8 %collective-permute-start.6 = (bf16[2,2,2,1,128,384]{4,5,2,1,3,0:T(8,128)(2,1)}, bf16[2,2,2,1,128,384]{4,5,2,1,3,0:T(8,128)(2,1)}, u32[]{:S(2)}, u32[]{:S(2)}) collective-permute-start(bf16[2,2,2,1,128,384]{4,5,2,1,3,0:T(8,128)(2,1)} %pad_maximum_fusion.20), channel_id=1, source_target_pairs={{0,4},{4,0},{8,12},{12,8},{16,20},{20,16},{24,28},{28,24},{1,5},{5... | collective-permute-start | bytes 2359304 | tf_op jit(solution)/shard_map/ppermute | solution.py:49
  83.9 76.6 %collective-permute-start.7 = (bf16[1024,384]{1,0:T(8,128)(2,1)}, bf16[1024,384]{1,0:T(8,128)(2,1)}, u32[]{:S(2)}, u32[]{:S(2)}) collective-permute-start(bf16[1024,384]{1,0:T(8,128)(2,1)} %bitcast.10.w_ref), channel_id=1, source_target_pairs={{0,2},{1,3},{2,0},{3,1},{4,6},{5,7},{6,4},{7,5},{8,10},{9,11},{10,... | collective-permute-start | bytes 2359304 | tf_op jit(solution)/shard_map/ppermute | solution.py:49
  86.6 22.1 %collective-permute-start.13 = (bf16[2,2,2,1,128,128]{4,5,2,1,3,0:T(8,128)(2,1)}, bf16[2,2,2,1,128,128]{4,5,2,1,3,0:T(8,128)(2,1)}, u32[]{:S(2)}, u32[]{:S(2)}) collective-permute-start(bf16[2,2,2,1,128,128]{4,5,2,1,3,0:T(8,128)(2,1)} %pad_maximum_fusion.27), channel_id=1, source_target_pairs={{0,4},{4,0},{8,12},{12,8},{16,20},{20,16},{24,28},{28,24},{1,5},{5... | collective-permute-start | bytes 786440 | tf_op jit(solution)/shard_map/ppermute | solution.py:49
  89.1 81.3 %collective-permute-start.14 = (bf16[1024,128]{1,0:T(8,128)(2,1)}, bf16[1024,128]{1,0:T(8,128)(2,1)}, u32[]{:S(2)}, u32[]{:S(2)}) collective-permute-start(bf16[1024,128]{1,0:T(8,128)(2,1)} %bitcast.17.wo_ref), channel_id=1, source_target_pairs={{0,2},{1,3},{2,0},{3,1},{4,6},{5,7},{6,4},{7,5},{8,10},{9,11},{10,... | collective-permute-start | bytes 786440 | tf_op jit(solution)/shard_map/ppermute | solution.py:49
  108.7 20.8 %collective-permute-start.23 = (bf16[1,2,2,1,128,512]{4,5,2,1,3,0:T(8,128)(2,1)S(1)}, bf16[1,2,2,1,128,512]{4,5,2,1,3,0:T(8,128)(2,1)S(1)}, u32[]{:S(2)}, u32[]{:S(2)}) collective-permute-start(bf16[1,2,2,1,128,512]{4,5,2,1,3,0:T(8,128)(2,1)S(1)} %bitcast.389), channel_id=1, source_target_pairs={{0,2},{1,3},{2,0},{3,1},{4,6},{5,7},{6,4},{7,5},{8,10},{9,11},{10,... | collective-permute-start | bytes 1572872 | tf_op jit(solution)/shard_map/ppermute | solution.py:49
  114.7 16.5 %collective-permute-start.20 = (bf16[2,2,1,128,512]{3,4,1,0,2:T(8,128)(2,1)S(1)}, bf16[2,2,1,128,512]{3,4,1,0,2:T(8,128)(2,1)}, u32[]{:S(2)}, u32[]{:S(2)}) collective-permute-start(bf16[2,2,1,128,512]{3,4,1,0,2:T(8,128)(2,1)S(1)} %copy-done.49), channel_id=1, source_target_pairs={{0,4},{4,0},{8,12},{12,8},{16,20},{20,16},{24,28},{28,24},{1,5},{5... | collective-permute-start | bytes 1572872 | tf_op jit(solution)/shard_map/ppermute | solution.py:49
  130.8 52.0 %collective-permute-start.25 = (bf16[2,2,2,1,128,512]{4,5,2,1,3,0:T(8,128)(2,1)}, bf16[2,2,2,1,128,512]{4,5,2,1,3,0:T(8,128)(2,1)}, u32[]{:S(2)}, u32[]{:S(2)}) collective-permute-start(bf16[2,2,2,1,128,512]{4,5,2,1,3,0:T(8,128)(2,1)} %pad_maximum_fusion.9), channel_id=1, source_target_pairs={{0,4},{4,0},{8,12},{12,8},{16,20},{20,16},{24,28},{28,24},{1,5},{5... | collective-permute-start | bytes 3145736 | tf_op jit(solution)/shard_map/ppermute | solution.py:49
  133.8 40.8 %collective-permute-start.26 = (bf16[1,2,2,1,128,512]{4,5,2,1,3,0:T(8,128)(2,1)S(1)}, bf16[1,2,2,1,128,512]{4,5,2,1,3,0:T(8,128)(2,1)}, u32[]{:S(2)}, u32[]{:S(2)}) collective-permute-start(bf16[1,2,2,1,128,512]{4,5,2,1,3,0:T(8,128)(2,1)S(1)} %bitcast.377), channel_id=1, source_target_pairs={{0,2},{1,3},{2,0},{3,1},{4,6},{5,7},{6,4},{7,5},{8,10},{9,11},{10,... | collective-permute-start | bytes 1572872 | tf_op jit(solution)/shard_map/ppermute | solution.py:49
  135.2 42.1 %collective-permute-start.24 = (bf16[2,2,1,128,512]{3,4,1,0,2:T(8,128)(2,1)S(1)}, bf16[2,2,1,128,512]{3,4,1,0,2:T(8,128)(2,1)}, u32[]{:S(2)}, u32[]{:S(2)}) collective-permute-start(bf16[2,2,1,128,512]{3,4,1,0,2:T(8,128)(2,1)S(1)} %copy-done.43), channel_id=1, source_target_pairs={{0,4},{4,0},{8,12},{12,8},{16,20},{20,16},{24,28},{28,24},{1,5},{5... | collective-permute-start | bytes 1572872 | tf_op jit(solution)/shard_map/ppermute | solution.py:49
  174.3 91.5 %collective-permute-start.28 = (bf16[1024,512]{1,0:T(8,128)(2,1)}, bf16[1024,512]{1,0:T(8,128)(2,1)}, u32[]{:S(2)}, u32[]{:S(2)}) collective-permute-start(bf16[1024,512]{1,0:T(8,128)(2,1)} %bitcast.30.w_ref), channel_id=1, source_target_pairs={{0,2},{1,3},{2,0},{3,1},{4,6},{5,7},{6,4},{7,5},{8,10},{9,11},{10,... | collective-permute-start | bytes 3145736 | tf_op jit(solution)/shard_map/ppermute | solution.py:49
  176.8 59.7 %collective-permute-start.27 = (bf16[2,2,2,1,128,512]{4,5,2,1,3,0:T(8,128)(2,1)}, bf16[2,2,2,1,128,512]{4,5,2,1,3,0:T(8,128)(2,1)}, u32[]{:S(2)}, u32[]{:S(2)}) collective-permute-start(bf16[2,2,2,1,128,512]{4,5,2,1,3,0:T(8,128)(2,1)} %pad_maximum_fusion.11), channel_id=1, source_target_pairs={{0,4},{4,0},{8,12},{12,8},{16,20},{20,16},{24,28},{28,24},{1,5},{5... | collective-permute-start | bytes 3145736 | tf_op jit(solution)/shard_map/ppermute | solution.py:49
  179.9 94.9 %collective-permute-start.29 = (bf16[1024,512]{1,0:T(8,128)(2,1)}, bf16[1024,512]{1,0:T(8,128)(2,1)}, u32[]{:S(2)}, u32[]{:S(2)}) collective-permute-start(bf16[1024,512]{1,0:T(8,128)(2,1)} %bitcast.399), channel_id=1, source_target_pairs={{0,2},{1,3},{2,0},{3,1},{4,6},{5,7},{6,4},{7,5},{8,10},{9,11},{10,... | collective-permute-start | bytes 3145736 | tf_op jit(solution)/shard_map/ppermute | solution.py:49
  182.7 51.2 %collective-permute-start.33 = (bf16[1,1,1024,256]{3,2,1,0:T(8,128)(2,1)S(1)}, bf16[1,1,1024,256]{3,2,1,0:T(8,128)(2,1)}, u32[]{:S(2)}, u32[]{:S(2)}) collective-permute-start(bf16[1,1,1024,256]{3,2,1,0:T(8,128)(2,1)S(1)} %constant_dynamic-slice_fusion.19), channel_id=1, source_target_pairs={{0,2},{1,3},{2,0},{3,1},{4,6},{5,7},{6,4},{7,5},{8,10},{9,11},{10,... | collective-permute-start | bytes 1572872 | tf_op jit(solution)/shard_map/ppermute | solution.py:49
  188.9 54.0 %collective-permute-start.17 = (bf16[1,512,1024]{2,1,0:T(8,128)(2,1)}, bf16[1,512,1024]{2,1,0:T(8,128)(2,1)}, u32[]{:S(2)}, u32[]{:S(2)}) collective-permute-start(bf16[1,512,1024]{2,1,0:T(8,128)(2,1)} %fusion.9), channel_id=1, source_target_pairs={{0,1},{1,0},{2,3},{3,2},{4,5},{5,4},{6,7},{7,6},{8,9},{9,8},{10,11... | collective-permute-start | bytes 3145736 | tf_op jit(solution)/shard_map/ppermute | solution.py:49
  236.2 42.9 %collective-permute-start.34 = (bf16[2,1,1,512,256]{4,3,2,0,1:T(8,128)(2,1)}, bf16[2,1,1,512,256]{4,3,2,0,1:T(8,128)(2,1)}, u32[]{:S(2)}, u32[]{:S(2)}) collective-permute-start(bf16[2,1,1,512,256]{4,3,2,0,1:T(8,128)(2,1)} %constant_dynamic-slice_fusion.18), channel_id=1, source_target_pairs={{0,1},{1,0},{2,3},{3,2},{4,5},{5,4},{6,7},{7,6},{8,9},{9,8},{10,11... | collective-permute-start | bytes 1572872 | tf_op jit(solution)/shard_map/ppermute | solution.py:49
  292.2 18.2 %collective-permute-start.35 = (bf16[1,512,1024]{2,1,0:T(8,128)(2,1)}, bf16[1,512,1024]{2,1,0:T(8,128)(2,1)}, u32[]{:S(2)}, u32[]{:S(2)}) collective-permute-start(bf16[1,512,1024]{2,1,0:T(8,128)(2,1)} %convert_bitcast_fusion.1), channel_id=1, source_target_pairs={{0,1},{1,0},{2,3},{3,2},{4,5},{5,4},{6,7},{7,6},{8,9},{9,8},{10,11... | collective-permute-start | bytes 3145736 | tf_op jit(solution)/shard_map/ppermute | solution.py:49
  352.9 33.1 %collective-permute-start.67 = (bf16[2,2,2,1,128,512]{4,5,2,1,3,0:T(8,128)(2,1)}, bf16[2,2,2,1,128,512]{4,5,2,1,3,0:T(8,128)(2,1)}, u32[]{:S(2)}, u32[]{:S(2)}) collective-permute-start(bf16[2,2,2,1,128,512]{4,5,2,1,3,0:T(8,128)(2,1)} %fusion.12), channel_id=1, source_target_pairs={{0,4},{4,0},{8,12},{12,8},{16,20},{20,16},{24,28},{28,24},{1,5},{5... | collective-permute-start | bytes 3145736 | tf_op jit(solution)/shard_map/ppermute | solution.py:49
  353.4 35.4 %collective-permute-start.65 = (bf16[1024,512]{1,0:T(8,128)(2,1)}, bf16[1024,512]{1,0:T(8,128)(2,1)}, u32[]{:S(2)}, u32[]{:S(2)}) collective-permute-start(bf16[1024,512]{1,0:T(8,128)(2,1)} %convolution_convert_fusion.2), channel_id=1, source_target_pairs={{0,2},{1,3},{2,0},{3,1},{4,6},{5,7},{6,4},{7,5},{8,10},{9,11},{10,... | collective-permute-start | bytes 3145736 | tf_op jit(solution)/shard_map/ppermute | solution.py:49
  354.8 46.9 %collective-permute-start.61 = (bf16[2,2,2,1,128,512]{5,4,2,1,3,0:T(8,128)(2,1)}, bf16[2,2,2,1,128,512]{5,4,2,1,3,0:T(8,128)(2,1)}, u32[]{:S(2)}, u32[]{:S(2)}) collective-permute-start(bf16[2,2,2,1,128,512]{5,4,2,1,3,0:T(8,128)(2,1)} %fusion.15), channel_id=1, source_target_pairs={{0,4},{4,0},{8,12},{12,8},{16,20},{20,16},{24,28},{28,24},{1,5},{5... | collective-permute-start | bytes 3145736 | tf_op jit(solution)/shard_map/ppermute | solution.py:49
  377.7 26.8 %collective-permute-start.36 = (bf16[1,512,1024]{2,1,0:T(8,128)(2,1)}, bf16[1,512,1024]{2,1,0:T(8,128)(2,1)}, u32[]{:S(2)}, u32[]{:S(2)}) collective-permute-start(bf16[1,512,1024]{2,1,0:T(8,128)(2,1)} %dynamic-slice_convert_fusion.1), channel_id=1, source_target_pairs={{0,1},{1,0},{2,3},{3,2},{4,5},{5,4},{6,7},{7,6},{8,9},{9,8},{10,11... | collective-permute-start | bytes 3145736 | tf_op jit(solution)/shard_map/ppermute | solution.py:49
  384.2 26.3 %collective-permute-start.59 = (bf16[1024,512]{1,0:T(8,128)(2,1)}, bf16[1024,512]{1,0:T(8,128)(2,1)}, u32[]{:S(2)}, u32[]{:S(2)}) collective-permute-start(bf16[1024,512]{1,0:T(8,128)(2,1)} %convolution_convert_fusion.6), channel_id=1, source_target_pairs={{0,2},{1,3},{2,0},{3,1},{4,6},{5,7},{6,4},{7,5},{8,10},{9,11},{10,... | collective-permute-start | bytes 3145736 | tf_op jit(solution)/shard_map/ppermute | solution.py:49
  388.4 42.4 %collective-permute-start.68 = (bf16[1,2,2,1,128,512]{4,5,2,1,3,0:T(8,128)(2,1)}, bf16[1,2,2,1,128,512]{4,5,2,1,3,0:T(8,128)(2,1)}, u32[]{:S(2)}, u32[]{:S(2)}) collective-permute-start(bf16[1,2,2,1,128,512]{4,5,2,1,3,0:T(8,128)(2,1)} %slice.330), channel_id=1, source_target_pairs={{0,2},{1,3},{2,0},{3,1},{4,6},{5,7},{6,4},{7,5},{8,10},{9,11},{10,... | collective-permute-start | bytes 1572872 | tf_op jit(solution)/shard_map/ppermute | solution.py:49
  393.5 38.8 %collective-permute-start.66 = (bf16[2,2,1,128,512]{3,4,2,1,0:T(8,128)(2,1)}, bf16[2,2,1,128,512]{3,4,2,1,0:T(8,128)(2,1)}, u32[]{:S(2)}, u32[]{:S(2)}) collective-permute-start(bf16[2,2,1,128,512]{3,4,2,1,0:T(8,128)(2,1)} %copy.352), channel_id=1, source_target_pairs={{0,4},{4,0},{8,12},{12,8},{16,20},{20,16},{24,28},{28,24},{1,5},{5... | collective-permute-start | bytes 1572872 | tf_op jit(solution)/shard_map/ppermute | solution.py:49
  404.2 31.6 %collective-permute-start.62 = (bf16[1,2,2,1,128,512]{5,4,2,1,3,0:T(8,128)(2,1)}, bf16[1,2,2,1,128,512]{5,4,2,1,3,0:T(8,128)(2,1)}, u32[]{:S(2)}, u32[]{:S(2)}) collective-permute-start(bf16[1,2,2,1,128,512]{5,4,2,1,3,0:T(8,128)(2,1)} %slice.327), channel_id=1, source_target_pairs={{0,2},{1,3},{2,0},{3,1},{4,6},{5,7},{6,4},{7,5},{8,10},{9,11},{10,... | collective-permute-start | bytes 1572872 | tf_op jit(solution)/shard_map/ppermute | solution.py:49
  413.0 21.7 %collective-permute-start.60 = (bf16[2,2,1,128,512]{4,3,2,1,0:T(8,128)(2,1)}, bf16[2,2,1,128,512]{4,3,2,1,0:T(8,128)(2,1)}, u32[]{:S(2)}, u32[]{:S(2)}) collective-permute-start(bf16[2,2,1,128,512]{4,3,2,1,0:T(8,128)(2,1)} %constant_dynamic-slice_fusion.4), channel_id=1, source_target_pairs={{0,4},{4,0},{8,12},{12,8},{16,20},{20,16},{24,28},{28,24},{1,5},{5... | collective-permute-start | bytes 1572872 | tf_op jit(solution)/shard_map/ppermute | solution.py:49
  413.5 17.2 %collective-permute-start.49 = (f32[6,1,256]{2,1,0:T(1,128)S(1)}, f32[6,1,256]{2,1,0:T(1,128)S(1)}, u32[]{:S(2)}, u32[]{:S(2)}) collective-permute-start(f32[6,1,256]{2,1,0:T(1,128)S(1)} %fusion.68), channel_id=1, source_target_pairs={{0,2},{1,3},{2,0},{3,1},{4,6},{5,7},{6,4},{7,5},{8,10},{9,11},{10,... | collective-permute-start | bytes 18440 | tf_op jit(solution)/shard_map/ppermute | solution.py:49
  434.6 97.1 %collective-permute-start.69 = (bf16[2,1,1,128,1024]{3,4,2,1,0:T(8,128)(2,1)}, bf16[2,1,1,128,1024]{3,4,2,1,0:T(8,128)(2,1)}, u32[]{:S(2)}, u32[]{:S(2)}) collective-permute-start(bf16[2,1,1,128,1024]{3,4,2,1,0:T(8,128)(2,1)} %fusion.38), channel_id=1, source_target_pairs={{0,8},{4,12},{8,0},{12,4},{16,24},{20,28},{24,16},{28,20},{1,9},{5... | collective-permute-start | bytes 1572872 | tf_op jit(solution)/shard_map/ppermute | solution.py:49
  438.1 97.9 %collective-permute-start.63 = (bf16[2,1,1,128,1024]{4,3,2,1,0:T(8,128)(2,1)}, bf16[2,1,1,128,1024]{4,3,2,1,0:T(8,128)(2,1)}, u32[]{:S(2)}, u32[]{:S(2)}) collective-permute-start(bf16[2,1,1,128,1024]{4,3,2,1,0:T(8,128)(2,1)} %fusion.40), channel_id=1, source_target_pairs={{0,8},{4,12},{8,0},{12,4},{16,24},{20,28},{24,16},{28,20},{1,9},{5... | collective-permute-start | bytes 1572872 | tf_op jit(solution)/shard_map/ppermute | solution.py:49
  500.1 56.2 %collective-permute-start.55 = (bf16[2,2,2,1,128,128]{4,5,2,1,3,0:T(8,128)(2,1)}, bf16[2,2,2,1,128,128]{4,5,2,1,3,0:T(8,128)(2,1)}, u32[]{:S(2)}, u32[]{:S(2)}) collective-permute-start(bf16[2,2,2,1,128,128]{4,5,2,1,3,0:T(8,128)(2,1)} %fusion.56), channel_id=1, source_target_pairs={{0,4},{4,0},{8,12},{12,8},{16,20},{20,16},{24,28},{28,24},{1,5},{5... | collective-permute-start | bytes 786440 | tf_op jit(solution)/shard_map/ppermute | solution.py:49
  500.6 52.0 %collective-permute-start.53 = (bf16[1024,128]{1,0:T(8,128)(2,1)}, bf16[1024,128]{1,0:T(8,128)(2,1)}, u32[]{:S(2)}, u32[]{:S(2)}) collective-permute-start(bf16[1024,128]{1,0:T(8,128)(2,1)} %convolution_convert_fusion.14), channel_id=1, source_target_pairs={{0,2},{1,3},{2,0},{3,1},{4,6},{5,7},{6,4},{7,5},{8,10},{9,11},{10,... | collective-permute-start | bytes 786440 | tf_op jit(solution)/shard_map/ppermute | solution.py:49
  513.0 21.5 %collective-permute-start.47 = (f32[1536]{0:T(1024)S(1)}, f32[1536]{0:T(1024)S(1)}, u32[]{:S(2)}, u32[]{:S(2)}) collective-permute-start(f32[1536]{0:T(1024)S(1)} %pad_maximum_fusion.32), channel_id=1, source_target_pairs={{0,2},{1,3},{2,0},{3,1},{4,6},{5,7},{6,4},{7,5},{8,10},{9,11},{10,... | collective-permute-start | bytes 18440 | tf_op jit(solution)/shard_map/ppermute | solution.py:49
  531.8 59.7 %collective-permute-start.43 = (bf16[2,2,2,1,128,384]{4,5,2,1,3,0:T(8,128)(2,1)}, bf16[2,2,2,1,128,384]{4,5,2,1,3,0:T(8,128)(2,1)}, u32[]{:S(2)}, u32[]{:S(2)}) collective-permute-start(bf16[2,2,2,1,128,384]{4,5,2,1,3,0:T(8,128)(2,1)} %fusion.34), channel_id=1, source_target_pairs={{0,4},{4,0},{8,12},{12,8},{16,20},{20,16},{24,28},{28,24},{1,5},{5... | collective-permute-start | bytes 2359304 | tf_op jit(solution)/shard_map/ppermute | solution.py:49
  534.6 60.0 %collective-permute-start.41 = (bf16[1024,384]{1,0:T(8,128)(2,1)}, bf16[1024,384]{1,0:T(8,128)(2,1)}, u32[]{:S(2)}, u32[]{:S(2)}) collective-permute-start(bf16[1024,384]{1,0:T(8,128)(2,1)} %convolution_convert_fusion.10), channel_id=1, source_target_pairs={{0,2},{1,3},{2,0},{3,1},{4,6},{5,7},{6,4},{7,5},{8,10},{9,11},{10,... | collective-permute-start | bytes 2359304 | tf_op jit(solution)/shard_map/ppermute | solution.py:49
  550.8 47.4 %collective-permute-start.38 = (bf16[1,512,1024]{2,1,0:T(8,128)(2,1)}, bf16[1,512,1024]{2,1,0:T(8,128)(2,1)}, u32[]{:S(2)}, u32[]{:S(2)}) collective-permute-start(bf16[1,512,1024]{2,1,0:T(8,128)(2,1)} %dynamic-slice_convert_fusion), channel_id=1, source_target_pairs={{0,1},{1,0},{2,3},{3,2},{4,5},{5,4},{6,7},{7,6},{8,9},{9,8},{10,11... | collective-permute-start | bytes 3145736 | tf_op jit(solution)/shard_map/ppermute | solution.py:49
  552.6 21.6 %collective-permute-start.70 = (bf16[1,1,1,128,1024]{3,4,2,1,0:T(8,128)(2,1)}, bf16[1,1,1,128,1024]{3,4,2,1,0:T(8,128)(2,1)}, u32[]{:S(2)}, u32[]{:S(2)}) collective-permute-start(bf16[1,1,1,128,1024]{3,4,2,1,0:T(8,128)(2,1)} %constant_dynamic-slice_fusion), channel_id=1, source_target_pairs={{0,16},{4,20},{8,24},{12,28},{16,0},{20,4},{24,8},{28,12},{1,17},{... | collective-permute-start | bytes 786440 | tf_op jit(solution)/shard_map/ppermute | solution.py:49
  556.3 28.1 %collective-permute-start.64 = (bf16[1,1,1,128,1024]{4,3,2,1,0:T(8,128)(2,1)}, bf16[1,1,1,128,1024]{4,3,2,1,0:T(8,128)(2,1)}, u32[]{:S(2)}, u32[]{:S(2)}) collective-permute-start(bf16[1,1,1,128,1024]{4,3,2,1,0:T(8,128)(2,1)} %constant_dynamic-slice_fusion.3), channel_id=1, source_target_pairs={{0,16},{4,20},{8,24},{12,28},{16,0},{20,4},{24,8},{28,12},{1,17},{... | collective-permute-start | bytes 786440 | tf_op jit(solution)/shard_map/ppermute | solution.py:49
  590.0 30.1 %collective-permute-start.58 = (bf16[1,1,1,128,256]{3,4,2,1,0:T(8,128)(2,1)}, bf16[1,1,1,128,256]{3,4,2,1,0:T(8,128)(2,1)}, u32[]{:S(2)}, u32[]{:S(2)}) collective-permute-start(bf16[1,1,1,128,256]{3,4,2,1,0:T(8,128)(2,1)} %constant_dynamic-slice_fusion.5), channel_id=1, source_target_pairs={{0,16},{4,20},{8,24},{12,28},{16,0},{20,4},{24,8},{28,12},{1,17},{... | collective-permute-start | bytes 196616 | tf_op jit(solution)/shard_map/ppermute | solution.py:49
  608.7 22.6 %collective-permute-start.40 = (bf16[1,1,1024,256]{3,2,1,0:T(8,128)(2,1)S(1)}, bf16[1,1,1024,256]{3,2,1,0:T(8,128)(2,1)S(1)}, u32[]{:S(2)}, u32[]{:S(2)}) collective-permute-start(bf16[1,1,1024,256]{3,2,1,0:T(8,128)(2,1)S(1)} %constant_dynamic-slice_fusion.15), channel_id=1, source_target_pairs={{0,2},{1,3},{2,0},{3,1},{4,6},{5,7},{6,4},{7,5},{8,10},{9,11},{10,... | collective-permute-start | bytes 1572872 | tf_op jit(solution)/shard_map/ppermute | solution.py:49
  (125 other events, 859.3 us)

commit v3 on v2

v3 whole, which is shorter than its diff:
```python
import functools
import math

import jax
import jax.numpy as jnp
from jax import lax
from jax.experimental import pallas as pl
from jax.experimental.pallas import tpu as pltpu
from jax.sharding import PartitionSpec as P

DH = 64
NORM_EPS = 1e-06
MASKED = -1000000000.0
LONGEST = 256
F32 = jnp.float32
BF16 = jnp.bfloat16


def nn(left, right):
    return lax.dot_general(left, right, (((1,), (0,)), ((), ())), preferred_element_type=F32)


def nt(left, right):
    return lax.dot_general(left, right, (((1,), (1,)), ((), ())), preferred_element_type=F32)


def tn(left, right):
    return lax.dot_general(left, right, (((0,), (0,)), ((), ())), preferred_element_type=F32)


def after(block, *others):
    return lax.optimization_barrier((block,) + others)[0]


def pick(block, bit, dim):
    return lax.dynamic_slice_in_dim(block, bit, 1, dim)


def bits_of(count):
    return [1 << b for b in reversed(range(count.bit_length() - 1))]


class Stage:
    def __init__(self, axis, count, mask, index):
        self.axis, self.pairs = axis, [(i, i ^ mask) for i in range(count)]
        self.bit = (index // mask) % 2

    def trade(self, block):
        return lax.ppermute(block, self.axis, self.pairs)

    def join(self, mine, other, dim):
        low = self.bit == 0
        return jnp.concatenate(
            (jnp.where(low, mine, other), jnp.where(low, other, mine)), axis=dim
        )

    def gather(self, block, dim):
        return self.join(block, self.trade(block), dim)

    def swap(self, block, split, dim):
        keep = pick(block, self.bit, split)
        return self.join(keep, self.trade(pick(block, 1 - self.bit, split)), dim)

    def reduce(self, block, dim):
        got = self.trade(pick(block, 1 - self.bit, dim))
        return add(pick(block, self.bit, dim), got)


def add(mine, other):
    return (mine.astype(F32) + other.astype(F32)).astype(mine.dtype)


def tiles_of(length):
    return min(256, length), min(128, length)


def key_windows(labels):
    rows, step = tiles_of(labels.shape[0])
    first, last = labels[::rows], labels[rows - 1 :: rows]
    start = jnp.sum(labels[None, :] < first[:, None], axis=1)
    stop = jnp.sum(labels[None, :] <= last[:, None], axis=1)
    block = start // step
    return jnp.stack((block, (stop - 1) // step + 1 - block)).astype(jnp.int32)


def for_each_block(windows, length, run):
    rows, step = tiles_of(length)
    reach = -(-(LONGEST - 1) // step)
    most = min(length // step, rows // step + 2 * reach)

    def one(i, carry):
        q0 = pl.multiple_of(i * rows, rows)
        k0 = pl.multiple_of(windows[0, i] * step, step)
        for n in range(1, most + 1):
            pl.when(windows[1, i] == n)(functools.partial(run, q0, k0, rows, n * step))
        return carry

    lax.fori_loop(0, length // rows, one, 0)


def attend_kernel(windows, q_ref, k_ref, v_ref, lab_col, lab_row, ctx_ref, lse_ref):
    length, lanes = q_ref.shape[1:]

    def run(q0, k0, rows, span):
        q = q_ref[0, pl.ds(q0, rows), :]
        k = k_ref[0, pl.ds(k0, span), :]
        v_t = v_ref[0, pl.ds(k0, span), :].T
        same = lab_col[pl.ds(k0, span), :] == lab_row[:, pl.ds(q0, rows)]
        head = lax.broadcasted_iota(jnp.int32, (span, lanes), 1) // DH
        outs = []
        for h in range(lanes // DH):
            scores = nt(jnp.where(head == h, k, jnp.zeros_like(k)), q)
            scores = jnp.where(same, scores, MASKED)
            top = jnp.max(scores, axis=0, keepdims=True)
            shifted = jnp.exp(scores - top)
            total = jnp.sum(shifted, axis=0, keepdims=True)
            outs.append(nn(v_t[h * DH : (h + 1) * DH, :], shifted.astype(BF16)) / total)
            lse_ref[0, h : h + 1, pl.ds(q0, rows)] = top + jnp.log(total)
        ctx_ref[0, pl.ds(q0, rows), :] = jnp.concatenate(outs, axis=0).T.astype(BF16)

    for_each_block(windows, length, run)


def attend_back_kernel(
    windows, q_ref, k_ref, v_ref, do_ref, lse_ref, lab_col, lab_row, gp_ref, sum_ref, dk_acc, dv_acc
):
    length, lanes = q_ref.shape[1:]
    scale = 1.0 / math.sqrt(DH)
    dk_acc[...] = jnp.zeros_like(dk_acc)
    dv_acc[...] = jnp.zeros_like(dv_acc)
    sum_ref[...] = jnp.zeros_like(sum_ref)

    def run(q0, k0, rows, span):
        q = q_ref[0, pl.ds(q0, rows), :]
        do = do_ref[0, pl.ds(q0, rows), :]
        k = k_ref[0, pl.ds(k0, span), :]
        v = v_ref[0, pl.ds(k0, span), :]
        k_t = k.T
        same = lab_col[pl.ds(k0, span), :] == lab_row[:, pl.ds(q0, rows)]
        head = lax.broadcasted_iota(jnp.int32, (span, lanes), 1) // DH
        head_q = lax.broadcasted_iota(jnp.int32, (rows, lanes), 1) // DH
        dqs = []
        dk = dv = None
        for h in range(lanes // DH):
            only = lambda a, own: jnp.where(own == h, a, jnp.zeros_like(a))
            scores = jnp.where(same, nt(only(k, head), q), MASKED)
            prob = jnp.exp(scores - lse_ref[0, h : h + 1, pl.ds(q0, rows)])
            weighted = prob * nt(only(v, head), do)
            row_dot = jnp.sum(weighted, axis=0, keepdims=True)
            dscore = (weighted - prob * row_dot).astype(BF16)
            dv_h = nn(prob.astype(BF16), only(do, head_q))
            dk_h = nn(dscore, only(q, head_q))
            dv = dv_h if dv is None else dv + dv_h
            dk = dk_h if dk is None else dk + dk_h
            dqs.append(nn(k_t[h * DH : (h + 1) * DH, :], dscore))
        dq = jnp.concatenate(dqs, axis=0).T * scale
        gp_ref[0, pl.ds(q0, rows), :lanes] = dq.astype(BF16)
        sum_ref[0, 0:1, :] += jnp.sum(dq, axis=0, keepdims=True)
        dk_acc[pl.ds(k0, span), :] += dk
        dv_acc[pl.ds(k0, span), :] += dv

    for_each_block(windows, length, run)
    gp_ref[0, :, lanes : 2 * lanes] = dk_acc[...].astype(BF16)
    gp_ref[0, :, 2 * lanes :] = dv_acc[...].astype(BF16)
    sum_ref[0, 1:2, :] = jnp.sum(dv_acc[...], axis=0, keepdims=True)


def struct(shape, dtype):
    return jax.ShapeDtypeStruct(shape, dtype)


def fixed(a):
    return pl.BlockSpec(a.shape, lambda i, *_: (0,) * len(a.shape))


def slab(a):
    return pl.BlockSpec((1,) + a.shape[1:], lambda i, *_: (i,) + (0,) * (len(a.shape) - 1))


def launch(kernel, grid, scalars, operands, specs, outs, out_specs, scratch, flops, name, aliases=None):
    moved = sum(math.prod(a.shape) * a.dtype.itemsize for a in list(operands) + list(outs))
    return pl.pallas_call(
        kernel,
        grid_spec=pltpu.PrefetchScalarGridSpec(
            num_scalar_prefetch=len(scalars),
            grid=(grid,),
            in_specs=specs,
            out_specs=out_specs,
            scratch_shapes=scratch,
        ),
        out_shape=outs,
        input_output_aliases=aliases or {},
        cost_estimate=pl.CostEstimate(flops=flops, transcendentals=0, bytes_accessed=moved),
        name=name,
    )(*scalars, *operands)


def attend(windows, q, k, v, lab_col, lab_row):
    slabs, length, lanes = q.shape
    operands = [q, k, v, lab_col, lab_row]
    specs = [slab(q)] * 3 + [fixed(lab_col), fixed(lab_row)]
    outs = [struct(q.shape, BF16), struct((slabs, lanes // DH, length), F32)]
    return launch(
        attend_kernel, slabs, [windows], operands, specs, outs, [slab(a) for a in outs], [],
        40 * slabs * length * 640 * lanes, "attend",
    )


def attend_back(windows, q, k, v, do, lse, lab_col, lab_row):
    slabs, length, lanes = q.shape
    operands = [q, k, v, do, lse, lab_col, lab_row]
    specs = [slab(a) for a in operands[:5]] + [fixed(lab_col), fixed(lab_row)]
    outs = [struct((slabs, length, 3 * lanes), BF16), struct((slabs, 2, lanes), F32)]
    return launch(
        attend_back_kernel, slabs, [windows], operands, specs, outs, [slab(a) for a in outs],
        [pltpu.VMEM((length, lanes), F32)] * 2, 60 * slabs * length * 640 * lanes, "attend_back",
    )


def row_tile(length):
    return min(256, length)


def tall(a, tile):
    if len(a.shape) == 2:
        return pl.BlockSpec((tile, a.shape[1]), lambda i, *_: (i, 0))
    return pl.BlockSpec((a.shape[0], tile, a.shape[2]), lambda i, *_: (0, i, 0))


def tall_from(a, tile, per):
    if len(a.shape) == 2:
        return pl.BlockSpec((tile, a.shape[1]), lambda i, at: (at[0] * per + i, 0))
    return pl.BlockSpec((a.shape[0], tile, a.shape[2]), lambda i, at: (0, at[0] * per + i, 0))


def project_kernel(x_ref, b_ref, *refs):
    count = b_ref.shape[0]
    weights, (q_ref, k_ref, v_ref) = refs[:count], refs[count:]
    lanes = q_ref.shape[2]
    scale = 1.0 / math.sqrt(DH)
    x = x_ref[...]
    for i in range(count):
        projected = nn(x, weights[i][...]) + b_ref[i]
        q_ref[i] = (projected[:, :lanes].astype(BF16).astype(F32) * scale).astype(BF16)
        k_ref[i] = projected[:, lanes : 2 * lanes].astype(BF16)
        v_ref[i] = projected[:, 2 * lanes :].astype(BF16)


def project(x, weights, bias):
    length, model = x.shape
    lanes = weights[0].shape[1] // 3
    tile = row_tile(length)
    outs = [struct((len(weights), length, lanes), BF16)] * 3
    return launch(
        project_kernel, length // tile, [], [x, bias] + weights,
        [tall(x, tile), fixed(bias)] + [fixed(w) for w in weights], outs,
        [tall(a, tile) for a in outs], [], 6 * length * model * lanes * len(weights), "project",
    )


def context_out_kernel(at, ctx_ref, *refs):
    weights, out_ref = refs[:-1], refs[-1]
    lanes = ctx_ref.shape[2]
    left = jnp.concatenate([ctx_ref[i] for i in range(len(weights))], axis=1)
    right = jnp.concatenate([w[:, w.shape[1] - lanes :] for w in weights], axis=1)
    out_ref[...] = nt(left, right).astype(out_ref.dtype)


def context_out(at, ctx, weights, part, dtype):
    tile = row_tile(part)
    model = weights[0].shape[0]
    out = struct((part, model), dtype)
    return launch(
        context_out_kernel, part // tile, [at], [ctx] + weights,
        [tall_from(ctx, tile, part // tile)] + [fixed(w) for w in weights], [out], [tall(out, tile)], [],
        2 * part * model * ctx.shape[0] * ctx.shape[2], "context_out",
    )[0]


def context_back_kernel(ga_ref, *refs):
    weights, out_ref = refs[:-1], refs[-1]
    lanes = out_ref.shape[2]
    right = jnp.concatenate([w[:, w.shape[1] - lanes :] for w in weights], axis=1)
    grad = nn(ga_ref[...], right).astype(BF16)
    for i in range(len(weights)):
        out_ref[i] = grad[:, i * lanes : (i + 1) * lanes]


def context_back(ga, weights, lanes):
    tile = row_tile(ga.shape[0])
    out = struct((len(weights), ga.shape[0], lanes), BF16)
    return launch(
        context_back_kernel, ga.shape[0] // tile, [], [ga] + weights,
        [tall(ga, tile)] + [fixed(w) for w in weights], [out], [tall(out, tile)], [],
        2 * math.prod(ga.shape) * lanes * len(weights), "context_back",
    )[0]


def ffn_in_kernel(y_ref, b_ref, *refs):
    count = b_ref.shape[0]
    wide = b_ref.shape[2]
    weights, (act_ref, slope_ref) = refs[:count], refs[-2:]
    y = y_ref[...]
    for i in range(count):
        inner = nn(y, weights[i][:, :wide]) + b_ref[i]
        share = 0.5 + 0.5 * lax.erf(inner * math.sqrt(0.5))
        density = jnp.exp(-0.5 * inner * inner) * (1.0 / math.sqrt(2.0 * math.pi))
        act_ref[i] = (inner * share).astype(BF16)
        slope_ref[i] = (share + inner * density).astype(BF16)


def place(a, tile, first):
    return pl.BlockSpec((a.shape[0], tile, a.shape[2]), lambda i, *_: (0, first + i, 0))


def ffn_in(y, bias, weights, ways, place_at, earlier):
    part, model = y.shape
    tile = row_tile(part)
    first = place_at * (part // tile)
    wide = bias.shape[2]
    count = len(weights)
    out = struct((count, part * ways, wide), BF16)
    anywhere = [pl.BlockSpec(memory_space=pl.ANY)] * len(earlier)
    return launch(
        ffn_in_kernel, part // tile, [], [y, bias] + weights + earlier,
        [tall(y, tile), fixed(bias)] + [fixed(w) for w in weights] + anywhere,
        [out, out], [place(out, tile, first)] * 2, [],
        6 * part * model * wide * count, "ffn_in",
        {2 + count + i: i for i in range(len(earlier))},
    )


def ffn_out_kernel(act_ref, *refs):
    weights, out_ref = refs[:-1], refs[-1]
    total = nt(act_ref[0], weights[0][...])
    for i in range(1, len(weights)):
        total += nt(act_ref[i], weights[i][...])
    out_ref[...] = total.astype(out_ref.dtype)


def ffn_out(act, weights, part, place_at, dtype):
    tile = row_tile(part)
    model = weights[0].shape[0]
    out = struct((part, model), dtype)
    return launch(
        ffn_out_kernel, part // tile, [], [act] + weights,
        [place(act, tile, place_at * (part // tile))] + [fixed(w) for w in weights],
        [out], [tall(out, tile)], [], 2 * part * model * act.shape[0] * act.shape[2], "ffn_out",
    )[0]


def ffn_back_kernel(gb_ref, slope_ref, *refs):
    count = slope_ref.shape[0]
    wide = slope_ref.shape[2]
    outs, ins = refs[:count], refs[count : 2 * count]
    gi_ref, sum_ref, out_ref = refs[-3:]
    gb = gb_ref[...]
    total = None
    sums = []
    for i in range(count):
        grad = nn(gb, outs[i][...]) * slope_ref[i].astype(F32)
        low = grad.astype(BF16)
        gi_ref[i] = low
        sums.append(jnp.sum(grad, axis=0, keepdims=True))
        term = nt(low, ins[i][:, :wide])
        total = term if total is None else total + term
    out_ref[...] = total.astype(out_ref.dtype)

    @pl.when(pl.program_id(0) == 0)
    def _():
        sum_ref[...] = jnp.zeros_like(sum_ref)

    for i in range(count):
        sum_ref[i] += sums[i]


def ffn_back(gb, slope, outs_w, ins_w, place_at, earlier, dtype):
    part, model = gb.shape
    tile = row_tile(part)
    first = place_at * (part // tile)
    count, _, wide = slope.shape
    anywhere = [pl.BlockSpec(memory_space=pl.ANY)] * len(earlier)
    outs = [struct(slope.shape, BF16), struct((count, 1, wide), F32), struct((part, model), dtype)]
    return launch(
        ffn_back_kernel, part // tile, [], [gb, slope] + outs_w + ins_w + earlier,
        [tall(gb, tile), place(slope, tile, first)] + [fixed(w) for w in outs_w + ins_w] + anywhere,
        outs, [place(outs[0], tile, first), fixed(outs[1]), tall(outs[2], tile)], [],
        4 * part * model * wide * count, "ffn_back",
        {2 + 2 * count + i: i for i in range(len(earlier))},
    )


def inputs_back_kernel(at, gp_ref, *refs):
    weights, out_ref = refs[:-1], refs[-1]
    total = nt(gp_ref[0], weights[0][...])
    for i in range(1, len(weights)):
        total += nt(gp_ref[i], weights[i][...])
    out_ref[...] = total.astype(out_ref.dtype)


def inputs_back(at, gp, weights, part, dtype):
    tile = row_tile(part)
    model = weights[0].shape[0]
    out = struct((part, model), dtype)
    return launch(
        inputs_back_kernel, part // tile, [at], [gp] + weights,
        [tall_from(gp, tile, part // tile)] + [fixed(w) for w in weights], [out], [tall(out, tile)], [],
        2 * part * model * gp.shape[0] * gp.shape[2], "inputs_back",
    )[0]


def weight_grad(left, right):
    length, model = left.shape
    count, _, wide = right.shape
    out = struct((count, model, wide), BF16)

    def kernel(left_ref, right_ref, out_ref, left_t):
        @pl.when(pl.program_id(0) == 0)
        def _():
            left_t[...] = left_ref[...].T

        out_ref[0] = nn(left_t[...], right_ref[0]).astype(BF16)

    stack = launch(
        kernel, count, [], [left, right], [fixed(left), slab(right)], [out], [slab(out)],
        [pltpu.VMEM((model, length), BF16)], 2 * length * model * wide * count, "weight_grad",
    )[0]
    return [stack[i] for i in range(count)]


def norm_rows(hidden):
    mean = jnp.mean(hidden, axis=1, keepdims=True)
    square = jnp.mean(hidden * hidden, axis=1, keepdims=True)
    inv_std = lax.rsqrt(square - mean * mean + NORM_EPS)
    return (hidden - mean) * inv_std, inv_std


def norm_rows_back(incoming, centred, inv_std, gain):
    scaled = incoming * gain
    first = jnp.mean(scaled, axis=1, keepdims=True)
    second = jnp.mean(scaled * centred, axis=1, keepdims=True)
    return inv_std * (scaled - first - centred * second)


def add_sums(sum_ref, terms):
    @pl.when(pl.program_id(0) == 0)
    def _():
        sum_ref[...] = jnp.zeros_like(sum_ref)

    for i, term in enumerate(terms):
        sum_ref[i : i + 1, :] += jnp.sum(term, axis=0, keepdims=True)


def norm_a_kernel(at, mine_ref, got_ref, x_ref, vec_ref, centred_ref, inv_ref, y_ref):
    hidden = mine_ref[...] + got_ref[...].astype(F32) + x_ref[...].astype(F32) + vec_ref[0]
    centred, inv_std = norm_rows(hidden)
    centred_ref[...] = centred
    inv_ref[...] = inv_std
    y_ref[...] = (centred * vec_ref[1] + vec_ref[2]).astype(BF16)


def norm_a(at, mine, got, x, vec):
    part, model = mine.shape
    tile = row_tile(part)
    outs = [struct((part, model), F32), struct((part, 1), F32), struct((part, model), BF16)]
    return launch(
        norm_a_kernel, part // tile, [at], [mine, got, x, vec],
        [tall(mine, tile), tall(got, tile), tall_from(x, tile, part // tile), fixed(vec)],
        outs, [tall(a, tile) for a in outs], [], 20 * part * model, "norm_a",
    )


def norm_b_kernel(mine_ref, got_ref, centred_a_ref, cot_ref, vec_ref, out_ref, grad_ref, low_ref, sum_ref):
    normed = centred_a_ref[...] * vec_ref[1] + vec_ref[2]
    hidden = mine_ref[...] + got_ref[...].astype(F32) + vec_ref[3] + normed
    centred, inv_std = norm_rows(hidden)
    out_ref[...] = (centred * vec_ref[4] + vec_ref[5]).astype(BF16)
    incoming = cot_ref[...].astype(F32)
    grad = norm_rows_back(incoming, centred, inv_std, vec_ref[4])
    grad_ref[...] = grad
    low_ref[...] = grad.astype(BF16)
    add_sums(sum_ref, (grad, incoming * centred, incoming))


def norm_b(mine, got, centred_a, cot, vec):
    part, model = mine.shape
    tile = row_tile(part)
    outs = [struct((part, model), BF16), struct((part, model), F32), struct((part, model), BF16), struct((3, model), F32)]
    return launch(
        norm_b_kernel, part // tile, [], [mine, got, centred_a, cot, vec],
        [tall(a, tile) for a in (mine, got, centred_a, cot)] + [fixed(vec)],
        outs, [tall(a, tile) for a in outs[:3]] + [fixed(outs[3])], [], 40 * part * model, "norm_b",
    )


def norm_a_back_kernel(mine_ref, got_ref, gb_ref, centred_ref, inv_ref, vec_ref, grad_ref, low_ref, sum_ref):
    incoming = mine_ref[...] + got_ref[...].astype(F32) + gb_ref[...]
    centred = centred_ref[...]
    grad = norm_rows_back(incoming, centred, inv_ref[...], vec_ref[1])
    grad_ref[...] = grad
    low_ref[...] = grad.astype(BF16)
    add_sums(sum_ref, (grad, incoming * centred, incoming))


def norm_a_back(mine, got, gb, centred, inv, vec):
    part, model = mine.shape
    tile = row_tile(part)
    outs = [struct((part, model), F32), struct((part, model), BF16), struct((3, model), F32)]
    return launch(
        norm_a_back_kernel, part // tile, [], [mine, got, gb, centred, inv, vec],
        [tall(a, tile) for a in (mine, got, gb, centred, inv)] + [fixed(vec)],
        outs, [tall(a, tile) for a in outs[:2]] + [fixed(outs[2])], [], 30 * part * model, "norm_a_back",
    )


def body(
    rows,
    cols,
    tokens,
    segments,
    wqkv,
    bias_qv,
    wo,
    bias_o,
    gain_a,
    shift_a,
    w_in,
    bias_in,
    w_out,
    bias_out,
    gain_b,
    shift_b,
    cotangent,
):
    seqs, length = segments.shape
    ways = cols // seqs
    width = tokens.shape[1]
    model = width * cols
    heads = wqkv.shape[1] // (3 * DH)
    lanes = heads * DH // 2
    hid = w_in.shape[1]
    part = length // ways
    own_rows = wqkv.shape[0]
    row, col = lax.axis_index("row"), lax.axis_index("col")
    seq, way = col // ways, col % ways
    by_seq = [Stage("col", cols, mask * ways, col) for mask in bits_of(seqs)]
    by_way = [Stage("col", cols, mask, col) for mask in bits_of(ways)]
    by_row = [Stage("row", rows, mask, row) for mask in bits_of(rows)]
    ns, nw, nr = len(by_seq), len(by_way), len(by_row)
    far, near = by_row[:-1], by_row[-1]
    parts = range(ways)
    at = [((way ^ p) * jnp.ones((1,), jnp.int32)).astype(jnp.int32) for p in parts]

    def gather_far(one, two):
        halves = [h.reshape((1,) * nr + h.shape) for h in (one, two)]
        for i, stage in enumerate(far):
            both = jnp.stack(halves)
            got = stage.trade(both)
            halves = [stage.join(both[h], got[h], i) for h in range(2)]
        return halves

    def gather_near(block):
        return near.gather(block, nr - 1).reshape(model, -1)

    def gather_last(one, two):
        ones, twos = [gather_near(one)], [two]
        for stage in by_seq:
            twos = twos + [stage.trade(b) for b in twos]
        two = after(two, ones[0])
        twos = [gather_near(b) for b in [two] + twos[1:]]
        for stage in by_seq:
            ones = ones + [stage.trade(b) for b in ones]
        return [b for j in range(seqs) for b in (ones[j], twos[j])]

    def halves_of(weight):
        half = weight.shape[1] // 2
        return weight[:, :half], weight[:, half:]

    by_kind = wqkv.reshape(own_rows, 2, heads // 2, 3, DH).transpose(1, 0, 3, 2, 4)
    by_kind = by_kind.reshape(2, own_rows, -1)
    far_qkv = gather_far(by_kind[0], by_kind[1])

    labels = lax.dynamic_slice_in_dim(segments, seq, 1, 0)[0]
    windows = key_windows(labels)
    lab_col, lab_row = labels[:, None], labels[None, :]

    def exchange(array, split, whole):
        blocks = [array]
        for stage in split + whole:
            both = blocks[0] if len(blocks) == 1 else jnp.concatenate(blocks, axis=1)
            if stage in split:
                both = both.reshape(2, both.shape[0] // 2, both.shape[1])
                mine, sent = pick(both, stage.bit, 0)[0], pick(both, 1 - stage.bit, 0)[0]
            else:
                mine = sent = both
            got = stage.trade(sent)
            low = stage.bit == 0
            blocks = [
                half
                for i in range(len(blocks))
                for a, b in [(mine[:, i * width : (i + 1) * width], got[:, i * width : (i + 1) * width])]
                for half in (jnp.where(low, a, b), jnp.where(low, b, a))
            ]
        return jnp.concatenate(blocks, axis=1)

    def to_features(array):
        blocks = [array]
        for stage in by_seq + by_way:
            half = blocks[0].shape[1] // 2
            both = blocks[0] if len(blocks) == 1 else jnp.concatenate(blocks, axis=0)
            mine = lax.dynamic_slice_in_dim(both, stage.bit * half, half, 1)
            got = stage.trade(lax.dynamic_slice_in_dim(both, (1 - stage.bit) * half, half, 1))
            low = stage.bit == 0
            count = array.shape[0]
            blocks = [
                half_rows
                for i in range(len(blocks))
                for a, b in [(mine[i * count : (i + 1) * count], got[i * count : (i + 1) * count])]
                for half_rows in (jnp.where(low, a, b), jnp.where(low, b, a))
            ]
        return jnp.concatenate(blocks, axis=0)

    whole_x = exchange(after(tokens, far_qkv[0]), by_seq, by_way)
    vectors = jnp.concatenate(
        [v.reshape(-1, width) for v in (bias_o, gain_a, shift_a, bias_out, gain_b, shift_b, bias_qv, bias_in)]
    )
    vectors = after(vectors, far_qkv[0])
    pairs = [vectors]
    for stage in by_seq:
        pairs = pairs + [stage.trade(v) for v in pairs]
    blocks = [vectors[:6]]
    for i, stage in enumerate(by_seq):
        got = jnp.concatenate([p[:6] for p in pairs[1 << i : 2 << i]], axis=1)
        low = stage.bit == 0
        both = jnp.concatenate(blocks, axis=1)
        blocks = [
            half
            for k in range(len(blocks))
            for a, b in [(both[:, k * width : (k + 1) * width], got[:, k * width : (k + 1) * width])]
            for half in (jnp.where(low, a, b), jnp.where(low, b, a))
        ]
    for stage in by_way:
        both = jnp.concatenate(blocks, axis=1)
        got = stage.trade(both)
        low = stage.bit == 0
        blocks = [
            half
            for k in range(len(blocks))
            for a, b in [(both[:, k * width : (k + 1) * width], got[:, k * width : (k + 1) * width])]
            for half in (jnp.where(low, a, b), jnp.where(low, b, a))
        ]
    vec = jnp.concatenate(blocks, axis=1).astype(F32)[:, None, :]
    nq = bias_qv.shape[0] // width
    q_biases, in_biases = [], []
    for j in range(seqs):
        both = pairs[j][6 : 6 + nq].astype(F32).reshape(2, heads // 2, 2, DH)
        both = both.transpose(0, 2, 1, 3).reshape(2, 2, lanes)
        q_biases.append(jnp.concatenate((both[:, :1], jnp.zeros_like(both[:, :1]), both[:, 1:]), axis=1))
        in_biases.append(pairs[j][6 + nq :].astype(F32).reshape(2, 1, hid // 2))
    q_bias = jnp.concatenate(q_biases, axis=0).reshape(2 * seqs, 1, 3 * lanes)
    in_bias = jnp.concatenate(in_biases, axis=0)

    qkv_all = gather_last(*far_qkv)
    wo_t, out_t = halves_of(wo.T), halves_of(w_out.T)
    both_in = [jnp.concatenate((a, b), axis=1) for a, b in zip(halves_of(w_in), wo_t)]
    far_in = gather_far(*[after(b, *far_qkv) for b in both_in])
    far_out = gather_far(*[after(b, *far_in) for b in out_t])
    in_all = gather_last(*[after(b, qkv_all[0], qkv_all[3]) for b in far_in])
    out_all = gather_last(*[after(b, in_all[0], in_all[3]) for b in far_out])
    cot = exchange(after(cotangent, qkv_all[2]), by_seq + by_way, [])

    def gather_parts(own):
        blocks = {0: own}
        for mask, stage in zip(bits_of(ways), by_way):
            for p in list(blocks):
                blocks[p ^ mask] = stage.trade(blocks[p])
        return [blocks[p] for p in parts]

    def scatter_parts(make):
        terms = {p: make(p, F32 if p == 0 else BF16) for p in reversed(parts)}
        for mask, stage in list(zip(bits_of(ways), by_way))[:-1]:
            for p in [q for q in terms if q & mask]:
                got = stage.trade(terms.pop(p))
                terms[p ^ mask] = add(terms[p ^ mask], got)
        return terms[0], by_way[-1].trade(terms[1])

    def whole_rows(blocks):
        blocks = list(blocks)
        for mask, stage in zip(reversed(bits_of(ways)), reversed(by_way)):
            low = stage.bit == 0
            for p in parts:
                if not p & mask:
                    a, b = blocks[p], blocks[p | mask]
                    blocks[p], blocks[p | mask] = jnp.where(low, a, b), jnp.where(low, b, a)
        return jnp.concatenate(blocks, axis=0)

    def scatter_first(blocks):
        ones, twos = blocks[0::2], blocks[1::2]
        fold = lambda b: near.reduce(b.reshape((2,) * nr + (own_rows, -1)), nr - 1)
        for stage in reversed(by_seq):
            count = len(ones) // 2
            ones = [add(ones[j], stage.trade(ones[count + j])) for j in range(count)]
        twos = [fold(b) for b in reversed(twos)][::-1]
        for stage in reversed(by_seq):
            count = len(twos) // 2
            twos = [add(twos[j], stage.trade(twos[count + j])) for j in range(count)]
        return fold(ones[0]), twos[0]

    def scatter_far(one, two):
        for i, stage in reversed(list(enumerate(far))):
            halves = (one, two)
            sent = jnp.stack([pick(b, 1 - stage.bit, i) for b in halves])
            got = stage.trade(sent)
            one, two = [add(pick(b, stage.bit, i), got[h]) for h, b in enumerate(halves)]
        return one.reshape(own_rows, -1).astype(F32), two.reshape(own_rows, -1).astype(F32)

    q, k, v = project(whole_x, qkv_all, q_bias)
    context, lse = attend(windows, q, k, v, lab_col, lab_row)
    mine, got = scatter_parts(lambda p, dtype: context_out(at[p], context, in_all, part, dtype))
    centred_a, inv_a, y = norm_a(at[0], mine, got, whole_x, vec)
    y_parts = gather_parts(y)
    earlier = []
    for p in parts:
        earlier = ffn_in(y_parts[p], in_bias, in_all, ways, p, list(earlier))
    active, slope = earlier
    mine, got = scatter_parts(lambda p, dtype: ffn_out(active, out_all, part, p, dtype))
    output, grad_b, gb, sums_b = norm_b(mine, got, centred_a, cot, vec)

    gb_parts = gather_parts(gb)
    output = to_features(after(output, gb_parts[-1]))
    terms, sum_in, earlier = {}, 0.0, []
    for p in parts:
        grad_inner, sums, terms[p] = ffn_back(
            gb_parts[p], slope, out_all, in_all, p, earlier, F32 if p == 0 else BF16
        )
        earlier = [grad_inner]
        sum_in = sum_in + sums
    mine, got = scatter_parts(lambda p, dtype: terms[p])
    grad_w_out = weight_grad(jnp.concatenate(gb_parts, axis=0), active)
    grad_w_in = weight_grad(jnp.concatenate(y_parts, axis=0), grad_inner)
    first_out = scatter_first(grad_w_out)
    grad_a, ga, sums_a = norm_a_back(mine, got, grad_b, centred_a, inv_a, vec)
    whole_ga = whole_rows(gather_parts(ga))
    grad_context = context_back(whole_ga, in_all, lanes)
    first_in = scatter_first([after(b, *first_out) for b in grad_w_in])
    out_halves = scatter_far(*first_out)
    grad_projected, sum_projected = attend_back(windows, q, k, v, grad_context, lse, lab_col, lab_row)
    in_halves = scatter_far(*first_in)
    grad_wo = weight_grad(whole_ga, context)
    grad_wqkv = weight_grad(whole_x, grad_projected)
    last = scatter_first([jnp.concatenate(two, axis=1) for two in zip(grad_wqkv, grad_wo)])
    mine, got = scatter_parts(lambda p, dtype: inputs_back(at[p], grad_projected, qkv_all, part, dtype))
    grad_tokens = to_features((mine + got.astype(F32) + grad_a).astype(BF16)).astype(F32)
    qkv_halves = scatter_far(*last)

    per_hidden = []
    for j in range(seqs):
        two = sum_projected[2 * j : 2 * j + 2].reshape(2, 2, heads // 2, DH).transpose(0, 2, 1, 3)
        per_hidden.append(jnp.concatenate((two.reshape(-1), sum_in[2 * j : 2 * j + 2].reshape(-1))))
    block = jnp.concatenate((sums_a, sums_b), axis=0)
    for stage in by_seq + by_way:
        half = block.shape[1] // 2
        got = stage.trade(lax.dynamic_slice_in_dim(block, (1 - stage.bit) * half, half, 1))
        block = lax.dynamic_slice_in_dim(block, stage.bit * half, half, 1) + got
    for stage in reversed(by_seq):
        count = len(per_hidden) // 2
        per_hidden = [per_hidden[j] + stage.trade(per_hidden[count + j]) for j in range(count)]
    sums = jnp.concatenate((per_hidden[0], block.reshape(-1)))
    for stage in by_row:
        sums = sums + stage.trade(sums)
    nqv = bias_qv.shape[0]
    sum_qv, sum_in = sums[:nqv], sums[nqv : nqv + hid]
    rest = sums[nqv + hid :].reshape(6, width)
    split = 3 * lanes
    grad_qkv = jnp.stack([h[:, :split] for h in qkv_halves])
    grad_qkv = grad_qkv.reshape(2, own_rows, 3, heads // 2, DH).transpose(1, 0, 3, 2, 4)
    return (
        output,
        grad_tokens,
        grad_qkv.reshape(own_rows, -1),
        sum_qv,
        jnp.concatenate([h[:, split:] for h in qkv_halves], axis=1).T,
        rest[0],
        rest[1],
        rest[2],
        jnp.concatenate(in_halves, axis=1),
        sum_in,
        jnp.concatenate(out_halves, axis=1).T,
        rest[3],
        rest[4],
        rest[5],
    )


def solution(mesh):
    tile, across, down, flat = P("row", "col"), P("row", None), P("col", "row"), P("col")
    in_specs = (tile, across, tile, flat, down, flat, flat, flat, tile, flat, down, flat, flat, flat, tile)
    out_specs = (tile, tile, tile, flat, down, flat, flat, flat, tile, flat, down, flat, flat, flat)
    rows, cols = mesh.shape["row"], mesh.shape["col"]

    def layer(*args):
        return body(rows, cols, *args)

    return jax.shard_map(layer, mesh=mesh, in_specs=in_specs, out_specs=out_specs, check_vma=False)
```

time: 640 us -> 521 us (0.81)
  matrix products: 93.3 us -> 0 us
  Pallas kernels: 118 us -> 173 us
  waiting for transfers between devices: 184 us -> 136 us
  local copies, waits for them, and re-layouts: 76.2 us -> 55.6 us
  other arithmetic: 93.8 us -> 80.2 us
    dot_general x29 -> x0, matrix products: 93.3 us -> none  [the longest x13 51.1 us: nt(): lax.dot_general(left, right, (((1,), (1,)), ((), ())), preferred_element_...]
    pallas_call x16 -> x21, Pallas kernels: 118 us -> 173 us  [launch(): pl.pallas_call(kernel, grid_spec=pltpu.PrefetchScalarGridSpec(num_scalar_...]
    ppermute x71 -> x65, waiting for transfers between devices: 184 us -> 136 us  [trade(): return lax.ppermute(block, self.axis, self.pairs)]
    slice x17, local copies, waits for them, and re-layouts: 17.9 us -> 4.85 us  [the longest x1 3.08 us: weight_grad(): return [stack[i] for i in range(count)]]
    squeeze x4 -> x6, local copies, waits for them, and re-layouts: 0.33 us -> 13.3 us  [the longest x3 9.2 us: weight_grad(): return [stack[i] for i in range(count)]]
    reduce_sum x7 -> x0, other arithmetic: 12.3 us -> none  [the longest x5 8.68 us: body(): jnp.sum(v, axis=0)]
    another operation x24 -> x13, local copies, waits for them, and re-layouts: 11.2 us -> 0.96 us  [the longest x12 0.96 us: scatter_far(): sent = jnp.stack([pick(b, 1 - stage.bit, i) for b in halves])]
    concatenate x10 -> x21, other arithmetic: 9.6 us -> 18.8 us  [the longest x3 4.59 us: body(): jnp.concatenate(two, axis=1)]
  transfers between devices with their start and end apart: 71 -> 65, of which waited for: 23 -> 21; matrix products, arithmetic and copies ran while one was open for 34% -> 24% of each run, Pallas kernels for 17% -> 31%
where the time goes in v3:
time: 521 us; the launch traced here: 514 us
  Pallas kernels  173 us (33%)
  waiting for transfers between devices  136 us (26%)
  other arithmetic  80.2 us (15%)
  starting transfers between devices  66.8 us (13%)
  local copies, waits for them, and re-layouts  55.6 us (11%)
    pallas_call x21, Pallas kernels, launch(): pl.pallas_call(kernel, grid_spec=pltpu.PrefetchScalarGridSpec(num_scalar_...  173 us
    ppermute x65, waiting for transfers between devices, trade(): return lax.ppermute(block, self.axis, self.pairs)  136 us
    ppermute x65, starting transfers between devices, trade(): return lax.ppermute(block, self.axis, self.pairs)  66.8 us
    convert_element_type x18, other arithmetic, add(): return (mine.astype(F32) + other.astype(F32)).astype(mine.dtype)  19.3 us
    unnamed x129, local copies, waits for them, and re-layouts  16.3 us
    select_n x16, other arithmetic, join(): jnp.where(low, mine, other)  13 us
  transfers between devices with their start and end apart: 65, of which 21 were waited for; matrix products, arithmetic and copies ran while one was open for 24% of the time, Pallas kernels for 31%

profile of v3, /device:TPU:0, one launch (start us, length us, event | category | flops | bytes accessed | tf_op | source)
XLA Modules:
  0.0 514.4 jit_solution(12832191280700989400)
XLA Ops:
  2.0 4.1 collective-permute-start
  8.4 6.8 %collective-permute-done = bf16[2,1,1,1,128,384]{4,5,3,2,1,0:T(8,128)(2,1)S(1)} collective-permute-done((bf16[2,1,1,1,128,384]{4,5,3,2,1,0:T(8,128)(2,1)S(1)}, bf16[2,1,1,1,128,384]{4,5,3,2,1,0:T(8,128)(2,1)S(1)}, u32[]{:S(2)}, u32[]{:S(2)}) %collective-permute-start) | collective-permute-done | bytes 196640 | tf_op jit(solution)/shard_map/ppermute | solution.py:49
  18.1 7.7 %collective-permute-done.1 = bf16[2,2,1,1,128,384]{4,5,1,3,2,0:T(8,128)(2,1)S(1)} collective-permute-done((bf16[2,2,1,1,128,384]{4,5,1,3,2,0:T(8,128)(2,1)S(1)}, bf16[2,2,1,1,128,384]{4,5,1,3,2,0:T(8,128)(2,1)S(1)}, u32[]{:S(2)}, u32[]{:S(2)}) %collective-permute-start.1) | collective-permute-done | bytes 393248 | tf_op jit(solution)/shard_map/ppermute | solution.py:49
  29.4 3.4 collective-permute-start.10
  37.6 8.7 %collective-permute-done.10 = bf16[2,1,1,1,128,640]{5,4,3,2,1,0:T(8,128)(2,1)S(1)} collective-permute-done((bf16[2,1,1,1,128,640]{5,4,3,2,1,0:T(8,128)(2,1)S(1)}, bf16[2,1,1,1,128,640]{5,4,3,2,1,0:T(8,128)(2,1)S(1)}, u32[]{:S(2)}, u32[]{:S(2)}) %collective-permute-start.10) | collective-permute-done | bytes 327712 | tf_op jit(solution)/shard_map/ppermute | solution.py:49
  55.7 14.5 %collective-permute-done.9 = bf16[2,2,1,128,384]{3,4,2,1,0:T(8,128)(2,1)S(1)} collective-permute-done((bf16[2,2,1,128,384]{3,4,2,1,0:T(8,128)(2,1)}, bf16[2,2,1,128,384]{3,4,2,1,0:T(8,128)(2,1)S(1)}, u32[]{:S(2)}, u32[]{:S(2)}) %collective-permute-start.9) | collective-permute-done | bytes 393248 | tf_op jit(solution)/shard_map/ppermute | solution.py:49
  77.1 3.4 collective-permute-start.20
  88.8 2.7 collective-permute-done.20
  96.5 8.6 %project.1 = (bf16[4,1024,128]{2,1,0:T(8,128)(2,1)}, bf16[4,1024,128]{2,1,0:T(8,128)(2,1)}, bf16[4,1024,128]{2,1,0:T(8,128)(2,1)}) custom-call(bf16[1024,1024]{1,0:T(8,128)(2,1)} %pad_maximum_fusion.x_ref.left_ref, f32[4,1,384]{2,1,0:T(1,128)} %reshape.1330.b_ref, bf16[1024,384]{1,0:T(8,128)(2,1)} %bitcast.433, bf16[1024,384]{1,0:T(8,128)(2,1)} %bitcast.439, ...), custom_call_target="tpu_custom_call" | custom-call | flops 3221225472 | bytes 8394752 | tf_op jit(solution)/shard_map/project/pallas_call | solution.py:182
  105.1 18.7 %attend.1 = (bf16[4,1024,128]{2,1,0:T(8,128)(2,1)}, f32[4,2,1024]{2,1,0:T(2,128)}) custom-call(s32[2,4]{1,0:T(2,128)} %pad_add_fusion.windows, bf16[4,1024,128]{2,1,0:T(8,128)(2,1)} %get-tuple-element.63.q_ref, bf16[4,1024,128]{2,1,0:T(8,128)(2,1)} %get-tuple-element.64.k_ref, bf16[4,1024,128]{2,1,0:T(8,128)(2,1)} %get-tuple-element.65.v_ref, ...), custom_call_target="tpu_custom_call" | custom-call | flops 13421772800 | bytes 4235264 | tf_op jit(solution)/shard_map/attend/pallas_call | solution.py:182
  129.2 28.1 %collective-permute-done.16 = bf16[2,2,1,128,640]{4,3,2,1,0:T(8,128)(2,1)S(1)} collective-permute-done((bf16[2,2,1,128,640]{4,3,2,1,0:T(8,128)(2,1)}, bf16[2,2,1,128,640]{4,3,2,1,0:T(8,128)(2,1)S(1)}, u32[]{:S(2)}, u32[]{:S(2)}) %collective-permute-start.16) | collective-permute-done | bytes 655392 | tf_op jit(solution)/shard_map/ppermute | solution.py:49
  164.2 4.4 context_out.3
  169.9 2.7 collective-permute-done.25
  178.0 4.6 context_out.2.mine_ref
  182.6 5.1 collective-permute-done.26
  190.0 3.9 norm_a.1
  199.3 7.7 %ffn_in.2 = (bf16[4,1024,512]{2,1,0:T(8,128)(2,1)}, bf16[4,1024,512]{2,1,0:T(8,128)(2,1)}) custom-call(bf16[512,1024]{1,0:T(8,128)(2,1)} %get-tuple-element.72.y_ref, f32[4,1,512]{2,1,0:T(1,128)} %maximum_convert_fusion.3.b_ref, bf16[1024,640]{1,0:T(8,128)(2,1)} %bitcast.400, bf16[1024,640]{1,0:T(8,128)(2,1)} %bitcast.414, bf16[1024,640]{1,0:T(8,128)(2,1)} %copy-done.3, ...), custom_call_target="tpu_custom_call" | custom-call | flops 6442450944 | bytes 14688256 | tf_op jit(solution)/shard_map/ffn_in/pallas_call | solution.py:182
  206.9 7.9 %ffn_in.3 = (bf16[4,1024,512]{2,1,0:T(8,128)(2,1)}, bf16[4,1024,512]{2,1,0:T(8,128)(2,1)}) custom-call(bf16[512,1024]{1,0:T(8,128)(2,1)} %collective-permute-done.19.y_ref, f32[4,1,512]{2,1,0:T(1,128)} %maximum_convert_fusion.3.b_ref, bf16[1024,640]{1,0:T(8,128)(2,1)} %bitcast.401, ...), custom_call_target="tpu_custom_call", output_to_operand_aliasing={{0}: (6, {}), {1}: (7, {})} | custom-call | flops 6442450944 | bytes 23076864 | tf_op jit(solution)/shard_map/ffn_in/pallas_call | solution.py:182
  215.8 6.0 %ffn_out.3 = bf16[512,1024]{1,0:T(8,128)(2,1)} custom-call(bf16[4,1024,512]{2,1,0:T(8,128)(2,1)} %get-tuple-element.75.act_ref.right_ref, bf16[1024,512]{1,0:T(8,128)(2,1)} %bitcast.420, bf16[1024,512]{1,0:T(8,128)(2,1)} %bitcast.428, bf16[1024,512]{1,0:T(8,128)(2,1)} %copy-done.5, bf16[1024,512]{1,0:T(8,128)(2,1)} %bitcast.424), custom_call_target="tpu_custom_call" | custom-call | flops 2147483648 | bytes 9437184 | tf_op jit(solution)/shard_map/ffn_out/pallas_call | solution.py:182
  224.5 6.1 %ffn_out.2.mine_ref = f32[512,1024]{1,0:T(8,128)} custom-call(bf16[4,1024,512]{2,1,0:T(8,128)(2,1)} %get-tuple-element.75.act_ref.right_ref, bf16[1024,512]{1,0:T(8,128)(2,1)} %bitcast.421, bf16[1024,512]{1,0:T(8,128)(2,1)} %bitcast.429, bf16[1024,512]{1,0:T(8,128)(2,1)} %copy-done.5, bf16[1024,512]{1,0:T(8,128)(2,1)} %bitcast.425), custom_call_target="tpu_custom_call" | custom-call | flops 2147483648 | bytes 10485760 | tf_op jit(solution)/shard_map/ffn_out/pallas_call | solution.py:182
  231.6 5.6 %norm_b.1 = (bf16[512,1024]{1,0:T(8,128)(2,1)}, f32[512,1024]{1,0:T(8,128)}, bf16[512,1024]{1,0:T(8,128)(2,1)}, f32[3,1024]{1,0:T(4,128)}) custom-call(f32[512,1024]{1,0:T(8,128)} %ffn_out.2.mine_ref, bf16[512,1024]{1,0:T(8,128)(2,1)} %copy-done.39, f32[512,1024]{1,0:T(8,128)} %get-tuple-element.81.centred_a_ref.centred_ref, ...), custom_call_target="tpu_custom_call" | custom-call | flops 20971520 | bytes 10522624 | tf_op jit(solution)/shard_map/norm_b/pallas_call | solution.py:182
  237.3 2.9 pad_maximum_fusion.2.left_ref
  240.2 10.9 %ffn_back.2 = (bf16[4,1024,512]{2,1,0:T(8,128)(2,1)}, f32[4,1,512]{2,1,0:T(1,128)}, f32[512,1024]{1,0:T(8,128)}) custom-call(bf16[512,1024]{1,0:T(8,128)(2,1)} %get-tuple-element.84.gb_ref, bf16[4,1024,512]{2,1,0:T(8,128)(2,1)} %get-tuple-element.86.slope_ref, bf16[1024,512]{1,0:T(8,128)(2,1)} %bitcast.422, bf16[1024,512]{1,0:T(8,128)(2,1)} %bitcast.430, ...), custom_call_target="tpu_custom_call" | custom-call | flops 4294967296 | bytes 20979712 | tf_op jit(solution)/shard_map/ffn_back/pallas_call | solution.py:182
  252.7 9.0 %weight_grad.7 = bf16[4,1024,512]{2,1,0:T(8,128)(2,1)} custom-call(bf16[1024,1024]{1,0:T(8,128)(2,1)} %pad_maximum_fusion.3.left_ref, bf16[4,1024,512]{2,1,0:T(8,128)(2,1)} %get-tuple-element.75.act_ref.right_ref), custom_call_target="tpu_custom_call" | custom-call | flops 4294967296 | bytes 10485760 | tf_op jit(solution)/shard_map/weight_grad/pallas_call | solution.py:182
  261.7 3.1 fusion.44
  267.9 10.6 %ffn_back.3 = (bf16[4,1024,512]{2,1,0:T(8,128)(2,1)}, f32[4,1,512]{2,1,0:T(1,128)}, bf16[512,1024]{1,0:T(8,128)(2,1)}) custom-call(bf16[512,1024]{1,0:T(8,128)(2,1)} %copy-done.10, bf16[4,1024,512]{2,1,0:T(8,128)(2,1)} %get-tuple-element.86.slope_ref, bf16[1024,512]{1,0:T(8,128)(2,1)} %bitcast.423, ...), custom_call_target="tpu_custom_call", output_to_operand_aliasing={{0}: (10, {})} | custom-call | flops 4294967296 | bytes 24125440 | tf_op jit(solution)/shard_map/ffn_back/pallas_call | solution.py:182
  278.5 9.2 %weight_grad.6 = bf16[4,1024,512]{2,1,0:T(8,128)(2,1)} custom-call(bf16[1024,1024]{1,0:T(8,128)(2,1)} %pad_maximum_fusion.2.left_ref, bf16[4,1024,512]{2,1,0:T(8,128)(2,1)} %get-tuple-element.101.right_ref), custom_call_target="tpu_custom_call" | custom-call | flops 4294967296 | bytes 10485760 | tf_op jit(solution)/shard_map/weight_grad/pallas_call | solution.py:182
  287.7 4.1 slice_bitcast_fusion.5
  300.9 6.9 %collective-permute-done.31 = bf16[512,512]{1,0:T(8,128)(2,1)} collective-permute-done((bf16[512,512]{1,0:T(8,128)(2,1)}, bf16[512,512]{1,0:T(8,128)(2,1)}, u32[]{:S(2)}, u32[]{:S(2)}) %collective-permute-start.31) | collective-permute-done | bytes 524320 | tf_op jit(solution)/shard_map/ppermute | solution.py:49
  313.8 5.4 %norm_a_back.1 = (f32[512,1024]{1,0:T(8,128)}, bf16[512,1024]{1,0:T(8,128)(2,1)}, f32[3,1024]{1,0:T(4,128)}) custom-call(f32[512,1024]{1,0:T(8,128)} %get-tuple-element.87.mine_ref, bf16[512,1024]{1,0:T(8,128)(2,1)} %collective-permute-done.33.got_ref, f32[512,1024]{1,0:T(8,128)} %get-tuple-element.90.gb_ref, ...), custom_call_target="tpu_custom_call" | custom-call | flops 15728640 | bytes 10524672 | tf_op jit(solution)/shard_map/norm_a_back/pallas_call | solution.py:182
  340.7 6.3 %weight_grad.5 = bf16[4,1024,128]{2,1,0:T(8,128)(2,1)} custom-call(bf16[1024,1024]{1,0:T(8,128)(2,1)} %pad_maximum_fusion.1.ga_ref.left_ref, bf16[4,1024,128]{2,1,0:T(8,128)(2,1)} %get-tuple-element.66.ctx_ref.right_ref), custom_call_target="tpu_custom_call" | custom-call | flops 1073741824 | bytes 4194304 | tf_op jit(solution)/shard_map/weight_grad/pallas_call | solution.py:182
  349.0 6.1 %context_back.1.do_ref = bf16[4,1024,128]{2,1,0:T(8,128)(2,1)} custom-call(bf16[1024,1024]{1,0:T(8,128)(2,1)} %pad_maximum_fusion.1.ga_ref.left_ref, bf16[1024,640]{1,0:T(8,128)(2,1)} %bitcast.404, bf16[1024,640]{1,0:T(8,128)(2,1)} %bitcast.418, bf16[1024,640]{1,0:T(8,128)(2,1)} %copy-done.3, bf16[1024,640]{1,0:T(8,128)(2,1)} %bitcast.411), custom_call_target="tpu_custom_call" | custom-call | flops 1073741824 | bytes 8388608 | tf_op jit(solution)/shard_map/context_back/pallas_call | solution.py:182
  355.0 22.0 %attend_back.1 = (bf16[4,1024,384]{2,1,0:T(8,128)(2,1)}, f32[4,2,128]{2,1,0:T(2,128)}) custom-call(s32[2,4]{1,0:T(2,128)} %pad_add_fusion.windows, bf16[4,1024,128]{2,1,0:T(8,128)(2,1)} %get-tuple-element.63.q_ref, bf16[4,1024,128]{2,1,0:T(8,128)(2,1)} %get-tuple-element.64.k_ref, bf16[4,1024,128]{2,1,0:T(8,128)(2,1)} %get-tuple-element.65.v_ref, ...), custom_call_target="tpu_custom_call" | custom-call | flops 20132659200 | bytes 7385088 | tf_op jit(solution)/shard_map/attend_back/pallas_call | solution.py:182
  377.1 8.6 %weight_grad.4 = bf16[4,1024,384]{2,1,0:T(8,128)(2,1)} custom-call(bf16[1024,1024]{1,0:T(8,128)(2,1)} %pad_maximum_fusion.x_ref.left_ref, bf16[4,1024,384]{2,1,0:T(8,128)(2,1)} %get-tuple-element.94.gp_ref.right_ref), custom_call_target="tpu_custom_call" | custom-call | flops 3221225472 | bytes 8388608 | tf_op jit(solution)/shard_map/weight_grad/pallas_call | solution.py:182
  385.7 3.0 slice_bitcast_fusion.7
  389.8 3.0 collective-permute-start.38
  400.1 5.5 %inputs_back.3 = bf16[512,1024]{1,0:T(8,128)(2,1)} custom-call(s32[1]{0:T(128)} %bitcast.62.at, bf16[4,1024,384]{2,1,0:T(8,128)(2,1)} %get-tuple-element.94.gp_ref.right_ref, bf16[1024,384]{1,0:T(8,128)(2,1)} %bitcast.434, bf16[1024,384]{1,0:T(8,128)(2,1)} %bitcast.440, bf16[1024,384]{1,0:T(8,128)(2,1)} %copy-done.16, bf16[1024,384]{1,0:T(8,128)(2,1)} %bitcast.437), custom_call_target="tpu_custom_call" | custom-call | flops 1610612736 | bytes 7340032 | tf_op jit(solution)/shard_map/inputs_back/pallas_call | solution.py:182
  405.6 6.0 %inputs_back.2 = f32[512,1024]{1,0:T(8,128)} custom-call(s32[1]{0:T(128)} %bitcast.at, bf16[4,1024,384]{2,1,0:T(8,128)(2,1)} %get-tuple-element.94.gp_ref.right_ref, bf16[1024,384]{1,0:T(8,128)(2,1)} %bitcast.435, bf16[1024,384]{1,0:T(8,128)(2,1)} %bitcast.441, bf16[1024,384]{1,0:T(8,128)(2,1)} %copy-done.16, bf16[1024,384]{1,0:T(8,128)(2,1)} %bitcast.438), custom_call_target="tpu_custom_call" | custom-call | flops 1610612736 | bytes 8388608 | tf_op jit(solution)/shard_map/inputs_back/pallas_call | solution.py:182
  416.0 4.1 collective-permute-done.48
  420.1 3.6 collective-permute-done.49
  431.7 2.4 collective-permute-done.64
  439.5 9.4 %collective-permute-done.41 = bf16[2,2,1,128,512]{3,4,0,2,1:T(8,128)(2,1)S(1)} collective-permute-done((bf16[2,2,1,128,512]{3,4,0,2,1:T(8,128)(2,1)S(1)}, bf16[2,2,1,128,512]{3,4,0,2,1:T(8,128)(2,1)S(1)}, u32[]{:S(2)}, u32[]{:S(2)}) %collective-permute-start.41) | collective-permute-done | bytes 524320 | tf_op jit(solution)/shard_map/ppermute | solution.py:49
  459.9 2.5 add_convert_fusion.2
  470.6 5.0 collective-permute-done.39
  478.6 3.6 collective-permute-done.61
  485.1 11.7 %collective-permute-done.62 = bf16[2,1,1,1,128,512]{5,4,3,2,1,0:T(8,128)(2,1)S(1)} collective-permute-done((bf16[2,1,1,1,128,512]{5,4,3,2,1,0:T(8,128)(2,1)S(1)}, bf16[2,1,1,1,128,512]{5,4,3,2,1,0:T(8,128)(2,1)S(1)}, u32[]{:S(2)}, u32[]{:S(2)}) %collective-permute-start.62) | collective-permute-done | bytes 262176 | tf_op jit(solution)/shard_map/ppermute | solution.py:49
  497.9 3.4 collective-permute-start.44
  503.0 9.1 %collective-permute-done.44 = bf16[2,1,1,1,128,512]{4,5,3,2,1,0:T(8,128)(2,1)S(1)} collective-permute-done((bf16[2,1,1,1,128,512]{4,5,3,2,1,0:T(8,128)(2,1)S(1)}, bf16[2,1,1,1,128,512]{4,5,3,2,1,0:T(8,128)(2,1)S(1)}, u32[]{:S(2)}, u32[]{:S(2)}) %collective-permute-start.44) | collective-permute-done | bytes 262176 | tf_op jit(solution)/shard_map/ppermute | solution.py:49
  (448 shorter events, 173.9 us)
Async XLA Ops:
  25.9 22.3 %collective-permute-start.5 = (bf16[2,2,1,128,384]{3,4,2,1,0:T(8,128)(2,1)S(1)}, bf16[2,2,1,128,384]{3,4,2,1,0:T(8,128)(2,1)}, u32[]{:S(2)}, u32[]{:S(2)}) collective-permute-start(bf16[2,2,1,128,384]{3,4,2,1,0:T(8,128)(2,1)S(1)} %pad_maximum_fusion.28), channel_id=1, source_target_pairs={{0,4},{4,0},{8,12},{12,8},{16,20},{20,16},{24,28},{28,24},{1,5},{5... | collective-permute-start | bytes 1179656 | tf_op jit(solution)/shard_map/ppermute | solution.py:49
  28.8 23.0 %collective-permute-start.8 = (bf16[2,2,1,128,384]{3,4,2,1,0:T(8,128)(2,1)S(1)}, bf16[2,2,1,128,384]{3,4,2,1,0:T(8,128)(2,1)}, u32[]{:S(2)}, u32[]{:S(2)}) collective-permute-start(bf16[2,2,1,128,384]{3,4,2,1,0:T(8,128)(2,1)S(1)} %pad_maximum_fusion.29), channel_id=1, source_target_pairs={{0,2},{1,3},{2,0},{3,1},{4,6},{5,7},{6,4},{7,5},{8,10},{9,11},{10,... | collective-permute-start | bytes 1179656 | tf_op jit(solution)/shard_map/ppermute | solution.py:49
  29.4 16.9 %collective-permute-start.10 = (bf16[2,1,1,1,128,640]{5,4,3,2,1,0:T(8,128)(2,1)S(1)}, bf16[2,1,1,1,128,640]{5,4,3,2,1,0:T(8,128)(2,1)S(1)}, u32[]{:S(2)}, u32[]{:S(2)}) collective-permute-start(bf16[2,1,1,1,128,640]{5,4,3,2,1,0:T(8,128)(2,1)S(1)} %pad_maximum_fusion.30), channel_id=1, source_target_pairs={{0,16},{4,20},{8,24},{12,28},{16,0},{20,4},{24,8},{28,12},{1,17},{... | collective-permute-start | bytes 983048 | tf_op jit(solution)/shard_map/ppermute | solution.py:49
  33.9 19.5 %collective-permute-start.2 = (bf16[1024,256]{1,0:T(8,128)(2,1)}, bf16[1024,256]{1,0:T(8,128)(2,1)}, u32[]{:S(2)}, u32[]{:S(2)}) collective-permute-start(bf16[1024,256]{1,0:T(8,128)(2,1)} %dynamic-slice_bitcast_fusion.3), channel_id=1, source_target_pairs={{0,2},{1,3},{2,0},{3,1},{4,6},{5,7},{6,4},{7,5},{8,10},{9,11},{10,... | collective-permute-start | bytes 1572872 | tf_op jit(solution)/shard_map/ppermute | solution.py:49
  47.4 24.8 %collective-permute-start.11 = (bf16[2,2,1,1,128,640]{5,4,1,3,2,0:T(8,128)(2,1)}, bf16[2,2,1,1,128,640]{5,4,1,3,2,0:T(8,128)(2,1)}, u32[]{:S(2)}, u32[]{:S(2)}) collective-permute-start(bf16[2,2,1,1,128,640]{5,4,1,3,2,0:T(8,128)(2,1)} %pad_maximum_fusion.18), channel_id=1, source_target_pairs={{0,8},{4,12},{8,0},{12,4},{16,24},{20,28},{24,16},{28,20},{1,9},{5... | collective-permute-start | bytes 1966088 | tf_op jit(solution)/shard_map/ppermute | solution.py:49
  49.7 35.4 %collective-permute-start.7 = (bf16[1024,384]{1,0:T(8,128)(2,1)S(1)}, bf16[1024,384]{1,0:T(8,128)(2,1)S(1)}, u32[]{:S(2)}, u32[]{:S(2)}) collective-permute-start(bf16[1024,384]{1,0:T(8,128)(2,1)S(1)} %bitcast.432), channel_id=1, source_target_pairs={{0,2},{1,3},{2,0},{3,1},{4,6},{5,7},{6,4},{7,5},{8,10},{9,11},{10,... | collective-permute-start | bytes 2359304 | tf_op jit(solution)/shard_map/ppermute | solution.py:49
  51.3 20.0 %collective-permute-start.6 = (bf16[2,2,1,128,384]{3,4,2,1,0:T(8,128)(2,1)S(1)}, bf16[2,2,1,128,384]{3,4,2,1,0:T(8,128)(2,1)S(1)}, u32[]{:S(2)}, u32[]{:S(2)}) collective-permute-start(bf16[2,2,1,128,384]{3,4,2,1,0:T(8,128)(2,1)S(1)} %pad_maximum_fusion.29), channel_id=1, source_target_pairs={{0,4},{4,0},{8,12},{12,8},{16,20},{20,16},{24,28},{28,24},{1,5},{5... | collective-permute-start | bytes 1179656 | tf_op jit(solution)/shard_map/ppermute | solution.py:49
  51.8 18.4 %collective-permute-start.9 = (bf16[2,2,1,128,384]{3,4,2,1,0:T(8,128)(2,1)}, bf16[2,2,1,128,384]{3,4,2,1,0:T(8,128)(2,1)S(1)}, u32[]{:S(2)}, u32[]{:S(2)}) collective-permute-start(bf16[2,2,1,128,384]{3,4,2,1,0:T(8,128)(2,1)} %collective-permute-done.8), channel_id=1, source_target_pairs={{0,4},{4,0},{8,12},{12,8},{16,20},{20,16},{24,28},{28,24},{1,5},{5... | collective-permute-start | bytes 1179656 | tf_op jit(solution)/shard_map/ppermute | solution.py:49
  55.7 37.8 %collective-permute-start.3 = (bf16[1024,512]{1,0:T(8,128)(2,1)}, bf16[1024,512]{1,0:T(8,128)(2,1)}, u32[]{:S(2)}, u32[]{:S(2)}) collective-permute-start(bf16[1024,512]{1,0:T(8,128)(2,1)} %pad_maximum_fusion.7), channel_id=1, source_target_pairs={{0,1},{1,0},{2,3},{3,2},{4,5},{5,4},{6,7},{7,6},{8,9},{9,8},{10,11... | collective-permute-start | bytes 3145736 | tf_op jit(solution)/shard_map/ppermute | solution.py:49
  77.1 14.4 %collective-permute-start.20 = (bf16[2,1,1,1,128,512]{4,5,3,2,1,0:T(8,128)(2,1)}, bf16[2,1,1,1,128,512]{4,5,3,2,1,0:T(8,128)(2,1)}, u32[]{:S(2)}, u32[]{:S(2)}) collective-permute-start(bf16[2,1,1,1,128,512]{4,5,3,2,1,0:T(8,128)(2,1)} %pad_maximum_fusion.33), channel_id=1, source_target_pairs={{0,16},{4,20},{8,24},{12,28},{16,0},{20,4},{24,8},{28,12},{1,17},{... | collective-permute-start | bytes 786440 | tf_op jit(solution)/shard_map/ppermute | solution.py:49
  84.1 42.8 %collective-permute-start.15 = (bf16[2,2,1,128,640]{4,3,2,1,0:T(8,128)(2,1)}, bf16[2,2,1,128,640]{4,3,2,1,0:T(8,128)(2,1)}, u32[]{:S(2)}, u32[]{:S(2)}) collective-permute-start(bf16[2,2,1,128,640]{4,3,2,1,0:T(8,128)(2,1)} %pad_maximum_fusion.20), channel_id=1, source_target_pairs={{0,2},{1,3},{2,0},{3,1},{4,6},{5,7},{6,4},{7,5},{8,10},{9,11},{10,... | collective-permute-start | bytes 1966088 | tf_op jit(solution)/shard_map/ppermute | solution.py:49
  84.7 39.1 %collective-permute-start.12 = (bf16[2,2,1,128,640]{4,3,2,1,0:T(8,128)(2,1)}, bf16[2,2,1,128,640]{4,3,2,1,0:T(8,128)(2,1)}, u32[]{:S(2)}, u32[]{:S(2)}) collective-permute-start(bf16[2,2,1,128,640]{4,3,2,1,0:T(8,128)(2,1)} %pad_maximum_fusion.19), channel_id=1, source_target_pairs={{0,4},{4,0},{8,12},{12,8},{16,20},{20,16},{24,28},{28,24},{1,5},{5... | collective-permute-start | bytes 1966088 | tf_op jit(solution)/shard_map/ppermute | solution.py:49
  87.3 81.2 %collective-permute-start.28 = (bf16[1024,256]{1,0:T(8,128)(2,1)}, bf16[1024,256]{1,0:T(8,128)(2,1)}, u32[]{:S(2)}, u32[]{:S(2)}) collective-permute-start(bf16[1024,256]{1,0:T(8,128)(2,1)} %dynamic-slice_bitcast_fusion.2), channel_id=1, source_target_pairs={{0,2},{1,3},{2,0},{3,1},{4,6},{5,7},{6,4},{7,5},{8,10},{9,11},{10,... | collective-permute-start | bytes 1572872 | tf_op jit(solution)/shard_map/ppermute | solution.py:49
  93.5 35.4 %collective-permute-start.21 = (bf16[2,2,1,1,128,512]{4,5,1,3,2,0:T(8,128)(2,1)}, bf16[2,2,1,1,128,512]{4,5,1,3,2,0:T(8,128)(2,1)S(1)}, u32[]{:S(2)}, u32[]{:S(2)}) collective-permute-start(bf16[2,2,1,1,128,512]{4,5,1,3,2,0:T(8,128)(2,1)} %pad_maximum_fusion.21), channel_id=1, source_target_pairs={{0,8},{4,12},{8,0},{12,4},{16,24},{20,28},{24,16},{28,20},{1,9},{5... | collective-permute-start | bytes 1572872 | tf_op jit(solution)/shard_map/ppermute | solution.py:49
  125.3 37.9 %collective-permute-start.14 = (bf16[1024,640]{1,0:T(8,128)(2,1)S(1)}, bf16[1024,640]{1,0:T(8,128)(2,1)S(1)}, u32[]{:S(2)}, u32[]{:S(2)}) collective-permute-start(bf16[1024,640]{1,0:T(8,128)(2,1)S(1)} %bitcast.397), channel_id=1, source_target_pairs={{0,2},{1,3},{2,0},{3,1},{4,6},{5,7},{6,4},{7,5},{8,10},{9,11},{10,... | collective-permute-start | bytes 3932168 | tf_op jit(solution)/shard_map/ppermute | solution.py:49
  126.9 34.9 %collective-permute-start.13 = (bf16[2,2,1,128,640]{4,3,2,1,0:T(8,128)(2,1)S(1)}, bf16[2,2,1,128,640]{4,3,2,1,0:T(8,128)(2,1)S(1)}, u32[]{:S(2)}, u32[]{:S(2)}) collective-permute-start(bf16[2,2,1,128,640]{4,3,2,1,0:T(8,128)(2,1)S(1)} %copy-done.17), channel_id=1, source_target_pairs={{0,4},{4,0},{8,12},{12,8},{16,20},{20,16},{24,28},{28,24},{1,5},{5... | collective-permute-start | bytes 1966088 | tf_op jit(solution)/shard_map/ppermute | solution.py:49
  127.0 30.4 %collective-permute-start.16 = (bf16[2,2,1,128,640]{4,3,2,1,0:T(8,128)(2,1)}, bf16[2,2,1,128,640]{4,3,2,1,0:T(8,128)(2,1)S(1)}, u32[]{:S(2)}, u32[]{:S(2)}) collective-permute-start(bf16[2,2,1,128,640]{4,3,2,1,0:T(8,128)(2,1)} %collective-permute-done.15), channel_id=1, source_target_pairs={{0,4},{4,0},{8,12},{12,8},{16,20},{20,16},{24,28},{28,24},{1,5},{5... | collective-permute-start | bytes 1966088 | tf_op jit(solution)/shard_map/ppermute | solution.py:49
  168.6 21.4 %collective-permute-start.17 = (bf16[512,1024]{1,0:T(8,128)(2,1)}, bf16[512,1024]{1,0:T(8,128)(2,1)}, u32[]{:S(2)}, u32[]{:S(2)}) collective-permute-start(bf16[512,1024]{1,0:T(8,128)(2,1)} %context_out.3), channel_id=1, source_target_pairs={{0,1},{1,0},{2,3},{3,2},{4,5},{5,4},{6,7},{7,6},{8,9},{9,8},{10,11... | collective-permute-start | bytes 3145736 | tf_op jit(solution)/shard_map/ppermute | solution.py:49
  172.6 15.1 %collective-permute-start.26 = (bf16[2,2,1,128,512]{3,4,2,1,0:T(8,128)(2,1)}, bf16[2,2,1,128,512]{3,4,2,1,0:T(8,128)(2,1)}, u32[]{:S(2)}, u32[]{:S(2)}) collective-permute-start(bf16[2,2,1,128,512]{3,4,2,1,0:T(8,128)(2,1)} %collective-permute-done.25), channel_id=1, source_target_pairs={{0,4},{4,0},{8,12},{12,8},{16,20},{20,16},{24,28},{28,24},{1,5},{5... | collective-permute-start | bytes 1572872 | tf_op jit(solution)/shard_map/ppermute | solution.py:49
  175.0 21.6 %collective-permute-start.23 = (bf16[2,2,1,128,512]{3,4,2,1,0:T(8,128)(2,1)}, bf16[2,2,1,128,512]{3,4,2,1,0:T(8,128)(2,1)}, u32[]{:S(2)}, u32[]{:S(2)}) collective-permute-start(bf16[2,2,1,128,512]{3,4,2,1,0:T(8,128)(2,1)} %copy-done.23), channel_id=1, source_target_pairs={{0,4},{4,0},{8,12},{12,8},{16,20},{20,16},{24,28},{28,24},{1,5},{5... | collective-permute-start | bytes 1572872 | tf_op jit(solution)/shard_map/ppermute | solution.py:49
  177.5 44.7 %collective-permute-start.29 = (bf16[512,512]{1,0:T(8,128)(2,1)}, bf16[512,512]{1,0:T(8,128)(2,1)}, u32[]{:S(2)}, u32[]{:S(2)}) collective-permute-start(bf16[512,512]{1,0:T(8,128)(2,1)} %get-tuple-element.256), channel_id=1, source_target_pairs={{0,1},{1,0},{2,3},{3,2},{4,5},{5,4},{6,7},{7,6},{8,9},{9,8},{10,11... | collective-permute-start | bytes 1572872 | tf_op jit(solution)/shard_map/ppermute | solution.py:49
  177.5 37.3 %collective-permute-start.24 = (bf16[1024,512]{1,0:T(8,128)(2,1)S(1)}, bf16[1024,512]{1,0:T(8,128)(2,1)S(1)}, u32[]{:S(2)}, u32[]{:S(2)}) collective-permute-start(bf16[1024,512]{1,0:T(8,128)(2,1)S(1)} %bitcast.419), channel_id=1, source_target_pairs={{0,2},{1,3},{2,0},{3,1},{4,6},{5,7},{6,4},{7,5},{8,10},{9,11},{10,... | collective-permute-start | bytes 3145736 | tf_op jit(solution)/shard_map/ppermute | solution.py:49
  237.1 13.9 %collective-permute-start.30 = (bf16[512,1024]{1,0:T(8,128)(2,1)}, bf16[512,1024]{1,0:T(8,128)(2,1)S(1)}, u32[]{:S(2)}, u32[]{:S(2)}) collective-permute-start(bf16[512,1024]{1,0:T(8,128)(2,1)} %get-tuple-element.84.gb_ref), channel_id=1, source_target_pairs={{0,1},{1,0},{2,3},{3,2},{4,5},{5,4},{6,7},{7,6},{8,9},{9,8},{10,11... | collective-permute-start | bytes 3145736 | tf_op jit(solution)/shard_map/ppermute | solution.py:49
  265.9 32.5 %collective-permute-start.54 = (bf16[2,2,1,128,512]{3,4,0,2,1:T(8,128)(2,1)}, bf16[2,2,1,128,512]{3,4,0,2,1:T(8,128)(2,1)}, u32[]{:S(2)}, u32[]{:S(2)}) collective-permute-start(bf16[2,2,1,128,512]{3,4,0,2,1:T(8,128)(2,1)} %copy.510), channel_id=1, source_target_pairs={{0,4},{4,0},{8,12},{12,8},{16,20},{20,16},{24,28},{28,24},{1,5},{5... | collective-permute-start | bytes 1572872 | tf_op jit(solution)/shard_map/ppermute | solution.py:49
  266.5 43.6 %collective-permute-start.51 = (bf16[1024,512]{1,0:T(8,128)(2,1)}, bf16[1024,512]{1,0:T(8,128)(2,1)}, u32[]{:S(2)}, u32[]{:S(2)}) collective-permute-start(bf16[1024,512]{1,0:T(8,128)(2,1)} %get-tuple-element.198), channel_id=1, source_target_pairs={{0,2},{1,3},{2,0},{3,1},{4,6},{5,7},{6,4},{7,5},{8,10},{9,11},{10,... | collective-permute-start | bytes 3145736 | tf_op jit(solution)/shard_map/ppermute | solution.py:49
  292.7 15.1 %collective-permute-start.31 = (bf16[512,512]{1,0:T(8,128)(2,1)}, bf16[512,512]{1,0:T(8,128)(2,1)}, u32[]{:S(2)}, u32[]{:S(2)}) collective-permute-start(bf16[512,512]{1,0:T(8,128)(2,1)} %constant_dynamic-slice_fusion.16), channel_id=1, source_target_pairs={{0,2},{1,3},{2,0},{3,1},{4,6},{5,7},{6,4},{7,5},{8,10},{9,11},{10,... | collective-permute-start | bytes 1572872 | tf_op jit(solution)/shard_map/ppermute | solution.py:49
  296.5 26.4 %collective-permute-start.53 = (bf16[2,2,1,128,512]{3,4,0,2,1:T(8,128)(2,1)}, bf16[2,2,1,128,512]{3,4,0,2,1:T(8,128)(2,1)}, u32[]{:S(2)}, u32[]{:S(2)}) collective-permute-start(bf16[2,2,1,128,512]{3,4,0,2,1:T(8,128)(2,1)} %copy.508), channel_id=1, source_target_pairs={{0,4},{4,0},{8,12},{12,8},{16,20},{20,16},{24,28},{28,24},{1,5},{5... | collective-permute-start | bytes 1572872 | tf_op jit(solution)/shard_map/ppermute | solution.py:49
  298.2 15.5 %collective-permute-start.33 = (bf16[512,1024]{1,0:T(8,128)(2,1)}, bf16[512,1024]{1,0:T(8,128)(2,1)}, u32[]{:S(2)}, u32[]{:S(2)}) collective-permute-start(bf16[512,1024]{1,0:T(8,128)(2,1)} %get-tuple-element.89), channel_id=1, source_target_pairs={{0,1},{1,0},{2,3},{3,2},{4,5},{5,4},{6,7},{7,6},{8,9},{9,8},{10,11... | collective-permute-start | bytes 3145736 | tf_op jit(solution)/shard_map/ppermute | solution.py:49
  300.4 22.5 %collective-permute-start.55 = (bf16[2,2,1,128,512]{3,4,0,2,1:T(8,128)(2,1)}, bf16[2,2,1,128,512]{3,4,0,2,1:T(8,128)(2,1)}, u32[]{:S(2)}, u32[]{:S(2)}) collective-permute-start(bf16[2,2,1,128,512]{3,4,0,2,1:T(8,128)(2,1)} %add_convert_fusion.8), channel_id=1, source_target_pairs={{0,2},{1,3},{2,0},{3,1},{4,6},{5,7},{6,4},{7,5},{8,10},{9,11},{10,... | collective-permute-start | bytes 1572872 | tf_op jit(solution)/shard_map/ppermute | solution.py:49
  313.0 14.7 %collective-permute-start.52 = (bf16[2,2,1,128,512]{3,4,2,1,0:T(8,128)(2,1)}, bf16[2,2,1,128,512]{3,4,2,1,0:T(8,128)(2,1)}, u32[]{:S(2)}, u32[]{:S(2)}) collective-permute-start(bf16[2,2,1,128,512]{3,4,2,1,0:T(8,128)(2,1)} %copy.506), channel_id=1, source_target_pairs={{0,4},{4,0},{8,12},{12,8},{16,20},{20,16},{24,28},{28,24},{1,5},{5... | collective-permute-start | bytes 1572872 | tf_op jit(solution)/shard_map/ppermute | solution.py:49
  319.2 18.6 %collective-permute-start.34 = (bf16[512,1024]{1,0:T(8,128)(2,1)}, bf16[512,1024]{1,0:T(8,128)(2,1)}, u32[]{:S(2)}, u32[]{:S(2)}) collective-permute-start(bf16[512,1024]{1,0:T(8,128)(2,1)} %get-tuple-element.92), channel_id=1, source_target_pairs={{0,1},{1,0},{2,3},{3,2},{4,5},{5,4},{6,7},{7,6},{8,9},{9,8},{10,11... | collective-permute-start | bytes 3145736 | tf_op jit(solution)/shard_map/ppermute | solution.py:49
  329.8 81.8 %collective-permute-start.63 = (bf16[2,2,1,1,128,512]{4,5,1,3,2,0:T(8,128)(2,1)}, bf16[2,2,1,1,128,512]{4,5,1,3,2,0:T(8,128)(2,1)}, u32[]{:S(2)}, u32[]{:S(2)}) collective-permute-start(bf16[2,2,1,1,128,512]{4,5,1,3,2,0:T(8,128)(2,1)} %pad_maximum_fusion.26), channel_id=1, source_target_pairs={{0,8},{4,12},{8,0},{12,4},{16,24},{20,28},{24,16},{28,20},{1,9},{5... | collective-permute-start | bytes 1572872 | tf_op jit(solution)/shard_map/ppermute | solution.py:49
  331.8 104.5 %collective-permute-start.56 = (bf16[1024,512]{1,0:T(8,128)(2,1)}, bf16[1024,512]{1,0:T(8,128)(2,1)}, u32[]{:S(2)}, u32[]{:S(2)}) collective-permute-start(bf16[1024,512]{1,0:T(8,128)(2,1)} %get-tuple-element.103), channel_id=1, source_target_pairs={{0,2},{1,3},{2,0},{3,1},{4,6},{5,7},{6,4},{7,5},{8,10},{9,11},{10,... | collective-permute-start | bytes 3145736 | tf_op jit(solution)/shard_map/ppermute | solution.py:49
  334.0 115.7 %collective-permute-start.58 = (bf16[2,2,1,128,512]{4,3,0,2,1:T(8,128)(2,1)}, bf16[2,2,1,128,512]{4,3,0,2,1:T(8,128)(2,1)}, u32[]{:S(2)}, u32[]{:S(2)}) collective-permute-start(bf16[2,2,1,128,512]{4,3,0,2,1:T(8,128)(2,1)} %copy.512), channel_id=1, source_target_pairs={{0,4},{4,0},{8,12},{12,8},{16,20},{20,16},{24,28},{28,24},{1,5},{5... | collective-permute-start | bytes 1572872 | tf_op jit(solution)/shard_map/ppermute | solution.py:49
  336.8 87.6 %collective-permute-start.59 = (bf16[2,2,1,128,512]{4,3,0,2,1:T(8,128)(2,1)}, bf16[2,2,1,128,512]{4,3,0,2,1:T(8,128)(2,1)}, u32[]{:S(2)}, u32[]{:S(2)}) collective-permute-start(bf16[2,2,1,128,512]{4,3,0,2,1:T(8,128)(2,1)} %copy.514), channel_id=1, source_target_pairs={{0,4},{4,0},{8,12},{12,8},{16,20},{20,16},{24,28},{28,24},{1,5},{5... | collective-permute-start | bytes 1572872 | tf_op jit(solution)/shard_map/ppermute | solution.py:49
  389.8 64.8 %collective-permute-start.38 = (bf16[1024,512]{1,0:T(8,128)(2,1)}, bf16[1024,512]{1,0:T(8,128)(2,1)}, u32[]{:S(2)}, u32[]{:S(2)}) collective-permute-start(bf16[1024,512]{1,0:T(8,128)(2,1)} %pad_maximum_fusion.14), channel_id=1, source_target_pairs={{0,2},{1,3},{2,0},{3,1},{4,6},{5,7},{6,4},{7,5},{8,10},{9,11},{10,... | collective-permute-start | bytes 3145736 | tf_op jit(solution)/shard_map/ppermute | solution.py:49
  428.2 40.9 %collective-permute-start.40 = (bf16[2,2,1,128,512]{3,4,0,2,1:T(8,128)(2,1)}, bf16[2,2,1,128,512]{3,4,0,2,1:T(8,128)(2,1)}, u32[]{:S(2)}, u32[]{:S(2)}) collective-permute-start(bf16[2,2,1,128,512]{3,4,0,2,1:T(8,128)(2,1)} %fusion.3), channel_id=1, source_target_pairs={{0,4},{4,0},{8,12},{12,8},{16,20},{20,16},{24,28},{28,24},{1,5},{5... | collective-permute-start | bytes 1572872 | tf_op jit(solution)/shard_map/ppermute | solution.py:49
  434.1 14.8 %collective-permute-start.41 = (bf16[2,2,1,128,512]{3,4,0,2,1:T(8,128)(2,1)S(1)}, bf16[2,2,1,128,512]{3,4,0,2,1:T(8,128)(2,1)S(1)}, u32[]{:S(2)}, u32[]{:S(2)}) collective-permute-start(bf16[2,2,1,128,512]{3,4,0,2,1:T(8,128)(2,1)S(1)} %copy-done.41), channel_id=1, source_target_pairs={{0,4},{4,0},{8,12},{12,8},{16,20},{20,16},{24,28},{28,24},{1,5},{5... | collective-permute-start | bytes 1572872 | tf_op jit(solution)/shard_map/ppermute | solution.py:49
  436.2 15.2 %collective-permute-start.60 = (bf16[2,2,1,128,512]{4,3,0,2,1:T(8,128)(2,1)S(1)}, bf16[2,2,1,128,512]{4,3,0,2,1:T(8,128)(2,1)S(1)}, u32[]{:S(2)}, u32[]{:S(2)}) collective-permute-start(bf16[2,2,1,128,512]{4,3,0,2,1:T(8,128)(2,1)S(1)} %add_convert_fusion.4), channel_id=1, source_target_pairs={{0,2},{1,3},{2,0},{3,1},{4,6},{5,7},{6,4},{7,5},{8,10},{9,11},{10,... | collective-permute-start | bytes 1572872 | tf_op jit(solution)/shard_map/ppermute | solution.py:49
  449.8 16.4 %collective-permute-start.57 = (bf16[2,2,1,128,512]{4,3,2,1,0:T(8,128)(2,1)}, bf16[2,2,1,128,512]{4,3,2,1,0:T(8,128)(2,1)}, u32[]{:S(2)}, u32[]{:S(2)}) collective-permute-start(bf16[2,2,1,128,512]{4,3,2,1,0:T(8,128)(2,1)} %constant_dynamic-slice_fusion.4), channel_id=1, source_target_pairs={{0,4},{4,0},{8,12},{12,8},{16,20},{20,16},{24,28},{28,24},{1,5},{5... | collective-permute-start | bytes 1572872 | tf_op jit(solution)/shard_map/ppermute | solution.py:49
  451.5 17.7 %collective-permute-start.42 = (bf16[2,2,1,128,512]{3,4,0,2,1:T(8,128)(2,1)}, bf16[2,2,1,128,512]{3,4,0,2,1:T(8,128)(2,1)}, u32[]{:S(2)}, u32[]{:S(2)}) collective-permute-start(bf16[2,2,1,128,512]{3,4,0,2,1:T(8,128)(2,1)} %add_convert_fusion.12), channel_id=1, source_target_pairs={{0,2},{1,3},{2,0},{3,1},{4,6},{5,7},{6,4},{7,5},{8,10},{9,11},{10,... | collective-permute-start | bytes 1572872 | tf_op jit(solution)/shard_map/ppermute | solution.py:49
  459.3 16.4 %collective-permute-start.39 = (bf16[2,2,1,128,512]{3,4,2,1,0:T(8,128)(2,1)}, bf16[2,2,1,128,512]{3,4,2,1,0:T(8,128)(2,1)}, u32[]{:S(2)}, u32[]{:S(2)}) collective-permute-start(bf16[2,2,1,128,512]{3,4,2,1,0:T(8,128)(2,1)} %copy.504), channel_id=1, source_target_pairs={{0,4},{4,0},{8,12},{12,8},{16,20},{20,16},{24,28},{28,24},{1,5},{5... | collective-permute-start | bytes 1572872 | tf_op jit(solution)/shard_map/ppermute | solution.py:49
  465.6 19.0 %collective-permute-start.36 = (bf16[512,512]{1,0:T(8,128)(2,1)}, bf16[512,512]{1,0:T(8,128)(2,1)S(1)}, u32[]{:S(2)}, u32[]{:S(2)}) collective-permute-start(bf16[512,512]{1,0:T(8,128)(2,1)} %constant_dynamic-slice_fusion.15), channel_id=1, source_target_pairs={{0,2},{1,3},{2,0},{3,1},{4,6},{5,7},{6,4},{7,5},{8,10},{9,11},{10,... | collective-permute-start | bytes 1572872 | tf_op jit(solution)/shard_map/ppermute | solution.py:49
  467.5 14.8 %collective-permute-start.61 = (bf16[2,2,1,1,128,512]{5,4,1,3,2,0:T(8,128)(2,1)S(1)}, bf16[2,2,1,1,128,512]{5,4,1,3,2,0:T(8,128)(2,1)S(1)}, u32[]{:S(2)}, u32[]{:S(2)}) collective-permute-start(bf16[2,2,1,1,128,512]{5,4,1,3,2,0:T(8,128)(2,1)S(1)} %pad_maximum_fusion.25), channel_id=1, source_target_pairs={{0,8},{4,12},{8,0},{12,4},{16,24},{20,28},{24,16},{28,20},{1,9},{5... | collective-permute-start | bytes 1572872 | tf_op jit(solution)/shard_map/ppermute | solution.py:49
  477.0 20.7 %collective-permute-start.43 = (bf16[2,2,1,1,128,512]{4,5,1,3,2,0:T(8,128)(2,1)S(1)}, bf16[2,2,1,1,128,512]{4,5,1,3,2,0:T(8,128)(2,1)S(1)}, u32[]{:S(2)}, u32[]{:S(2)}) collective-permute-start(bf16[2,2,1,1,128,512]{4,5,1,3,2,0:T(8,128)(2,1)S(1)} %pad_maximum_fusion.24), channel_id=1, source_target_pairs={{0,8},{4,12},{8,0},{12,4},{16,24},{20,28},{24,16},{28,20},{1,9},{5... | collective-permute-start | bytes 1572872 | tf_op jit(solution)/shard_map/ppermute | solution.py:49
  482.5 14.3 %collective-permute-start.62 = (bf16[2,1,1,1,128,512]{5,4,3,2,1,0:T(8,128)(2,1)S(1)}, bf16[2,1,1,1,128,512]{5,4,3,2,1,0:T(8,128)(2,1)S(1)}, u32[]{:S(2)}, u32[]{:S(2)}) collective-permute-start(bf16[2,1,1,1,128,512]{5,4,3,2,1,0:T(8,128)(2,1)S(1)} %pad_maximum_fusion.37), channel_id=1, source_target_pairs={{0,16},{4,20},{8,24},{12,28},{16,0},{20,4},{24,8},{28,12},{1,17},{... | collective-permute-start | bytes 786440 | tf_op jit(solution)/shard_map/ppermute | solution.py:49
  485.0 16.4 %collective-permute-start.37 = (bf16[1024,256]{1,0:T(8,128)(2,1)S(1)}, bf16[1024,256]{1,0:T(8,128)(2,1)S(1)}, u32[]{:S(2)}, u32[]{:S(2)}) collective-permute-start(bf16[1024,256]{1,0:T(8,128)(2,1)S(1)} %get-tuple-element.244), channel_id=1, source_target_pairs={{0,1},{1,0},{2,3},{3,2},{4,5},{5,4},{6,7},{7,6},{8,9},{9,8},{10,11... | collective-permute-start | bytes 1572872 | tf_op jit(solution)/shard_map/ppermute | solution.py:49
  497.9 14.1 %collective-permute-start.44 = (bf16[2,1,1,1,128,512]{4,5,3,2,1,0:T(8,128)(2,1)S(1)}, bf16[2,1,1,1,128,512]{4,5,3,2,1,0:T(8,128)(2,1)S(1)}, u32[]{:S(2)}, u32[]{:S(2)}) collective-permute-start(bf16[2,1,1,1,128,512]{4,5,3,2,1,0:T(8,128)(2,1)S(1)} %pad_maximum_fusion.36), channel_id=1, source_target_pairs={{0,16},{4,20},{8,24},{12,28},{16,0},{20,4},{24,8},{28,12},{1,17},{... | collective-permute-start | bytes 786440 | tf_op jit(solution)/shard_map/ppermute | solution.py:49
  (75 other events, 630.4 us)

commit v4 on v3

--- a/solution.py
+++ b/solution.py
@@ -12,6 +12,7 @@
 NORM_EPS = 1e-06
 MASKED = -1000000000.0
 LONGEST = 256
+COL = ("seq", "way")
 F32 = jnp.float32
 BF16 = jnp.bfloat16
 
@@ -233,6 +234,29 @@
     return pl.BlockSpec((a.shape[0], tile, a.shape[2]), lambda i, at: (0, at[0] * per + i, 0))
 
 
+class Slab:
+    def __init__(self, array, width, block, order):
+        self.array, self.width = array, width
+        shape = (array.shape[0], 1, array.shape[2], width)
+        self.spec = pl.BlockSpec(shape, lambda i, at: (0, at[1 + order], 0, block))
+
+
+def arrays(slabs):
+    return [w.array for w in slabs]
+
+
+def specs_of(slabs):
+    return [w.spec for w in slabs]
+
+
+def rows_of(slab):
+    return slab.array.shape[0] * slab.array.shape[2]
+
+
+def flat(ref):
+    return ref[:, 0].reshape(ref.shape[0] * ref.shape[2], ref.shape[3])
+
+
 def project_kernel(x_ref, b_ref, *refs):
     count = b_ref.shape[0]
     weights, (q_ref, k_ref, v_ref) = refs[:count], refs[count:]
@@ -260,49 +284,49 @@
 
 def context_out_kernel(at, ctx_ref, *refs):
     weights, out_ref = refs[:-1], refs[-1]
-    lanes = ctx_ref.shape[2]
-    left = jnp.concatenate([ctx_ref[i] for i in range(len(weights))], axis=1)
-    right = jnp.concatenate([w[:, w.shape[1] - lanes :] for w in weights], axis=1)
+    left = jnp.concatenate([ctx_ref[i] for i in range(ctx_ref.shape[0])], axis=1)
+    right = jnp.concatenate([flat(w) for w in weights], axis=1)
     out_ref[...] = nt(left, right).astype(out_ref.dtype)
 
 
 def context_out(at, ctx, weights, part, dtype):
     tile = row_tile(part)
-    model = weights[0].shape[0]
+    model = rows_of(weights[0])
     out = struct((part, model), dtype)
     return launch(
-        context_out_kernel, part // tile, [at], [ctx] + weights,
-        [tall_from(ctx, tile, part // tile)] + [fixed(w) for w in weights], [out], [tall(out, tile)], [],
+        context_out_kernel, part // tile, [at], [ctx] + arrays(weights),
+        [tall_from(ctx, tile, part // tile)] + specs_of(weights), [out], [tall(out, tile)], [],
         2 * part * model * ctx.shape[0] * ctx.shape[2], "context_out",
     )[0]
 
 
-def context_back_kernel(ga_ref, *refs):
+def context_back_kernel(at, ga_ref, *refs):
     weights, out_ref = refs[:-1], refs[-1]
     lanes = out_ref.shape[2]
-    right = jnp.concatenate([w[:, w.shape[1] - lanes :] for w in weights], axis=1)
+    right = jnp.concatenate([flat(w) for w in weights], axis=1)
     grad = nn(ga_ref[...], right).astype(BF16)
-    for i in range(len(weights)):
+    for i in range(out_ref.shape[0]):
         out_ref[i] = grad[:, i * lanes : (i + 1) * lanes]
 
 
-def context_back(ga, weights, lanes):
+def context_back(at, ga, weights):
+    lanes = weights[0].width // 2
     tile = row_tile(ga.shape[0])
-    out = struct((len(weights), ga.shape[0], lanes), BF16)
-    return launch(
-        context_back_kernel, ga.shape[0] // tile, [], [ga] + weights,
-        [tall(ga, tile)] + [fixed(w) for w in weights], [out], [tall(out, tile)], [],
-        2 * math.prod(ga.shape) * lanes * len(weights), "context_back",
+    count = 2 * len(weights)
+    out = struct((count, ga.shape[0], lanes), BF16)
+    return launch(
+        context_back_kernel, ga.shape[0] // tile, [at], [ga] + arrays(weights),
+        [tall(ga, tile)] + specs_of(weights), [out], [tall(out, tile)], [],
+        2 * math.prod(ga.shape) * lanes * count, "context_back",
     )[0]
 
 
-def ffn_in_kernel(y_ref, b_ref, *refs):
+def ffn_in_kernel(at, y_ref, b_ref, *refs):
     count = b_ref.shape[0]
-    wide = b_ref.shape[2]
     weights, (act_ref, slope_ref) = refs[:count], refs[-2:]
     y = y_ref[...]
     for i in range(count):
-        inner = nn(y, weights[i][:, :wide]) + b_ref[i]
+        inner = nn(y, flat(weights[i])) + b_ref[i]
         share = 0.5 + 0.5 * lax.erf(inner * math.sqrt(0.5))
         density = jnp.exp(-0.5 * inner * inner) * (1.0 / math.sqrt(2.0 * math.pi))
         act_ref[i] = (inner * share).astype(BF16)
@@ -313,7 +337,7 @@
     return pl.BlockSpec((a.shape[0], tile, a.shape[2]), lambda i, *_: (0, first + i, 0))
 
 
-def ffn_in(y, bias, weights, ways, place_at, earlier):
+def ffn_in(at, y, bias, weights, ways, place_at, earlier):
     part, model = y.shape
     tile = row_tile(part)
     first = place_at * (part // tile)
@@ -322,47 +346,46 @@
     out = struct((count, part * ways, wide), BF16)
     anywhere = [pl.BlockSpec(memory_space=pl.ANY)] * len(earlier)
     return launch(
-        ffn_in_kernel, part // tile, [], [y, bias] + weights + earlier,
-        [tall(y, tile), fixed(bias)] + [fixed(w) for w in weights] + anywhere,
+        ffn_in_kernel, part // tile, [at], [y, bias] + arrays(weights) + earlier,
+        [tall(y, tile), fixed(bias)] + specs_of(weights) + anywhere,
         [out, out], [place(out, tile, first)] * 2, [],
         6 * part * model * wide * count, "ffn_in",
-        {2 + count + i: i for i in range(len(earlier))},
-    )
-
-
-def ffn_out_kernel(act_ref, *refs):
+        {3 + count + i: i for i in range(len(earlier))},
+    )
+
+
+def ffn_out_kernel(at, act_ref, *refs):
     weights, out_ref = refs[:-1], refs[-1]
-    total = nt(act_ref[0], weights[0][...])
+    total = nt(act_ref[0], flat(weights[0]))
     for i in range(1, len(weights)):
-        total += nt(act_ref[i], weights[i][...])
+        total += nt(act_ref[i], flat(weights[i]))
     out_ref[...] = total.astype(out_ref.dtype)
 
 
-def ffn_out(act, weights, part, place_at, dtype):
+def ffn_out(at, act, weights, part, place_at, dtype):
     tile = row_tile(part)
-    model = weights[0].shape[0]
+    model = rows_of(weights[0])
     out = struct((part, model), dtype)
     return launch(
-        ffn_out_kernel, part // tile, [], [act] + weights,
-        [place(act, tile, place_at * (part // tile))] + [fixed(w) for w in weights],
+        ffn_out_kernel, part // tile, [at], [act] + arrays(weights),
+        [place(act, tile, place_at * (part // tile))] + specs_of(weights),
         [out], [tall(out, tile)], [], 2 * part * model * act.shape[0] * act.shape[2], "ffn_out",
     )[0]
 
 
-def ffn_back_kernel(gb_ref, slope_ref, *refs):
+def ffn_back_kernel(at, gb_ref, slope_ref, *refs):
     count = slope_ref.shape[0]
-    wide = slope_ref.shape[2]
     outs, ins = refs[:count], refs[count : 2 * count]
     gi_ref, sum_ref, out_ref = refs[-3:]
     gb = gb_ref[...]
     total = None
     sums = []
     for i in range(count):
-        grad = nn(gb, outs[i][...]) * slope_ref[i].astype(F32)
+        grad = nn(gb, flat(outs[i])) * slope_ref[i].astype(F32)
         low = grad.astype(BF16)
         gi_ref[i] = low
         sums.append(jnp.sum(grad, axis=0, keepdims=True))
-        term = nt(low, ins[i][:, :wide])
+        term = nt(low, flat(ins[i]))
         total = term if total is None else total + term
     out_ref[...] = total.astype(out_ref.dtype)
 
@@ -374,7 +397,7 @@
         sum_ref[i] += sums[i]
 
 
-def ffn_back(gb, slope, outs_w, ins_w, place_at, earlier, dtype):
+def ffn_back(at, gb, slope, outs_w, ins_w, place_at, earlier, dtype):
     part, model = gb.shape
     tile = row_tile(part)
     first = place_at * (part // tile)
@@ -382,11 +405,11 @@
     anywhere = [pl.BlockSpec(memory_space=pl.ANY)] * len(earlier)
     outs = [struct(slope.shape, BF16), struct((count, 1, wide), F32), struct((part, model), dtype)]
     return launch(
-        ffn_back_kernel, part // tile, [], [gb, slope] + outs_w + ins_w + earlier,
-        [tall(gb, tile), place(slope, tile, first)] + [fixed(w) for w in outs_w + ins_w] + anywhere,
+        ffn_back_kernel, part // tile, [at], [gb, slope] + arrays(outs_w + ins_w) + earlier,
+        [tall(gb, tile), place(slope, tile, first)] + specs_of(outs_w + ins_w) + anywhere,
         outs, [place(outs[0], tile, first), fixed(outs[1]), tall(outs[2], tile)], [],
         4 * part * model * wide * count, "ffn_back",
-        {2 + 2 * count + i: i for i in range(len(earlier))},
+        {3 + 2 * count + i: i for i in range(len(earlier))},
     )
 
 
@@ -409,23 +432,68 @@
     )[0]
 
 
-def weight_grad(left, right):
-    length, model = left.shape
-    count, _, wide = right.shape
-    out = struct((count, model, wide), BF16)
-
-    def kernel(left_ref, right_ref, out_ref, left_t):
+def transpose_into(left_t, lefts):
+    first = 0
+    for left in lefts:
+        left_t[:, first : first + left.shape[0]] = left[...].T
+        first += left.shape[0]
+
+
+def weight_grad(lefts, right):
+    count, length, wide = right.shape
+    model = lefts[0].shape[1]
+    out = struct((model, wide), BF16)
+    parts = len(lefts)
+
+    def kernel(*refs):
+        right_ref, outs = refs[parts], refs[parts + 1 : parts + 1 + count]
+        left_t, slots, sems = refs[-3:]
+        copies = [pltpu.make_async_copy(slots.at[k % 2], outs[k], sems.at[k % 2]) for k in range(count)]
+
+        def step(k):
+            if k == 0:
+                transpose_into(left_t, refs[:parts])
+            if k > 1:
+                copies[k - 2].wait()
+            slots[k % 2] = nn(left_t[...], right_ref[0]).astype(BF16)
+            copies[k].start()
+            if k == count - 1:
+                for last in copies[max(k - 1, 0) :]:
+                    last.wait()
+
+        for k in range(count):
+            pl.when(pl.program_id(0) == k)(functools.partial(step, k))
+
+    return launch(
+        kernel, count, [], list(lefts) + [right], [fixed(a) for a in lefts] + [slab(right)], [out] * count,
+        [pl.BlockSpec(memory_space=pl.ANY)] * count,
+        [pltpu.VMEM((model, length), BF16), pltpu.VMEM((2, model, wide), BF16), pltpu.SemaphoreType.DMA((2,))],
+        2 * length * model * wide * count, "weight_grad",
+    )
+
+
+def weight_grad_shards(at, lefts, right, rows, seqs):
+    count, length, wide = right.shape
+    model = lefts[0].shape[1]
+    halves = count // seqs
+    out = struct((rows, seqs, model // rows, wide * halves), BF16)
+    parts = len(lefts)
+
+    def kernel(at_ref, *refs):
+        right_ref, out_ref, left_t = refs[parts:]
+
         @pl.when(pl.program_id(0) == 0)
         def _():
-            left_t[...] = left_ref[...].T
-
-        out_ref[0] = nn(left_t[...], right_ref[0]).astype(BF16)
-
-    stack = launch(
-        kernel, count, [], [left, right], [fixed(left), slab(right)], [out], [slab(out)],
-        [pltpu.VMEM((model, length), BF16)], 2 * length * model * wide * count, "weight_grad",
+            transpose_into(left_t, refs[:parts])
+
+        made = nn(left_t[...], right_ref[0]).astype(BF16)
+        out_ref[:, 0] = made.reshape(out_ref.shape[0], out_ref.shape[2], wide)
+
+    spec = pl.BlockSpec((rows, 1, model // rows, wide), lambda i, at: (0, at[1 + i // halves], 0, i % halves))
+    return launch(
+        kernel, count, [at], list(lefts) + [right], [fixed(a) for a in lefts] + [slab(right)], [out], [spec],
+        [pltpu.VMEM((model, length), BF16)], 2 * length * model * wide * count, "weight_grad_shards",
     )[0]
-    return [stack[i] for i in range(count)]
 
 
 def norm_rows(hidden):
@@ -541,15 +609,18 @@
     hid = w_in.shape[1]
     part = length // ways
     own_rows = wqkv.shape[0]
-    row, col = lax.axis_index("row"), lax.axis_index("col")
+    row, col = lax.axis_index("row"), lax.axis_index(COL)
     seq, way = col // ways, col % ways
-    by_seq = [Stage("col", cols, mask * ways, col) for mask in bits_of(seqs)]
-    by_way = [Stage("col", cols, mask, col) for mask in bits_of(ways)]
+    by_seq = [Stage(COL, cols, mask * ways, col) for mask in bits_of(seqs)]
+    by_way = [Stage(COL, cols, mask, col) for mask in bits_of(ways)]
     by_row = [Stage("row", rows, mask, row) for mask in bits_of(rows)]
     ns, nw, nr = len(by_seq), len(by_way), len(by_row)
     far, near = by_row[:-1], by_row[-1]
     parts = range(ways)
-    at = [((way ^ p) * jnp.ones((1,), jnp.int32)).astype(jnp.int32) for p in parts]
+    orders = [0]
+    for mask in bits_of(seqs):
+        orders = orders + [o ^ mask for o in orders]
+    at = [jnp.stack([way ^ p] + [seq ^ o for o in orders]).astype(jnp.int32) for p in parts]
 
     def gather_far(one, two):
         halves = [h.reshape((1,) * nr + h.shape) for h in (one, two)]
@@ -661,12 +732,18 @@
     in_bias = jnp.concatenate(in_biases, axis=0)
 
     qkv_all = gather_last(*far_qkv)
-    wo_t, out_t = halves_of(wo.T), halves_of(w_out.T)
-    both_in = [jnp.concatenate((a, b), axis=1) for a, b in zip(halves_of(w_in), wo_t)]
-    far_in = gather_far(*[after(b, *far_qkv) for b in both_in])
-    far_out = gather_far(*[after(b, *far_in) for b in out_t])
-    in_all = gather_last(*[after(b, qkv_all[0], qkv_all[3]) for b in far_in])
-    out_all = gather_last(*[after(b, in_all[0], in_all[3]) for b in far_out])
+    everyone = ("row", "seq")
+
+    def shards(weight):
+        whole = lax.all_gather(weight, everyone, axis=0, tiled=True)
+        return whole.reshape(rows, seqs, own_rows, weight.shape[1])
+
+    whole_in = shards(jnp.concatenate((w_in, wo.T), axis=1))
+    whole_out = shards(w_out.T)
+    pairs_of = [(j, h) for j in range(seqs) for h in range(2)]
+    in_all = [Slab(whole_in, hid // 2, h, j) for j, h in pairs_of]
+    wo_all = [Slab(whole_in, 2 * lanes, hid // (2 * lanes), j) for j in range(seqs)]
+    out_all = [Slab(whole_out, hid // 2, h, j) for j, h in pairs_of]
     cot = exchange(after(cotangent, qkv_all[2]), by_seq + by_way, [])
 
     def gather_parts(own):
@@ -716,38 +793,39 @@
 
     q, k, v = project(whole_x, qkv_all, q_bias)
     context, lse = attend(windows, q, k, v, lab_col, lab_row)
-    mine, got = scatter_parts(lambda p, dtype: context_out(at[p], context, in_all, part, dtype))
+    mine, got = scatter_parts(lambda p, dtype: context_out(at[p], context, wo_all, part, dtype))
     centred_a, inv_a, y = norm_a(at[0], mine, got, whole_x, vec)
     y_parts = gather_parts(y)
     earlier = []
     for p in parts:
-        earlier = ffn_in(y_parts[p], in_bias, in_all, ways, p, list(earlier))
+        earlier = ffn_in(at[0], y_parts[p], in_bias, in_all, ways, p, list(earlier))
     active, slope = earlier
-    mine, got = scatter_parts(lambda p, dtype: ffn_out(active, out_all, part, p, dtype))
+    mine, got = scatter_parts(lambda p, dtype: ffn_out(at[0], active, out_all, part, p, dtype))
     output, grad_b, gb, sums_b = norm_b(mine, got, centred_a, cot, vec)
 
     gb_parts = gather_parts(gb)
     output = to_features(after(output, gb_parts[-1]))
+    grad_w_out = weight_grad_shards(at[0], gb_parts, active, rows, seqs)
+    out_sum = lax.psum_scatter(
+        grad_w_out.reshape(rows * seqs * own_rows, hid), everyone, scatter_dimension=0, tiled=True
+    )
     terms, sum_in, earlier = {}, 0.0, []
     for p in parts:
         grad_inner, sums, terms[p] = ffn_back(
-            gb_parts[p], slope, out_all, in_all, p, earlier, F32 if p == 0 else BF16
+            at[0], after(gb_parts[p], grad_w_out), slope, out_all, in_all, p, earlier, F32 if p == 0 else BF16
         )
         earlier = [grad_inner]
         sum_in = sum_in + sums
     mine, got = scatter_parts(lambda p, dtype: terms[p])
-    grad_w_out = weight_grad(jnp.concatenate(gb_parts, axis=0), active)
-    grad_w_in = weight_grad(jnp.concatenate(y_parts, axis=0), grad_inner)
-    first_out = scatter_first(grad_w_out)
+    grad_w_in = weight_grad(y_parts, grad_inner)
     grad_a, ga, sums_a = norm_a_back(mine, got, grad_b, centred_a, inv_a, vec)
     whole_ga = whole_rows(gather_parts(ga))
-    grad_context = context_back(whole_ga, in_all, lanes)
-    first_in = scatter_first([after(b, *first_out) for b in grad_w_in])
-    out_halves = scatter_far(*first_out)
+    grad_context = context_back(at[0], whole_ga, wo_all)
+    first_in = scatter_first(grad_w_in)
     grad_projected, sum_projected = attend_back(windows, q, k, v, grad_context, lse, lab_col, lab_row)
     in_halves = scatter_far(*first_in)
-    grad_wo = weight_grad(whole_ga, context)
-    grad_wqkv = weight_grad(whole_x, grad_projected)
+    grad_wo = weight_grad([whole_ga], context)
+    grad_wqkv = weight_grad([whole_x], grad_projected)
     last = scatter_first([jnp.concatenate(two, axis=1) for two in zip(grad_wqkv, grad_wo)])
     mine, got = scatter_parts(lambda p, dtype: inputs_back(at[p], grad_projected, qkv_all, part, dtype))
     grad_tokens = to_features((mine + got.astype(F32) + grad_a).astype(BF16)).astype(F32)
@@ -785,7 +863,7 @@
         rest[2],
         jnp.concatenate(in_halves, axis=1),
         sum_in,
-        jnp.concatenate(out_halves, axis=1).T,
+        out_sum.astype(F32).T,
         rest[3],
         rest[4],
         rest[5],
@@ -793,12 +871,24 @@
 
 
 def solution(mesh):
-    tile, across, down, flat = P("row", "col"), P("row", None), P("col", "row"), P("col")
-    in_specs = (tile, across, tile, flat, down, flat, flat, flat, tile, flat, down, flat, flat, flat, tile)
-    out_specs = (tile, tile, tile, flat, down, flat, flat, flat, tile, flat, down, flat, flat, flat)
     rows, cols = mesh.shape["row"], mesh.shape["col"]
-
-    def layer(*args):
-        return body(rows, cols, *args)
-
-    return jax.shard_map(layer, mesh=mesh, in_specs=in_specs, out_specs=out_specs, check_vma=False)
+    tile, across, down, flat_col = P("row", COL), P("row", None), P(COL, "row"), P(COL)
+    in_specs = (
+        tile, across, tile, flat_col, down, flat_col, flat_col, flat_col,
+        tile, flat_col, down, flat_col, flat_col, flat_col, tile,
+    )
+    out_specs = (
+        tile, tile, tile, flat_col, down, flat_col, flat_col, flat_col,
+        tile, flat_col, down, flat_col, flat_col, flat_col,
+    )
+
+    def run(*args):
+        seqs = args[1].shape[0] // rows
+        fine = jax.sharding.Mesh(mesh.devices.reshape(rows, seqs, cols // seqs), ("row",) + COL)
+
+        def layer(*local):
+            return body(rows, cols, *local)
+
+        return jax.shard_map(layer, mesh=fine, in_specs=in_specs, out_specs=out_specs, check_vma=False)(*args)
+
+    return run

time: 521 us -> 552 us (1.060)
  waiting for transfers between devices: 136 us -> 224 us
  other arithmetic: 80.2 us -> 50.5 us
  starting transfers between devices: 66.8 us -> 39.3 us
  local copies, waits for them, and re-layouts: 55.6 us -> 36 us
  between operations: 2.6 us -> 15.4 us
  Pallas kernels: 173 us -> 179 us
    all_gather x0 -> x2, waiting for transfers between devices: none -> 53.1 us  [shards(): whole = lax.all_gather(weight, everyone, axis=0, tiled=True)]
    ppermute x65 -> x44, waiting for transfers between devices: 136 us -> 170 us  [trade(): return lax.ppermute(block, self.axis, self.pairs)]
    ppermute x65 -> x44, starting transfers between devices: 66.8 us -> 39.2 us  [trade(): return lax.ppermute(block, self.axis, self.pairs)]
    select_n x16 -> x6, other arithmetic: 13 us -> 3.48 us  [join(): jnp.where(low, mine, other)]
    squeeze x3 -> x0, local copies, waits for them, and re-layouts: 9.2 us -> none  [weight_grad(): return [stack[i] for i in range(count)]]
    concatenate x18 -> x6, other arithmetic: 8.67 us -> 0.37 us  [join(): jnp.concatenate((jnp.where(low, mine, other), jnp.where(low, other, mine)...]
    convert_element_type x18 -> x12, other arithmetic: 19.3 us -> 12.2 us  [add(): return (mine.astype(F32) + other.astype(F32)).astype(mine.dtype)]
    pallas_call x21, Pallas kernels: 173 us -> 179 us  [launch(): pl.pallas_call(kernel, grid_spec=pltpu.PrefetchScalarGridSpec(num_scalar_...]
  transfers between devices with their start and end apart: 65 -> 47, of which waited for: 21 -> 20; matrix products, arithmetic and copies ran while one was open for 24% -> 14% of each run, Pallas kernels for 31% -> 30%
where the time goes in v4:
time: 552 us; the launch traced here: 544 us
  waiting for transfers between devices  224 us (41%)
  Pallas kernels  179 us (32%)
  other arithmetic  50.5 us (9%)
  starting transfers between devices  39.3 us (7%)
  local copies, waits for them, and re-layouts  36 us (7%)
  between operations  15.4 us (3%)
    pallas_call x21, Pallas kernels, launch(): pl.pallas_call(kernel, grid_spec=pltpu.PrefetchScalarGridSpec(num_scalar_...  179 us
    ppermute x44, waiting for transfers between devices, trade(): return lax.ppermute(block, self.axis, self.pairs)  170 us
    all_gather x2, waiting for transfers between devices, shards(): whole = lax.all_gather(weight, everyone, axis=0, tiled=True)  53.1 us
    ppermute x44, starting transfers between devices, trade(): return lax.ppermute(block, self.axis, self.pairs)  39.2 us
    unnamed x90, local copies, waits for them, and re-layouts  17.8 us
    convert_element_type x12, other arithmetic, add(): return (mine.astype(F32) + other.astype(F32)).astype(mine.dtype)  12.2 us
  transfers between devices with their start and end apart: 47, of which 20 were waited for; matrix products, arithmetic and copies ran while one was open for 14% of the time, Pallas kernels for 30%

profile of v4, /device:TPU:0, one launch (start us, length us, event | category | flops | bytes accessed | tf_op | source)
XLA Modules:
  0.0 544.0 jit_solution(13414880690398400577)
XLA Ops:
  11.2 4.1 collective-permute-start
  16.0 8.5 %collective-permute-done = bf16[2,1,1,1,128,384]{4,5,3,2,1,0:T(8,128)(2,1)S(1)} collective-permute-done((bf16[2,1,1,1,128,384]{4,5,3,2,1,0:T(8,128)(2,1)S(1)}, bf16[2,1,1,1,128,384]{4,5,3,2,1,0:T(8,128)(2,1)S(1)}, u32[]{:S(2)}, u32[]{:S(2)}) %collective-permute-start) | collective-permute-done | bytes 196640 | tf_op jit(solution)/shard_map/ppermute | solution.py:50
  28.3 12.8 %collective-permute-done.1 = bf16[2,2,1,1,128,384]{4,5,1,3,2,0:T(8,128)(2,1)S(1)} collective-permute-done((bf16[2,2,1,1,128,384]{4,5,1,3,2,0:T(8,128)(2,1)S(1)}, bf16[2,2,1,1,128,384]{4,5,1,3,2,0:T(8,128)(2,1)S(1)}, u32[]{:S(2)}, u32[]{:S(2)}) %collective-permute-start.1) | collective-permute-done | bytes 393248 | tf_op jit(solution)/shard_map/ppermute | solution.py:50
  46.8 10.1 %collective-permute-done.5 = bf16[2,2,1,128,384]{3,4,2,1,0:T(8,128)(2,1)} collective-permute-done((bf16[2,2,1,128,384]{3,4,2,1,0:T(8,128)(2,1)S(1)}, bf16[2,2,1,128,384]{3,4,2,1,0:T(8,128)(2,1)}, u32[]{:S(2)}, u32[]{:S(2)}) %collective-permute-start.5) | collective-permute-done | bytes 393248 | tf_op jit(solution)/shard_map/ppermute | solution.py:50
  59.9 14.8 %collective-permute-done.2 = bf16[1024,256]{1,0:T(8,128)(2,1)S(1)} collective-permute-done((bf16[1024,256]{1,0:T(8,128)(2,1)S(1)}, bf16[1024,256]{1,0:T(8,128)(2,1)S(1)}, u32[]{:S(2)}, u32[]{:S(2)}) %collective-permute-start.2) | collective-permute-done | bytes 524320 | tf_op jit(solution)/shard_map/ppermute | solution.py:50
  81.7 16.9 %collective-permute-done.9 = bf16[2,2,1,128,384]{3,4,2,1,0:T(8,128)(2,1)} collective-permute-done((bf16[2,2,1,128,384]{3,4,2,1,0:T(8,128)(2,1)}, bf16[2,2,1,128,384]{3,4,2,1,0:T(8,128)(2,1)}, u32[]{:S(2)}, u32[]{:S(2)}) %collective-permute-start.9) | collective-permute-done | bytes 393248 | tf_op jit(solution)/shard_map/ppermute | solution.py:50
  104.0 10.0 %collective-permute-done.7.refs_2_ = bf16[1024,384]{1,0:T(8,128)(2,1)S(1)} collective-permute-done((bf16[1024,384]{1,0:T(8,128)(2,1)S(1)}, bf16[1024,384]{1,0:T(8,128)(2,1)S(1)}, u32[]{:S(2)}, u32[]{:S(2)}) %collective-permute-start.7) | collective-permute-done | bytes 786464 | tf_op jit(solution)/shard_map/ppermute | solution.py:50
  115.0 8.6 %project.1 = (bf16[4,1024,128]{2,1,0:T(8,128)(2,1)}, bf16[4,1024,128]{2,1,0:T(8,128)(2,1)}, bf16[4,1024,128]{2,1,0:T(8,128)(2,1)}) custom-call(bf16[1024,1024]{1,0:T(8,128)(2,1)} %pad_maximum_fusion.x_ref.refs_0_, f32[4,1,384]{2,1,0:T(1,128)} %reshape.877.b_ref, bf16[1024,384]{1,0:T(8,128)(2,1)} %bitcast.279, bf16[1024,384]{1,0:T(8,128)(2,1)} %bitcast.282, ...), custom_call_target="tpu_custom_call" | custom-call | flops 3221225472 | bytes 8394752 | tf_op jit(solution)/shard_map/project/pallas_call | solution.py:183
  123.5 20.1 %attend.1 = (bf16[4,1024,128]{2,1,0:T(8,128)(2,1)}, f32[4,2,1024]{2,1,0:T(2,128)}) custom-call(s32[2,4]{1,0:T(2,128)} %pad_add_fusion.windows, bf16[4,1024,128]{2,1,0:T(8,128)(2,1)} %get-tuple-element.63.q_ref, bf16[4,1024,128]{2,1,0:T(8,128)(2,1)} %get-tuple-element.64.k_ref, bf16[4,1024,128]{2,1,0:T(8,128)(2,1)} %get-tuple-element.65.v_ref, ...), custom_call_target="tpu_custom_call" | custom-call | flops 13421772800 | bytes 4235264 | tf_op jit(solution)/shard_map/attend/pallas_call | solution.py:183
  143.6 3.9 context_out.3
  151.2 4.0 context_out.2.mine_ref
  156.2 4.5 norm_a.1
  164.2 53.1 %all-gather.5.cloned.1.call-done = bf16[2048,1024]{0,1:T(8,128)(2,1)} async-done(((bf16[128,1024]{0,1:T(8,128)(2,1)}), bf16[2048,1024]{0,1:T(8,128)(2,1)}) %all-gather.5.cloned.1.call-update) | async-done | bytes 4194320 | tf_op jit(solution)/shard_map/all_gather | solution.py:738
  217.3 6.4 %copy.394 = bf16[2048,1024]{1,0:T(8,128)(2,1)} copy(bf16[2048,1024]{0,1:T(8,128)(2,1)} %all-gather.5.cloned.1.call-done) | data formatting | bytes 8388608 | tf_op jit(solution)/shard_map/all_gather | solution.py:738
  223.7 8.1 %ffn_in.2 = (bf16[4,1024,512]{2,1,0:T(8,128)(2,1)}, bf16[4,1024,512]{2,1,0:T(8,128)(2,1)}) custom-call(s32[3]{0:T(128)} %add_add_fusion.at.at_ref, bf16[512,1024]{1,0:T(8,128)(2,1)} %get-tuple-element.67.y_ref.refs_0_, f32[4,1,512]{2,1,0:T(1,128)} %maximum_convert_fusion.3.b_ref, bf16[8,2,128,1280]{3,2,1,0:T(8,128)(2,1)} %bitcast.244, ...), custom_call_target="tpu_custom_call" | custom-call | flops 6442450944 | bytes 30416896 | tf_op jit(solution)/shard_map/ffn_in/pallas_call | solution.py:183
  232.8 8.1 %ffn_in.3 = (bf16[4,1024,512]{2,1,0:T(8,128)(2,1)}, bf16[4,1024,512]{2,1,0:T(8,128)(2,1)}) custom-call(s32[3]{0:T(128)} %add_add_fusion.at.at_ref, bf16[512,1024]{1,0:T(8,128)(2,1)} %copy-done.6, f32[4,1,512]{2,1,0:T(1,128)} %maximum_convert_fusion.3.b_ref, bf16[8,2,128,1280]{3,2,1,0:T(8,128)(2,1)} %bitcast.248, ...), custom_call_target="tpu_custom_call", output_to_operand_aliasing={{0}: (7, {}), {1}: (8, {})} | custom-call | flops 6442450944 | bytes 38805504 | tf_op jit(solution)/shard_map/ffn_in/pallas_call | solution.py:183
  240.9 6.6 %ffn_out.3 = bf16[512,1024]{1,0:T(8,128)(2,1)} custom-call(s32[3]{0:T(128)} %add_add_fusion.at.at_ref, bf16[4,1024,512]{2,1,0:T(8,128)(2,1)} %get-tuple-element.70.act_ref.refs_2_, bf16[8,2,128,1024]{3,2,1,0:T(8,128)(2,1)} %bitcast.262, bf16[8,2,128,1024]{3,2,1,0:T(8,128)(2,1)} %bitcast.263, bf16[8,2,128,1024]{3,2,1,0:T(8,128)(2,1)} %bitcast.264, ...), custom_call_target="tpu_custom_call" | custom-call | flops 2147483648 | bytes 22020096 | tf_op jit(solution)/shard_map/ffn_out/pallas_call | solution.py:183
  248.8 7.1 %ffn_out.2.mine_ref = f32[512,1024]{1,0:T(8,128)} custom-call(s32[3]{0:T(128)} %add_add_fusion.at.at_ref, bf16[4,1024,512]{2,1,0:T(8,128)(2,1)} %get-tuple-element.70.act_ref.refs_2_, bf16[8,2,128,1024]{3,2,1,0:T(8,128)(2,1)} %bitcast.266, bf16[8,2,128,1024]{3,2,1,0:T(8,128)(2,1)} %bitcast.267, bf16[8,2,128,1024]{3,2,1,0:T(8,128)(2,1)} %bitcast.268, ...), custom_call_target="tpu_custom_call" | custom-call | flops 2147483648 | bytes 23068672 | tf_op jit(solution)/shard_map/ffn_out/pallas_call | solution.py:183
  256.8 5.5 %norm_b.1 = (bf16[512,1024]{1,0:T(8,128)(2,1)}, f32[512,1024]{1,0:T(8,128)}, bf16[512,1024]{1,0:T(8,128)(2,1)}, f32[3,1024]{1,0:T(4,128)}) custom-call(f32[512,1024]{1,0:T(8,128)} %ffn_out.2.mine_ref, bf16[512,1024]{1,0:T(8,128)(2,1)} %copy-done.16, f32[512,1024]{1,0:T(8,128)} %get-tuple-element.71.centred_a_ref.centred_ref, ...), custom_call_target="tpu_custom_call" | custom-call | flops 20971520 | bytes 10522624 | tf_op jit(solution)/shard_map/norm_b/pallas_call | solution.py:183
  263.0 2.5 collective-permute-done.16.refs_1_.gb_ref
  266.5 9.7 %weight_grad_shards.1 = bf16[8,2,128,1024]{3,2,1,0:T(8,128)(2,1)} custom-call(s32[3]{0:T(128)} %add_add_fusion.at.at_ref, bf16[512,1024]{1,0:T(8,128)(2,1)} %get-tuple-element.76.refs_0_.gb_ref, bf16[512,1024]{1,0:T(8,128)(2,1)} %copy-done.7, bf16[4,1024,512]{2,1,0:T(8,128)(2,1)} %get-tuple-element.70.act_ref.refs_2_), custom_call_target="tpu_custom_call" | custom-call | flops 4294967296 | bytes 10485760 | tf_op jit(solution)/shard_map/weight_grad_shards/pallas_call | solution.py:183
  279.1 11.5 %ffn_back.2 = (bf16[4,1024,512]{2,1,0:T(8,128)(2,1)}, f32[4,1,512]{2,1,0:T(1,128)}, f32[512,1024]{1,0:T(8,128)}) custom-call(s32[3]{0:T(128)} %add_add_fusion.at.at_ref, bf16[512,1024]{1,0:T(8,128)(2,1)} %get-tuple-element.76.refs_0_.gb_ref, bf16[4,1024,512]{2,1,0:T(8,128)(2,1)} %get-tuple-element.77.slope_ref, bf16[8,2,128,1024]{3,2,1,0:T(8,128)(2,1)} %bitcast.270, ...), custom_call_target="tpu_custom_call" | custom-call | flops 4294967296 | bytes 49291264 | tf_op jit(solution)/shard_map/ffn_back/pallas_call | solution.py:183
  290.6 11.2 %ffn_back.3 = (bf16[4,1024,512]{2,1,0:T(8,128)(2,1)}, f32[4,1,512]{2,1,0:T(1,128)}, bf16[512,1024]{1,0:T(8,128)(2,1)}) custom-call(s32[3]{0:T(128)} %add_add_fusion.at.at_ref, bf16[512,1024]{1,0:T(8,128)(2,1)} %copy-done.7, bf16[4,1024,512]{2,1,0:T(8,128)(2,1)} %get-tuple-element.77.slope_ref, ...), custom_call_target="tpu_custom_call", output_to_operand_aliasing={{0}: (11, {})} | custom-call | flops 4294967296 | bytes 52436992 | tf_op jit(solution)/shard_map/ffn_back/pallas_call | solution.py:183
  301.9 8.4 %weight_grad.5 = (bf16[1024,512]{1,0:T(8,128)(2,1)}, bf16[1024,512]{1,0:T(8,128)(2,1)}, bf16[1024,512]{1,0:T(8,128)(2,1)}, bf16[1024,512]{1,0:T(8,128)(2,1)}) custom-call(bf16[512,1024]{1,0:T(8,128)(2,1)} %get-tuple-element.67.y_ref.refs_0_, bf16[512,1024]{1,0:T(8,128)(2,1)} %copy-done.6, bf16[4,1024,512]{2,1,0:T(8,128)(2,1)} %get-tuple-element.101.refs_2_), custom_call_target="tpu_custom_call" | custom-call | flops 4294967296 | bytes 10485760 | tf_op jit(solution)/shard_map/weight_grad/pallas_call | solution.py:183
  317.5 29.9 %collective-permute-done.40 = bf16[2,2,1,128,512]{4,3,0,2,1:T(8,128)(2,1)S(1)} collective-permute-done((bf16[2,2,1,128,512]{4,3,0,2,1:T(8,128)(2,1)S(1)}, bf16[2,2,1,128,512]{4,3,0,2,1:T(8,128)(2,1)S(1)}, u32[]{:S(2)}, u32[]{:S(2)}) %collective-permute-start.40) | collective-permute-done | bytes 524320 | tf_op jit(solution)/shard_map/ppermute | solution.py:50
  349.3 5.7 %norm_a_back.1 = (f32[512,1024]{1,0:T(8,128)}, bf16[512,1024]{1,0:T(8,128)(2,1)}, f32[3,1024]{1,0:T(4,128)}) custom-call(f32[512,1024]{1,0:T(8,128)} %get-tuple-element.78.mine_ref, bf16[512,1024]{1,0:T(8,128)(2,1)} %copy-done.14, f32[512,1024]{1,0:T(8,128)} %get-tuple-element.82.gb_ref, f32[512,1024]{1,0:T(8,128)} %get-tuple-element.71.centred_a_ref.centred_ref, ...), custom_call_target="tpu_custom_call" | custom-call | flops 15728640 | bytes 10524672 | tf_op jit(solution)/shard_map/norm_a_back/pallas_call | solution.py:183
  355.8 2.0 collective-permute-start.32
  357.8 9.2 %collective-permute-done.37 = bf16[1024,512]{1,0:T(8,128)(2,1)} collective-permute-done((bf16[1024,512]{1,0:T(8,128)(2,1)}, bf16[1024,512]{1,0:T(8,128)(2,1)}, u32[]{:S(2)}, u32[]{:S(2)}) %collective-permute-start.37) | collective-permute-done | bytes 1048608 | tf_op jit(solution)/shard_map/ppermute | solution.py:50
  369.3 2.8 collective-permute-start.38
  373.3 20.0 %collective-permute-done.41 = bf16[2,2,1,128,512]{4,3,0,2,1:T(8,128)(2,1)} collective-permute-done((bf16[2,2,1,128,512]{4,3,0,2,1:T(8,128)(2,1)}, bf16[2,2,1,128,512]{4,3,0,2,1:T(8,128)(2,1)}, u32[]{:S(2)}, u32[]{:S(2)}) %collective-permute-start.41) | collective-permute-done | bytes 524320 | tf_op jit(solution)/shard_map/ppermute | solution.py:50
  402.0 5.5 %context_back.1.do_ref = bf16[4,1024,128]{2,1,0:T(8,128)(2,1)} custom-call(s32[3]{0:T(128)} %add_add_fusion.at.at_ref, bf16[1024,1024]{1,0:T(8,128)(2,1)} %pad_maximum_fusion.1.ga_ref.refs_0_, bf16[8,2,128,1280]{3,2,1,0:T(8,128)(2,1)} %bitcast.260, bf16[8,2,128,1280]{3,2,1,0:T(8,128)(2,1)} %bitcast.261), custom_call_target="tpu_custom_call" | custom-call | flops 1073741824 | bytes 13631488 | tf_op jit(solution)/shard_map/context_back/pallas_call | solution.py:183
  407.5 24.1 %attend_back.1 = (bf16[4,1024,384]{2,1,0:T(8,128)(2,1)}, f32[4,2,128]{2,1,0:T(2,128)}) custom-call(s32[2,4]{1,0:T(2,128)} %pad_add_fusion.windows, bf16[4,1024,128]{2,1,0:T(8,128)(2,1)} %get-tuple-element.63.q_ref, bf16[4,1024,128]{2,1,0:T(8,128)(2,1)} %get-tuple-element.64.k_ref, bf16[4,1024,128]{2,1,0:T(8,128)(2,1)} %get-tuple-element.65.v_ref, ...), custom_call_target="tpu_custom_call" | custom-call | flops 20132659200 | bytes 7385088 | tf_op jit(solution)/shard_map/attend_back/pallas_call | solution.py:183
  432.5 2.5 collective-permute-start.31
  434.9 5.7 %weight_grad.4 = (bf16[1024,128]{1,0:T(8,128)(2,1)}, bf16[1024,128]{1,0:T(8,128)(2,1)}, bf16[1024,128]{1,0:T(8,128)(2,1)}, bf16[1024,128]{1,0:T(8,128)(2,1)}) custom-call(bf16[1024,1024]{1,0:T(8,128)(2,1)} %pad_maximum_fusion.1.ga_ref.refs_0_, bf16[4,1024,128]{2,1,0:T(8,128)(2,1)} %get-tuple-element.66.ctx_ref.refs_1_), custom_call_target="tpu_custom_call" | custom-call | flops 1073741824 | bytes 4194304 | tf_op jit(solution)/shard_map/weight_grad/pallas_call | solution.py:183
  440.7 8.3 %weight_grad.3 = (bf16[1024,384]{1,0:T(8,128)(2,1)}, bf16[1024,384]{1,0:T(8,128)(2,1)}, bf16[1024,384]{1,0:T(8,128)(2,1)}, bf16[1024,384]{1,0:T(8,128)(2,1)}) custom-call(bf16[1024,1024]{1,0:T(8,128)(2,1)} %pad_maximum_fusion.x_ref.refs_0_, bf16[4,1024,384]{2,1,0:T(8,128)(2,1)} %get-tuple-element.86.gp_ref.refs_1_), custom_call_target="tpu_custom_call" | custom-call | flops 3221225472 | bytes 8388608 | tf_op jit(solution)/shard_map/weight_grad/pallas_call | solution.py:183
  454.6 2.1 pad_maximum_fusion.6
  459.0 2.2 collective-permute-start.34
  463.6 3.0 collective-permute-start.35
  466.6 6.2 %inputs_back.3 = bf16[512,1024]{1,0:T(8,128)(2,1)} custom-call(s32[3]{0:T(128)} %add_add_fusion.1.at, bf16[4,1024,384]{2,1,0:T(8,128)(2,1)} %get-tuple-element.86.gp_ref.refs_1_, bf16[1024,384]{1,0:T(8,128)(2,1)} %bitcast.280, bf16[1024,384]{1,0:T(8,128)(2,1)} %bitcast.283, bf16[1024,384]{1,0:T(8,128)(2,1)} %copy-done.4, bf16[1024,384]{1,0:T(8,128)(2,1)} %bitcast.286), custom_call_target="tpu_custom_call" | custom-call | flops 1610612736 | bytes 7340032 | tf_op jit(solution)/shard_map/inputs_back/pallas_call | solution.py:183
  472.9 6.3 %inputs_back.2 = f32[512,1024]{1,0:T(8,128)} custom-call(s32[3]{0:T(128)} %add_add_fusion.at.at_ref, bf16[4,1024,384]{2,1,0:T(8,128)(2,1)} %get-tuple-element.86.gp_ref.refs_1_, bf16[1024,384]{1,0:T(8,128)(2,1)} %bitcast.281, bf16[1024,384]{1,0:T(8,128)(2,1)} %bitcast.284, bf16[1024,384]{1,0:T(8,128)(2,1)} %copy-done.4, bf16[1024,384]{1,0:T(8,128)(2,1)} %bitcast.287), custom_call_target="tpu_custom_call" | custom-call | flops 1610612736 | bytes 8388608 | tf_op jit(solution)/shard_map/inputs_back/pallas_call | solution.py:183
  484.1 2.0 add_convert_fusion.8
  486.1 2.1 collective-permute-start.28
  492.3 2.5 add_convert_fusion.2
  496.3 4.9 collective-permute-done.28
  502.8 2.1 collective-permute-done.25
  507.1 5.1 collective-permute-done.22
  512.6 7.0 %collective-permute-done.29 = bf16[2,2,1,1,128,512]{4,5,1,3,2,0:T(8,128)(2,1)S(1)} collective-permute-done((bf16[2,2,1,1,128,512]{4,5,1,3,2,0:T(8,128)(2,1)S(1)}, bf16[2,2,1,1,128,512]{4,5,1,3,2,0:T(8,128)(2,1)S(1)}, u32[]{:S(2)}, u32[]{:S(2)}) %collective-permute-start.29) | collective-permute-done | bytes 524320 | tf_op jit(solution)/shard_map/ppermute | solution.py:50
  521.5 11.8 %collective-permute-done.30 = bf16[2,1,1,1,128,512]{4,5,3,2,1,0:T(8,128)(2,1)S(1)} collective-permute-done((bf16[2,1,1,1,128,512]{4,5,3,2,1,0:T(8,128)(2,1)S(1)}, bf16[2,1,1,1,128,512]{4,5,3,2,1,0:T(8,128)(2,1)S(1)}, u32[]{:S(2)}, u32[]{:S(2)}) %collective-permute-start.30) | collective-permute-done | bytes 262176 | tf_op jit(solution)/shard_map/ppermute | solution.py:50
  (320 shorter events, 99.1 us)
Async XLA Ops:
  7.2 136.4 %all-gather.3.cloned.1.call-start = ((), (), s32[]{:S(2)}) async-start(), calls=%async_computation.1 | async-start | bytes 5570560 | tf_op jit(solution)/shard_map/all_gather | solution.py:738
  9.9 207.4 %all-gather.5.cloned.1.call-start = ((), (), s32[]{:S(2)}) async-start(), calls=%async_computation.2 | async-start | bytes 4456448 | tf_op jit(solution)/shard_map/all_gather | solution.py:738
  11.2 13.2 %collective-permute-start = (bf16[2,1,1,1,128,384]{4,5,3,2,1,0:T(8,128)(2,1)S(1)}, bf16[2,1,1,1,128,384]{4,5,3,2,1,0:T(8,128)(2,1)S(1)}, u32[]{:S(2)}, u32[]{:S(2)}) collective-permute-start(bf16[2,1,1,1,128,384]{4,5,3,2,1,0:T(8,128)(2,1)S(1)} %pad_maximum_fusion.20), channel_id=1, source_target_pairs={{0,16},{4,20},{8,24},{12,28},{16,0},{20,4},{24,8},{28,12},{1,17},{... | collective-permute-start | bytes 589832 | tf_op jit(solution)/shard_map/ppermute | solution.py:50
  15.4 519.7 %reduce-scatter.4.cloned.1.call-start = ((), (), s32[]{:S(2)}) async-start(), calls=%async_computation.3 | async-start | bytes 4456448
  24.6 16.4 %collective-permute-start.1 = (bf16[2,2,1,1,128,384]{4,5,1,3,2,0:T(8,128)(2,1)S(1)}, bf16[2,2,1,1,128,384]{4,5,1,3,2,0:T(8,128)(2,1)S(1)}, u32[]{:S(2)}, u32[]{:S(2)}) collective-permute-start(bf16[2,2,1,1,128,384]{4,5,1,3,2,0:T(8,128)(2,1)S(1)} %pad_maximum_fusion.14), channel_id=1, source_target_pairs={{0,8},{4,12},{8,0},{12,4},{16,24},{20,28},{24,16},{28,20},{1,9},{5... | collective-permute-start | bytes 1179656 | tf_op jit(solution)/shard_map/ppermute | solution.py:50
  41.2 15.7 %collective-permute-start.5 = (bf16[2,2,1,128,384]{3,4,2,1,0:T(8,128)(2,1)S(1)}, bf16[2,2,1,128,384]{3,4,2,1,0:T(8,128)(2,1)}, u32[]{:S(2)}, u32[]{:S(2)}) collective-permute-start(bf16[2,2,1,128,384]{3,4,2,1,0:T(8,128)(2,1)S(1)} %pad_maximum_fusion.15), channel_id=1, source_target_pairs={{0,4},{4,0},{8,12},{12,8},{16,20},{20,16},{24,28},{28,24},{1,5},{5... | collective-permute-start | bytes 1179656 | tf_op jit(solution)/shard_map/ppermute | solution.py:50
  42.8 3.9 collective-permute-start.4
  44.5 33.6 %collective-permute-start.8 = (bf16[2,2,1,128,384]{3,4,2,1,0:T(8,128)(2,1)S(1)}, bf16[2,2,1,128,384]{3,4,2,1,0:T(8,128)(2,1)}, u32[]{:S(2)}, u32[]{:S(2)}) collective-permute-start(bf16[2,2,1,128,384]{3,4,2,1,0:T(8,128)(2,1)S(1)} %pad_maximum_fusion.16), channel_id=1, source_target_pairs={{0,2},{1,3},{2,0},{3,1},{4,6},{5,7},{6,4},{7,5},{8,10},{9,11},{10,... | collective-permute-start | bytes 1179656 | tf_op jit(solution)/shard_map/ppermute | solution.py:50
  45.1 29.6 %collective-permute-start.2 = (bf16[1024,256]{1,0:T(8,128)(2,1)S(1)}, bf16[1024,256]{1,0:T(8,128)(2,1)S(1)}, u32[]{:S(2)}, u32[]{:S(2)}) collective-permute-start(bf16[1024,256]{1,0:T(8,128)(2,1)S(1)} %dynamic-slice_bitcast_fusion.3), channel_id=1, source_target_pairs={{0,2},{1,3},{2,0},{3,1},{4,6},{5,7},{6,4},{7,5},{8,10},{9,11},{10,... | collective-permute-start | bytes 1572872 | tf_op jit(solution)/shard_map/ppermute | solution.py:50
  58.5 19.1 %copy-start.3 = (bf16[2,2,2,128,384]{4,3,2,1,0:T(8,128)(2,1)}, bf16[2,2,2,128,384]{4,3,2,1,0:T(8,128)(2,1)S(1)}, u32[]{:S(2)}) copy-start(bf16[2,2,2,128,384]{4,3,2,1,0:T(8,128)(2,1)S(1)} %copy.379) | copy-start | bytes 2359300
  58.5 20.9 %collective-permute-start.6 = (bf16[2,2,1,128,384]{3,4,2,1,0:T(8,128)(2,1)S(1)}, bf16[2,2,1,128,384]{3,4,2,1,0:T(8,128)(2,1)}, u32[]{:S(2)}, u32[]{:S(2)}) collective-permute-start(bf16[2,2,1,128,384]{3,4,2,1,0:T(8,128)(2,1)S(1)} %pad_maximum_fusion.16), channel_id=1, source_target_pairs={{0,4},{4,0},{8,12},{12,8},{16,20},{20,16},{24,28},{28,24},{1,5},{5... | collective-permute-start | bytes 1179656 | tf_op jit(solution)/shard_map/ppermute | solution.py:50
  76.9 24.1 %collective-permute-start.3 = (bf16[1024,512]{1,0:T(8,128)(2,1)}, bf16[1024,512]{1,0:T(8,128)(2,1)}, u32[]{:S(2)}, u32[]{:S(2)}) collective-permute-start(bf16[1024,512]{1,0:T(8,128)(2,1)} %pad_maximum_fusion.2), channel_id=1, source_target_pairs={{0,1},{1,0},{2,3},{3,2},{4,5},{5,4},{6,7},{7,6},{8,9},{9,8},{10,11... | collective-permute-start | bytes 3145736 | tf_op jit(solution)/shard_map/ppermute | solution.py:50
  77.6 36.5 %collective-permute-start.7 = (bf16[1024,384]{1,0:T(8,128)(2,1)S(1)}, bf16[1024,384]{1,0:T(8,128)(2,1)S(1)}, u32[]{:S(2)}, u32[]{:S(2)}) collective-permute-start(bf16[1024,384]{1,0:T(8,128)(2,1)S(1)} %bitcast.278), channel_id=1, source_target_pairs={{0,2},{1,3},{2,0},{3,1},{4,6},{5,7},{6,4},{7,5},{8,10},{9,11},{10,... | collective-permute-start | bytes 2359304 | tf_op jit(solution)/shard_map/ppermute | solution.py:50
  78.0 20.5 %collective-permute-start.9 = (bf16[2,2,1,128,384]{3,4,2,1,0:T(8,128)(2,1)}, bf16[2,2,1,128,384]{3,4,2,1,0:T(8,128)(2,1)}, u32[]{:S(2)}, u32[]{:S(2)}) collective-permute-start(bf16[2,2,1,128,384]{3,4,2,1,0:T(8,128)(2,1)} %collective-permute-done.8), channel_id=1, source_target_pairs={{0,4},{4,0},{8,12},{12,8},{16,20},{20,16},{24,28},{28,24},{1,5},{5... | collective-permute-start | bytes 1179656 | tf_op jit(solution)/shard_map/ppermute | solution.py:50
  147.6 7.6 %collective-permute-start.10 = (bf16[512,1024]{1,0:T(8,128)(2,1)}, bf16[512,1024]{1,0:T(8,128)(2,1)S(1)}, u32[]{:S(2)}, u32[]{:S(2)}) collective-permute-start(bf16[512,1024]{1,0:T(8,128)(2,1)} %context_out.3), channel_id=1, source_target_pairs={{0,1},{1,0},{2,3},{3,2},{4,5},{5,4},{6,7},{7,6},{8,9},{9,8},{10,11... | collective-permute-start | bytes 3145736 | tf_op jit(solution)/shard_map/ppermute | solution.py:50
  148.3 14.4 %collective-permute-start.14 = (bf16[1024,256]{1,0:T(8,128)(2,1)S(1)}, bf16[1024,256]{1,0:T(8,128)(2,1)}, u32[]{:S(2)}, u32[]{:S(2)}) collective-permute-start(bf16[1024,256]{1,0:T(8,128)(2,1)S(1)} %dynamic-slice_bitcast_fusion.2), channel_id=1, source_target_pairs={{0,2},{1,3},{2,0},{3,1},{4,6},{5,7},{6,4},{7,5},{8,10},{9,11},{10,... | collective-permute-start | bytes 1572872 | tf_op jit(solution)/shard_map/ppermute | solution.py:50
  148.4 2.0 collective-permute-start.11
  160.7 71.1 %collective-permute-start.12 = (bf16[512,1024]{1,0:T(8,128)(2,1)}, bf16[512,1024]{1,0:T(8,128)(2,1)S(1)}, u32[]{:S(2)}, u32[]{:S(2)}) collective-permute-start(bf16[512,1024]{1,0:T(8,128)(2,1)} %get-tuple-element.67.y_ref.refs_0_), channel_id=1, source_target_pairs={{0,1},{1,0},{2,3},{3,2},{4,5},{5,4},{6,7},{7,6},{8,9},{9,8},{10,11... | collective-permute-start | bytes 3145736 | tf_op jit(solution)/shard_map/ppermute | solution.py:50
  164.1 83.4 %collective-permute-start.15 = (bf16[512,512]{1,0:T(8,128)(2,1)S(1)}, bf16[512,512]{1,0:T(8,128)(2,1)S(1)}, u32[]{:S(2)}, u32[]{:S(2)}) collective-permute-start(bf16[512,512]{1,0:T(8,128)(2,1)S(1)} %get-tuple-element.247), channel_id=1, source_target_pairs={{0,1},{1,0},{2,3},{3,2},{4,5},{5,4},{6,7},{7,6},{8,9},{9,8},{10,11... | collective-permute-start | bytes 1572872 | tf_op jit(solution)/shard_map/ppermute | solution.py:50
  247.5 8.4 %collective-permute-start.13 = (bf16[512,1024]{1,0:T(8,128)(2,1)}, bf16[512,1024]{1,0:T(8,128)(2,1)S(1)}, u32[]{:S(2)}, u32[]{:S(2)}) collective-permute-start(bf16[512,1024]{1,0:T(8,128)(2,1)} %ffn_out.3), channel_id=1, source_target_pairs={{0,1},{1,0},{2,3},{3,2},{4,5},{5,4},{6,7},{7,6},{8,9},{9,8},{10,11... | collective-permute-start | bytes 3145736 | tf_op jit(solution)/shard_map/ppermute | solution.py:50
  262.4 3.1 collective-permute-start.16
  277.5 37.8 %collective-permute-start.17 = (bf16[512,512]{1,0:T(8,128)(2,1)S(1)}, bf16[512,512]{1,0:T(8,128)(2,1)}, u32[]{:S(2)}, u32[]{:S(2)}) collective-permute-start(bf16[512,512]{1,0:T(8,128)(2,1)S(1)} %constant_dynamic-slice_fusion.14), channel_id=1, source_target_pairs={{0,2},{1,3},{2,0},{3,1},{4,6},{5,7},{6,4},{7,5},{8,10},{9,11},{10,... | collective-permute-start | bytes 1572872 | tf_op jit(solution)/shard_map/ppermute | solution.py:50
  301.8 46.5 %collective-permute-start.19 = (bf16[512,1024]{1,0:T(8,128)(2,1)}, bf16[512,1024]{1,0:T(8,128)(2,1)S(1)}, u32[]{:S(2)}, u32[]{:S(2)}) collective-permute-start(bf16[512,1024]{1,0:T(8,128)(2,1)} %get-tuple-element.81), channel_id=1, source_target_pairs={{0,1},{1,0},{2,3},{3,2},{4,5},{5,4},{6,7},{7,6},{8,9},{9,8},{10,11... | collective-permute-start | bytes 3145736 | tf_op jit(solution)/shard_map/ppermute | solution.py:50
  312.6 60.7 %collective-permute-start.39 = (bf16[2,2,1,128,512]{4,3,0,2,1:T(8,128)(2,1)}, bf16[2,2,1,128,512]{4,3,0,2,1:T(8,128)(2,1)}, u32[]{:S(2)}, u32[]{:S(2)}) collective-permute-start(bf16[2,2,1,128,512]{4,3,0,2,1:T(8,128)(2,1)} %copy.422), channel_id=1, source_target_pairs={{0,4},{4,0},{8,12},{12,8},{16,20},{20,16},{24,28},{28,24},{1,5},{5... | collective-permute-start | bytes 1572872 | tf_op jit(solution)/shard_map/ppermute | solution.py:50
  314.0 52.9 %collective-permute-start.37 = (bf16[1024,512]{1,0:T(8,128)(2,1)}, bf16[1024,512]{1,0:T(8,128)(2,1)}, u32[]{:S(2)}, u32[]{:S(2)}) collective-permute-start(bf16[1024,512]{1,0:T(8,128)(2,1)} %get-tuple-element.103), channel_id=1, source_target_pairs={{0,2},{1,3},{2,0},{3,1},{4,6},{5,7},{6,4},{7,5},{8,10},{9,11},{10,... | collective-permute-start | bytes 3145736 | tf_op jit(solution)/shard_map/ppermute | solution.py:50
  314.6 32.7 %collective-permute-start.40 = (bf16[2,2,1,128,512]{4,3,0,2,1:T(8,128)(2,1)S(1)}, bf16[2,2,1,128,512]{4,3,0,2,1:T(8,128)(2,1)S(1)}, u32[]{:S(2)}, u32[]{:S(2)}) collective-permute-start(bf16[2,2,1,128,512]{4,3,0,2,1:T(8,128)(2,1)S(1)} %copy.424), channel_id=1, source_target_pairs={{0,4},{4,0},{8,12},{12,8},{16,20},{20,16},{24,28},{28,24},{1,5},{5... | collective-permute-start | bytes 1572872 | tf_op jit(solution)/shard_map/ppermute | solution.py:50
  317.5 51.9 %collective-permute-start.18 = (bf16[1024,256]{1,0:T(8,128)(2,1)}, bf16[1024,256]{1,0:T(8,128)(2,1)}, u32[]{:S(2)}, u32[]{:S(2)}) collective-permute-start(bf16[1024,256]{1,0:T(8,128)(2,1)} %get-tuple-element.241), channel_id=1, source_target_pairs={{0,1},{1,0},{2,3},{3,2},{4,5},{5,4},{6,7},{7,6},{8,9},{9,8},{10,11... | collective-permute-start | bytes 1572872 | tf_op jit(solution)/shard_map/ppermute | solution.py:50
  348.3 45.0 %collective-permute-start.41 = (bf16[2,2,1,128,512]{4,3,0,2,1:T(8,128)(2,1)}, bf16[2,2,1,128,512]{4,3,0,2,1:T(8,128)(2,1)}, u32[]{:S(2)}, u32[]{:S(2)}) collective-permute-start(bf16[2,2,1,128,512]{4,3,0,2,1:T(8,128)(2,1)} %add_convert_fusion.4), channel_id=1, source_target_pairs={{0,2},{1,3},{2,0},{3,1},{4,6},{5,7},{6,4},{7,5},{8,10},{9,11},{10,... | collective-permute-start | bytes 1572872 | tf_op jit(solution)/shard_map/ppermute | solution.py:50
  355.8 40.0 %collective-permute-start.32 = (f32[6,512]{1,0:T(8,128)S(1)}, f32[6,512]{1,0:T(8,128)S(1)}, u32[]{:S(2)}, u32[]{:S(2)}) collective-permute-start(f32[6,512]{1,0:T(8,128)S(1)} %fusion.23), channel_id=1, source_target_pairs={{0,2},{1,3},{2,0},{3,1},{4,6},{5,7},{6,4},{7,5},{8,10},{9,11},{10,... | collective-permute-start | bytes 36872 | tf_op jit(solution)/shard_map/ppermute | solution.py:50
  367.0 32.2 %collective-permute-start.20 = (bf16[512,1024]{1,0:T(8,128)(2,1)}, bf16[512,1024]{1,0:T(8,128)(2,1)}, u32[]{:S(2)}, u32[]{:S(2)}) collective-permute-start(bf16[512,1024]{1,0:T(8,128)(2,1)} %get-tuple-element.84), channel_id=1, source_target_pairs={{0,1},{1,0},{2,3},{3,2},{4,5},{5,4},{6,7},{7,6},{8,9},{9,8},{10,11... | collective-permute-start | bytes 3145736 | tf_op jit(solution)/shard_map/ppermute | solution.py:50
  369.3 27.7 %collective-permute-start.38 = (bf16[2,2,1,128,512]{4,3,2,1,0:T(8,128)(2,1)}, bf16[2,2,1,128,512]{4,3,2,1,0:T(8,128)(2,1)}, u32[]{:S(2)}, u32[]{:S(2)}) collective-permute-start(bf16[2,2,1,128,512]{4,3,2,1,0:T(8,128)(2,1)} %constant_dynamic-slice_fusion.4), channel_id=1, source_target_pairs={{0,4},{4,0},{8,12},{12,8},{16,20},{20,16},{24,28},{28,24},{1,5},{5... | collective-permute-start | bytes 1572872 | tf_op jit(solution)/shard_map/ppermute | solution.py:50
  395.8 1.2 collective-permute-start.33
  399.1 57.5 %collective-permute-start.42 = (bf16[2,2,1,1,128,512]{5,4,1,3,2,0:T(8,128)(2,1)}, bf16[2,2,1,1,128,512]{5,4,1,3,2,0:T(8,128)(2,1)}, u32[]{:S(2)}, u32[]{:S(2)}) collective-permute-start(bf16[2,2,1,1,128,512]{5,4,1,3,2,0:T(8,128)(2,1)} %pad_maximum_fusion.13), channel_id=1, source_target_pairs={{0,8},{4,12},{8,0},{12,4},{16,24},{20,28},{24,16},{28,20},{1,9},{5... | collective-permute-start | bytes 1572872 | tf_op jit(solution)/shard_map/ppermute | solution.py:50
  432.5 26.5 %collective-permute-start.31 = (f32[1536]{0:T(1024)S(1)}, f32[1536]{0:T(1024)S(1)}, u32[]{:S(2)}, u32[]{:S(2)}) collective-permute-start(f32[1536]{0:T(1024)S(1)} %pad_maximum_fusion.25), channel_id=1, source_target_pairs={{0,2},{1,3},{2,0},{3,1},{4,6},{5,7},{6,4},{7,5},{8,10},{9,11},{10,... | collective-permute-start | bytes 18440 | tf_op jit(solution)/shard_map/ppermute | solution.py:50
  451.3 45.0 %collective-permute-start.26 = (bf16[2,2,1,128,512]{3,4,0,2,1:T(8,128)(2,1)}, bf16[2,2,1,128,512]{3,4,0,2,1:T(8,128)(2,1)}, u32[]{:S(2)}, u32[]{:S(2)}) collective-permute-start(bf16[2,2,1,128,512]{3,4,0,2,1:T(8,128)(2,1)} %copy.418), channel_id=1, source_target_pairs={{0,4},{4,0},{8,12},{12,8},{16,20},{20,16},{24,28},{28,24},{1,5},{5... | collective-permute-start | bytes 1572872 | tf_op jit(solution)/shard_map/ppermute | solution.py:50
  452.6 31.5 %collective-permute-start.27 = (bf16[2,2,1,128,512]{3,4,0,2,1:T(8,128)(2,1)}, bf16[2,2,1,128,512]{3,4,0,2,1:T(8,128)(2,1)}, u32[]{:S(2)}, u32[]{:S(2)}) collective-permute-start(bf16[2,2,1,128,512]{3,4,0,2,1:T(8,128)(2,1)} %copy.420), channel_id=1, source_target_pairs={{0,4},{4,0},{8,12},{12,8},{16,20},{20,16},{24,28},{28,24},{1,5},{5... | collective-permute-start | bytes 1572872 | tf_op jit(solution)/shard_map/ppermute | solution.py:50
  456.6 31.6 %collective-permute-start.24 = (bf16[1024,512]{1,0:T(8,128)(2,1)}, bf16[1024,512]{1,0:T(8,128)(2,1)S(1)}, u32[]{:S(2)}, u32[]{:S(2)}) collective-permute-start(bf16[1024,512]{1,0:T(8,128)(2,1)} %pad_maximum_fusion.6), channel_id=1, source_target_pairs={{0,2},{1,3},{2,0},{3,1},{4,6},{5,7},{6,4},{7,5},{8,10},{9,11},{10,... | collective-permute-start | bytes 3145736 | tf_op jit(solution)/shard_map/ppermute | solution.py:50
  459.0 4.7 collective-permute-start.34
  461.9 20.5 %collective-permute-start.43 = (bf16[2,1,1,1,128,512]{5,4,3,2,1,0:T(8,128)(2,1)}, bf16[2,1,1,1,128,512]{5,4,3,2,1,0:T(8,128)(2,1)}, u32[]{:S(2)}, u32[]{:S(2)}) collective-permute-start(bf16[2,1,1,1,128,512]{5,4,3,2,1,0:T(8,128)(2,1)} %pad_maximum_fusion.19), channel_id=1, source_target_pairs={{0,16},{4,20},{8,24},{12,28},{16,0},{20,4},{24,8},{28,12},{1,17},{... | collective-permute-start | bytes 786440 | tf_op jit(solution)/shard_map/ppermute | solution.py:50
  463.6 9.2 %collective-permute-start.35 = (f32[3072]{0:T(1024)S(1)}, f32[3072]{0:T(1024)S(1)}, u32[]{:S(2)}, u32[]{:S(2)}) collective-permute-start(f32[3072]{0:T(1024)S(1)} %fusion.33), channel_id=1, source_target_pairs={{0,8},{4,12},{8,0},{12,4},{16,24},{20,28},{24,16},{28,20},{1,9},{5... | collective-permute-start | bytes 36872 | tf_op jit(solution)/shard_map/ppermute | solution.py:50
  472.8 7.7 %collective-permute-start.36 = (f32[3072]{0:T(1024)S(1)}, f32[3072]{0:T(1024)S(1)}, u32[]{:S(2)}, u32[]{:S(2)}) collective-permute-start(f32[3072]{0:T(1024)S(1)} %add.267), channel_id=1, source_target_pairs={{0,4},{4,0},{8,12},{12,8},{16,20},{20,16},{24,28},{28,24},{1,5},{5... | collective-permute-start | bytes 36872 | tf_op jit(solution)/shard_map/ppermute | solution.py:50
  480.5 11.7 %collective-permute-start.21 = (bf16[512,1024]{1,0:T(8,128)(2,1)}, bf16[512,1024]{1,0:T(8,128)(2,1)}, u32[]{:S(2)}, u32[]{:S(2)}) collective-permute-start(bf16[512,1024]{1,0:T(8,128)(2,1)} %inputs_back.3), channel_id=1, source_target_pairs={{0,1},{1,0},{2,3},{3,2},{4,5},{5,4},{6,7},{7,6},{8,9},{9,8},{10,11... | collective-permute-start | bytes 3145736 | tf_op jit(solution)/shard_map/ppermute | solution.py:50
  486.1 15.2 %collective-permute-start.28 = (bf16[2,2,1,128,512]{3,4,0,2,1:T(8,128)(2,1)}, bf16[2,2,1,128,512]{3,4,0,2,1:T(8,128)(2,1)}, u32[]{:S(2)}, u32[]{:S(2)}) collective-permute-start(bf16[2,2,1,128,512]{3,4,0,2,1:T(8,128)(2,1)} %add_convert_fusion.8), channel_id=1, source_target_pairs={{0,2},{1,3},{2,0},{3,1},{4,6},{5,7},{6,4},{7,5},{8,10},{9,11},{10,... | collective-permute-start | bytes 1572872 | tf_op jit(solution)/shard_map/ppermute | solution.py:50
  490.4 14.5 %collective-permute-start.25 = (bf16[2,2,1,128,512]{3,4,2,1,0:T(8,128)(2,1)}, bf16[2,2,1,128,512]{3,4,2,1,0:T(8,128)(2,1)}, u32[]{:S(2)}, u32[]{:S(2)}) collective-permute-start(bf16[2,2,1,128,512]{3,4,2,1,0:T(8,128)(2,1)} %copy.416), channel_id=1, source_target_pairs={{0,4},{4,0},{8,12},{12,8},{16,20},{20,16},{24,28},{28,24},{1,5},{5... | collective-permute-start | bytes 1572872 | tf_op jit(solution)/shard_map/ppermute | solution.py:50
  496.2 16.0 %collective-permute-start.22 = (bf16[512,512]{1,0:T(8,128)(2,1)S(1)}, bf16[512,512]{1,0:T(8,128)(2,1)S(1)}, u32[]{:S(2)}, u32[]{:S(2)}) collective-permute-start(bf16[512,512]{1,0:T(8,128)(2,1)S(1)} %constant_dynamic-slice_fusion.13), channel_id=1, source_target_pairs={{0,2},{1,3},{2,0},{3,1},{4,6},{5,7},{6,4},{7,5},{8,10},{9,11},{10,... | collective-permute-start | bytes 1572872 | tf_op jit(solution)/shard_map/ppermute | solution.py:50
  506.2 13.4 %collective-permute-start.29 = (bf16[2,2,1,1,128,512]{4,5,1,3,2,0:T(8,128)(2,1)S(1)}, bf16[2,2,1,1,128,512]{4,5,1,3,2,0:T(8,128)(2,1)S(1)}, u32[]{:S(2)}, u32[]{:S(2)}) collective-permute-start(bf16[2,2,1,1,128,512]{4,5,1,3,2,0:T(8,128)(2,1)S(1)} %pad_maximum_fusion.12), channel_id=1, source_target_pairs={{0,8},{4,12},{8,0},{12,4},{16,24},{20,28},{24,16},{28,20},{1,9},{5... | collective-permute-start | bytes 1572872 | tf_op jit(solution)/shard_map/ppermute | solution.py:50
  512.6 7.4 %collective-permute-start.23 = (bf16[1024,256]{1,0:T(8,128)(2,1)S(1)}, bf16[1024,256]{1,0:T(8,128)(2,1)S(1)}, u32[]{:S(2)}, u32[]{:S(2)}) collective-permute-start(bf16[1024,256]{1,0:T(8,128)(2,1)S(1)} %get-tuple-element.235), channel_id=1, source_target_pairs={{0,1},{1,0},{2,3},{3,2},{4,5},{5,4},{6,7},{7,6},{8,9},{9,8},{10,11... | collective-permute-start | bytes 1572872 | tf_op jit(solution)/shard_map/ppermute | solution.py:50
  519.9 13.4 %collective-permute-start.30 = (bf16[2,1,1,1,128,512]{4,5,3,2,1,0:T(8,128)(2,1)S(1)}, bf16[2,1,1,1,128,512]{4,5,3,2,1,0:T(8,128)(2,1)S(1)}, u32[]{:S(2)}, u32[]{:S(2)}) collective-permute-start(bf16[2,1,1,1,128,512]{4,5,3,2,1,0:T(8,128)(2,1)S(1)} %pad_maximum_fusion.18), channel_id=1, source_target_pairs={{0,16},{4,20},{8,24},{12,28},{16,0},{20,4},{24,8},{28,12},{1,17},{... | collective-permute-start | bytes 786440 | tf_op jit(solution)/shard_map/ppermute | solution.py:50
  (39 other events, 280.7 us)
Sparse Core Ops, SparseCore 0:
  11.3 115.0 all-gather.2
  129.1 88.1 all-gather.4
  276.3 137.6 reduce-scatter.3

commit v5 on v4

--- a/solution.py
+++ b/solution.py
@@ -13,6 +13,7 @@
 MASKED = -1000000000.0
 LONGEST = 256
 COL = ("seq", "way")
+SHARE = 1
 F32 = jnp.float32
 BF16 = jnp.bfloat16
 
@@ -65,6 +66,10 @@
     def reduce(self, block, dim):
         got = self.trade(pick(block, 1 - self.bit, dim))
         return add(pick(block, self.bit, dim), got)
+
+
+def add_three(mine, one, two):
+    return (mine.astype(F32) + one.astype(F32) + two.astype(F32)).astype(mine.dtype)
 
 
 def add(mine, other):
@@ -191,26 +196,30 @@
         ),
         out_shape=outs,
         input_output_aliases=aliases or {},
-        cost_estimate=pl.CostEstimate(flops=flops, transcendentals=0, bytes_accessed=moved),
+        cost_estimate=pl.CostEstimate(flops=flops // SHARE, transcendentals=0, bytes_accessed=moved // SHARE),
         name=name,
     )(*scalars, *operands)
 
 
-def attend(windows, q, k, v, lab_col, lab_row):
-    slabs, length, lanes = q.shape
+def slab_from(a, first):
+    return pl.BlockSpec((1,) + a.shape[1:], lambda i, *_: (first + i,) + (0,) * (len(a.shape) - 1))
+
+
+def attend(windows, q, k, v, lab_col, lab_row, first, slabs):
+    _, length, lanes = q.shape
     operands = [q, k, v, lab_col, lab_row]
-    specs = [slab(q)] * 3 + [fixed(lab_col), fixed(lab_row)]
-    outs = [struct(q.shape, BF16), struct((slabs, lanes // DH, length), F32)]
+    specs = [slab_from(q, first)] * 3 + [fixed(lab_col), fixed(lab_row)]
+    outs = [struct((slabs,) + q.shape[1:], BF16), struct((slabs, lanes // DH, length), F32)]
     return launch(
         attend_kernel, slabs, [windows], operands, specs, outs, [slab(a) for a in outs], [],
         40 * slabs * length * 640 * lanes, "attend",
     )
 
 
-def attend_back(windows, q, k, v, do, lse, lab_col, lab_row):
-    slabs, length, lanes = q.shape
+def attend_back(windows, q, k, v, do, lse, lab_col, lab_row, first, slabs):
+    _, length, lanes = q.shape
     operands = [q, k, v, do, lse, lab_col, lab_row]
-    specs = [slab(a) for a in operands[:5]] + [fixed(lab_col), fixed(lab_row)]
+    specs = [slab_from(a, first) for a in operands[:4]] + [slab(lse), fixed(lab_col), fixed(lab_row)]
     outs = [struct((slabs, length, 3 * lanes), BF16), struct((slabs, 2, lanes), F32)]
     return launch(
         attend_back_kernel, slabs, [windows], operands, specs, outs, [slab(a) for a in outs],
@@ -241,6 +250,12 @@
         self.spec = pl.BlockSpec(shape, lambda i, at: (0, at[1 + order], 0, block))
 
 
+class Whole:
+    def __init__(self, array, width, block):
+        self.array, self.width = array, width
+        self.spec = pl.BlockSpec((array.shape[0], width), lambda i, *_: (0, block))
+
+
 def arrays(slabs):
     return [w.array for w in slabs]
 
@@ -250,10 +265,13 @@
 
 
 def rows_of(slab):
-    return slab.array.shape[0] * slab.array.shape[2]
+    shape = slab.array.shape
+    return shape[0] if len(shape) == 2 else shape[0] * shape[2]
 
 
 def flat(ref):
+    if len(ref.shape) == 2:
+        return ref[...]
     return ref[:, 0].reshape(ref.shape[0] * ref.shape[2], ref.shape[3])
 
 
@@ -282,37 +300,36 @@
     )
 
 
-def context_out_kernel(at, ctx_ref, *refs):
-    weights, out_ref = refs[:-1], refs[-1]
-    left = jnp.concatenate([ctx_ref[i] for i in range(ctx_ref.shape[0])], axis=1)
-    right = jnp.concatenate([flat(w) for w in weights], axis=1)
-    out_ref[...] = nt(left, right).astype(out_ref.dtype)
-
-
-def context_out(at, ctx, weights, part, dtype):
+def context_out(at, stacks, weights, part, dtype):
     tile = row_tile(part)
     model = rows_of(weights[0])
+    per, _, lanes = stacks[0].shape
     out = struct((part, model), dtype)
-    return launch(
-        context_out_kernel, part // tile, [at], [ctx] + arrays(weights),
-        [tall_from(ctx, tile, part // tile)] + specs_of(weights), [out], [tall(out, tile)], [],
-        2 * part * model * ctx.shape[0] * ctx.shape[2], "context_out",
+
+    def kernel(at_ref, *refs):
+        left = jnp.concatenate([ctx[i] for ctx in refs[: len(stacks)] for i in range(per)], axis=1)
+        right = jnp.concatenate([flat(w)[:, w.shape[-1] - lanes :] for w in refs[len(stacks) : -1]], axis=1)
+        refs[-1][...] = nt(left, right).astype(refs[-1].dtype)
+
+    return launch(
+        kernel, part // tile, [at], list(stacks) + arrays(weights),
+        [tall_from(a, tile, part // tile) for a in stacks] + specs_of(weights), [out], [tall(out, tile)], [],
+        2 * part * model * lanes * len(weights), "context_out",
     )[0]
 
 
 def context_back_kernel(at, ga_ref, *refs):
     weights, out_ref = refs[:-1], refs[-1]
     lanes = out_ref.shape[2]
-    right = jnp.concatenate([flat(w) for w in weights], axis=1)
+    right = jnp.concatenate([flat(w)[:, w.shape[-1] - lanes :] for w in weights], axis=1)
     grad = nn(ga_ref[...], right).astype(BF16)
     for i in range(out_ref.shape[0]):
         out_ref[i] = grad[:, i * lanes : (i + 1) * lanes]
 
 
-def context_back(at, ga, weights):
-    lanes = weights[0].width // 2
+def context_back(at, ga, weights, lanes):
     tile = row_tile(ga.shape[0])
-    count = 2 * len(weights)
+    count = len(weights)
     out = struct((count, ga.shape[0], lanes), BF16)
     return launch(
         context_back_kernel, ga.shape[0] // tile, [at], [ga] + arrays(weights),
@@ -413,49 +430,61 @@
     )
 
 
-def inputs_back_kernel(at, gp_ref, *refs):
-    weights, out_ref = refs[:-1], refs[-1]
-    total = nt(gp_ref[0], weights[0][...])
-    for i in range(1, len(weights)):
-        total += nt(gp_ref[i], weights[i][...])
-    out_ref[...] = total.astype(out_ref.dtype)
-
-
-def inputs_back(at, gp, weights, part, dtype):
+def inputs_back(at, stacks, weights, part, dtype):
     tile = row_tile(part)
     model = weights[0].shape[0]
     out = struct((part, model), dtype)
-    return launch(
-        inputs_back_kernel, part // tile, [at], [gp] + weights,
-        [tall_from(gp, tile, part // tile)] + [fixed(w) for w in weights], [out], [tall(out, tile)], [],
-        2 * part * model * gp.shape[0] * gp.shape[2], "inputs_back",
+    per = stacks[0].shape[0]
+
+    def kernel(at_ref, *refs):
+        grads, rest, out_ref = refs[: len(stacks)], refs[len(stacks) : -1], refs[-1]
+        total = None
+        for i, weight in enumerate(rest):
+            term = nt(grads[i // per][i % per], weight[...])
+            total = term if total is None else total + term
+        out_ref[...] = total.astype(out_ref.dtype)
+
+    return launch(
+        kernel, part // tile, [at], list(stacks) + weights,
+        [tall_from(a, tile, part // tile) for a in stacks] + [fixed(w) for w in weights], [out], [tall(out, tile)], [],
+        2 * part * model * weights[0].shape[1] * len(weights), "inputs_back",
     )[0]
 
 
 def transpose_into(left_t, lefts):
     first = 0
     for left in lefts:
-        left_t[:, first : first + left.shape[0]] = left[...].T
+        left_t[:, pl.ds(first, left.shape[0])] = left[...].T
         first += left.shape[0]
 
 
-def weight_grad(lefts, right):
-    count, length, wide = right.shape
-    model = lefts[0].shape[1]
-    out = struct((model, wide), BF16)
-    parts = len(lefts)
+def weight_grad(pairs):
+    count = pairs[0][1].shape[0]
+    length, model = pairs[0][1].shape[1], pairs[0][0][0].shape[1]
+    wides = [right.shape[2] for _, right, _ in pairs]
+    out = struct((model, sum(wides)), BF16)
+    lefts = [left for group, _, _ in pairs for left in group]
+    rights = [right for _, right, _ in pairs]
+    many = len(pairs)
 
     def kernel(*refs):
-        right_ref, outs = refs[parts], refs[parts + 1 : parts + 1 + count]
-        left_t, slots, sems = refs[-3:]
+        left_refs, refs = refs[: len(lefts)], refs[len(lefts) :]
+        right_refs, outs = refs[:many], refs[many : many + count]
+        left_t, slots, sems = refs[many + count :]
         copies = [pltpu.make_async_copy(slots.at[k % 2], outs[k], sems.at[k % 2]) for k in range(count)]
 
         def step(k):
             if k == 0:
-                transpose_into(left_t, refs[:parts])
+                first = 0
+                for n, (group, _, _) in enumerate(pairs):
+                    transpose_into(left_t.at[n], left_refs[first : first + len(group)])
+                    first += len(group)
             if k > 1:
                 copies[k - 2].wait()
-            slots[k % 2] = nn(left_t[...], right_ref[0]).astype(BF16)
+            column = 0
+            for n, wide in enumerate(wides):
+                slots[k % 2, :, column : column + wide] = nn(left_t[n], right_refs[n][0]).astype(BF16)
+                column += wide
             copies[k].start()
             if k == count - 1:
                 for last in copies[max(k - 1, 0) :]:
@@ -465,35 +494,71 @@
             pl.when(pl.program_id(0) == k)(functools.partial(step, k))
 
     return launch(
-        kernel, count, [], list(lefts) + [right], [fixed(a) for a in lefts] + [slab(right)], [out] * count,
-        [pl.BlockSpec(memory_space=pl.ANY)] * count,
-        [pltpu.VMEM((model, length), BF16), pltpu.VMEM((2, model, wide), BF16), pltpu.SemaphoreType.DMA((2,))],
-        2 * length * model * wide * count, "weight_grad",
-    )
-
-
-def weight_grad_shards(at, lefts, right, rows, seqs):
+        kernel, count, [], lefts + rights, [fixed(a) for a in lefts] + [slab_from(a, f) for _, a, f in pairs],
+        [out] * count, [pl.BlockSpec(memory_space=pl.ANY)] * count,
+        [
+            pltpu.VMEM((many, model, length), BF16),
+            pltpu.VMEM((2,) + out.shape, BF16),
+            pltpu.SemaphoreType.DMA((2,)),
+        ],
+        2 * length * model * sum(wides) * count, "weight_grad",
+    )
+
+
+def weight_grad_shards(at, lefts, right, ring, near, seqs):
     count, length, wide = right.shape
     model = lefts[0].shape[1]
     halves = count // seqs
-    out = struct((rows, seqs, model // rows, wide * halves), BF16)
+    own = model // (ring * near)
+    out = struct((near, seqs, own, wide * halves), BF16)
     parts = len(lefts)
+    block = near * own
 
     def kernel(at_ref, *refs):
-        right_ref, out_ref, left_t = refs[parts:]
+        right_ref, outs, left_t = refs[parts], refs[parts + 1 : -1], refs[-1]
 
         @pl.when(pl.program_id(0) == 0)
         def _():
             transpose_into(left_t, refs[:parts])
 
-        made = nn(left_t[...], right_ref[0]).astype(BF16)
-        out_ref[:, 0] = made.reshape(out_ref.shape[0], out_ref.shape[2], wide)
-
-    spec = pl.BlockSpec((rows, 1, model // rows, wide), lambda i, at: (0, at[1 + i // halves], 0, i % halves))
-    return launch(
-        kernel, count, [at], list(lefts) + [right], [fixed(a) for a in lefts] + [slab(right)], [out], [spec],
-        [pltpu.VMEM((model, length), BF16)], 2 * length * model * wide * count, "weight_grad_shards",
-    )[0]
+        for k in range(ring):
+            first = pl.multiple_of(((at_ref[1 + seqs] + k) % ring) * block, block)
+            made = nn(left_t[pl.ds(first, block), :], right_ref[0]).astype(BF16)
+            outs[k][:, 0] = made.reshape(near, own, wide)
+
+    spec = pl.BlockSpec((near, 1, own, wide), lambda i, at: (0, at[1 + i // halves], 0, i % halves))
+    return launch(
+        kernel, count, [at], list(lefts) + [right], [fixed(a) for a in lefts] + [slab(right)], [out] * ring,
+        [spec] * ring, [pltpu.VMEM((model, length), BF16)], 2 * length * model * wide * count, "weight_grad_shards",
+    )
+
+
+def assemble(place, pieces):
+    ring = len(pieces)
+    each = [p if isinstance(p, list) else [p] for p in pieces]
+    shape = pieces[0].shape[1:]
+    out = struct((ring,) + shape, BF16)
+    operands = [a for p in each for a in p]
+
+    def kernel(place_ref, *refs):
+        sources, outs, sems = list(refs[: len(operands)]), refs[len(operands) : -1], refs[-1]
+        copies = []
+        for k, p in enumerate(each):
+            spot = (place_ref[0] + k) % ring
+            own = [sources.pop(0) for _ in p]
+            for h in range(2):
+                source = own[h] if len(own) == 2 else own[0].at[h]
+                copies.append(pltpu.make_async_copy(source, outs[h].at[spot], sems.at[2 * k + h]))
+        for copy in copies:
+            copy.start()
+        for copy in copies:
+            copy.wait()
+
+    anywhere = pl.BlockSpec(memory_space=pl.ANY)
+    return launch(
+        kernel, 1, [place], operands, [anywhere] * len(operands), [out] * 2, [fixed(out)] * 2,
+        [pltpu.SemaphoreType.DMA((2 * ring,))], 0, "assemble",
+    )
 
 
 def norm_rows(hidden):
@@ -615,32 +680,67 @@
     by_way = [Stage(COL, cols, mask, col) for mask in bits_of(ways)]
     by_row = [Stage("row", rows, mask, row) for mask in bits_of(rows)]
     ns, nw, nr = len(by_seq), len(by_way), len(by_row)
-    far, near = by_row[:-1], by_row[-1]
+    outer, near = by_row[:-1], by_row[-1]
     parts = range(ways)
     orders = [0]
     for mask in bits_of(seqs):
         orders = orders + [o ^ mask for o in orders]
-    at = [jnp.stack([way ^ p] + [seq ^ o for o in orders]).astype(jnp.int32) for p in parts]
-
-    def gather_far(one, two):
-        halves = [h.reshape((1,) * nr + h.shape) for h in (one, two)]
-        for i, stage in enumerate(far):
-            both = jnp.stack(halves)
-            got = stage.trade(both)
-            halves = [stage.join(both[h], got[h], i) for h in range(2)]
-        return halves
-
-    def gather_near(block):
-        return near.gather(block, nr - 1).reshape(model, -1)
-
-    def gather_last(one, two):
-        ones, twos = [gather_near(one)], [two]
+    ring = rows // 2
+    place = row // 2
+    at = [jnp.stack([way ^ p] + [seq ^ o for o in orders] + [place]).astype(jnp.int32) for p in parts]
+    here = place.reshape(1).astype(jnp.int32)
+
+    def turn(block, step):
+        return lax.ppermute(block, "row", [(i, (i + 2 * step) % rows) for i in range(rows)])
+
+    def turn_first(piece):
+        return turn(piece, 1), turn(piece, -1)
+
+    def turn_rest(piece, got):
+        plus, minus = got
+        pieces = {0: piece, ring - 1: plus, 1: minus}
+        for k in range(2, ring // 2):
+            plus, minus = turn(plus, 1), turn(minus, -1)
+            pieces[ring - k], pieces[k] = plus, minus
+        pieces[ring // 2] = [turn(plus[0], 1), turn(minus[1], -1)]
+        return [pieces[k] for k in range(ring)]
+
+    def held(block, mark):
+        return after(block, *mark) if mark else block
+
+    def spread(halves):
+        one, two = [h[None, None] for h in halves]
+        return one, two, near.trade(one), by_seq[0].trade(two)
+
+    def spread_rest(one, two, one_got, two_got):
+        one, two = near.join(one, one_got, 0), by_seq[0].join(two, two_got, 1)
+        return one, two, by_seq[0].trade(one), near.trade(two)
+
+    def spread_end(one, two, one_got, two_got):
+        return jnp.stack((by_seq[0].join(one, one_got, 1), near.join(two, two_got, 0)))
+
+    def whole_shards(pieces):
+        return [g.reshape((rows,) + g.shape[2:]) for g in assemble(here, pieces)]
+
+    def last_first(one, two):
+        twos = [two]
         for stage in by_seq:
             twos = twos + [stage.trade(b) for b in twos]
-        two = after(two, ones[0])
-        twos = [gather_near(b) for b in [two] + twos[1:]]
+        return near.trade(one), twos[1:]
+
+    def last_rest(one, two, one_got, two_got):
+        def whole(block, got):
+            return near.join(block, got, nr - 1).reshape(model, -1)
+
+        twos = [two] + two_got
+        twos_got = [near.trade(b) for b in twos]
+        ones = [whole(one, one_got)]
         for stage in by_seq:
             ones = ones + [stage.trade(b) for b in ones]
+        return ones, twos, twos_got
+
+    def last_end(ones, twos, twos_got):
+        twos = [near.join(b, g, nr - 1).reshape(model, -1) for b, g in zip(twos, twos_got)]
         return [b for j in range(seqs) for b in (ones[j], twos[j])]
 
     def halves_of(weight):
@@ -649,13 +749,24 @@
 
     by_kind = wqkv.reshape(own_rows, 2, heads // 2, 3, DH).transpose(1, 0, 3, 2, 4)
     by_kind = by_kind.reshape(2, own_rows, -1)
-    far_qkv = gather_far(by_kind[0], by_kind[1])
+    def by_bits(pieces):
+        return [b.reshape((2,) * (nr - 1) + (1,) + b.shape[1:]) for b in assemble(here, pieces)]
+
+    wo_t = halves_of(wo.T)
+    qkv_got = turn_first(by_kind)
+    in_piece = jnp.stack([jnp.concatenate((a, b), axis=1) for a, b in zip(halves_of(w_in), wo_t)])
+    qkv_pieces = turn_rest(by_kind, qkv_got)
+    in_got = turn_first(after(in_piece, *qkv_got))
+    out_shards = spread(halves_of(w_out.T))
+    out_first = out_shards[2:]
+    out_shards = spread_rest(*out_shards)
+    far_qkv = by_bits(qkv_pieces)
 
     labels = lax.dynamic_slice_in_dim(segments, seq, 1, 0)[0]
     windows = key_windows(labels)
     lab_col, lab_row = labels[:, None], labels[None, :]
 
-    def exchange(array, split, whole):
+    def exchange(array, split, whole, mark=()):
         blocks = [array]
         for stage in split + whole:
             both = blocks[0] if len(blocks) == 1 else jnp.concatenate(blocks, axis=1)
@@ -664,7 +775,7 @@
                 mine, sent = pick(both, stage.bit, 0)[0], pick(both, 1 - stage.bit, 0)[0]
             else:
                 mine = sent = both
-            got = stage.trade(sent)
+            got = held(stage.trade(sent), mark)
             low = stage.bit == 0
             blocks = [
                 half
@@ -691,11 +802,27 @@
             ]
         return jnp.concatenate(blocks, axis=0)
 
-    whole_x = exchange(after(tokens, far_qkv[0]), by_seq, by_way)
+    def widen(array, whole):
+        for stage in whole:
+            got = stage.trade(array)
+            low = stage.bit == 0
+            array = jnp.concatenate(
+                [
+                    half
+                    for i in range(array.shape[1] // width)
+                    for a, b in [(array[:, i * width : (i + 1) * width], got[:, i * width : (i + 1) * width])]
+                    for half in (jnp.where(low, a, b), jnp.where(low, b, a))
+                ],
+                axis=1,
+            )
+        return array
+
+    half_x = exchange(after(tokens, *out_first), by_seq, [])
     vectors = jnp.concatenate(
         [v.reshape(-1, width) for v in (bias_o, gain_a, shift_a, bias_out, gain_b, shift_b, bias_qv, bias_in)]
     )
-    vectors = after(vectors, far_qkv[0])
+    vectors = after(vectors, half_x)
+    whole_x = widen(half_x, by_way)
     pairs = [vectors]
     for stage in by_seq:
         pairs = pairs + [stage.trade(v) for v in pairs]
@@ -731,20 +858,15 @@
     q_bias = jnp.concatenate(q_biases, axis=0).reshape(2 * seqs, 1, 3 * lanes)
     in_bias = jnp.concatenate(in_biases, axis=0)
 
-    qkv_all = gather_last(*far_qkv)
-    everyone = ("row", "seq")
-
-    def shards(weight):
-        whole = lax.all_gather(weight, everyone, axis=0, tiled=True)
-        return whole.reshape(rows, seqs, own_rows, weight.shape[1])
-
-    whole_in = shards(jnp.concatenate((w_in, wo.T), axis=1))
-    whole_out = shards(w_out.T)
+    qkv_first = last_first(*far_qkv)
+    qkv_rest = last_rest(*far_qkv, *qkv_first)
+    in_pieces = turn_rest(in_piece, [after(g, *far_qkv) for g in in_got])
+    far_in = by_bits(in_pieces)
+    in_first = last_first(*[after(b, qkv_rest[0][0], *qkv_first[1]) for b in far_in])
+    qkv_all = last_end(*qkv_rest)
+    out_piece = spread_end(*out_shards[:2], *[after(b, *far_qkv) for b in out_shards[2:]])
+    out_got = turn_first(after(out_piece, *far_in))
     pairs_of = [(j, h) for j in range(seqs) for h in range(2)]
-    in_all = [Slab(whole_in, hid // 2, h, j) for j, h in pairs_of]
-    wo_all = [Slab(whole_in, 2 * lanes, hid // (2 * lanes), j) for j in range(seqs)]
-    out_all = [Slab(whole_out, hid // 2, h, j) for j, h in pairs_of]
-    cot = exchange(after(cotangent, qkv_all[2]), by_seq + by_way, [])
 
     def gather_parts(own):
         blocks = {0: own}
@@ -771,71 +893,135 @@
                     blocks[p], blocks[p | mask] = jnp.where(low, a, b), jnp.where(low, b, a)
         return jnp.concatenate(blocks, axis=0)
 
-    def scatter_first(blocks):
-        ones, twos = blocks[0::2], blocks[1::2]
-        fold = lambda b: near.reduce(b.reshape((2,) * nr + (own_rows, -1)), nr - 1)
-        for stage in reversed(by_seq):
-            count = len(ones) // 2
-            ones = [add(ones[j], stage.trade(ones[count + j])) for j in range(count)]
-        twos = [fold(b) for b in reversed(twos)][::-1]
-        for stage in reversed(by_seq):
-            count = len(twos) // 2
-            twos = [add(twos[j], stage.trade(twos[count + j])) for j in range(count)]
-        return fold(ones[0]), twos[0]
-
-    def scatter_far(one, two):
-        for i, stage in reversed(list(enumerate(far))):
+    def fold_start(block):
+        block = block.reshape((2,) * nr + (own_rows, -1))
+        return block, near.trade(pick(block, 1 - near.bit, nr - 1))
+
+    def fold_end(block, got):
+        return add(pick(block, near.bit, nr - 1), got)
+
+    def across_start(blocks):
+        count = len(blocks) // 2
+        return blocks[:count], [by_seq[-1].trade(b) for b in blocks[count:]]
+
+    def across_end(mine, gots):
+        blocks = [add(m, g) for m, g in zip(mine, gots)]
+        for stage in list(reversed(by_seq))[1:]:
+            count = len(blocks) // 2
+            blocks = [add(blocks[j], stage.trade(blocks[count + j])) for j in range(count)]
+        return blocks[0]
+
+    def scatter_far(one, two, marks=()):
+        for n, (i, stage) in enumerate(reversed(list(enumerate(outer)))):
             halves = (one, two)
             sent = jnp.stack([pick(b, 1 - stage.bit, i) for b in halves])
-            got = stage.trade(sent)
+            got = held(stage.trade(sent), marks[n] if n < len(marks) else ())
             one, two = [add(pick(b, stage.bit, i), got[h]) for h, b in enumerate(halves)]
         return one.reshape(own_rows, -1).astype(F32), two.reshape(own_rows, -1).astype(F32)
 
     q, k, v = project(whole_x, qkv_all, q_bias)
-    context, lse = attend(windows, q, k, v, lab_col, lab_row)
-    mine, got = scatter_parts(lambda p, dtype: context_out(at[p], context, wo_all, part, dtype))
+    contexts, lses, ready = [], [], [in_first[0], *in_first[1]]
+    for j in range(seqs):
+        context, lse = attend(windows, after(q, *contexts, *ready) if j else q, k, v, lab_col, lab_row, 2 * j, 2)
+        contexts, lses = contexts + [context], lses + [lse]
+        if j == 0:
+            in_first = after(in_first[0], context), [after(b, context) for b in in_first[1]]
+            in_rest = last_rest(*far_in, *in_first)
+    contexts = [after(c, *contexts, *out_got) for c in contexts]
+    out_pieces = turn_rest(out_piece, [after(g, contexts[-1]) for g in out_got])
+    in_blocks = last_end(*in_rest)
+    in_all = [Whole(b, hid // 2, 0) for b in in_blocks]
+    aligned = lanes % 128 == 0
+    wo_all = [Whole(b, lanes, hid // 2 // lanes) if aligned else Whole(b, b.shape[1], 0) for b in in_blocks]
+    mine, got = scatter_parts(lambda p, dtype: context_out(at[p], contexts, wo_all, part, dtype))
     centred_a, inv_a, y = norm_a(at[0], mine, got, whole_x, vec)
     y_parts = gather_parts(y)
     earlier = []
     for p in parts:
         earlier = ffn_in(at[0], y_parts[p], in_bias, in_all, ways, p, list(earlier))
     active, slope = earlier
+    whole_out = whole_shards([after(p, active) if not isinstance(p, list) else [after(b, active) for b in p] for p in out_pieces])
+    out_all = [Slab(whole_out[h], hid // 2, 0, j) for j, h in pairs_of]
+    cot = exchange(after(cotangent, contexts[-1]), by_seq + by_way, [], (active,))
     mine, got = scatter_parts(lambda p, dtype: ffn_out(at[0], active, out_all, part, p, dtype))
     output, grad_b, gb, sums_b = norm_b(mine, got, centred_a, cot, vec)
 
     gb_parts = gather_parts(gb)
     output = to_features(after(output, gb_parts[-1]))
-    grad_w_out = weight_grad_shards(at[0], gb_parts, active, rows, seqs)
-    out_sum = lax.psum_scatter(
-        grad_w_out.reshape(rows * seqs * own_rows, hid), everyone, scatter_dimension=0, tiled=True
-    )
+    chunks = weight_grad_shards(at[0], gb_parts, active, ring, 2, seqs)
+    plus, minus = turn(chunks[ring // 2][0], 1), turn(chunks[ring // 2][1], -1)
+    tie = (chunks[0],)
     terms, sum_in, earlier = {}, 0.0, []
     for p in parts:
         grad_inner, sums, terms[p] = ffn_back(
-            at[0], after(gb_parts[p], grad_w_out), slope, out_all, in_all, p, earlier, F32 if p == 0 else BF16
+            at[0], after(gb_parts[p], *tie), slope, out_all, in_all, p, earlier, F32 if p == 0 else BF16
         )
         earlier = [grad_inner]
+        if p == parts[-1]:
+            firsts = plus, minus
+            plus, minus = after(plus, grad_inner), after(minus, grad_inner)
+            for far in reversed(range(1, ring // 2)):
+                up, down = chunks[far], chunks[ring - far]
+                if far == ring // 2 - 1:
+                    up = jnp.stack((add(up[0], plus), up[1]))
+                    down = jnp.stack((down[0], add(down[1], minus)))
+                else:
+                    up, down = add(up, plus), add(down, minus)
+                tie = (up, down)
+                plus, minus = turn(up, 1), turn(down, -1)
         sum_in = sum_in + sums
     mine, got = scatter_parts(lambda p, dtype: terms[p])
-    grad_w_in = weight_grad(y_parts, grad_inner)
-    grad_a, ga, sums_a = norm_a_back(mine, got, grad_b, centred_a, inv_a, vec)
+    grad_w_in = weight_grad([(y_parts, after(grad_inner, *firsts), 0)])
+    grad_a, ga, sums_a = norm_a_back(mine, got, after(grad_b, grad_w_in[0]), centred_a, inv_a, vec)
     whole_ga = whole_rows(gather_parts(ga))
-    grad_context = context_back(at[0], whole_ga, wo_all)
-    first_in = scatter_first(grad_w_in)
-    grad_projected, sum_projected = attend_back(windows, q, k, v, grad_context, lse, lab_col, lab_row)
-    in_halves = scatter_far(*first_in)
-    grad_wo = weight_grad([whole_ga], context)
-    grad_wqkv = weight_grad([whole_x], grad_projected)
-    last = scatter_first([jnp.concatenate(two, axis=1) for two in zip(grad_wqkv, grad_wo)])
-    mine, got = scatter_parts(lambda p, dtype: inputs_back(at[p], grad_projected, qkv_all, part, dtype))
-    grad_tokens = to_features((mine + got.astype(F32) + grad_a).astype(BF16)).astype(F32)
-    qkv_halves = scatter_far(*last)
+    grad_context = context_back(at[0], whole_ga, wo_all, lanes)
+    ones_mine, ones_got = across_start(grad_w_in[0::2])
+    twos_in = [fold_start(b) for b in grad_w_in[1::2]]
+    gots = ones_got + [g for _, g in twos_in] + [plus, minus]
+    stacks, sums_p, made, later = {}, [], {}, []
+    ready = grad_context
+    for j in reversed(range(seqs)):
+        projected, sums = attend_back(
+            windows, q, k, v, after(grad_context, ready), lses[j], lab_col, lab_row, 2 * j, 2
+        )
+        if j == seqs - 1:
+            projected = after(projected, *gots)
+        made[j] = weight_grad([([whole_x], projected, 0), ([whole_ga], contexts[j], 0)])
+        ready = made[j][0]
+        stacks[j], sums_p = projected, [sums] + sums_p
+        if j == seqs - 1:
+            ones_got, twos_got = [held(g, (projected,)) for g in ones_got], [held(g, (projected,)) for _, g in twos_in]
+            one_in = fold_start(across_end(ones_mine, ones_got))
+            two_in = across_start([fold_end(b, g) for (b, _), g in zip(twos_in, twos_got)])
+            later = [one_in[1]] + two_in[1]
+            out_sum = add_three(chunks[0], after(plus, projected), after(minus, projected))
+            out_sum = near.reduce(after(out_sum, ready), 0)
+    sum_projected = jnp.concatenate(sums_p, axis=0)
+    for stage in reversed(by_seq):
+        out_sum = stage.reduce(after(out_sum, ready), 1)
+    halves_in = fold_end(one_in[0], held(one_in[1], (ready,))), across_end(two_in[0], [held(g, (ready,)) for g in two_in[1]])
+    ones_mine, ones_got = across_start([made[j][0] for j in range(seqs)])
+    twos_last = [fold_start(made[j][1]) for j in range(seqs)]
+    gots = ones_got + [g for _, g in twos_last]
+    stacks = [after(stacks[j], ready, *later) for j in range(seqs)]
+    term = {1: inputs_back(at[1], stacks, qkv_all, part, BF16)} if ways == 2 else {}
+    tied = [after(a, *gots[:1], *term.values()) for a in stacks]
+    mine, got = scatter_parts(
+        lambda p, dtype: term[p] if p in term else inputs_back(at[p], tied, qkv_all, part, dtype)
+    )
+    ones_got, twos_got = [held(g, tuple(term.values())) for g in ones_got], [g for _, g in twos_last]
+    one_last = fold_start(across_end(ones_mine, ones_got))
+    two_last = across_start([fold_end(b, g) for (b, _), g in zip(twos_last, twos_got)])
+    in_halves = scatter_far(*halves_in, [(mine,)])
+    grad_tokens = to_features((after(mine, one_last[1]) + got.astype(F32) + grad_a).astype(BF16)).astype(F32)
+    qkv_halves = scatter_far(fold_end(*one_last), across_end(*two_last))
 
     per_hidden = []
     for j in range(seqs):
         two = sum_projected[2 * j : 2 * j + 2].reshape(2, 2, heads // 2, DH).transpose(0, 2, 1, 3)
         per_hidden.append(jnp.concatenate((two.reshape(-1), sum_in[2 * j : 2 * j + 2].reshape(-1))))
-    block = jnp.concatenate((sums_a, sums_b), axis=0)
+    block = after(jnp.concatenate((sums_a, sums_b), axis=0), one_last[0])
+    per_hidden = [after(v, one_last[0]) for v in per_hidden]
     for stage in by_seq + by_way:
         half = block.shape[1] // 2
         got = stage.trade(lax.dynamic_slice_in_dim(block, (1 - stage.bit) * half, half, 1))
@@ -863,7 +1049,7 @@
         rest[2],
         jnp.concatenate(in_halves, axis=1),
         sum_in,
-        out_sum.astype(F32).T,
+        out_sum.reshape(own_rows, hid).astype(F32).T,
         rest[3],
         rest[4],
         rest[5],

time: 552 us -> 432 us (0.78)
  waiting for transfers between devices: 224 us -> 59.4 us
  starting transfers between devices: 39.3 us -> 82 us
  between operations: 15.4 us -> 2.37 us
  Pallas kernels: 179 us -> 189 us
    ppermute x44 -> x53, waiting for transfers between devices: 170 us -> 48.5 us  [trade(): return lax.ppermute(block, self.axis, self.pairs)]
    all_gather x2 -> x0, waiting for transfers between devices: 53.1 us -> none  [shards(): whole = lax.all_gather(weight, everyone, axis=0, tiled=True)]
    ppermute x0 -> x16, starting transfers between devices: none -> 28.8 us  [turn(): lax.ppermute(block, 'row', [(i, (i + 2 * step) % rows) for i in range(row...]
    ppermute x44 -> x53, starting transfers between devices: 39.2 us -> 53.2 us  [trade(): return lax.ppermute(block, self.axis, self.pairs)]
    ppermute x0 -> x16, waiting for transfers between devices: none -> 11 us  [turn(): lax.ppermute(block, 'row', [(i, (i + 2 * step) % rows) for i in range(row...]
    pallas_call x21 -> x26, Pallas kernels: 179 us -> 189 us  [launch(): pl.pallas_call(kernel, grid_spec=pltpu.PrefetchScalarGridSpec(num_scalar_...]
    squeeze x0 -> x7, local copies, waits for them, and re-layouts: none -> 6.65 us  [the longest x6 4.32 us: turn_rest(): pieces[ring // 2] = [turn(plus[0], 1), turn(minus[1], -1)]]
    all_gather x1 -> x0, local copies, waits for them, and re-layouts: 6.41 us -> none  [shards(): whole = lax.all_gather(weight, everyone, axis=0, tiled=True)]
  transfers between devices with their start and end apart: 47 -> 69, of which waited for: 20 -> 22; matrix products, arithmetic and copies ran while one was open for 14% -> 19% of each run, Pallas kernels for 30% -> 36%
where the time goes in v5:
time: 432 us; the launch traced here: 426 us
  Pallas kernels  189 us (44%)
  starting transfers between devices  82 us (19%)
  waiting for transfers between devices  59.4 us (14%)
  other arithmetic  55.3 us (13%)
  local copies, waits for them, and re-layouts  38 us (9%)
    pallas_call x26, Pallas kernels, launch(): pl.pallas_call(kernel, grid_spec=pltpu.PrefetchScalarGridSpec(num_scalar_...  189 us
    ppermute x53, starting transfers between devices, trade(): return lax.ppermute(block, self.axis, self.pairs)  53.2 us
    ppermute x53, waiting for transfers between devices, trade(): return lax.ppermute(block, self.axis, self.pairs)  48.5 us
    ppermute x16, starting transfers between devices, turn(): lax.ppermute(block, 'row', [(i, (i + 2 * step) % rows) for i in range(row...  28.8 us
    unnamed x131, local copies, waits for them, and re-layouts  19.4 us
    convert_element_type x13, other arithmetic, add(): return (mine.astype(F32) + other.astype(F32)).astype(mine.dtype)  12.5 us
    ppermute x16, waiting for transfers between devices, turn(): lax.ppermute(block, 'row', [(i, (i + 2 * step) % rows) for i in range(row...  11 us
  transfers between devices with their start and end apart: 69, of which 22 were waited for; matrix products, arithmetic and copies ran while one was open for 19% of the time, Pallas kernels for 36%

profile of v5, /device:TPU:0, one launch (start us, length us, event | category | flops | bytes accessed | tf_op | source)
XLA Modules:
  0.0 426.0 jit_solution(615740650239520381)
XLA Ops:
  2.2 3.1 collective-permute-start.6
  18.2 3.8 collective-permute-start.8
  26.0 4.2 collective-permute-start.14
  45.9 3.6 collective-permute-start.17
  53.0 2.5 assemble.4
  56.1 3.9 collective-permute-start.23
  66.4 4.6 %collective-permute-done.13 = bf16[2,2,1,128,384]{4,3,2,1,0:T(8,128)(2,1)S(1)} collective-permute-done((bf16[2,2,1,128,384]{4,3,2,1,0:T(8,128)(2,1)}, bf16[2,2,1,128,384]{4,3,2,1,0:T(8,128)(2,1)S(1)}, u32[]{:S(2)}, u32[]{:S(2)}) %collective-permute-start.13) | collective-permute-done | bytes 393248 | tf_op jit(solution)/shard_map/ppermute | solution.py:51
  77.1 4.7 %collective-permute-done.11.refs_2_.refs_4_ = bf16[1024,384]{1,0:T(8,128)(2,1)S(1)} collective-permute-done((bf16[1024,384]{1,0:T(8,128)(2,1)S(1)}, bf16[1024,384]{1,0:T(8,128)(2,1)S(1)}, u32[]{:S(2)}, u32[]{:S(2)}) %collective-permute-start.11) | collective-permute-done | bytes 786464 | tf_op jit(solution)/shard_map/ppermute | solution.py:51
  83.3 8.4 %project.1 = (bf16[4,1024,128]{2,1,0:T(8,128)(2,1)}, bf16[4,1024,128]{2,1,0:T(8,128)(2,1)}, bf16[4,1024,128]{2,1,0:T(8,128)(2,1)}) custom-call(bf16[1024,1024]{1,0:T(8,128)(2,1)} %pad_maximum_fusion.x_ref.refs_0_, f32[4,1,384]{2,1,0:T(1,128)} %reshape.567.b_ref, bf16[1024,384]{1,0:T(8,128)(2,1)} %bitcast.272, bf16[1024,384]{1,0:T(8,128)(2,1)} %bitcast.275, ...), custom_call_target="tpu_custom_call" | custom-call | flops 3221225472 | bytes 8394752 | tf_op jit(solution)/shard_map/project/pallas_call | solution.py:188
  91.7 10.3 %attend.2 = (bf16[2,1024,128]{2,1,0:T(8,128)(2,1)}, f32[2,2,1024]{2,1,0:T(2,128)}) custom-call(s32[2,4]{1,0:T(2,128)} %pad_add_fusion.windows, bf16[4,1024,128]{2,1,0:T(8,128)(2,1)} %get-tuple-element.132.q_ref, bf16[4,1024,128]{2,1,0:T(8,128)(2,1)} %get-tuple-element.122.k_ref, bf16[4,1024,128]{2,1,0:T(8,128)(2,1)} %get-tuple-element.123.v_ref, ...), custom_call_target="tpu_custom_call" | custom-call | flops 6710886400 | bytes 3694592 | tf_op jit(solution)/shard_map/attend/pallas_call | solution.py:188
  107.5 10.4 %attend.3 = (bf16[2,1024,128]{2,1,0:T(8,128)(2,1)}, f32[2,2,1024]{2,1,0:T(2,128)}) custom-call(s32[2,4]{1,0:T(2,128)} %pad_add_fusion.windows, bf16[4,1024,128]{2,1,0:T(8,128)(2,1)} %get-tuple-element.132.q_ref, bf16[4,1024,128]{2,1,0:T(8,128)(2,1)} %get-tuple-element.122.k_ref, bf16[4,1024,128]{2,1,0:T(8,128)(2,1)} %get-tuple-element.123.v_ref, ...), custom_call_target="tpu_custom_call" | custom-call | flops 6710886400 | bytes 3694592 | tf_op jit(solution)/shard_map/attend/pallas_call | solution.py:188
  120.4 6.6 %collective-permute-done.25.refs_4_.refs_2_.refs_6_ = bf16[1024,640]{1,0:T(8,128)(2,1)S(1)} collective-permute-done((bf16[1024,640]{1,0:T(8,128)(2,1)S(1)}, bf16[1024,640]{1,0:T(8,128)(2,1)S(1)}, u32[]{:S(2)}, u32[]{:S(2)}) %collective-permute-start.25) | collective-permute-done | bytes 1310752 | tf_op jit(solution)/shard_map/ppermute | solution.py:51
  128.1 4.0 context_out.3
  137.9 4.0 context_out.2.mine_ref
  142.9 4.5 %norm_a.1 = (f32[512,1024]{1,0:T(8,128)}, f32[512,1]{1,0:T(8,128)}, bf16[512,1024]{1,0:T(8,128)(2,1)}) custom-call(s32[4]{0:T(128)} %add_add_fusion.at_ref.at, f32[512,1024]{1,0:T(8,128)} %context_out.2.mine_ref, bf16[512,1024]{1,0:T(8,128)(2,1)} %copy-done.24, bf16[1024,1024]{1,0:T(8,128)(2,1)} %pad_maximum_fusion.x_ref.refs_0_, ...), custom_call_target="tpu_custom_call" | custom-call | flops 10485760 | bytes 8415232 | tf_op jit(solution)/shard_map/norm_a/pallas_call | solution.py:188
  150.4 2.5 collective-permute-start.30
  152.9 8.0 %ffn_in.2 = (bf16[4,1024,512]{2,1,0:T(8,128)(2,1)}, bf16[4,1024,512]{2,1,0:T(8,128)(2,1)}) custom-call(s32[4]{0:T(128)} %add_add_fusion.at_ref.at, bf16[512,1024]{1,0:T(8,128)(2,1)} %get-tuple-element.141.y_ref.refs_0_, f32[4,1,512]{2,1,0:T(1,128)} %maximum_convert_fusion.3.b_ref, bf16[1024,640]{1,0:T(8,128)(2,1)} %bitcast.252, bf16[1024,640]{1,0:T(8,128)(2,1)} %bitcast.259, ...), custom_call_target="tpu_custom_call" | custom-call | flops 6442450944 | bytes 14688256 | tf_op jit(solution)/shard_map/ffn_in/pallas_call | solution.py:188
  161.0 8.1 %ffn_in.3 = (bf16[4,1024,512]{2,1,0:T(8,128)(2,1)}, bf16[4,1024,512]{2,1,0:T(8,128)(2,1)}) custom-call(s32[4]{0:T(128)} %add_add_fusion.at_ref.at, bf16[512,1024]{1,0:T(8,128)(2,1)} %collective-permute-done.29.y_ref.refs_1_, f32[4,1,512]{2,1,0:T(1,128)} %maximum_convert_fusion.3.b_ref, ...), custom_call_target="tpu_custom_call", output_to_operand_aliasing={{0}: (7, {}), {1}: (8, {})} | custom-call | flops 6442450944 | bytes 23076864 | tf_op jit(solution)/shard_map/ffn_in/pallas_call | solution.py:188
  169.1 5.0 %collective-permute-done.31.refs_3_ = bf16[2,2,128,512]{3,2,1,0:T(8,128)(2,1)S(1)} collective-permute-done((bf16[2,2,128,512]{3,2,1,0:T(8,128)(2,1)S(1)}, bf16[2,2,128,512]{3,2,1,0:T(8,128)(2,1)S(1)}, u32[]{:S(2)}, u32[]{:S(2)}) %collective-permute-start.31) | collective-permute-done | bytes 524320 | tf_op jit(solution)/shard_map/ppermute | solution.py:694
  176.3 4.2 assemble.5
  180.5 6.6 %ffn_out.3 = bf16[512,1024]{1,0:T(8,128)(2,1)} custom-call(s32[4]{0:T(128)} %add_add_fusion.at_ref.at, bf16[4,1024,512]{2,1,0:T(8,128)(2,1)} %get-tuple-element.144.act_ref.refs_2_, bf16[8,2,128,512]{3,2,1,0:T(8,128)(2,1)} %bitcast.233, bf16[8,2,128,512]{3,2,1,0:T(8,128)(2,1)} %bitcast.241, bf16[8,2,128,512]{3,2,1,0:T(8,128)(2,1)} %bitcast.234, ...), custom_call_target="tpu_custom_call" | custom-call | flops 2147483648 | bytes 13631488 | tf_op jit(solution)/shard_map/ffn_out/pallas_call | solution.py:188
  187.8 6.8 %ffn_out.2.mine_ref = f32[512,1024]{1,0:T(8,128)} custom-call(s32[4]{0:T(128)} %add_add_fusion.at_ref.at, bf16[4,1024,512]{2,1,0:T(8,128)(2,1)} %get-tuple-element.144.act_ref.refs_2_, bf16[8,2,128,512]{3,2,1,0:T(8,128)(2,1)} %bitcast.235, bf16[8,2,128,512]{3,2,1,0:T(8,128)(2,1)} %bitcast.243, bf16[8,2,128,512]{3,2,1,0:T(8,128)(2,1)} %bitcast.236, ...), custom_call_target="tpu_custom_call" | custom-call | flops 2147483648 | bytes 14680064 | tf_op jit(solution)/shard_map/ffn_out/pallas_call | solution.py:188
  196.8 5.4 %norm_b.1 = (bf16[512,1024]{1,0:T(8,128)(2,1)}, f32[512,1024]{1,0:T(8,128)}, bf16[512,1024]{1,0:T(8,128)(2,1)}, f32[3,1024]{1,0:T(4,128)}) custom-call(f32[512,1024]{1,0:T(8,128)} %ffn_out.2.mine_ref, bf16[512,1024]{1,0:T(8,128)(2,1)} %copy-done.25, f32[512,1024]{1,0:T(8,128)} %get-tuple-element.154.centred_a_ref.centred_ref, ...), custom_call_target="tpu_custom_call" | custom-call | flops 20971520 | bytes 10522624 | tf_op jit(solution)/shard_map/norm_b/pallas_call | solution.py:188
  202.4 2.7 collective-permute-done.35.refs_1_.gb_ref
  206.2 9.8 %weight_grad_shards.1 = (bf16[2,2,128,1024]{3,2,1,0:T(8,128)(2,1)}, bf16[2,2,128,1024]{3,2,1,0:T(8,128)(2,1)}, bf16[2,2,128,1024]{3,2,1,0:T(8,128)(2,1)}, bf16[2,2,128,1024]{3,2,1,0:T(8,128)(2,1)}) custom-call(s32[4]{0:T(128)} %add_add_fusion.at_ref.at, bf16[512,1024]{1,0:T(8,128)(2,1)} %get-tuple-element.162.refs_0_.gb_ref, bf16[512,1024]{1,0:T(8,128)(2,1)} %copy-done.10, ...), custom_call_target="tpu_custom_call" | custom-call | flops 4294967296 | bytes 10485760 | tf_op jit(solution)/shard_map/weight_grad_shards/pallas_call | solution.py:188
  216.0 2.3 slice_bitcast_fusion
  220.5 11.2 %ffn_back.2 = (bf16[4,1024,512]{2,1,0:T(8,128)(2,1)}, f32[4,1,512]{2,1,0:T(1,128)}, f32[512,1024]{1,0:T(8,128)}) custom-call(s32[4]{0:T(128)} %add_add_fusion.at_ref.at, bf16[512,1024]{1,0:T(8,128)(2,1)} %get-tuple-element.162.refs_0_.gb_ref, bf16[4,1024,512]{2,1,0:T(8,128)(2,1)} %get-tuple-element.163.slope_ref, bf16[8,2,128,512]{3,2,1,0:T(8,128)(2,1)} %bitcast.237, ...), custom_call_target="tpu_custom_call" | custom-call | flops 4294967296 | bytes 25174016 | tf_op jit(solution)/shard_map/ffn_back/pallas_call | solution.py:188
  231.7 11.2 %ffn_back.3 = (bf16[4,1024,512]{2,1,0:T(8,128)(2,1)}, f32[4,1,512]{2,1,0:T(1,128)}, bf16[512,1024]{1,0:T(8,128)(2,1)}) custom-call(s32[4]{0:T(128)} %add_add_fusion.at_ref.at, bf16[512,1024]{1,0:T(8,128)(2,1)} %copy-done.10, bf16[4,1024,512]{2,1,0:T(8,128)(2,1)} %get-tuple-element.163.slope_ref, ...), custom_call_target="tpu_custom_call", output_to_operand_aliasing={{0}: (11, {})} | custom-call | flops 4294967296 | bytes 28319744 | tf_op jit(solution)/shard_map/ffn_back/pallas_call | solution.py:188
  247.9 2.5 collective-permute-start.46
  250.4 8.4 %weight_grad.3 = (bf16[1024,512]{1,0:T(8,128)(2,1)}, bf16[1024,512]{1,0:T(8,128)(2,1)}, bf16[1024,512]{1,0:T(8,128)(2,1)}, bf16[1024,512]{1,0:T(8,128)(2,1)}) custom-call(bf16[512,1024]{1,0:T(8,128)(2,1)} %get-tuple-element.141.y_ref.refs_0_, bf16[512,1024]{1,0:T(8,128)(2,1)} %collective-permute-done.29.y_ref.refs_1_, ...), custom_call_target="tpu_custom_call" | custom-call | flops 4294967296 | bytes 10485760 | tf_op jit(solution)/shard_map/weight_grad/pallas_call | solution.py:188
  260.4 5.5 %norm_a_back.1 = (f32[512,1024]{1,0:T(8,128)}, bf16[512,1024]{1,0:T(8,128)(2,1)}, f32[3,1024]{1,0:T(4,128)}) custom-call(f32[512,1024]{1,0:T(8,128)} %get-tuple-element.164.mine_ref, bf16[512,1024]{1,0:T(8,128)(2,1)} %collective-permute-done.38.got_ref, f32[512,1024]{1,0:T(8,128)} %get-tuple-element.173.gb_ref, ...), custom_call_target="tpu_custom_call" | custom-call | flops 15728640 | bytes 10524672 | tf_op jit(solution)/shard_map/norm_a_back/pallas_call | solution.py:188
  276.7 5.7 %context_back.1.do_ref = bf16[4,1024,128]{2,1,0:T(8,128)(2,1)} custom-call(s32[4]{0:T(128)} %add_add_fusion.at_ref.at, bf16[1024,1024]{1,0:T(8,128)(2,1)} %pad_maximum_fusion.1.ga_ref.refs_1_, bf16[1024,640]{1,0:T(8,128)(2,1)} %bitcast.256, bf16[1024,640]{1,0:T(8,128)(2,1)} %bitcast.263, bf16[1024,640]{1,0:T(8,128)(2,1)} %copy-done.3, ...), custom_call_target="tpu_custom_call" | custom-call | flops 1073741824 | bytes 8388608 | tf_op jit(solution)/shard_map/context_back/pallas_call | solution.py:188
  282.4 12.0 %attend_back.2 = (bf16[2,1024,384]{2,1,0:T(8,128)(2,1)}, f32[2,2,128]{2,1,0:T(2,128)}) custom-call(s32[2,4]{1,0:T(2,128)} %pad_add_fusion.windows, bf16[4,1024,128]{2,1,0:T(8,128)(2,1)} %get-tuple-element.132.q_ref, bf16[4,1024,128]{2,1,0:T(8,128)(2,1)} %get-tuple-element.122.k_ref, bf16[4,1024,128]{2,1,0:T(8,128)(2,1)} %get-tuple-element.123.v_ref, ...), custom_call_target="tpu_custom_call" | custom-call | flops 10066329600 | bytes 5793792 | tf_op jit(solution)/shard_map/attend_back/pallas_call | solution.py:188
  295.8 2.6 collective-permute-done.42
  298.4 7.6 %weight_grad.4 = (bf16[1024,512]{1,0:T(8,128)(2,1)}, bf16[1024,512]{1,0:T(8,128)(2,1)}) custom-call(bf16[1024,1024]{1,0:T(8,128)(2,1)} %pad_maximum_fusion.x_ref.refs_0_, bf16[1024,1024]{1,0:T(8,128)(2,1)} %pad_maximum_fusion.1.ga_ref.refs_1_, bf16[2,1024,384]{2,1,0:T(8,128)(2,1)} %get-tuple-element.197.refs_2_.refs_1_, ...), custom_call_target="tpu_custom_call" | custom-call | flops 2147483648 | bytes 8388608 | tf_op jit(solution)/shard_map/weight_grad/pallas_call | solution.py:188
  307.6 2.5 add_convert_fusion
  318.4 12.3 %attend_back.3 = (bf16[2,1024,384]{2,1,0:T(8,128)(2,1)}, f32[2,2,128]{2,1,0:T(2,128)}) custom-call(s32[2,4]{1,0:T(2,128)} %pad_add_fusion.windows, bf16[4,1024,128]{2,1,0:T(8,128)(2,1)} %get-tuple-element.132.q_ref, bf16[4,1024,128]{2,1,0:T(8,128)(2,1)} %get-tuple-element.122.k_ref, bf16[4,1024,128]{2,1,0:T(8,128)(2,1)} %get-tuple-element.123.v_ref, ...), custom_call_target="tpu_custom_call" | custom-call | flops 10066329600 | bytes 5793792 | tf_op jit(solution)/shard_map/attend_back/pallas_call | solution.py:188
  330.8 7.3 %weight_grad.5 = (bf16[1024,512]{1,0:T(8,128)(2,1)}, bf16[1024,512]{1,0:T(8,128)(2,1)}) custom-call(bf16[1024,1024]{1,0:T(8,128)(2,1)} %pad_maximum_fusion.x_ref.refs_0_, bf16[1024,1024]{1,0:T(8,128)(2,1)} %pad_maximum_fusion.1.ga_ref.refs_1_, bf16[2,1024,384]{2,1,0:T(8,128)(2,1)} %get-tuple-element.196.refs_2_.refs_0_, ...), custom_call_target="tpu_custom_call" | custom-call | flops 2147483648 | bytes 8388608 | tf_op jit(solution)/shard_map/weight_grad/pallas_call | solution.py:188
  356.1 6.3 %inputs_back.2 = bf16[512,1024]{1,0:T(8,128)(2,1)} custom-call(s32[4]{0:T(128)} %add_add_fusion.1.at_ref, bf16[2,1024,384]{2,1,0:T(8,128)(2,1)} %get-tuple-element.196.refs_2_.refs_0_, bf16[2,1024,384]{2,1,0:T(8,128)(2,1)} %get-tuple-element.197.refs_2_.refs_1_, bf16[1024,384]{1,0:T(8,128)(2,1)} %bitcast.273, bf16[1024,384]{1,0:T(8,128)(2,1)} %bitcast.276, ...), custom_call_target="tpu_custom_call" | custom-call | flops 1610612736 | bytes 7340032 | tf_op jit(solution)/shard_map/inputs_back/pallas_call | solution.py:188
  367.8 6.4 %inputs_back.3 = f32[512,1024]{1,0:T(8,128)} custom-call(s32[4]{0:T(128)} %add_add_fusion.at_ref.at, bf16[2,1024,384]{2,1,0:T(8,128)(2,1)} %get-tuple-element.196.refs_2_.refs_0_, bf16[2,1024,384]{2,1,0:T(8,128)(2,1)} %get-tuple-element.197.refs_2_.refs_1_, bf16[1024,384]{1,0:T(8,128)(2,1)} %bitcast.274, bf16[1024,384]{1,0:T(8,128)(2,1)} %bitcast.277, ...), custom_call_target="tpu_custom_call" | custom-call | flops 1610612736 | bytes 8388608 | tf_op jit(solution)/shard_map/inputs_back/pallas_call | solution.py:188
  379.6 4.2 collective-permute-start.62
  385.5 2.9 collective-permute-start.66
  390.0 3.5 collective-permute-done.63
  394.6 2.7 collective-permute-done.64
  399.2 2.5 collective-permute-start.57
  404.5 6.5 %collective-permute-done.57 = bf16[2,2,1,1,128,512]{4,5,1,3,2,0:T(8,128)(2,1)S(1)} collective-permute-done((bf16[2,2,1,1,128,512]{4,5,1,3,2,0:T(8,128)(2,1)S(1)}, bf16[2,2,1,1,128,512]{4,5,1,3,2,0:T(8,128)(2,1)S(1)}, u32[]{:S(2)}, u32[]{:S(2)}) %collective-permute-start.57) | collective-permute-done | bytes 524320 | tf_op jit(solution)/shard_map/ppermute | solution.py:51
  412.6 2.3 collective-permute-done.52
  416.2 6.3 %collective-permute-done.58 = bf16[2,1,1,1,128,512]{4,5,3,2,1,0:T(8,128)(2,1)S(1)} collective-permute-done((bf16[2,1,1,1,128,512]{4,5,3,2,1,0:T(8,128)(2,1)S(1)}, bf16[2,1,1,1,128,512]{4,5,3,2,1,0:T(8,128)(2,1)S(1)}, u32[]{:S(2)}, u32[]{:S(2)}) %collective-permute-start.58) | collective-permute-done | bytes 262176 | tf_op jit(solution)/shard_map/ppermute | solution.py:51
  (424 shorter events, 151.2 us)
Async XLA Ops:
  2.2 15.9 %collective-permute-start.6 = (bf16[2,128,384]{2,1,0:T(8,128)(2,1)S(1)}, bf16[2,128,384]{2,1,0:T(8,128)(2,1)S(1)}, u32[]{:S(2)}, u32[]{:S(2)}) collective-permute-start(bf16[2,128,384]{2,1,0:T(8,128)(2,1)S(1)} %copy.324.refs_0_), channel_id=1, source_target_pairs={{0,8},{4,12},{8,16},{12,20},{16,24},{20,28},{24,0},{28,4},{1,9},{5... | collective-permute-start | bytes 589832 | tf_op jit(solution)/shard_map/ppermute | solution.py:694
  5.3 12.9 %collective-permute-start.5 = (bf16[2,128,384]{2,1,0:T(8,128)(2,1)S(1)}, bf16[2,128,384]{2,1,0:T(8,128)(2,1)S(1)}, u32[]{:S(2)}, u32[]{:S(2)}) collective-permute-start(bf16[2,128,384]{2,1,0:T(8,128)(2,1)S(1)} %copy.324.refs_0_), channel_id=1, source_target_pairs={{0,24},{4,28},{8,0},{12,4},{16,8},{20,12},{24,16},{28,20},{1,25},{... | collective-permute-start | bytes 589832 | tf_op jit(solution)/shard_map/ppermute | solution.py:694
  16.0 16.4 %collective-permute-start.20 = (bf16[2,1,128,512]{3,2,1,0:T(8,128)(2,1)}, bf16[2,1,128,512]{3,2,1,0:T(8,128)(2,1)}, u32[]{:S(2)}, u32[]{:S(2)}) collective-permute-start(bf16[2,1,128,512]{3,2,1,0:T(8,128)(2,1)} %pad_maximum_fusion.18), channel_id=1, source_target_pairs={{0,2},{1,3},{2,0},{3,1},{4,6},{5,7},{6,4},{7,5},{8,10},{9,11},{10,... | collective-permute-start | bytes 786440 | tf_op jit(solution)/shard_map/ppermute | solution.py:51
  17.5 16.3 %collective-permute-start.21 = (bf16[1,2,128,512]{3,2,1,0:T(8,128)(2,1)S(1)}, bf16[1,2,128,512]{3,2,1,0:T(8,128)(2,1)}, u32[]{:S(2)}, u32[]{:S(2)}) collective-permute-start(bf16[1,2,128,512]{3,2,1,0:T(8,128)(2,1)S(1)} %pad_maximum_fusion.19), channel_id=1, source_target_pairs={{0,4},{4,0},{8,12},{12,8},{16,20},{20,16},{24,28},{28,24},{1,5},{5... | collective-permute-start | bytes 786440 | tf_op jit(solution)/shard_map/ppermute | solution.py:51
  22.1 17.9 %collective-permute-start.2 = (bf16[1024,256]{1,0:T(8,128)(2,1)S(1)}, bf16[1024,256]{1,0:T(8,128)(2,1)}, u32[]{:S(2)}, u32[]{:S(2)}) collective-permute-start(bf16[1024,256]{1,0:T(8,128)(2,1)S(1)} %dynamic-slice_bitcast_fusion.3), channel_id=1, source_target_pairs={{0,2},{1,3},{2,0},{3,1},{4,6},{5,7},{6,4},{7,5},{8,10},{9,11},{10,... | collective-permute-start | bytes 1572872 | tf_op jit(solution)/shard_map/ppermute | solution.py:51
  24.7 13.1 %collective-permute-start.15 = (bf16[2,128,640]{2,1,0:T(8,128)(2,1)S(1)}, bf16[2,128,640]{2,1,0:T(8,128)(2,1)S(1)}, u32[]{:S(2)}, u32[]{:S(2)}) collective-permute-start(bf16[2,128,640]{2,1,0:T(8,128)(2,1)S(1)} %pad_maximum_fusion.17.refs_0_), channel_id=1, source_target_pairs={{0,8},{4,12},{8,16},{12,20},{16,24},{20,28},{24,0},{28,4},{1,9},{5... | collective-permute-start | bytes 983048 | tf_op jit(solution)/shard_map/ppermute | solution.py:694
  26.0 13.1 %collective-permute-start.14 = (bf16[2,128,640]{2,1,0:T(8,128)(2,1)S(1)}, bf16[2,128,640]{2,1,0:T(8,128)(2,1)S(1)}, u32[]{:S(2)}, u32[]{:S(2)}) collective-permute-start(bf16[2,128,640]{2,1,0:T(8,128)(2,1)S(1)} %pad_maximum_fusion.17.refs_0_), channel_id=1, source_target_pairs={{0,24},{4,28},{8,0},{12,4},{16,8},{20,12},{24,16},{28,20},{1,25},{... | collective-permute-start | bytes 983048 | tf_op jit(solution)/shard_map/ppermute | solution.py:694
  32.4 28.9 %collective-permute-start.12 = (bf16[2,2,1,128,384]{4,3,2,1,0:T(8,128)(2,1)}, bf16[2,2,1,128,384]{4,3,2,1,0:T(8,128)(2,1)}, u32[]{:S(2)}, u32[]{:S(2)}) collective-permute-start(bf16[2,2,1,128,384]{4,3,2,1,0:T(8,128)(2,1)} %bitcast.305), channel_id=1, source_target_pairs={{0,2},{1,3},{2,0},{3,1},{4,6},{5,7},{6,4},{7,5},{8,10},{9,11},{10,... | collective-permute-start | bytes 1179656 | tf_op jit(solution)/shard_map/ppermute | solution.py:51
  33.8 28.9 %collective-permute-start.10 = (bf16[2,2,1,128,384]{4,3,2,1,0:T(8,128)(2,1)}, bf16[2,2,1,128,384]{4,3,2,1,0:T(8,128)(2,1)}, u32[]{:S(2)}, u32[]{:S(2)}) collective-permute-start(bf16[2,2,1,128,384]{4,3,2,1,0:T(8,128)(2,1)} %bitcast.306), channel_id=1, source_target_pairs={{0,4},{4,0},{8,12},{12,8},{16,20},{20,16},{24,28},{28,24},{1,5},{5... | collective-permute-start | bytes 1179656 | tf_op jit(solution)/shard_map/ppermute | solution.py:51
  37.8 18.3 %collective-permute-start.9 = (bf16[2,2,1,128,384]{4,3,2,1,0:T(8,128)(2,1)}, bf16[2,2,1,128,384]{4,3,2,1,0:T(8,128)(2,1)}, u32[]{:S(2)}, u32[]{:S(2)}) collective-permute-start(bf16[2,2,1,128,384]{4,3,2,1,0:T(8,128)(2,1)} %bitcast.21), channel_id=1, source_target_pairs={{0,4},{4,0},{8,12},{12,8},{16,20},{20,16},{24,28},{28,24},{1,5},{5... | collective-permute-start | bytes 1179656 | tf_op jit(solution)/shard_map/ppermute | solution.py:51
  39.1 11.3 %collective-permute-start.16 = (bf16[128,640]{1,0:T(8,128)(2,1)}, bf16[128,640]{1,0:T(8,128)(2,1)S(1)}, u32[]{:S(2)}, u32[]{:S(2)}) collective-permute-start(bf16[128,640]{1,0:T(8,128)(2,1)} %slice_bitcast_fusion.7), channel_id=1, source_target_pairs={{0,8},{4,12},{8,16},{12,20},{16,24},{20,28},{24,0},{28,4},{1,9},{5... | collective-permute-start | bytes 491528 | tf_op jit(solution)/shard_map/ppermute | solution.py:694
  50.3 23.5 %collective-permute-start.3 = (bf16[1024,512]{1,0:T(8,128)(2,1)}, bf16[1024,512]{1,0:T(8,128)(2,1)S(1)}, u32[]{:S(2)}, u32[]{:S(2)}) collective-permute-start(bf16[1024,512]{1,0:T(8,128)(2,1)} %pad_maximum_fusion.5), channel_id=1, source_target_pairs={{0,1},{1,0},{2,3},{3,2},{4,5},{5,4},{6,7},{7,6},{8,9},{9,8},{10,11... | collective-permute-start | bytes 3145736 | tf_op jit(solution)/shard_map/ppermute | solution.py:51
  55.5 62.4 %collective-permute-start.22 = (bf16[2,2,2,128,512]{4,3,2,1,0:T(8,128)(2,1)}, bf16[2,2,2,128,512]{4,3,2,1,0:T(8,128)(2,1)}, u32[]{:S(2)}, u32[]{:S(2)}) collective-permute-start(bf16[2,2,2,128,512]{4,3,2,1,0:T(8,128)(2,1)} %pad_maximum_fusion.6.refs_0_), channel_id=1, source_target_pairs={{0,8},{4,12},{8,16},{12,20},{16,24},{20,28},{24,0},{28,4},{1,9},{5... | collective-permute-start | bytes 3145736 | tf_op jit(solution)/shard_map/ppermute | solution.py:694
  56.1 61.8 %collective-permute-start.23 = (bf16[2,2,2,128,512]{4,3,2,1,0:T(8,128)(2,1)}, bf16[2,2,2,128,512]{4,3,2,1,0:T(8,128)(2,1)}, u32[]{:S(2)}, u32[]{:S(2)}) collective-permute-start(bf16[2,2,2,128,512]{4,3,2,1,0:T(8,128)(2,1)} %pad_maximum_fusion.6.refs_0_), channel_id=1, source_target_pairs={{0,24},{4,28},{8,0},{12,4},{16,8},{20,12},{24,16},{28,20},{1,25},{... | collective-permute-start | bytes 3145736 | tf_op jit(solution)/shard_map/ppermute | solution.py:694
  61.3 20.5 %collective-permute-start.11 = (bf16[1024,384]{1,0:T(8,128)(2,1)S(1)}, bf16[1024,384]{1,0:T(8,128)(2,1)S(1)}, u32[]{:S(2)}, u32[]{:S(2)}) collective-permute-start(bf16[1024,384]{1,0:T(8,128)(2,1)S(1)} %bitcast.271), channel_id=1, source_target_pairs={{0,2},{1,3},{2,0},{3,1},{4,6},{5,7},{6,4},{7,5},{8,10},{9,11},{10,... | collective-permute-start | bytes 2359304 | tf_op jit(solution)/shard_map/ppermute | solution.py:51
  71.1 34.0 %collective-permute-start.19 = (bf16[2,2,1,128,640]{4,3,2,1,0:T(8,128)(2,1)S(1)}, bf16[2,2,1,128,640]{4,3,2,1,0:T(8,128)(2,1)}, u32[]{:S(2)}, u32[]{:S(2)}) collective-permute-start(bf16[2,2,1,128,640]{4,3,2,1,0:T(8,128)(2,1)S(1)} %bitcast.300), channel_id=1, source_target_pairs={{0,2},{1,3},{2,0},{3,1},{4,6},{5,7},{6,4},{7,5},{8,10},{9,11},{10,... | collective-permute-start | bytes 1966088 | tf_op jit(solution)/shard_map/ppermute | solution.py:51
  73.8 30.0 %collective-permute-start.24 = (bf16[2,2,1,128,640]{4,3,2,1,0:T(8,128)(2,1)S(1)}, bf16[2,2,1,128,640]{4,3,2,1,0:T(8,128)(2,1)}, u32[]{:S(2)}, u32[]{:S(2)}) collective-permute-start(bf16[2,2,1,128,640]{4,3,2,1,0:T(8,128)(2,1)S(1)} %bitcast.301), channel_id=1, source_target_pairs={{0,4},{4,0},{8,12},{12,8},{16,20},{20,16},{24,28},{28,24},{1,5},{5... | collective-permute-start | bytes 1966088 | tf_op jit(solution)/shard_map/ppermute | solution.py:51
  81.7 20.3 %collective-permute-start.18 = (bf16[2,2,1,128,640]{4,3,2,1,0:T(8,128)(2,1)S(1)}, bf16[2,2,1,128,640]{4,3,2,1,0:T(8,128)(2,1)S(1)}, u32[]{:S(2)}, u32[]{:S(2)}) collective-permute-start(bf16[2,2,1,128,640]{4,3,2,1,0:T(8,128)(2,1)S(1)} %bitcast.303), channel_id=1, source_target_pairs={{0,4},{4,0},{8,12},{12,8},{16,20},{20,16},{24,28},{28,24},{1,5},{5... | collective-permute-start | bytes 1966088 | tf_op jit(solution)/shard_map/ppermute | solution.py:51
  102.3 24.7 %collective-permute-start.25 = (bf16[1024,640]{1,0:T(8,128)(2,1)S(1)}, bf16[1024,640]{1,0:T(8,128)(2,1)S(1)}, u32[]{:S(2)}, u32[]{:S(2)}) collective-permute-start(bf16[1024,640]{1,0:T(8,128)(2,1)S(1)} %bitcast.249), channel_id=1, source_target_pairs={{0,2},{1,3},{2,0},{3,1},{4,6},{5,7},{6,4},{7,5},{8,10},{9,11},{10,... | collective-permute-start | bytes 3932168 | tf_op jit(solution)/shard_map/ppermute | solution.py:51
  105.0 12.8 %collective-permute-start.26 = (bf16[2,2,1,128,640]{4,3,2,1,0:T(8,128)(2,1)}, bf16[2,2,1,128,640]{4,3,2,1,0:T(8,128)(2,1)S(1)}, u32[]{:S(2)}, u32[]{:S(2)}) collective-permute-start(bf16[2,2,1,128,640]{4,3,2,1,0:T(8,128)(2,1)} %collective-permute-done.19), channel_id=1, source_target_pairs={{0,4},{4,0},{8,12},{12,8},{16,20},{20,16},{24,28},{28,24},{1,5},{5... | collective-permute-start | bytes 1966088 | tf_op jit(solution)/shard_map/ppermute | solution.py:51
  136.5 32.6 %collective-permute-start.33 = (bf16[1024,256]{1,0:T(8,128)(2,1)}, bf16[1024,256]{1,0:T(8,128)(2,1)}, u32[]{:S(2)}, u32[]{:S(2)}) collective-permute-start(bf16[1024,256]{1,0:T(8,128)(2,1)} %dynamic-slice_bitcast_fusion.2), channel_id=1, source_target_pairs={{0,2},{1,3},{2,0},{3,1},{4,6},{5,7},{6,4},{7,5},{8,10},{9,11},{10,... | collective-permute-start | bytes 1572872 | tf_op jit(solution)/shard_map/ppermute | solution.py:51
  147.4 13.6 %collective-permute-start.29 = (bf16[512,1024]{1,0:T(8,128)(2,1)}, bf16[512,1024]{1,0:T(8,128)(2,1)}, u32[]{:S(2)}, u32[]{:S(2)}) collective-permute-start(bf16[512,1024]{1,0:T(8,128)(2,1)} %get-tuple-element.141.y_ref.refs_0_), channel_id=1, source_target_pairs={{0,1},{1,0},{2,3},{3,2},{4,5},{5,4},{6,7},{7,6},{8,9},{9,8},{10,11... | collective-permute-start | bytes 3145736 | tf_op jit(solution)/shard_map/ppermute | solution.py:51
  148.5 25.6 %collective-permute-start.31 = (bf16[2,2,128,512]{3,2,1,0:T(8,128)(2,1)S(1)}, bf16[2,2,128,512]{3,2,1,0:T(8,128)(2,1)S(1)}, u32[]{:S(2)}, u32[]{:S(2)}) collective-permute-start(bf16[2,2,128,512]{3,2,1,0:T(8,128)(2,1)S(1)} %slice_bitcast_fusion.2), channel_id=1, source_target_pairs={{0,24},{4,28},{8,0},{12,4},{16,8},{20,12},{24,16},{28,20},{1,25},{... | collective-permute-start | bytes 1572872 | tf_op jit(solution)/shard_map/ppermute | solution.py:694
  150.4 25.1 %collective-permute-start.30 = (bf16[2,2,128,512]{3,2,1,0:T(8,128)(2,1)}, bf16[2,2,128,512]{3,2,1,0:T(8,128)(2,1)S(1)}, u32[]{:S(2)}, u32[]{:S(2)}) collective-permute-start(bf16[2,2,128,512]{3,2,1,0:T(8,128)(2,1)} %slice_bitcast_fusion.3), channel_id=1, source_target_pairs={{0,8},{4,12},{8,16},{12,20},{16,24},{20,28},{24,0},{28,4},{1,9},{5... | collective-permute-start | bytes 1572872 | tf_op jit(solution)/shard_map/ppermute | solution.py:694
  218.3 27.3 %collective-permute-start.40 = (bf16[2,128,1024]{2,1,0:T(8,128)(2,1)}, bf16[2,128,1024]{2,1,0:T(8,128)(2,1)}, u32[]{:S(2)}, u32[]{:S(2)}) collective-permute-start(bf16[2,128,1024]{2,1,0:T(8,128)(2,1)} %get-tuple-element.356), channel_id=1, source_target_pairs={{0,24},{4,28},{8,0},{12,4},{16,8},{20,12},{24,16},{28,20},{1,25},{... | collective-permute-start | bytes 1572872 | tf_op jit(solution)/shard_map/ppermute | solution.py:694
  219.0 31.4 %collective-permute-start.39 = (bf16[2,128,1024]{2,1,0:T(8,128)(2,1)}, bf16[2,128,1024]{2,1,0:T(8,128)(2,1)S(1)}, u32[]{:S(2)}, u32[]{:S(2)}) collective-permute-start(bf16[2,128,1024]{2,1,0:T(8,128)(2,1)} %get-tuple-element.357), channel_id=1, source_target_pairs={{0,8},{4,12},{8,16},{12,20},{16,24},{20,28},{24,0},{28,4},{1,9},{5... | collective-permute-start | bytes 1572872 | tf_op jit(solution)/shard_map/ppermute | solution.py:694
  243.0 17.4 %collective-permute-start.38 = (bf16[512,1024]{1,0:T(8,128)(2,1)}, bf16[512,1024]{1,0:T(8,128)(2,1)}, u32[]{:S(2)}, u32[]{:S(2)}) collective-permute-start(bf16[512,1024]{1,0:T(8,128)(2,1)} %get-tuple-element.167), channel_id=1, source_target_pairs={{0,1},{1,0},{2,3},{3,2},{4,5},{5,4},{6,7},{7,6},{8,9},{9,8},{10,11... | collective-permute-start | bytes 3145736 | tf_op jit(solution)/shard_map/ppermute | solution.py:51
  244.9 14.1 %collective-permute-start.36 = (bf16[512,512]{1,0:T(8,128)(2,1)}, bf16[512,512]{1,0:T(8,128)(2,1)}, u32[]{:S(2)}, u32[]{:S(2)}) collective-permute-start(bf16[512,512]{1,0:T(8,128)(2,1)} %constant_dynamic-slice_fusion.17), channel_id=1, source_target_pairs={{0,2},{1,3},{2,0},{3,1},{4,6},{5,7},{6,4},{7,5},{8,10},{9,11},{10,... | collective-permute-start | bytes 1572872 | tf_op jit(solution)/shard_map/ppermute | solution.py:51
  247.9 46.9 %collective-permute-start.46 = (bf16[2,2,128,1024]{3,2,1,0:T(8,128)(2,1)}, bf16[2,2,128,1024]{3,2,1,0:T(8,128)(2,1)}, u32[]{:S(2)}, u32[]{:S(2)}) collective-permute-start(bf16[2,2,128,1024]{3,2,1,0:T(8,128)(2,1)} %pad_maximum_fusion.11), channel_id=1, source_target_pairs={{0,24},{4,28},{8,0},{12,4},{16,8},{20,12},{24,16},{28,20},{1,25},{... | collective-permute-start | bytes 3145736 | tf_op jit(solution)/shard_map/ppermute | solution.py:694
  267.7 28.1 %collective-permute-start.45 = (bf16[2,2,128,1024]{3,2,1,0:T(8,128)(2,1)}, bf16[2,2,128,1024]{3,2,1,0:T(8,128)(2,1)}, u32[]{:S(2)}, u32[]{:S(2)}) collective-permute-start(bf16[2,2,128,1024]{3,2,1,0:T(8,128)(2,1)} %pad_maximum_fusion.10), channel_id=1, source_target_pairs={{0,8},{4,12},{8,16},{12,20},{16,24},{20,28},{24,0},{28,4},{1,9},{5... | collective-permute-start | bytes 3145736 | tf_op jit(solution)/shard_map/ppermute | solution.py:694
  269.5 24.9 %collective-permute-start.43 = (bf16[2,2,1,128,512]{4,3,0,2,1:T(8,128)(2,1)}, bf16[2,2,1,128,512]{4,3,0,2,1:T(8,128)(2,1)}, u32[]{:S(2)}, u32[]{:S(2)}) collective-permute-start(bf16[2,2,1,128,512]{4,3,0,2,1:T(8,128)(2,1)} %copy.368), channel_id=1, source_target_pairs={{0,4},{4,0},{8,12},{12,8},{16,20},{20,16},{24,28},{28,24},{1,5},{5... | collective-permute-start | bytes 1572872 | tf_op jit(solution)/shard_map/ppermute | solution.py:51
  272.0 22.9 %collective-permute-start.44 = (bf16[2,2,1,128,512]{4,3,0,2,1:T(8,128)(2,1)}, bf16[2,2,1,128,512]{4,3,0,2,1:T(8,128)(2,1)S(1)}, u32[]{:S(2)}, u32[]{:S(2)}) collective-permute-start(bf16[2,2,1,128,512]{4,3,0,2,1:T(8,128)(2,1)} %copy.369), channel_id=1, source_target_pairs={{0,4},{4,0},{8,12},{12,8},{16,20},{20,16},{24,28},{28,24},{1,5},{5... | collective-permute-start | bytes 1572872 | tf_op jit(solution)/shard_map/ppermute | solution.py:51
  273.7 24.8 %collective-permute-start.42 = (bf16[1024,512]{1,0:T(8,128)(2,1)}, bf16[1024,512]{1,0:T(8,128)(2,1)S(1)}, u32[]{:S(2)}, u32[]{:S(2)}) collective-permute-start(bf16[1024,512]{1,0:T(8,128)(2,1)} %get-tuple-element.179), channel_id=1, source_target_pairs={{0,2},{1,3},{2,0},{3,1},{4,6},{5,7},{6,4},{7,5},{8,10},{9,11},{10,... | collective-permute-start | bytes 3145736 | tf_op jit(solution)/shard_map/ppermute | solution.py:51
  306.1 58.5 %collective-permute-start.49 = (bf16[1024,512]{1,0:T(8,128)(2,1)}, bf16[1024,512]{1,0:T(8,128)(2,1)}, u32[]{:S(2)}, u32[]{:S(2)}) collective-permute-start(bf16[1024,512]{1,0:T(8,128)(2,1)} %get-tuple-element.187), channel_id=1, source_target_pairs={{0,2},{1,3},{2,0},{3,1},{4,6},{5,7},{6,4},{7,5},{8,10},{9,11},{10,... | collective-permute-start | bytes 3145736 | tf_op jit(solution)/shard_map/ppermute | solution.py:51
  310.9 33.9 %collective-permute-start.67 = (bf16[1,2,128,1024]{3,2,1,0:T(8,128)(2,1)}, bf16[1,2,128,1024]{3,2,1,0:T(8,128)(2,1)}, u32[]{:S(2)}, u32[]{:S(2)}) collective-permute-start(bf16[1,2,128,1024]{3,2,1,0:T(8,128)(2,1)} %constant_dynamic-slice_fusion.1), channel_id=1, source_target_pairs={{0,4},{4,0},{8,12},{12,8},{16,20},{20,16},{24,28},{28,24},{1,5},{5... | collective-permute-start | bytes 1572872 | tf_op jit(solution)/shard_map/ppermute | solution.py:51
  313.6 34.7 %collective-permute-start.47 = (bf16[2,2,1,128,512]{4,3,2,1,0:T(8,128)(2,1)}, bf16[2,2,1,128,512]{4,3,2,1,0:T(8,128)(2,1)}, u32[]{:S(2)}, u32[]{:S(2)}) collective-permute-start(bf16[2,2,1,128,512]{4,3,2,1,0:T(8,128)(2,1)} %constant_dynamic-slice_fusion.14), channel_id=1, source_target_pairs={{0,4},{4,0},{8,12},{12,8},{16,20},{20,16},{24,28},{28,24},{1,5},{5... | collective-permute-start | bytes 1572872 | tf_op jit(solution)/shard_map/ppermute | solution.py:51
  315.0 33.5 %collective-permute-start.48 = (bf16[2,2,1,128,512]{4,3,0,2,1:T(8,128)(2,1)}, bf16[2,2,1,128,512]{4,3,0,2,1:T(8,128)(2,1)}, u32[]{:S(2)}, u32[]{:S(2)}) collective-permute-start(bf16[2,2,1,128,512]{4,3,0,2,1:T(8,128)(2,1)} %add_convert_fusion.12), channel_id=1, source_target_pairs={{0,2},{1,3},{2,0},{3,1},{4,6},{5,7},{6,4},{7,5},{8,10},{9,11},{10,... | collective-permute-start | bytes 1572872 | tf_op jit(solution)/shard_map/ppermute | solution.py:51
  316.7 36.2 %collective-permute-start.55 = (bf16[2,2,1,128,512]{3,4,0,2,1:T(8,128)(2,1)}, bf16[2,2,1,128,512]{3,4,0,2,1:T(8,128)(2,1)}, u32[]{:S(2)}, u32[]{:S(2)}) collective-permute-start(bf16[2,2,1,128,512]{3,4,0,2,1:T(8,128)(2,1)} %copy.376), channel_id=1, source_target_pairs={{0,4},{4,0},{8,12},{12,8},{16,20},{20,16},{24,28},{28,24},{1,5},{5... | collective-permute-start | bytes 1572872 | tf_op jit(solution)/shard_map/ppermute | solution.py:51
  344.8 43.6 %collective-permute-start.54 = (bf16[2,2,1,128,512]{3,4,0,2,1:T(8,128)(2,1)}, bf16[2,2,1,128,512]{3,4,0,2,1:T(8,128)(2,1)}, u32[]{:S(2)}, u32[]{:S(2)}) collective-permute-start(bf16[2,2,1,128,512]{3,4,0,2,1:T(8,128)(2,1)} %copy.374), channel_id=1, source_target_pairs={{0,4},{4,0},{8,12},{12,8},{16,20},{20,16},{24,28},{28,24},{1,5},{5... | collective-permute-start | bytes 1572872 | tf_op jit(solution)/shard_map/ppermute | solution.py:51
  348.3 14.1 %collective-permute-start.68 = (bf16[1,1,128,1024]{3,2,1,0:T(8,128)(2,1)S(1)}, bf16[1,1,128,1024]{3,2,1,0:T(8,128)(2,1)}, u32[]{:S(2)}, u32[]{:S(2)}) collective-permute-start(bf16[1,1,128,1024]{3,2,1,0:T(8,128)(2,1)S(1)} %constant_dynamic-slice_fusion), channel_id=1, source_target_pairs={{0,2},{1,3},{2,0},{3,1},{4,6},{5,7},{6,4},{7,5},{8,10},{9,11},{10,... | collective-permute-start | bytes 786440 | tf_op jit(solution)/shard_map/ppermute | solution.py:51
  352.2 21.9 %collective-permute-start.65 = (bf16[2,2,1,1,128,512]{5,4,1,3,2,0:T(8,128)(2,1)}, bf16[2,2,1,1,128,512]{5,4,1,3,2,0:T(8,128)(2,1)}, u32[]{:S(2)}, u32[]{:S(2)}) collective-permute-start(bf16[2,2,1,1,128,512]{5,4,1,3,2,0:T(8,128)(2,1)} %pad_maximum_fusion.16), channel_id=1, source_target_pairs={{0,8},{4,12},{8,0},{12,4},{16,24},{20,28},{24,16},{28,20},{1,9},{5... | collective-permute-start | bytes 1572872 | tf_op jit(solution)/shard_map/ppermute | solution.py:51
  355.0 33.5 %collective-permute-start.56 = (bf16[2,2,1,128,512]{3,4,0,2,1:T(8,128)(2,1)}, bf16[2,2,1,128,512]{3,4,0,2,1:T(8,128)(2,1)}, u32[]{:S(2)}, u32[]{:S(2)}) collective-permute-start(bf16[2,2,1,128,512]{3,4,0,2,1:T(8,128)(2,1)} %add_convert_fusion.9), channel_id=1, source_target_pairs={{0,2},{1,3},{2,0},{3,1},{4,6},{5,7},{6,4},{7,5},{8,10},{9,11},{10,... | collective-permute-start | bytes 1572872 | tf_op jit(solution)/shard_map/ppermute | solution.py:51
  362.4 39.4 %collective-permute-start.51 = (bf16[512,1024]{1,0:T(8,128)(2,1)}, bf16[512,1024]{1,0:T(8,128)(2,1)}, u32[]{:S(2)}, u32[]{:S(2)}) collective-permute-start(bf16[512,1024]{1,0:T(8,128)(2,1)} %inputs_back.2), channel_id=1, source_target_pairs={{0,1},{1,0},{2,3},{3,2},{4,5},{5,4},{6,7},{7,6},{8,9},{9,8},{10,11... | collective-permute-start | bytes 3145736 | tf_op jit(solution)/shard_map/ppermute | solution.py:51
  366.8 11.2 %collective-permute-start.59 = (f32[1536]{0:T(1024)S(1)}, f32[1536]{0:T(1024)S(1)}, u32[]{:S(2)}, u32[]{:S(2)}) collective-permute-start(f32[1536]{0:T(1024)S(1)} %pad_maximum_fusion.26), channel_id=1, source_target_pairs={{0,2},{1,3},{2,0},{3,1},{4,6},{5,7},{6,4},{7,5},{8,10},{9,11},{10,... | collective-permute-start | bytes 18440 | tf_op jit(solution)/shard_map/ppermute | solution.py:51
  378.0 21.0 %collective-permute-start.50 = (bf16[2,2,1,128,512]{3,4,2,1,0:T(8,128)(2,1)S(1)}, bf16[2,2,1,128,512]{3,4,2,1,0:T(8,128)(2,1)S(1)}, u32[]{:S(2)}, u32[]{:S(2)}) collective-permute-start(bf16[2,2,1,128,512]{3,4,2,1,0:T(8,128)(2,1)S(1)} %copy.371), channel_id=1, source_target_pairs={{0,4},{4,0},{8,12},{12,8},{16,20},{20,16},{24,28},{28,24},{1,5},{5... | collective-permute-start | bytes 1572872 | tf_op jit(solution)/shard_map/ppermute | solution.py:51
  385.5 16.3 %collective-permute-start.66 = (bf16[2,1,1,1,128,512]{5,4,3,2,1,0:T(8,128)(2,1)S(1)}, bf16[2,1,1,1,128,512]{5,4,3,2,1,0:T(8,128)(2,1)S(1)}, u32[]{:S(2)}, u32[]{:S(2)}) collective-permute-start(bf16[2,1,1,1,128,512]{5,4,3,2,1,0:T(8,128)(2,1)S(1)} %pad_maximum_fusion.21), channel_id=1, source_target_pairs={{0,16},{4,20},{8,24},{12,28},{16,0},{20,4},{24,8},{28,12},{1,17},{... | collective-permute-start | bytes 786440 | tf_op jit(solution)/shard_map/ppermute | solution.py:51
  399.2 11.7 %collective-permute-start.57 = (bf16[2,2,1,1,128,512]{4,5,1,3,2,0:T(8,128)(2,1)S(1)}, bf16[2,2,1,1,128,512]{4,5,1,3,2,0:T(8,128)(2,1)S(1)}, u32[]{:S(2)}, u32[]{:S(2)}) collective-permute-start(bf16[2,2,1,1,128,512]{4,5,1,3,2,0:T(8,128)(2,1)S(1)} %pad_maximum_fusion.15), channel_id=1, source_target_pairs={{0,8},{4,12},{8,0},{12,4},{16,24},{20,28},{24,16},{28,20},{1,9},{5... | collective-permute-start | bytes 1572872 | tf_op jit(solution)/shard_map/ppermute | solution.py:51
  411.2 11.3 %collective-permute-start.58 = (bf16[2,1,1,1,128,512]{4,5,3,2,1,0:T(8,128)(2,1)S(1)}, bf16[2,1,1,1,128,512]{4,5,3,2,1,0:T(8,128)(2,1)S(1)}, u32[]{:S(2)}, u32[]{:S(2)}) collective-permute-start(bf16[2,1,1,1,128,512]{4,5,3,2,1,0:T(8,128)(2,1)S(1)} %pad_maximum_fusion.20), channel_id=1, source_target_pairs={{0,16},{4,20},{8,24},{12,28},{16,0},{20,4},{24,8},{28,12},{1,17},{... | collective-permute-start | bytes 786440 | tf_op jit(solution)/shard_map/ppermute | solution.py:51
  (81 other events, 522.2 us)

commit v6 on v5

--- a/solution.py
+++ b/solution.py
@@ -231,6 +231,10 @@
     return min(256, length)
 
 
+def product_tile(length):
+    return min(512, length)
+
+
 def tall(a, tile):
     if len(a.shape) == 2:
         return pl.BlockSpec((tile, a.shape[1]), lambda i, *_: (i, 0))
@@ -328,7 +332,7 @@
 
 
 def context_back(at, ga, weights, lanes):
-    tile = row_tile(ga.shape[0])
+    tile = product_tile(ga.shape[0])
     count = len(weights)
     out = struct((count, ga.shape[0], lanes), BF16)
     return launch(
@@ -522,15 +526,23 @@
             transpose_into(left_t, refs[:parts])
 
         for k in range(ring):
-            first = pl.multiple_of(((at_ref[1 + seqs] + k) % ring) * block, block)
-            made = nn(left_t[pl.ds(first, block), :], right_ref[0]).astype(BF16)
-            outs[k][:, 0] = made.reshape(near, own, wide)
+            first = pl.multiple_of(((at_ref[1 + seqs] + k + ring // 2) % ring) * block, block)
+            made = nn(left_t[pl.ds(first, block), :], right_ref[0]).astype(BF16).reshape(near, own, wide)
+            if k == 0:
+                for n in range(near):
+                    outs[n][0] = made[n]
+            else:
+                outs[near - 1 + k][:, 0] = made
 
     spec = pl.BlockSpec((near, 1, own, wide), lambda i, at: (0, at[1 + i // halves], 0, i % halves))
-    return launch(
-        kernel, count, [at], list(lefts) + [right], [fixed(a) for a in lefts] + [slab(right)], [out] * ring,
-        [spec] * ring, [pltpu.VMEM((model, length), BF16)], 2 * length * model * wide * count, "weight_grad_shards",
-    )
+    lone = pl.BlockSpec((1, own, wide), lambda i, at: (at[1 + i // halves], 0, i % halves))
+    shape = struct(out.shape[1:], BF16)
+    made = launch(
+        kernel, count, [at], list(lefts) + [right], [fixed(a) for a in lefts] + [slab(right)],
+        [shape] * near + [out] * (ring - 1), [lone] * near + [spec] * (ring - 1), [pltpu.VMEM((model, length), BF16)], 2 * length * model * wide * count, "weight_grad_shards",
+    )
+    arrays_of = [list(made[:near])] + list(made[near:])
+    return arrays_of[ring // 2 :] + arrays_of[: ring // 2]
 
 
 def assemble(place, pieces):
@@ -558,6 +570,26 @@
     return launch(
         kernel, 1, [place], operands, [anywhere] * len(operands), [out] * 2, [fixed(out)] * 2,
         [pltpu.SemaphoreType.DMA((2 * ring,))], 0, "assemble",
+    )
+
+
+def last_grads(halves, lanes):
+    own = halves[0][0].shape[0]
+    outs = [struct((own, 6 * lanes), F32), struct((2 * lanes, own), F32)]
+    operands = [a for pair in halves for a in pair]
+
+    def kernel(*refs):
+        qkv_ref, wo_ref = refs[-2:]
+        for h in range(2):
+            total = (refs[2 * h][...].astype(F32) + refs[2 * h + 1][...].astype(F32)).astype(BF16).astype(F32)
+            for n in range(lanes // DH):
+                for kind in range(3):
+                    to, start = (h * lanes // DH + n) * 3 * DH + kind * DH, kind * lanes + n * DH
+                    qkv_ref[:, to : to + DH] = total[:, start : start + DH]
+            wo_ref[h * lanes : (h + 1) * lanes, :] = total[:, 3 * lanes :].T
+
+    return launch(
+        kernel, 1, [], operands, [fixed(a) for a in operands], outs, [fixed(a) for a in outs], [], 0, "last_grads",
     )
 
 
@@ -911,11 +943,13 @@
             blocks = [add(blocks[j], stage.trade(blocks[count + j])) for j in range(count)]
         return blocks[0]
 
-    def scatter_far(one, two, marks=()):
+    def scatter_far(one, two, marks=(), split=False):
         for n, (i, stage) in enumerate(reversed(list(enumerate(outer)))):
             halves = (one, two)
             sent = jnp.stack([pick(b, 1 - stage.bit, i) for b in halves])
             got = held(stage.trade(sent), marks[n] if n < len(marks) else ())
+            if split and n == len(outer) - 1:
+                return [(pick(b, stage.bit, i).reshape(own_rows, -1), got[h].reshape(own_rows, -1)) for h, b in enumerate(halves)]
             one, two = [add(pick(b, stage.bit, i), got[h]) for h, b in enumerate(halves)]
         return one.reshape(own_rows, -1).astype(F32), two.reshape(own_rows, -1).astype(F32)
 
@@ -1000,28 +1034,38 @@
     for stage in reversed(by_seq):
         out_sum = stage.reduce(after(out_sum, ready), 1)
     halves_in = fold_end(one_in[0], held(one_in[1], (ready,))), across_end(two_in[0], [held(g, (ready,)) for g in two_in[1]])
-    ones_mine, ones_got = across_start([made[j][0] for j in range(seqs)])
-    twos_last = [fold_start(made[j][1]) for j in range(seqs)]
-    gots = ones_got + [g for _, g in twos_last]
-    stacks = [after(stacks[j], ready, *later) for j in range(seqs)]
-    term = {1: inputs_back(at[1], stacks, qkv_all, part, BF16)} if ways == 2 else {}
-    tied = [after(a, *gots[:1], *term.values()) for a in stacks]
-    mine, got = scatter_parts(
-        lambda p, dtype: term[p] if p in term else inputs_back(at[p], tied, qkv_all, part, dtype)
-    )
-    ones_got, twos_got = [held(g, tuple(term.values())) for g in ones_got], [g for _, g in twos_last]
-    one_last = fold_start(across_end(ones_mine, ones_got))
-    two_last = across_start([fold_end(b, g) for (b, _), g in zip(twos_last, twos_got)])
-    in_halves = scatter_far(*halves_in, [(mine,)])
-    grad_tokens = to_features((after(mine, one_last[1]) + got.astype(F32) + grad_a).astype(BF16)).astype(F32)
-    qkv_halves = scatter_far(fold_end(*one_last), across_end(*two_last))
 
     per_hidden = []
     for j in range(seqs):
         two = sum_projected[2 * j : 2 * j + 2].reshape(2, 2, heads // 2, DH).transpose(0, 2, 1, 3)
-        per_hidden.append(jnp.concatenate((two.reshape(-1), sum_in[2 * j : 2 * j + 2].reshape(-1))))
-    block = after(jnp.concatenate((sums_a, sums_b), axis=0), one_last[0])
-    per_hidden = [after(v, one_last[0]) for v in per_hidden]
+        per_hidden += [two.reshape(-1), sum_in[2 * j : 2 * j + 2].reshape(-1)]
+    small = jnp.concatenate([sums_a.reshape(-1), sums_b.reshape(-1)] + per_hidden)
+    for stage in outer:
+        small = small + stage.trade(small)
+
+    ones_mine, ones_got = across_start([made[j][0] for j in range(seqs)])
+    twos_last = [fold_start(made[j][1]) for j in range(seqs)]
+    ones_got = [held(g, (ready,)) for g in ones_got]
+    one_last = fold_start(across_end(ones_mine, ones_got))
+    stacks = [after(stacks[j], ready, *later, one_last[0], small) for j in range(seqs)]
+    term = {1: inputs_back(at[1], stacks, qkv_all, part, BF16)} if ways == 2 else {}
+    small = held(small, tuple(term.values()))
+    small_got = near.trade(small)
+    twos_got = [held(g, tuple(term.values())) for _, g in twos_last]
+    two_last = across_start([fold_end(b, g) for (b, _), g in zip(twos_last, twos_got)])
+    tied = [after(a, *twos_got, *term.values()) for a in stacks]
+    mine, got = scatter_parts(
+        lambda p, dtype: term[p] if p in term else inputs_back(at[p], tied, qkv_all, part, dtype)
+    )
+    in_halves = scatter_far(*halves_in, [tuple(term.values())])
+    mine = after(mine, one_last[1], *two_last[1], *in_halves, small_got)
+    grad_tokens = to_features((mine + got.astype(F32) + grad_a).astype(BF16)).astype(F32)
+    halves_last = fold_end(*one_last), across_end(*two_last)
+    finals = scatter_far(*halves_last, split=True)
+    grad_qkv, grad_wo = last_grads(finals, lanes)
+    small = after(small, *halves_last) + small_got
+    block = small[: 6 * model].reshape(6, model)
+    per_hidden = list(small[6 * model :].reshape(seqs, -1))
     for stage in by_seq + by_way:
         half = block.shape[1] // 2
         got = stage.trade(lax.dynamic_slice_in_dim(block, (1 - stage.bit) * half, half, 1))
@@ -1030,20 +1074,16 @@
         count = len(per_hidden) // 2
         per_hidden = [per_hidden[j] + stage.trade(per_hidden[count + j]) for j in range(count)]
     sums = jnp.concatenate((per_hidden[0], block.reshape(-1)))
-    for stage in by_row:
-        sums = sums + stage.trade(sums)
+
     nqv = bias_qv.shape[0]
     sum_qv, sum_in = sums[:nqv], sums[nqv : nqv + hid]
     rest = sums[nqv + hid :].reshape(6, width)
-    split = 3 * lanes
-    grad_qkv = jnp.stack([h[:, :split] for h in qkv_halves])
-    grad_qkv = grad_qkv.reshape(2, own_rows, 3, heads // 2, DH).transpose(1, 0, 3, 2, 4)
     return (
         output,
         grad_tokens,
-        grad_qkv.reshape(own_rows, -1),
+        grad_qkv,
         sum_qv,
-        jnp.concatenate([h[:, split:] for h in qkv_halves], axis=1).T,
+        grad_wo,
         rest[0],
         rest[1],
         rest[2],

time: 432 us -> 429 us (level)
  waiting for transfers between devices: 59.4 us -> 53.5 us
  other arithmetic: 55.3 us -> 60.4 us
    unnamed x131 -> x124, local copies, waits for them, and re-layouts: 19.4 us -> 15 us
    pallas_call x26 -> x27, Pallas kernels: 189 us -> 190 us  [launch(): pl.pallas_call(kernel, grid_spec=pltpu.PrefetchScalarGridSpec(num_scalar_...]
  transfers between devices with their start and end apart: 69 -> 69, of which waited for: 22 -> 21; matrix products, arithmetic and copies ran while one was open for 19% -> 20% of each run, Pallas kernels for 36% -> 36%
where the time goes in v6:
time: 429 us; the launch traced here: 423 us
  Pallas kernels  190 us (44%)
  starting transfers between devices  79.8 us (19%)
  other arithmetic  60.4 us (14%)
  waiting for transfers between devices  53.5 us (12%)
  local copies, waits for them, and re-layouts  36.9 us (9%)
    pallas_call x27, Pallas kernels, launch(): pl.pallas_call(kernel, grid_spec=pltpu.PrefetchScalarGridSpec(num_scalar_...  190 us
    ppermute x53, starting transfers between devices, trade(): return lax.ppermute(block, self.axis, self.pairs)  50.8 us
    ppermute x53, waiting for transfers between devices, trade(): return lax.ppermute(block, self.axis, self.pairs)  45.8 us
    ppermute x16, starting transfers between devices, turn(): lax.ppermute(block, 'row', [(i, (i + 2 * step) % rows) for i in range(row...  28.9 us
    convert_element_type x13, other arithmetic, add(): return (mine.astype(F32) + other.astype(F32)).astype(mine.dtype)  15.2 us
    unnamed x124, local copies, waits for them, and re-layouts  15 us
  transfers between devices with their start and end apart: 69, of which 21 were waited for; matrix products, arithmetic and copies ran while one was open for 20% of the time, Pallas kernels for 36%

profile of v6, /device:TPU:0, one launch (start us, length us, event | category | flops | bytes accessed | tf_op | source)
XLA Modules:
  0.0 422.7 jit_solution(16787647066137104600)
XLA Ops:
  2.2 3.1 collective-permute-start.6
  5.3 2.1 collective-permute-start.5
  18.2 3.8 collective-permute-start.8
  25.3 4.3 %collective-permute-start.14 = (bf16[2,128,640]{2,1,0:T(8,128)(2,1)S(1)}, bf16[2,128,640]{2,1,0:T(8,128)(2,1)S(1)}, u32[]{:S(2)}, u32[]{:S(2)}) collective-permute-start(bf16[2,128,640]{2,1,0:T(8,128)(2,1)S(1)} %pad_maximum_fusion.18.refs_0_), channel_id=1, source_target_pairs={{0,24},{4,28},{8,0},{12,4},{16,8},{20,12},{24,16},{28,20},{1,25},{... | collective-permute-start | bytes 983048 | tf_op jit(solution)/shard_map/ppermute | solution.py:726
  29.5 2.2 assemble.3
  43.2 2.6 collective-permute-done.4
  45.8 3.2 collective-permute-start.17
  52.6 2.5 assemble.4
  56.0 3.5 collective-permute-start.23
  65.6 4.6 %collective-permute-done.13 = bf16[2,2,1,128,384]{4,3,2,1,0:T(8,128)(2,1)S(1)} collective-permute-done((bf16[2,2,1,128,384]{4,3,2,1,0:T(8,128)(2,1)}, bf16[2,2,1,128,384]{4,3,2,1,0:T(8,128)(2,1)S(1)}, u32[]{:S(2)}, u32[]{:S(2)}) %collective-permute-start.13) | collective-permute-done | bytes 393248 | tf_op jit(solution)/shard_map/ppermute | solution.py:51
  77.7 3.5 collective-permute-done.11.refs_2_.refs_4_
  82.7 8.4 %project.1 = (bf16[4,1024,128]{2,1,0:T(8,128)(2,1)}, bf16[4,1024,128]{2,1,0:T(8,128)(2,1)}, bf16[4,1024,128]{2,1,0:T(8,128)(2,1)}) custom-call(bf16[1024,1024]{1,0:T(8,128)(2,1)} %pad_maximum_fusion.x_ref.refs_0_, f32[4,1,384]{2,1,0:T(1,128)} %reshape.535.b_ref, bf16[1024,384]{1,0:T(8,128)(2,1)} %bitcast.258, bf16[1024,384]{1,0:T(8,128)(2,1)} %bitcast.261, ...), custom_call_target="tpu_custom_call" | custom-call | flops 3221225472 | bytes 8394752 | tf_op jit(solution)/shard_map/project/pallas_call | solution.py:188
  91.1 10.3 %attend.2 = (bf16[2,1024,128]{2,1,0:T(8,128)(2,1)}, f32[2,2,1024]{2,1,0:T(2,128)}) custom-call(s32[2,4]{1,0:T(2,128)} %pad_add_fusion.windows, bf16[4,1024,128]{2,1,0:T(8,128)(2,1)} %get-tuple-element.136.q_ref, bf16[4,1024,128]{2,1,0:T(8,128)(2,1)} %get-tuple-element.126.k_ref, bf16[4,1024,128]{2,1,0:T(8,128)(2,1)} %get-tuple-element.127.v_ref, ...), custom_call_target="tpu_custom_call" | custom-call | flops 6710886400 | bytes 3694592 | tf_op jit(solution)/shard_map/attend/pallas_call | solution.py:188
  101.7 2.2 collective-permute-start.25
  107.4 10.4 %attend.3 = (bf16[2,1024,128]{2,1,0:T(8,128)(2,1)}, f32[2,2,1024]{2,1,0:T(2,128)}) custom-call(s32[2,4]{1,0:T(2,128)} %pad_add_fusion.windows, bf16[4,1024,128]{2,1,0:T(8,128)(2,1)} %get-tuple-element.136.q_ref, bf16[4,1024,128]{2,1,0:T(8,128)(2,1)} %get-tuple-element.126.k_ref, bf16[4,1024,128]{2,1,0:T(8,128)(2,1)} %get-tuple-element.127.v_ref, ...), custom_call_target="tpu_custom_call" | custom-call | flops 6710886400 | bytes 3694592 | tf_op jit(solution)/shard_map/attend/pallas_call | solution.py:188
  120.2 6.4 %collective-permute-done.25.refs_4_.refs_2_.refs_6_ = bf16[1024,640]{1,0:T(8,128)(2,1)S(1)} collective-permute-done((bf16[1024,640]{1,0:T(8,128)(2,1)S(1)}, bf16[1024,640]{1,0:T(8,128)(2,1)S(1)}, u32[]{:S(2)}, u32[]{:S(2)}) %collective-permute-start.25) | collective-permute-done | bytes 1310752 | tf_op jit(solution)/shard_map/ppermute | solution.py:51
  127.8 4.0 context_out.3
  137.3 4.0 context_out.2.mine_ref
  142.3 4.5 %norm_a.1 = (f32[512,1024]{1,0:T(8,128)}, f32[512,1]{1,0:T(8,128)}, bf16[512,1024]{1,0:T(8,128)(2,1)}) custom-call(s32[4]{0:T(128)} %add_add_fusion.at_ref.at, f32[512,1024]{1,0:T(8,128)} %context_out.2.mine_ref, bf16[512,1024]{1,0:T(8,128)(2,1)} %copy-done.24, bf16[1024,1024]{1,0:T(8,128)(2,1)} %pad_maximum_fusion.x_ref.refs_0_, ...), custom_call_target="tpu_custom_call" | custom-call | flops 10485760 | bytes 8415232 | tf_op jit(solution)/shard_map/norm_a/pallas_call | solution.py:188
  149.8 2.5 collective-permute-start.30
  152.3 8.1 %ffn_in.2 = (bf16[4,1024,512]{2,1,0:T(8,128)(2,1)}, bf16[4,1024,512]{2,1,0:T(8,128)(2,1)}) custom-call(s32[4]{0:T(128)} %add_add_fusion.at_ref.at, bf16[512,1024]{1,0:T(8,128)(2,1)} %get-tuple-element.145.y_ref.refs_0_, f32[4,1,512]{2,1,0:T(1,128)} %maximum_convert_fusion.2.b_ref, bf16[1024,640]{1,0:T(8,128)(2,1)} %bitcast.238, bf16[1024,640]{1,0:T(8,128)(2,1)} %bitcast.245, ...), custom_call_target="tpu_custom_call" | custom-call | flops 6442450944 | bytes 14688256 | tf_op jit(solution)/shard_map/ffn_in/pallas_call | solution.py:188
  161.4 8.3 %ffn_in.3 = (bf16[4,1024,512]{2,1,0:T(8,128)(2,1)}, bf16[4,1024,512]{2,1,0:T(8,128)(2,1)}) custom-call(s32[4]{0:T(128)} %add_add_fusion.at_ref.at, bf16[512,1024]{1,0:T(8,128)(2,1)} %copy-done.49, f32[4,1,512]{2,1,0:T(1,128)} %maximum_convert_fusion.2.b_ref, bf16[1024,640]{1,0:T(8,128)(2,1)} %bitcast.239, ...), custom_call_target="tpu_custom_call", output_to_operand_aliasing={{0}: (7, {}), {1}: (8, {})} | custom-call | flops 6442450944 | bytes 23076864 | tf_op jit(solution)/shard_map/ffn_in/pallas_call | solution.py:188
  170.5 3.0 collective-permute-done.31.refs_3_
  175.6 4.2 assemble.5
  179.8 6.6 %ffn_out.3 = bf16[512,1024]{1,0:T(8,128)(2,1)} custom-call(s32[4]{0:T(128)} %add_add_fusion.at_ref.at, bf16[4,1024,512]{2,1,0:T(8,128)(2,1)} %get-tuple-element.148.act_ref.refs_2_, bf16[8,2,128,512]{3,2,1,0:T(8,128)(2,1)} %bitcast.219, bf16[8,2,128,512]{3,2,1,0:T(8,128)(2,1)} %bitcast.227, bf16[8,2,128,512]{3,2,1,0:T(8,128)(2,1)} %bitcast.220, ...), custom_call_target="tpu_custom_call" | custom-call | flops 2147483648 | bytes 13631488 | tf_op jit(solution)/shard_map/ffn_out/pallas_call | solution.py:188
  187.2 6.8 %ffn_out.2.mine_ref = f32[512,1024]{1,0:T(8,128)} custom-call(s32[4]{0:T(128)} %add_add_fusion.at_ref.at, bf16[4,1024,512]{2,1,0:T(8,128)(2,1)} %get-tuple-element.148.act_ref.refs_2_, bf16[8,2,128,512]{3,2,1,0:T(8,128)(2,1)} %bitcast.221, bf16[8,2,128,512]{3,2,1,0:T(8,128)(2,1)} %bitcast.229, bf16[8,2,128,512]{3,2,1,0:T(8,128)(2,1)} %bitcast.222, ...), custom_call_target="tpu_custom_call" | custom-call | flops 2147483648 | bytes 14680064 | tf_op jit(solution)/shard_map/ffn_out/pallas_call | solution.py:188
  196.2 5.5 %norm_b.1 = (bf16[512,1024]{1,0:T(8,128)(2,1)}, f32[512,1024]{1,0:T(8,128)}, bf16[512,1024]{1,0:T(8,128)(2,1)}, f32[3,1024]{1,0:T(4,128)}) custom-call(f32[512,1024]{1,0:T(8,128)} %ffn_out.2.mine_ref, bf16[512,1024]{1,0:T(8,128)(2,1)} %copy-done.25, f32[512,1024]{1,0:T(8,128)} %get-tuple-element.158.centred_a_ref.centred_ref, ...), custom_call_target="tpu_custom_call" | custom-call | flops 20971520 | bytes 10522624 | tf_op jit(solution)/shard_map/norm_b/pallas_call | solution.py:188
  205.6 9.6 %weight_grad_shards.1 = (bf16[2,128,1024]{2,1,0:T(8,128)(2,1)}, bf16[2,128,1024]{2,1,0:T(8,128)(2,1)}, bf16[2,2,128,1024]{3,2,1,0:T(8,128)(2,1)}, bf16[2,2,128,1...) custom-call(s32[4]{0:T(128)} %add_add_fusion.at_ref.at, bf16[512,1024]{1,0:T(8,128)(2,1)} %get-tuple-element.166.refs_0_.gb_ref, ...), custom_call_target="tpu_custom_call" | custom-call | flops 4294967296 | bytes 10485760 | tf_op jit(solution)/shard_map/weight_grad_shards/pallas_call | solution.py:188
  217.3 11.2 %ffn_back.2 = (bf16[4,1024,512]{2,1,0:T(8,128)(2,1)}, f32[4,1,512]{2,1,0:T(1,128)}, f32[512,1024]{1,0:T(8,128)}) custom-call(s32[4]{0:T(128)} %add_add_fusion.at_ref.at, bf16[512,1024]{1,0:T(8,128)(2,1)} %get-tuple-element.166.refs_0_.gb_ref, bf16[4,1024,512]{2,1,0:T(8,128)(2,1)} %get-tuple-element.167.slope_ref, bf16[8,2,128,512]{3,2,1,0:T(8,128)(2,1)} %bitcast.223, ...), custom_call_target="tpu_custom_call" | custom-call | flops 4294967296 | bytes 25174016 | tf_op jit(solution)/shard_map/ffn_back/pallas_call | solution.py:188
  228.5 11.1 %ffn_back.3 = (bf16[4,1024,512]{2,1,0:T(8,128)(2,1)}, f32[4,1,512]{2,1,0:T(1,128)}, bf16[512,1024]{1,0:T(8,128)(2,1)}) custom-call(s32[4]{0:T(128)} %add_add_fusion.at_ref.at, bf16[512,1024]{1,0:T(8,128)(2,1)} %copy-done.9, bf16[4,1024,512]{2,1,0:T(8,128)(2,1)} %get-tuple-element.167.slope_ref, ...), custom_call_target="tpu_custom_call", output_to_operand_aliasing={{0}: (11, {})} | custom-call | flops 4294967296 | bytes 28319744 | tf_op jit(solution)/shard_map/ffn_back/pallas_call | solution.py:188
  245.0 2.6 collective-permute-start.46
  247.5 8.4 %weight_grad.3 = (bf16[1024,512]{1,0:T(8,128)(2,1)}, bf16[1024,512]{1,0:T(8,128)(2,1)}, bf16[1024,512]{1,0:T(8,128)(2,1)}, bf16[1024,512]{1,0:T(8,128)(2,1)}) custom-call(bf16[512,1024]{1,0:T(8,128)(2,1)} %get-tuple-element.145.y_ref.refs_0_, bf16[512,1024]{1,0:T(8,128)(2,1)} %copy-done.49, bf16[4,1024,512]{2,1,0:T(8,128)(2,1)} %get-tuple-element.176.refs_2_), custom_call_target="tpu_custom_call" | custom-call | flops 4294967296 | bytes 10485760 | tf_op jit(solution)/shard_map/weight_grad/pallas_call | solution.py:188
  258.4 5.5 %norm_a_back.1 = (f32[512,1024]{1,0:T(8,128)}, bf16[512,1024]{1,0:T(8,128)(2,1)}, f32[3,1024]{1,0:T(4,128)}) custom-call(f32[512,1024]{1,0:T(8,128)} %get-tuple-element.168.mine_ref, bf16[512,1024]{1,0:T(8,128)(2,1)} %collective-permute-done.38.got_ref, f32[512,1024]{1,0:T(8,128)} %get-tuple-element.178.gb_ref, ...), custom_call_target="tpu_custom_call" | custom-call | flops 15728640 | bytes 10524672 | tf_op jit(solution)/shard_map/norm_a_back/pallas_call | solution.py:188
  275.8 4.7 %context_back.1.do_ref = bf16[4,1024,128]{2,1,0:T(8,128)(2,1)} custom-call(s32[4]{0:T(128)} %add_add_fusion.at_ref.at, bf16[1024,1024]{1,0:T(8,128)(2,1)} %pad_maximum_fusion.1.ga_ref.refs_1_, bf16[1024,640]{1,0:T(8,128)(2,1)} %bitcast.242, bf16[1024,640]{1,0:T(8,128)(2,1)} %bitcast.249, bf16[1024,640]{1,0:T(8,128)(2,1)} %copy-done.3, ...), custom_call_target="tpu_custom_call" | custom-call | flops 1073741824 | bytes 8388608 | tf_op jit(solution)/shard_map/context_back/pallas_call | solution.py:188
  280.5 11.9 %attend_back.2 = (bf16[2,1024,384]{2,1,0:T(8,128)(2,1)}, f32[2,2,128]{2,1,0:T(2,128)}) custom-call(s32[2,4]{1,0:T(2,128)} %pad_add_fusion.windows, bf16[4,1024,128]{2,1,0:T(8,128)(2,1)} %get-tuple-element.136.q_ref, bf16[4,1024,128]{2,1,0:T(8,128)(2,1)} %get-tuple-element.126.k_ref, bf16[4,1024,128]{2,1,0:T(8,128)(2,1)} %get-tuple-element.127.v_ref, ...), custom_call_target="tpu_custom_call" | custom-call | flops 10066329600 | bytes 5793792 | tf_op jit(solution)/shard_map/attend_back/pallas_call | solution.py:188
  292.9 4.0 collective-permute-done.42
  297.0 7.3 %weight_grad.4 = (bf16[1024,512]{1,0:T(8,128)(2,1)}, bf16[1024,512]{1,0:T(8,128)(2,1)}) custom-call(bf16[1024,1024]{1,0:T(8,128)(2,1)} %pad_maximum_fusion.x_ref.refs_0_, bf16[1024,1024]{1,0:T(8,128)(2,1)} %pad_maximum_fusion.1.ga_ref.refs_1_, bf16[2,1024,384]{2,1,0:T(8,128)(2,1)} %get-tuple-element.213.refs_2_.refs_1_, ...), custom_call_target="tpu_custom_call" | custom-call | flops 2147483648 | bytes 8388608 | tf_op jit(solution)/shard_map/weight_grad/pallas_call | solution.py:188
  305.5 2.2 add_convert_fusion
  315.8 12.4 %attend_back.3 = (bf16[2,1024,384]{2,1,0:T(8,128)(2,1)}, f32[2,2,128]{2,1,0:T(2,128)}) custom-call(s32[2,4]{1,0:T(2,128)} %pad_add_fusion.windows, bf16[4,1024,128]{2,1,0:T(8,128)(2,1)} %get-tuple-element.136.q_ref, bf16[4,1024,128]{2,1,0:T(8,128)(2,1)} %get-tuple-element.126.k_ref, bf16[4,1024,128]{2,1,0:T(8,128)(2,1)} %get-tuple-element.127.v_ref, ...), custom_call_target="tpu_custom_call" | custom-call | flops 10066329600 | bytes 5793792 | tf_op jit(solution)/shard_map/attend_back/pallas_call | solution.py:188
  329.2 3.5 collective-permute-start.50
  332.7 7.3 %weight_grad.5 = (bf16[1024,512]{1,0:T(8,128)(2,1)}, bf16[1024,512]{1,0:T(8,128)(2,1)}) custom-call(bf16[1024,1024]{1,0:T(8,128)(2,1)} %pad_maximum_fusion.x_ref.refs_0_, bf16[1024,1024]{1,0:T(8,128)(2,1)} %pad_maximum_fusion.1.ga_ref.refs_1_, bf16[2,1024,384]{2,1,0:T(8,128)(2,1)} %get-tuple-element.212.refs_2_.refs_0_, ...), custom_call_target="tpu_custom_call" | custom-call | flops 2147483648 | bytes 8388608 | tf_op jit(solution)/shard_map/weight_grad/pallas_call | solution.py:188
  358.3 6.5 %inputs_back.2 = bf16[512,1024]{1,0:T(8,128)(2,1)} custom-call(s32[4]{0:T(128)} %add_add_fusion.1.at_ref, bf16[2,1024,384]{2,1,0:T(8,128)(2,1)} %get-tuple-element.212.refs_2_.refs_0_, bf16[2,1024,384]{2,1,0:T(8,128)(2,1)} %get-tuple-element.213.refs_2_.refs_1_, bf16[1024,384]{1,0:T(8,128)(2,1)} %bitcast.259, bf16[1024,384]{1,0:T(8,128)(2,1)} %bitcast.262, ...), custom_call_target="tpu_custom_call" | custom-call | flops 1610612736 | bytes 7340032 | tf_op jit(solution)/shard_map/inputs_back/pallas_call | solution.py:188
  374.9 6.3 %inputs_back.3 = f32[512,1024]{1,0:T(8,128)} custom-call(s32[4]{0:T(128)} %add_add_fusion.at_ref.at, bf16[2,1024,384]{2,1,0:T(8,128)(2,1)} %get-tuple-element.212.refs_2_.refs_0_, bf16[2,1024,384]{2,1,0:T(8,128)(2,1)} %get-tuple-element.213.refs_2_.refs_1_, bf16[1024,384]{1,0:T(8,128)(2,1)} %bitcast.260, bf16[1024,384]{1,0:T(8,128)(2,1)} %bitcast.263, ...), custom_call_target="tpu_custom_call" | custom-call | flops 1610612736 | bytes 8388608 | tf_op jit(solution)/shard_map/inputs_back/pallas_call | solution.py:188
  383.9 4.0 collective-permute-done.54
  394.4 2.5 add_convert_fusion.1
  398.8 5.2 %collective-permute-done.62 = bf16[2,2,1,1,128,512]{5,4,1,3,2,0:T(8,128)(2,1)S(1)} collective-permute-done((bf16[2,2,1,1,128,512]{5,4,1,3,2,0:T(8,128)(2,1)S(1)}, bf16[2,2,1,1,128,512]{5,4,1,3,2,0:T(8,128)(2,1)S(1)}, u32[]{:S(2)}, u32[]{:S(2)}) %collective-permute-start.62) | collective-permute-done | bytes 524320 | tf_op jit(solution)/shard_map/ppermute | solution.py:51
  407.5 3.9 collective-permute-done.60
  412.4 5.7 %collective-permute-done.63 = bf16[2,1,1,1,128,512]{5,4,3,2,1,0:T(8,128)(2,1)S(1)} collective-permute-done((bf16[2,1,1,1,128,512]{5,4,3,2,1,0:T(8,128)(2,1)S(1)}, bf16[2,1,1,1,128,512]{5,4,3,2,1,0:T(8,128)(2,1)S(1)}, u32[]{:S(2)}, u32[]{:S(2)}) %collective-permute-start.63) | collective-permute-done | bytes 262176 | tf_op jit(solution)/shard_map/ppermute | solution.py:51
  (410 shorter events, 154.1 us)
Async XLA Ops:
  2.2 15.9 %collective-permute-start.6 = (bf16[2,128,384]{2,1,0:T(8,128)(2,1)S(1)}, bf16[2,128,384]{2,1,0:T(8,128)(2,1)S(1)}, u32[]{:S(2)}, u32[]{:S(2)}) collective-permute-start(bf16[2,128,384]{2,1,0:T(8,128)(2,1)S(1)} %copy.284.refs_0_), channel_id=1, source_target_pairs={{0,8},{4,12},{8,16},{12,20},{16,24},{20,28},{24,0},{28,4},{1,9},{5... | collective-permute-start | bytes 589832 | tf_op jit(solution)/shard_map/ppermute | solution.py:726
  5.3 12.9 %collective-permute-start.5 = (bf16[2,128,384]{2,1,0:T(8,128)(2,1)S(1)}, bf16[2,128,384]{2,1,0:T(8,128)(2,1)S(1)}, u32[]{:S(2)}, u32[]{:S(2)}) collective-permute-start(bf16[2,128,384]{2,1,0:T(8,128)(2,1)S(1)} %copy.284.refs_0_), channel_id=1, source_target_pairs={{0,24},{4,28},{8,0},{12,4},{16,8},{20,12},{24,16},{28,20},{1,25},{... | collective-permute-start | bytes 589832 | tf_op jit(solution)/shard_map/ppermute | solution.py:726
  16.0 15.7 %collective-permute-start.20 = (bf16[2,1,128,512]{3,2,1,0:T(8,128)(2,1)}, bf16[2,1,128,512]{3,2,1,0:T(8,128)(2,1)}, u32[]{:S(2)}, u32[]{:S(2)}) collective-permute-start(bf16[2,1,128,512]{3,2,1,0:T(8,128)(2,1)} %pad_maximum_fusion.19), channel_id=1, source_target_pairs={{0,2},{1,3},{2,0},{3,1},{4,6},{5,7},{6,4},{7,5},{8,10},{9,11},{10,... | collective-permute-start | bytes 786440 | tf_op jit(solution)/shard_map/ppermute | solution.py:51
  17.5 15.7 %collective-permute-start.21 = (bf16[1,2,128,512]{3,2,1,0:T(8,128)(2,1)S(1)}, bf16[1,2,128,512]{3,2,1,0:T(8,128)(2,1)}, u32[]{:S(2)}, u32[]{:S(2)}) collective-permute-start(bf16[1,2,128,512]{3,2,1,0:T(8,128)(2,1)S(1)} %pad_maximum_fusion.20), channel_id=1, source_target_pairs={{0,4},{4,0},{8,12},{12,8},{16,20},{20,16},{24,28},{28,24},{1,5},{5... | collective-permute-start | bytes 786440 | tf_op jit(solution)/shard_map/ppermute | solution.py:51
  22.9 17.1 %collective-permute-start.2 = (bf16[1024,256]{1,0:T(8,128)(2,1)}, bf16[1024,256]{1,0:T(8,128)(2,1)}, u32[]{:S(2)}, u32[]{:S(2)}) collective-permute-start(bf16[1024,256]{1,0:T(8,128)(2,1)} %dynamic-slice_bitcast_fusion.3), channel_id=1, source_target_pairs={{0,2},{1,3},{2,0},{3,1},{4,6},{5,7},{6,4},{7,5},{8,10},{9,11},{10,... | collective-permute-start | bytes 1572872 | tf_op jit(solution)/shard_map/ppermute | solution.py:51
  24.9 12.2 %collective-permute-start.15 = (bf16[2,128,640]{2,1,0:T(8,128)(2,1)S(1)}, bf16[2,128,640]{2,1,0:T(8,128)(2,1)S(1)}, u32[]{:S(2)}, u32[]{:S(2)}) collective-permute-start(bf16[2,128,640]{2,1,0:T(8,128)(2,1)S(1)} %pad_maximum_fusion.18.refs_0_), channel_id=1, source_target_pairs={{0,8},{4,12},{8,16},{12,20},{16,24},{20,28},{24,0},{28,4},{1,9},{5... | collective-permute-start | bytes 983048 | tf_op jit(solution)/shard_map/ppermute | solution.py:726
  25.3 13.5 %collective-permute-start.14 = (bf16[2,128,640]{2,1,0:T(8,128)(2,1)S(1)}, bf16[2,128,640]{2,1,0:T(8,128)(2,1)S(1)}, u32[]{:S(2)}, u32[]{:S(2)}) collective-permute-start(bf16[2,128,640]{2,1,0:T(8,128)(2,1)S(1)} %pad_maximum_fusion.18.refs_0_), channel_id=1, source_target_pairs={{0,24},{4,28},{8,0},{12,4},{16,8},{20,12},{24,16},{28,20},{1,25},{... | collective-permute-start | bytes 983048 | tf_op jit(solution)/shard_map/ppermute | solution.py:726
  31.7 29.0 %collective-permute-start.12 = (bf16[2,2,1,128,384]{4,3,2,1,0:T(8,128)(2,1)}, bf16[2,2,1,128,384]{4,3,2,1,0:T(8,128)(2,1)}, u32[]{:S(2)}, u32[]{:S(2)}) collective-permute-start(bf16[2,2,1,128,384]{4,3,2,1,0:T(8,128)(2,1)} %bitcast.287), channel_id=1, source_target_pairs={{0,2},{1,3},{2,0},{3,1},{4,6},{5,7},{6,4},{7,5},{8,10},{9,11},{10,... | collective-permute-start | bytes 1179656 | tf_op jit(solution)/shard_map/ppermute | solution.py:51
  33.2 28.7 %collective-permute-start.10 = (bf16[2,2,1,128,384]{4,3,2,1,0:T(8,128)(2,1)}, bf16[2,2,1,128,384]{4,3,2,1,0:T(8,128)(2,1)}, u32[]{:S(2)}, u32[]{:S(2)}) collective-permute-start(bf16[2,2,1,128,384]{4,3,2,1,0:T(8,128)(2,1)} %bitcast.288), channel_id=1, source_target_pairs={{0,4},{4,0},{8,12},{12,8},{16,20},{20,16},{24,28},{28,24},{1,5},{5... | collective-permute-start | bytes 1179656 | tf_op jit(solution)/shard_map/ppermute | solution.py:51
  37.1 18.9 %collective-permute-start.9 = (bf16[2,2,1,128,384]{4,3,2,1,0:T(8,128)(2,1)S(1)}, bf16[2,2,1,128,384]{4,3,2,1,0:T(8,128)(2,1)}, u32[]{:S(2)}, u32[]{:S(2)}) collective-permute-start(bf16[2,2,1,128,384]{4,3,2,1,0:T(8,128)(2,1)S(1)} %bitcast.290), channel_id=1, source_target_pairs={{0,4},{4,0},{8,12},{12,8},{16,20},{20,16},{24,28},{28,24},{1,5},{5... | collective-permute-start | bytes 1179656 | tf_op jit(solution)/shard_map/ppermute | solution.py:51
  49.9 23.3 %collective-permute-start.3 = (bf16[1024,512]{1,0:T(8,128)(2,1)}, bf16[1024,512]{1,0:T(8,128)(2,1)}, u32[]{:S(2)}, u32[]{:S(2)}) collective-permute-start(bf16[1024,512]{1,0:T(8,128)(2,1)} %pad_maximum_fusion.5), channel_id=1, source_target_pairs={{0,1},{1,0},{2,3},{3,2},{4,5},{5,4},{6,7},{7,6},{8,9},{9,8},{10,11... | collective-permute-start | bytes 3145736 | tf_op jit(solution)/shard_map/ppermute | solution.py:51
  55.1 62.6 %collective-permute-start.22 = (bf16[2,2,2,128,512]{4,3,2,1,0:T(8,128)(2,1)}, bf16[2,2,2,128,512]{4,3,2,1,0:T(8,128)(2,1)}, u32[]{:S(2)}, u32[]{:S(2)}) collective-permute-start(bf16[2,2,2,128,512]{4,3,2,1,0:T(8,128)(2,1)} %pad_maximum_fusion.6.refs_0_), channel_id=1, source_target_pairs={{0,8},{4,12},{8,16},{12,20},{16,24},{20,28},{24,0},{28,4},{1,9},{5... | collective-permute-start | bytes 3145736 | tf_op jit(solution)/shard_map/ppermute | solution.py:726
  56.0 61.7 %collective-permute-start.23 = (bf16[2,2,2,128,512]{4,3,2,1,0:T(8,128)(2,1)}, bf16[2,2,2,128,512]{4,3,2,1,0:T(8,128)(2,1)}, u32[]{:S(2)}, u32[]{:S(2)}) collective-permute-start(bf16[2,2,2,128,512]{4,3,2,1,0:T(8,128)(2,1)} %pad_maximum_fusion.6.refs_0_), channel_id=1, source_target_pairs={{0,24},{4,28},{8,0},{12,4},{16,8},{20,12},{24,16},{28,20},{1,25},{... | collective-permute-start | bytes 3145736 | tf_op jit(solution)/shard_map/ppermute | solution.py:726
  60.7 20.5 %collective-permute-start.11 = (bf16[1024,384]{1,0:T(8,128)(2,1)S(1)}, bf16[1024,384]{1,0:T(8,128)(2,1)S(1)}, u32[]{:S(2)}, u32[]{:S(2)}) collective-permute-start(bf16[1024,384]{1,0:T(8,128)(2,1)S(1)} %bitcast.257), channel_id=1, source_target_pairs={{0,2},{1,3},{2,0},{3,1},{4,6},{5,7},{6,4},{7,5},{8,10},{9,11},{10,... | collective-permute-start | bytes 2359304 | tf_op jit(solution)/shard_map/ppermute | solution.py:51
  70.3 35.1 %collective-permute-start.19 = (bf16[2,2,1,128,640]{4,3,2,1,0:T(8,128)(2,1)}, bf16[2,2,1,128,640]{4,3,2,1,0:T(8,128)(2,1)}, u32[]{:S(2)}, u32[]{:S(2)}) collective-permute-start(bf16[2,2,1,128,640]{4,3,2,1,0:T(8,128)(2,1)} %bitcast.38), channel_id=1, source_target_pairs={{0,2},{1,3},{2,0},{3,1},{4,6},{5,7},{6,4},{7,5},{8,10},{9,11},{10,... | collective-permute-start | bytes 1966088 | tf_op jit(solution)/shard_map/ppermute | solution.py:51
  73.2 30.7 %collective-permute-start.24 = (bf16[2,2,1,128,640]{4,3,2,1,0:T(8,128)(2,1)}, bf16[2,2,1,128,640]{4,3,2,1,0:T(8,128)(2,1)}, u32[]{:S(2)}, u32[]{:S(2)}) collective-permute-start(bf16[2,2,1,128,640]{4,3,2,1,0:T(8,128)(2,1)} %bitcast.44), channel_id=1, source_target_pairs={{0,4},{4,0},{8,12},{12,8},{16,20},{20,16},{24,28},{28,24},{1,5},{5... | collective-permute-start | bytes 1966088 | tf_op jit(solution)/shard_map/ppermute | solution.py:51
  81.2 20.2 %collective-permute-start.18 = (bf16[2,2,1,128,640]{4,3,2,1,0:T(8,128)(2,1)S(1)}, bf16[2,2,1,128,640]{4,3,2,1,0:T(8,128)(2,1)S(1)}, u32[]{:S(2)}, u32[]{:S(2)}) collective-permute-start(bf16[2,2,1,128,640]{4,3,2,1,0:T(8,128)(2,1)S(1)} %bitcast.285), channel_id=1, source_target_pairs={{0,4},{4,0},{8,12},{12,8},{16,20},{20,16},{24,28},{28,24},{1,5},{5... | collective-permute-start | bytes 1966088 | tf_op jit(solution)/shard_map/ppermute | solution.py:51
  101.7 24.9 %collective-permute-start.25 = (bf16[1024,640]{1,0:T(8,128)(2,1)S(1)}, bf16[1024,640]{1,0:T(8,128)(2,1)S(1)}, u32[]{:S(2)}, u32[]{:S(2)}) collective-permute-start(bf16[1024,640]{1,0:T(8,128)(2,1)S(1)} %bitcast.235), channel_id=1, source_target_pairs={{0,2},{1,3},{2,0},{3,1},{4,6},{5,7},{6,4},{7,5},{8,10},{9,11},{10,... | collective-permute-start | bytes 3932168 | tf_op jit(solution)/shard_map/ppermute | solution.py:51
  105.4 12.3 %collective-permute-start.26 = (bf16[2,2,1,128,640]{4,3,2,1,0:T(8,128)(2,1)}, bf16[2,2,1,128,640]{4,3,2,1,0:T(8,128)(2,1)S(1)}, u32[]{:S(2)}, u32[]{:S(2)}) collective-permute-start(bf16[2,2,1,128,640]{4,3,2,1,0:T(8,128)(2,1)} %collective-permute-done.19), channel_id=1, source_target_pairs={{0,4},{4,0},{8,12},{12,8},{16,20},{20,16},{24,28},{28,24},{1,5},{5... | collective-permute-start | bytes 1966088 | tf_op jit(solution)/shard_map/ppermute | solution.py:51
  136.2 33.5 %collective-permute-start.33 = (bf16[1024,256]{1,0:T(8,128)(2,1)}, bf16[1024,256]{1,0:T(8,128)(2,1)S(1)}, u32[]{:S(2)}, u32[]{:S(2)}) collective-permute-start(bf16[1024,256]{1,0:T(8,128)(2,1)} %dynamic-slice_bitcast_fusion.2), channel_id=1, source_target_pairs={{0,2},{1,3},{2,0},{3,1},{4,6},{5,7},{6,4},{7,5},{8,10},{9,11},{10,... | collective-permute-start | bytes 1572872 | tf_op jit(solution)/shard_map/ppermute | solution.py:51
  146.8 13.6 %collective-permute-start.29 = (bf16[512,1024]{1,0:T(8,128)(2,1)}, bf16[512,1024]{1,0:T(8,128)(2,1)S(1)}, u32[]{:S(2)}, u32[]{:S(2)}) collective-permute-start(bf16[512,1024]{1,0:T(8,128)(2,1)} %get-tuple-element.145.y_ref.refs_0_), channel_id=1, source_target_pairs={{0,1},{1,0},{2,3},{3,2},{4,5},{5,4},{6,7},{7,6},{8,9},{9,8},{10,11... | collective-permute-start | bytes 3145736 | tf_op jit(solution)/shard_map/ppermute | solution.py:51
  147.9 25.6 %collective-permute-start.31 = (bf16[2,2,128,512]{3,2,1,0:T(8,128)(2,1)S(1)}, bf16[2,2,128,512]{3,2,1,0:T(8,128)(2,1)S(1)}, u32[]{:S(2)}, u32[]{:S(2)}) collective-permute-start(bf16[2,2,128,512]{3,2,1,0:T(8,128)(2,1)S(1)} %slice_bitcast_fusion), channel_id=1, source_target_pairs={{0,24},{4,28},{8,0},{12,4},{16,8},{20,12},{24,16},{28,20},{1,25},{... | collective-permute-start | bytes 1572872 | tf_op jit(solution)/shard_map/ppermute | solution.py:726
  149.8 25.0 %collective-permute-start.30 = (bf16[2,2,128,512]{3,2,1,0:T(8,128)(2,1)}, bf16[2,2,128,512]{3,2,1,0:T(8,128)(2,1)S(1)}, u32[]{:S(2)}, u32[]{:S(2)}) collective-permute-start(bf16[2,2,128,512]{3,2,1,0:T(8,128)(2,1)} %slice_bitcast_fusion.1), channel_id=1, source_target_pairs={{0,8},{4,12},{8,16},{12,20},{16,24},{20,28},{24,0},{28,4},{1,9},{5... | collective-permute-start | bytes 1572872 | tf_op jit(solution)/shard_map/ppermute | solution.py:726
  215.2 27.5 %collective-permute-start.40 = (bf16[2,128,1024]{2,1,0:T(8,128)(2,1)}, bf16[2,128,1024]{2,1,0:T(8,128)(2,1)}, u32[]{:S(2)}, u32[]{:S(2)}) collective-permute-start(bf16[2,128,1024]{2,1,0:T(8,128)(2,1)} %get-tuple-element.175), channel_id=1, source_target_pairs={{0,24},{4,28},{8,0},{12,4},{16,8},{20,12},{24,16},{28,20},{1,25},{... | collective-permute-start | bytes 1572872 | tf_op jit(solution)/shard_map/ppermute | solution.py:726
  215.9 31.6 %collective-permute-start.39 = (bf16[2,128,1024]{2,1,0:T(8,128)(2,1)}, bf16[2,128,1024]{2,1,0:T(8,128)(2,1)S(1)}, u32[]{:S(2)}, u32[]{:S(2)}) collective-permute-start(bf16[2,128,1024]{2,1,0:T(8,128)(2,1)} %get-tuple-element.174), channel_id=1, source_target_pairs={{0,8},{4,12},{8,16},{12,20},{16,24},{20,28},{24,0},{28,4},{1,9},{5... | collective-permute-start | bytes 1572872 | tf_op jit(solution)/shard_map/ppermute | solution.py:726
  239.8 18.6 %collective-permute-start.38 = (bf16[512,1024]{1,0:T(8,128)(2,1)}, bf16[512,1024]{1,0:T(8,128)(2,1)}, u32[]{:S(2)}, u32[]{:S(2)}) collective-permute-start(bf16[512,1024]{1,0:T(8,128)(2,1)} %get-tuple-element.171), channel_id=1, source_target_pairs={{0,1},{1,0},{2,3},{3,2},{4,5},{5,4},{6,7},{7,6},{8,9},{9,8},{10,11... | collective-permute-start | bytes 3145736 | tf_op jit(solution)/shard_map/ppermute | solution.py:51
  241.7 14.2 %collective-permute-start.36 = (bf16[512,512]{1,0:T(8,128)(2,1)}, bf16[512,512]{1,0:T(8,128)(2,1)}, u32[]{:S(2)}, u32[]{:S(2)}) collective-permute-start(bf16[512,512]{1,0:T(8,128)(2,1)} %constant_dynamic-slice_fusion.15), channel_id=1, source_target_pairs={{0,2},{1,3},{2,0},{3,1},{4,6},{5,7},{6,4},{7,5},{8,10},{9,11},{10,... | collective-permute-start | bytes 1572872 | tf_op jit(solution)/shard_map/ppermute | solution.py:51
  245.0 47.5 %collective-permute-start.46 = (bf16[2,2,128,1024]{3,2,1,0:T(8,128)(2,1)}, bf16[2,2,128,1024]{3,2,1,0:T(8,128)(2,1)}, u32[]{:S(2)}, u32[]{:S(2)}) collective-permute-start(bf16[2,2,128,1024]{3,2,1,0:T(8,128)(2,1)} %pad_maximum_fusion.11), channel_id=1, source_target_pairs={{0,24},{4,28},{8,0},{12,4},{16,8},{20,12},{24,16},{28,20},{1,25},{... | collective-permute-start | bytes 3145736 | tf_op jit(solution)/shard_map/ppermute | solution.py:726
  265.5 27.4 %collective-permute-start.45 = (bf16[2,2,128,1024]{3,2,1,0:T(8,128)(2,1)}, bf16[2,2,128,1024]{3,2,1,0:T(8,128)(2,1)}, u32[]{:S(2)}, u32[]{:S(2)}) collective-permute-start(bf16[2,2,128,1024]{3,2,1,0:T(8,128)(2,1)} %pad_maximum_fusion.10), channel_id=1, source_target_pairs={{0,8},{4,12},{8,16},{12,20},{16,24},{20,28},{24,0},{28,4},{1,9},{5... | collective-permute-start | bytes 3145736 | tf_op jit(solution)/shard_map/ppermute | solution.py:726
  266.5 26.0 %collective-permute-start.43 = (bf16[2,2,1,128,512]{4,3,0,2,1:T(8,128)(2,1)}, bf16[2,2,1,128,512]{4,3,0,2,1:T(8,128)(2,1)}, u32[]{:S(2)}, u32[]{:S(2)}) collective-permute-start(bf16[2,2,1,128,512]{4,3,0,2,1:T(8,128)(2,1)} %copy.321), channel_id=1, source_target_pairs={{0,4},{4,0},{8,12},{12,8},{16,20},{20,16},{24,28},{28,24},{1,5},{5... | collective-permute-start | bytes 1572872 | tf_op jit(solution)/shard_map/ppermute | solution.py:51
  268.9 23.5 %collective-permute-start.44 = (bf16[2,2,1,128,512]{4,3,0,2,1:T(8,128)(2,1)}, bf16[2,2,1,128,512]{4,3,0,2,1:T(8,128)(2,1)}, u32[]{:S(2)}, u32[]{:S(2)}) collective-permute-start(bf16[2,2,1,128,512]{4,3,0,2,1:T(8,128)(2,1)} %copy.322), channel_id=1, source_target_pairs={{0,4},{4,0},{8,12},{12,8},{16,20},{20,16},{24,28},{28,24},{1,5},{5... | collective-permute-start | bytes 1572872 | tf_op jit(solution)/shard_map/ppermute | solution.py:51
  271.8 25.2 %collective-permute-start.42 = (bf16[1024,512]{1,0:T(8,128)(2,1)}, bf16[1024,512]{1,0:T(8,128)(2,1)}, u32[]{:S(2)}, u32[]{:S(2)}) collective-permute-start(bf16[1024,512]{1,0:T(8,128)(2,1)} %get-tuple-element.184), channel_id=1, source_target_pairs={{0,2},{1,3},{2,0},{3,1},{4,6},{5,7},{6,4},{7,5},{8,10},{9,11},{10,... | collective-permute-start | bytes 3145736 | tf_op jit(solution)/shard_map/ppermute | solution.py:51
  304.3 52.5 %collective-permute-start.49 = (bf16[1024,512]{1,0:T(8,128)(2,1)}, bf16[1024,512]{1,0:T(8,128)(2,1)}, u32[]{:S(2)}, u32[]{:S(2)}) collective-permute-start(bf16[1024,512]{1,0:T(8,128)(2,1)} %get-tuple-element.192), channel_id=1, source_target_pairs={{0,2},{1,3},{2,0},{3,1},{4,6},{5,7},{6,4},{7,5},{8,10},{9,11},{10,... | collective-permute-start | bytes 3145736 | tf_op jit(solution)/shard_map/ppermute | solution.py:51
  308.5 38.6 %collective-permute-start.67 = (bf16[1,2,128,1024]{3,2,1,0:T(8,128)(2,1)}, bf16[1,2,128,1024]{3,2,1,0:T(8,128)(2,1)}, u32[]{:S(2)}, u32[]{:S(2)}) collective-permute-start(bf16[1,2,128,1024]{3,2,1,0:T(8,128)(2,1)} %constant_dynamic-slice_fusion.1), channel_id=1, source_target_pairs={{0,4},{4,0},{8,12},{12,8},{16,20},{20,16},{24,28},{28,24},{1,5},{5... | collective-permute-start | bytes 1572872 | tf_op jit(solution)/shard_map/ppermute | solution.py:51
  312.4 36.9 %collective-permute-start.47 = (bf16[2,2,1,128,512]{4,3,2,1,0:T(8,128)(2,1)}, bf16[2,2,1,128,512]{4,3,2,1,0:T(8,128)(2,1)}, u32[]{:S(2)}, u32[]{:S(2)}) collective-permute-start(bf16[2,2,1,128,512]{4,3,2,1,0:T(8,128)(2,1)} %constant_dynamic-slice_fusion.12), channel_id=1, source_target_pairs={{0,4},{4,0},{8,12},{12,8},{16,20},{20,16},{24,28},{28,24},{1,5},{5... | collective-permute-start | bytes 1572872 | tf_op jit(solution)/shard_map/ppermute | solution.py:51
  314.9 35.0 %collective-permute-start.48 = (bf16[2,2,1,128,512]{4,3,0,2,1:T(8,128)(2,1)}, bf16[2,2,1,128,512]{4,3,0,2,1:T(8,128)(2,1)S(1)}, u32[]{:S(2)}, u32[]{:S(2)}) collective-permute-start(bf16[2,2,1,128,512]{4,3,0,2,1:T(8,128)(2,1)} %add_convert_fusion.12), channel_id=1, source_target_pairs={{0,2},{1,3},{2,0},{3,1},{4,6},{5,7},{6,4},{7,5},{8,10},{9,11},{10,... | collective-permute-start | bytes 1572872 | tf_op jit(solution)/shard_map/ppermute | solution.py:51
  329.2 12.7 %collective-permute-start.50 = (f32[9216]{0:T(1024)S(1)}, f32[9216]{0:T(1024)S(1)}, u32[]{:S(2)}, u32[]{:S(2)}) collective-permute-start(f32[9216]{0:T(1024)S(1)} %constant_dynamic-update-slice_fusion), channel_id=1, source_target_pairs={{0,16},{4,20},{8,24},{12,28},{16,0},{20,4},{24,8},{28,12},{1,17},{... | collective-permute-start | bytes 110600 | tf_op jit(solution)/shard_map/ppermute | solution.py:51
  345.9 18.9 %collective-permute-start.53 = (bf16[2,2,1,128,512]{4,3,2,1,0:T(8,128)(2,1)}, bf16[2,2,1,128,512]{4,3,2,1,0:T(8,128)(2,1)}, u32[]{:S(2)}, u32[]{:S(2)}) collective-permute-start(bf16[2,2,1,128,512]{4,3,2,1,0:T(8,128)(2,1)} %constant_dynamic-slice_fusion.9), channel_id=1, source_target_pairs={{0,4},{4,0},{8,12},{12,8},{16,20},{20,16},{24,28},{28,24},{1,5},{5... | collective-permute-start | bytes 1572872 | tf_op jit(solution)/shard_map/ppermute | solution.py:51
  347.1 24.9 %collective-permute-start.52 = (bf16[2,2,1,128,512]{4,3,2,1,0:T(8,128)(2,1)}, bf16[2,2,1,128,512]{4,3,2,1,0:T(8,128)(2,1)}, u32[]{:S(2)}, u32[]{:S(2)}) collective-permute-start(bf16[2,2,1,128,512]{4,3,2,1,0:T(8,128)(2,1)} %constant_dynamic-slice_fusion.10), channel_id=1, source_target_pairs={{0,4},{4,0},{8,12},{12,8},{16,20},{20,16},{24,28},{28,24},{1,5},{5... | collective-permute-start | bytes 1572872 | tf_op jit(solution)/shard_map/ppermute | solution.py:51
  353.3 14.1 %collective-permute-start.56 = (bf16[2,2,1,1,128,512]{5,4,1,3,2,0:T(8,128)(2,1)}, bf16[2,2,1,1,128,512]{5,4,1,3,2,0:T(8,128)(2,1)}, u32[]{:S(2)}, u32[]{:S(2)}) collective-permute-start(bf16[2,2,1,1,128,512]{5,4,1,3,2,0:T(8,128)(2,1)} %pad_maximum_fusion.15), channel_id=1, source_target_pairs={{0,8},{4,12},{8,0},{12,4},{16,24},{20,28},{24,16},{28,20},{1,9},{5... | collective-permute-start | bytes 1572872 | tf_op jit(solution)/shard_map/ppermute | solution.py:51
  366.8 15.4 %collective-permute-start.55 = (bf16[2,2,1,128,512]{4,3,2,1,0:T(8,128)(2,1)}, bf16[2,2,1,128,512]{4,3,2,1,0:T(8,128)(2,1)S(1)}, u32[]{:S(2)}, u32[]{:S(2)}) collective-permute-start(bf16[2,2,1,128,512]{4,3,2,1,0:T(8,128)(2,1)} %add_convert_fusion.11), channel_id=1, source_target_pairs={{0,2},{1,3},{2,0},{3,1},{4,6},{5,7},{6,4},{7,5},{8,10},{9,11},{10,... | collective-permute-start | bytes 1572872 | tf_op jit(solution)/shard_map/ppermute | solution.py:51
  372.0 22.3 %collective-permute-start.59 = (bf16[512,1024]{1,0:T(8,128)(2,1)}, bf16[512,1024]{1,0:T(8,128)(2,1)}, u32[]{:S(2)}, u32[]{:S(2)}) collective-permute-start(bf16[512,1024]{1,0:T(8,128)(2,1)} %inputs_back.2), channel_id=1, source_target_pairs={{0,1},{1,0},{2,3},{3,2},{4,5},{5,4},{6,7},{7,6},{8,9},{9,8},{10,11... | collective-permute-start | bytes 3145736 | tf_op jit(solution)/shard_map/ppermute | solution.py:51
  372.9 15.0 %collective-permute-start.54 = (bf16[2,2,1,128,512]{4,3,0,2,1:T(8,128)(2,1)}, bf16[2,2,1,128,512]{4,3,0,2,1:T(8,128)(2,1)}, u32[]{:S(2)}, u32[]{:S(2)}) collective-permute-start(bf16[2,2,1,128,512]{4,3,0,2,1:T(8,128)(2,1)} %copy.324), channel_id=1, source_target_pairs={{0,4},{4,0},{8,12},{12,8},{16,20},{20,16},{24,28},{28,24},{1,5},{5... | collective-permute-start | bytes 1572872 | tf_op jit(solution)/shard_map/ppermute | solution.py:51
  374.0 15.1 %collective-permute-start.58 = (f32[9216]{0:T(1024)S(1)}, f32[9216]{0:T(1024)S(1)}, u32[]{:S(2)}, u32[]{:S(2)}) collective-permute-start(f32[9216]{0:T(1024)S(1)} %add.266), channel_id=1, source_target_pairs={{0,4},{4,0},{8,12},{12,8},{16,20},{20,16},{24,28},{28,24},{1,5},{5... | collective-permute-start | bytes 110600 | tf_op jit(solution)/shard_map/ppermute | solution.py:51
  391.4 12.6 %collective-permute-start.62 = (bf16[2,2,1,1,128,512]{5,4,1,3,2,0:T(8,128)(2,1)S(1)}, bf16[2,2,1,1,128,512]{5,4,1,3,2,0:T(8,128)(2,1)S(1)}, u32[]{:S(2)}, u32[]{:S(2)}) collective-permute-start(bf16[2,2,1,1,128,512]{5,4,1,3,2,0:T(8,128)(2,1)S(1)} %pad_maximum_fusion.16), channel_id=1, source_target_pairs={{0,8},{4,12},{8,0},{12,4},{16,24},{20,28},{24,16},{28,20},{1,9},{5... | collective-permute-start | bytes 1572872 | tf_op jit(solution)/shard_map/ppermute | solution.py:51
  394.3 17.5 %collective-permute-start.66 = (f32[6,256]{1,0:T(8,128)S(1)}, f32[6,256]{1,0:T(8,128)S(1)}, u32[]{:S(2)}, u32[]{:S(2)}) collective-permute-start(f32[6,256]{1,0:T(8,128)S(1)} %constant_dynamic-slice_fusion.2), channel_id=1, source_target_pairs={{0,1},{1,0},{2,3},{3,2},{4,5},{5,4},{6,7},{7,6},{8,9},{9,8},{10,11... | collective-permute-start | bytes 18440 | tf_op jit(solution)/shard_map/ppermute | solution.py:51
  396.9 14.5 %collective-permute-start.60 = (bf16[512,512]{1,0:T(8,128)(2,1)S(1)}, bf16[512,512]{1,0:T(8,128)(2,1)S(1)}, u32[]{:S(2)}, u32[]{:S(2)}) collective-permute-start(bf16[512,512]{1,0:T(8,128)(2,1)S(1)} %constant_dynamic-slice_fusion.6), channel_id=1, source_target_pairs={{0,2},{1,3},{2,0},{3,1},{4,6},{5,7},{6,4},{7,5},{8,10},{9,11},{10,... | collective-permute-start | bytes 1572872 | tf_op jit(solution)/shard_map/ppermute | solution.py:51
  405.5 12.6 %collective-permute-start.63 = (bf16[2,1,1,1,128,512]{5,4,3,2,1,0:T(8,128)(2,1)S(1)}, bf16[2,1,1,1,128,512]{5,4,3,2,1,0:T(8,128)(2,1)S(1)}, u32[]{:S(2)}, u32[]{:S(2)}) collective-permute-start(bf16[2,1,1,1,128,512]{5,4,3,2,1,0:T(8,128)(2,1)S(1)} %pad_maximum_fusion.22), channel_id=1, source_target_pairs={{0,16},{4,20},{8,24},{12,28},{16,0},{20,4},{24,8},{28,12},{1,17},{... | collective-permute-start | bytes 786440 | tf_op jit(solution)/shard_map/ppermute | solution.py:51
  (77 other events, 519.5 us)

commit v7 on v6

--- a/solution.py
+++ b/solution.py
@@ -223,7 +223,7 @@
     outs = [struct((slabs, length, 3 * lanes), BF16), struct((slabs, 2, lanes), F32)]
     return launch(
         attend_back_kernel, slabs, [windows], operands, specs, outs, [slab(a) for a in outs],
-        [pltpu.VMEM((length, lanes), F32)] * 2, 60 * slabs * length * 640 * lanes, "attend_back",
+        [pltpu.VMEM((length, lanes), F32)] * 2, 6 * slabs * length * 640 * lanes, "attend_back",
     )
 
 

time: 429 us -> 425 us (level)
  waiting for transfers between devices: 53.5 us -> 48 us
  Pallas kernels: 190 us -> 195 us
    pallas_call x27, Pallas kernels: 190 us -> 195 us  [launch(): pl.pallas_call(kernel, grid_spec=pltpu.PrefetchScalarGridSpec(num_scalar_...]
    ppermute x53, waiting for transfers between devices: 45.8 us -> 40.7 us  [trade(): return lax.ppermute(block, self.axis, self.pairs)]
    unnamed x124 -> x130, local copies, waits for them, and re-layouts: 15 us -> 15 us
  transfers between devices with their start and end apart: 69 -> 69, of which waited for: 21 -> 20; matrix products, arithmetic and copies ran while one was open for 20% -> 20% of each run, Pallas kernels for 36% -> 38%
where the time goes in v7:
time: 425 us; the launch traced here: 419 us
  Pallas kernels  195 us (46%)
  starting transfers between devices  77.9 us (18%)
  other arithmetic  58.5 us (14%)
  waiting for transfers between devices  48 us (11%)
  local copies, waits for them, and re-layouts  37 us (9%)
    pallas_call x27, Pallas kernels, launch(): pl.pallas_call(kernel, grid_spec=pltpu.PrefetchScalarGridSpec(num_scalar_...  195 us
    ppermute x53, starting transfers between devices, trade(): return lax.ppermute(block, self.axis, self.pairs)  48.9 us
    ppermute x53, waiting for transfers between devices, trade(): return lax.ppermute(block, self.axis, self.pairs)  40.7 us
    ppermute x16, starting transfers between devices, turn(): lax.ppermute(block, 'row', [(i, (i + 2 * step) % rows) for i in range(row...  28.9 us
    unnamed x130, local copies, waits for them, and re-layouts  15 us
    convert_element_type x13, other arithmetic, add(): return (mine.astype(F32) + other.astype(F32)).astype(mine.dtype)  13.1 us
  transfers between devices with their start and end apart: 69, of which 20 were waited for; matrix products, arithmetic and copies ran while one was open for 20% of the time, Pallas kernels for 38%

profile of v7, /device:TPU:0, one launch (start us, length us, event | category | flops | bytes accessed | tf_op | source)
XLA Modules:
  0.0 418.8 jit_solution(616716448093380029)
XLA Ops:
  2.2 3.1 collective-permute-start.6
  5.3 2.1 collective-permute-start.5
  18.2 3.8 collective-permute-start.8
  25.3 4.3 %collective-permute-start.14 = (bf16[2,128,640]{2,1,0:T(8,128)(2,1)S(1)}, bf16[2,128,640]{2,1,0:T(8,128)(2,1)S(1)}, u32[]{:S(2)}, u32[]{:S(2)}) collective-permute-start(bf16[2,128,640]{2,1,0:T(8,128)(2,1)S(1)} %pad_maximum_fusion.18.refs_0_), channel_id=1, source_target_pairs={{0,24},{4,28},{8,0},{12,4},{16,8},{20,12},{24,16},{28,20},{1,25},{... | collective-permute-start | bytes 983048 | tf_op jit(solution)/shard_map/ppermute | solution.py:726
  29.5 2.2 assemble.3
  43.2 2.6 collective-permute-done.4
  45.8 3.2 collective-permute-start.17
  52.6 2.5 assemble.4
  56.1 3.5 collective-permute-start.23
  65.6 4.6 %collective-permute-done.13 = bf16[2,2,1,128,384]{4,3,2,1,0:T(8,128)(2,1)S(1)} collective-permute-done((bf16[2,2,1,128,384]{4,3,2,1,0:T(8,128)(2,1)}, bf16[2,2,1,128,384]{4,3,2,1,0:T(8,128)(2,1)S(1)}, u32[]{:S(2)}, u32[]{:S(2)}) %collective-permute-start.13) | collective-permute-done | bytes 393248 | tf_op jit(solution)/shard_map/ppermute | solution.py:51
  77.7 3.5 collective-permute-done.11.refs_2_.refs_4_
  82.7 8.4 %project.1 = (bf16[4,1024,128]{2,1,0:T(8,128)(2,1)}, bf16[4,1024,128]{2,1,0:T(8,128)(2,1)}, bf16[4,1024,128]{2,1,0:T(8,128)(2,1)}) custom-call(bf16[1024,1024]{1,0:T(8,128)(2,1)} %pad_maximum_fusion.x_ref.refs_0_, f32[4,1,384]{2,1,0:T(1,128)} %reshape.535.b_ref, bf16[1024,384]{1,0:T(8,128)(2,1)} %bitcast.258, bf16[1024,384]{1,0:T(8,128)(2,1)} %bitcast.261, ...), custom_call_target="tpu_custom_call" | custom-call | flops 3221225472 | bytes 8394752 | tf_op jit(solution)/shard_map/project/pallas_call | solution.py:188
  91.1 11.4 %attend.2 = (bf16[2,1024,128]{2,1,0:T(8,128)(2,1)}, f32[2,2,1024]{2,1,0:T(2,128)}) custom-call(s32[2,4]{1,0:T(2,128)} %pad_add_fusion.windows, bf16[4,1024,128]{2,1,0:T(8,128)(2,1)} %get-tuple-element.136.q_ref, bf16[4,1024,128]{2,1,0:T(8,128)(2,1)} %get-tuple-element.126.k_ref, bf16[4,1024,128]{2,1,0:T(8,128)(2,1)} %get-tuple-element.127.v_ref, ...), custom_call_target="tpu_custom_call" | custom-call | flops 6710886400 | bytes 3694592 | tf_op jit(solution)/shard_map/attend/pallas_call | solution.py:188
  106.7 11.4 %attend.3 = (bf16[2,1024,128]{2,1,0:T(8,128)(2,1)}, f32[2,2,1024]{2,1,0:T(2,128)}) custom-call(s32[2,4]{1,0:T(2,128)} %pad_add_fusion.windows, bf16[4,1024,128]{2,1,0:T(8,128)(2,1)} %get-tuple-element.136.q_ref, bf16[4,1024,128]{2,1,0:T(8,128)(2,1)} %get-tuple-element.126.k_ref, bf16[4,1024,128]{2,1,0:T(8,128)(2,1)} %get-tuple-element.127.v_ref, ...), custom_call_target="tpu_custom_call" | custom-call | flops 6710886400 | bytes 3694592 | tf_op jit(solution)/shard_map/attend/pallas_call | solution.py:188
  120.6 6.0 %collective-permute-done.25.refs_4_.refs_2_.refs_6_ = bf16[1024,640]{1,0:T(8,128)(2,1)S(1)} collective-permute-done((bf16[1024,640]{1,0:T(8,128)(2,1)S(1)}, bf16[1024,640]{1,0:T(8,128)(2,1)S(1)}, u32[]{:S(2)}, u32[]{:S(2)}) %collective-permute-start.25) | collective-permute-done | bytes 1310752 | tf_op jit(solution)/shard_map/ppermute | solution.py:51
  127.8 4.0 context_out.3
  137.3 4.0 context_out.2.mine_ref
  142.3 4.5 %norm_a.1 = (f32[512,1024]{1,0:T(8,128)}, f32[512,1]{1,0:T(8,128)}, bf16[512,1024]{1,0:T(8,128)(2,1)}) custom-call(s32[4]{0:T(128)} %add_add_fusion.at_ref.at, f32[512,1024]{1,0:T(8,128)} %context_out.2.mine_ref, bf16[512,1024]{1,0:T(8,128)(2,1)} %copy-done.25, bf16[1024,1024]{1,0:T(8,128)(2,1)} %pad_maximum_fusion.x_ref.refs_0_, ...), custom_call_target="tpu_custom_call" | custom-call | flops 10485760 | bytes 8415232 | tf_op jit(solution)/shard_map/norm_a/pallas_call | solution.py:188
  149.8 2.5 collective-permute-start.30
  152.3 8.1 %ffn_in.2 = (bf16[4,1024,512]{2,1,0:T(8,128)(2,1)}, bf16[4,1024,512]{2,1,0:T(8,128)(2,1)}) custom-call(s32[4]{0:T(128)} %add_add_fusion.at_ref.at, bf16[512,1024]{1,0:T(8,128)(2,1)} %get-tuple-element.145.y_ref.refs_0_, f32[4,1,512]{2,1,0:T(1,128)} %maximum_convert_fusion.2.b_ref, bf16[1024,640]{1,0:T(8,128)(2,1)} %bitcast.238, bf16[1024,640]{1,0:T(8,128)(2,1)} %bitcast.245, ...), custom_call_target="tpu_custom_call" | custom-call | flops 6442450944 | bytes 14688256 | tf_op jit(solution)/shard_map/ffn_in/pallas_call | solution.py:188
  161.4 8.2 %ffn_in.3 = (bf16[4,1024,512]{2,1,0:T(8,128)(2,1)}, bf16[4,1024,512]{2,1,0:T(8,128)(2,1)}) custom-call(s32[4]{0:T(128)} %add_add_fusion.at_ref.at, bf16[512,1024]{1,0:T(8,128)(2,1)} %copy-done.52, f32[4,1,512]{2,1,0:T(1,128)} %maximum_convert_fusion.2.b_ref, bf16[1024,640]{1,0:T(8,128)(2,1)} %bitcast.239, ...), custom_call_target="tpu_custom_call", output_to_operand_aliasing={{0}: (7, {}), {1}: (8, {})} | custom-call | flops 6442450944 | bytes 23076864 | tf_op jit(solution)/shard_map/ffn_in/pallas_call | solution.py:188
  170.4 3.1 collective-permute-done.31.refs_3_
  175.6 4.2 %assemble.5 = (bf16[4,2,2,128,512]{4,3,2,1,0:T(8,128)(2,1)}, bf16[4,2,2,128,512]{4,3,2,1,0:T(8,128)(2,1)}) custom-call(s32[1]{0:T(128)} %bitcast.3.place_ref, bf16[2,2,2,128,512]{4,3,2,1,0:T(8,128)(2,1)} %pad_maximum_fusion.6.refs_0_, bf16[2,2,2,128,512]{4,3,2,1,0:T(8,128)(2,1)} %collective-permute-done.23.refs_1_, bf16[2,2,128,512]{3,2,1,0:T(8,128)(2,1)} %copy-done.34, ...), custom_call_target="tpu_custom_call" | custom-call | bytes 8388608 | tf_op jit(solution)/shard_map/assemble/pallas_call | solution.py:188
  179.9 6.6 %ffn_out.3 = bf16[512,1024]{1,0:T(8,128)(2,1)} custom-call(s32[4]{0:T(128)} %add_add_fusion.at_ref.at, bf16[4,1024,512]{2,1,0:T(8,128)(2,1)} %get-tuple-element.148.act_ref.refs_2_, bf16[8,2,128,512]{3,2,1,0:T(8,128)(2,1)} %bitcast.219, bf16[8,2,128,512]{3,2,1,0:T(8,128)(2,1)} %bitcast.227, bf16[8,2,128,512]{3,2,1,0:T(8,128)(2,1)} %bitcast.220, ...), custom_call_target="tpu_custom_call" | custom-call | flops 2147483648 | bytes 13631488 | tf_op jit(solution)/shard_map/ffn_out/pallas_call | solution.py:188
  187.2 6.8 %ffn_out.2.mine_ref = f32[512,1024]{1,0:T(8,128)} custom-call(s32[4]{0:T(128)} %add_add_fusion.at_ref.at, bf16[4,1024,512]{2,1,0:T(8,128)(2,1)} %get-tuple-element.148.act_ref.refs_2_, bf16[8,2,128,512]{3,2,1,0:T(8,128)(2,1)} %bitcast.221, bf16[8,2,128,512]{3,2,1,0:T(8,128)(2,1)} %bitcast.229, bf16[8,2,128,512]{3,2,1,0:T(8,128)(2,1)} %bitcast.222, ...), custom_call_target="tpu_custom_call" | custom-call | flops 2147483648 | bytes 14680064 | tf_op jit(solution)/shard_map/ffn_out/pallas_call | solution.py:188
  196.2 5.4 %norm_b.1 = (bf16[512,1024]{1,0:T(8,128)(2,1)}, f32[512,1024]{1,0:T(8,128)}, bf16[512,1024]{1,0:T(8,128)(2,1)}, f32[3,1024]{1,0:T(4,128)}) custom-call(f32[512,1024]{1,0:T(8,128)} %ffn_out.2.mine_ref, bf16[512,1024]{1,0:T(8,128)(2,1)} %copy-done.26, f32[512,1024]{1,0:T(8,128)} %get-tuple-element.158.centred_a_ref.centred_ref, ...), custom_call_target="tpu_custom_call" | custom-call | flops 20971520 | bytes 10522624 | tf_op jit(solution)/shard_map/norm_b/pallas_call | solution.py:188
  205.5 9.6 %weight_grad_shards.1 = (bf16[2,128,1024]{2,1,0:T(8,128)(2,1)}, bf16[2,128,1024]{2,1,0:T(8,128)(2,1)}, bf16[2,2,128,1024]{3,2,1,0:T(8,128)(2,1)}, bf16[2,2,128,1...) custom-call(s32[4]{0:T(128)} %add_add_fusion.at_ref.at, bf16[512,1024]{1,0:T(8,128)(2,1)} %get-tuple-element.166.refs_0_.gb_ref, ...), custom_call_target="tpu_custom_call" | custom-call | flops 4294967296 | bytes 10485760 | tf_op jit(solution)/shard_map/weight_grad_shards/pallas_call | solution.py:188
  217.3 11.2 %ffn_back.2 = (bf16[4,1024,512]{2,1,0:T(8,128)(2,1)}, f32[4,1,512]{2,1,0:T(1,128)}, f32[512,1024]{1,0:T(8,128)}) custom-call(s32[4]{0:T(128)} %add_add_fusion.at_ref.at, bf16[512,1024]{1,0:T(8,128)(2,1)} %get-tuple-element.166.refs_0_.gb_ref, bf16[4,1024,512]{2,1,0:T(8,128)(2,1)} %get-tuple-element.167.slope_ref, bf16[8,2,128,512]{3,2,1,0:T(8,128)(2,1)} %bitcast.223, ...), custom_call_target="tpu_custom_call" | custom-call | flops 4294967296 | bytes 25174016 | tf_op jit(solution)/shard_map/ffn_back/pallas_call | solution.py:188
  228.5 11.2 %ffn_back.3 = (bf16[4,1024,512]{2,1,0:T(8,128)(2,1)}, f32[4,1,512]{2,1,0:T(1,128)}, bf16[512,1024]{1,0:T(8,128)(2,1)}) custom-call(s32[4]{0:T(128)} %add_add_fusion.at_ref.at, bf16[512,1024]{1,0:T(8,128)(2,1)} %copy-done.9, bf16[4,1024,512]{2,1,0:T(8,128)(2,1)} %get-tuple-element.167.slope_ref, ...), custom_call_target="tpu_custom_call", output_to_operand_aliasing={{0}: (11, {})} | custom-call | flops 4294967296 | bytes 28319744 | tf_op jit(solution)/shard_map/ffn_back/pallas_call | solution.py:188
  245.0 2.6 collective-permute-start.46
  247.6 8.3 %weight_grad.3 = (bf16[1024,512]{1,0:T(8,128)(2,1)}, bf16[1024,512]{1,0:T(8,128)(2,1)}, bf16[1024,512]{1,0:T(8,128)(2,1)}, bf16[1024,512]{1,0:T(8,128)(2,1)}) custom-call(bf16[512,1024]{1,0:T(8,128)(2,1)} %get-tuple-element.145.y_ref.refs_0_, bf16[512,1024]{1,0:T(8,128)(2,1)} %copy-done.52, bf16[4,1024,512]{2,1,0:T(8,128)(2,1)} %get-tuple-element.176.refs_2_), custom_call_target="tpu_custom_call" | custom-call | flops 4294967296 | bytes 10485760 | tf_op jit(solution)/shard_map/weight_grad/pallas_call | solution.py:188
  258.4 5.5 %norm_a_back.1 = (f32[512,1024]{1,0:T(8,128)}, bf16[512,1024]{1,0:T(8,128)(2,1)}, f32[3,1024]{1,0:T(4,128)}) custom-call(f32[512,1024]{1,0:T(8,128)} %get-tuple-element.168.mine_ref, bf16[512,1024]{1,0:T(8,128)(2,1)} %collective-permute-done.38.got_ref, f32[512,1024]{1,0:T(8,128)} %get-tuple-element.178.gb_ref, ...), custom_call_target="tpu_custom_call" | custom-call | flops 15728640 | bytes 10524672 | tf_op jit(solution)/shard_map/norm_a_back/pallas_call | solution.py:188
  275.9 4.7 %context_back.1.do_ref = bf16[4,1024,128]{2,1,0:T(8,128)(2,1)} custom-call(s32[4]{0:T(128)} %add_add_fusion.at_ref.at, bf16[1024,1024]{1,0:T(8,128)(2,1)} %pad_maximum_fusion.1.ga_ref.refs_1_, bf16[1024,640]{1,0:T(8,128)(2,1)} %bitcast.242, bf16[1024,640]{1,0:T(8,128)(2,1)} %bitcast.249, bf16[1024,640]{1,0:T(8,128)(2,1)} %copy-done.3, ...), custom_call_target="tpu_custom_call" | custom-call | flops 1073741824 | bytes 8388608 | tf_op jit(solution)/shard_map/context_back/pallas_call | solution.py:188
  280.6 13.4 %attend_back.2 = (bf16[2,1024,384]{2,1,0:T(8,128)(2,1)}, f32[2,2,128]{2,1,0:T(2,128)}) custom-call(s32[2,4]{1,0:T(2,128)} %pad_add_fusion.windows, bf16[4,1024,128]{2,1,0:T(8,128)(2,1)} %get-tuple-element.136.q_ref, bf16[4,1024,128]{2,1,0:T(8,128)(2,1)} %get-tuple-element.126.k_ref, bf16[4,1024,128]{2,1,0:T(8,128)(2,1)} %get-tuple-element.127.v_ref, ...), custom_call_target="tpu_custom_call" | custom-call | flops 1006632960 | bytes 5793792 | tf_op jit(solution)/shard_map/attend_back/pallas_call | solution.py:188
  294.5 7.6 %weight_grad.4 = (bf16[1024,512]{1,0:T(8,128)(2,1)}, bf16[1024,512]{1,0:T(8,128)(2,1)}) custom-call(bf16[1024,1024]{1,0:T(8,128)(2,1)} %pad_maximum_fusion.x_ref.refs_0_, bf16[1024,1024]{1,0:T(8,128)(2,1)} %pad_maximum_fusion.1.ga_ref.refs_1_, bf16[2,1024,384]{2,1,0:T(8,128)(2,1)} %get-tuple-element.213.refs_2_.refs_1_, ...), custom_call_target="tpu_custom_call" | custom-call | flops 2147483648 | bytes 8388608 | tf_op jit(solution)/shard_map/weight_grad/pallas_call | solution.py:188
  303.3 2.5 add_convert_fusion
  311.8 13.9 %attend_back.3 = (bf16[2,1024,384]{2,1,0:T(8,128)(2,1)}, f32[2,2,128]{2,1,0:T(2,128)}) custom-call(s32[2,4]{1,0:T(2,128)} %pad_add_fusion.windows, bf16[4,1024,128]{2,1,0:T(8,128)(2,1)} %get-tuple-element.136.q_ref, bf16[4,1024,128]{2,1,0:T(8,128)(2,1)} %get-tuple-element.126.k_ref, bf16[4,1024,128]{2,1,0:T(8,128)(2,1)} %get-tuple-element.127.v_ref, ...), custom_call_target="tpu_custom_call" | custom-call | flops 1006632960 | bytes 5793792 | tf_op jit(solution)/shard_map/attend_back/pallas_call | solution.py:188
  326.7 2.2 collective-permute-start.50
  328.9 7.3 %weight_grad.5 = (bf16[1024,512]{1,0:T(8,128)(2,1)}, bf16[1024,512]{1,0:T(8,128)(2,1)}) custom-call(bf16[1024,1024]{1,0:T(8,128)(2,1)} %pad_maximum_fusion.x_ref.refs_0_, bf16[1024,1024]{1,0:T(8,128)(2,1)} %pad_maximum_fusion.1.ga_ref.refs_1_, bf16[2,1024,384]{2,1,0:T(8,128)(2,1)} %get-tuple-element.212.refs_2_.refs_0_, ...), custom_call_target="tpu_custom_call" | custom-call | flops 2147483648 | bytes 8388608 | tf_op jit(solution)/shard_map/weight_grad/pallas_call | solution.py:188
  342.1 2.2 collective-permute-start.53
  354.7 6.5 %inputs_back.2 = bf16[512,1024]{1,0:T(8,128)(2,1)} custom-call(s32[4]{0:T(128)} %add_add_fusion.1.at_ref, bf16[2,1024,384]{2,1,0:T(8,128)(2,1)} %get-tuple-element.212.refs_2_.refs_0_, bf16[2,1024,384]{2,1,0:T(8,128)(2,1)} %get-tuple-element.213.refs_2_.refs_1_, bf16[1024,384]{1,0:T(8,128)(2,1)} %bitcast.259, bf16[1024,384]{1,0:T(8,128)(2,1)} %bitcast.262, ...), custom_call_target="tpu_custom_call" | custom-call | flops 1610612736 | bytes 7340032 | tf_op jit(solution)/shard_map/inputs_back/pallas_call | solution.py:188
  370.8 6.3 %inputs_back.3 = f32[512,1024]{1,0:T(8,128)} custom-call(s32[4]{0:T(128)} %add_add_fusion.at_ref.at, bf16[2,1024,384]{2,1,0:T(8,128)(2,1)} %get-tuple-element.212.refs_2_.refs_0_, bf16[2,1024,384]{2,1,0:T(8,128)(2,1)} %get-tuple-element.213.refs_2_.refs_1_, bf16[1024,384]{1,0:T(8,128)(2,1)} %bitcast.260, bf16[1024,384]{1,0:T(8,128)(2,1)} %bitcast.263, ...), custom_call_target="tpu_custom_call" | custom-call | flops 1610612736 | bytes 8388608 | tf_op jit(solution)/shard_map/inputs_back/pallas_call | solution.py:188
  379.8 4.0 collective-permute-done.54
  391.1 2.5 add_convert_fusion.1
  394.7 5.2 %collective-permute-done.62 = bf16[2,2,1,1,128,512]{5,4,1,3,2,0:T(8,128)(2,1)S(1)} collective-permute-done((bf16[2,2,1,1,128,512]{5,4,1,3,2,0:T(8,128)(2,1)S(1)}, bf16[2,2,1,1,128,512]{5,4,1,3,2,0:T(8,128)(2,1)S(1)}, u32[]{:S(2)}, u32[]{:S(2)}) %collective-permute-start.62) | collective-permute-done | bytes 524320 | tf_op jit(solution)/shard_map/ppermute | solution.py:51
  401.5 3.0 collective-permute-start.63
  404.4 3.6 collective-permute-done.60
  409.0 5.3 %collective-permute-done.63 = bf16[2,1,1,1,128,512]{5,4,3,2,1,0:T(8,128)(2,1)S(1)} collective-permute-done((bf16[2,1,1,1,128,512]{5,4,3,2,1,0:T(8,128)(2,1)S(1)}, bf16[2,1,1,1,128,512]{5,4,3,2,1,0:T(8,128)(2,1)S(1)}, u32[]{:S(2)}, u32[]{:S(2)}) %collective-permute-start.63) | collective-permute-done | bytes 262176 | tf_op jit(solution)/shard_map/ppermute | solution.py:51
  (416 shorter events, 148.0 us)
Async XLA Ops:
  2.2 15.9 %collective-permute-start.6 = (bf16[2,128,384]{2,1,0:T(8,128)(2,1)S(1)}, bf16[2,128,384]{2,1,0:T(8,128)(2,1)S(1)}, u32[]{:S(2)}, u32[]{:S(2)}) collective-permute-start(bf16[2,128,384]{2,1,0:T(8,128)(2,1)S(1)} %copy.284.refs_0_), channel_id=1, source_target_pairs={{0,8},{4,12},{8,16},{12,20},{16,24},{20,28},{24,0},{28,4},{1,9},{5... | collective-permute-start | bytes 589832 | tf_op jit(solution)/shard_map/ppermute | solution.py:726
  5.3 12.9 %collective-permute-start.5 = (bf16[2,128,384]{2,1,0:T(8,128)(2,1)S(1)}, bf16[2,128,384]{2,1,0:T(8,128)(2,1)S(1)}, u32[]{:S(2)}, u32[]{:S(2)}) collective-permute-start(bf16[2,128,384]{2,1,0:T(8,128)(2,1)S(1)} %copy.284.refs_0_), channel_id=1, source_target_pairs={{0,24},{4,28},{8,0},{12,4},{16,8},{20,12},{24,16},{28,20},{1,25},{... | collective-permute-start | bytes 589832 | tf_op jit(solution)/shard_map/ppermute | solution.py:726
  16.0 15.7 %collective-permute-start.20 = (bf16[2,1,128,512]{3,2,1,0:T(8,128)(2,1)}, bf16[2,1,128,512]{3,2,1,0:T(8,128)(2,1)}, u32[]{:S(2)}, u32[]{:S(2)}) collective-permute-start(bf16[2,1,128,512]{3,2,1,0:T(8,128)(2,1)} %pad_maximum_fusion.19), channel_id=1, source_target_pairs={{0,2},{1,3},{2,0},{3,1},{4,6},{5,7},{6,4},{7,5},{8,10},{9,11},{10,... | collective-permute-start | bytes 786440 | tf_op jit(solution)/shard_map/ppermute | solution.py:51
  17.5 15.7 %collective-permute-start.21 = (bf16[1,2,128,512]{3,2,1,0:T(8,128)(2,1)S(1)}, bf16[1,2,128,512]{3,2,1,0:T(8,128)(2,1)}, u32[]{:S(2)}, u32[]{:S(2)}) collective-permute-start(bf16[1,2,128,512]{3,2,1,0:T(8,128)(2,1)S(1)} %pad_maximum_fusion.20), channel_id=1, source_target_pairs={{0,4},{4,0},{8,12},{12,8},{16,20},{20,16},{24,28},{28,24},{1,5},{5... | collective-permute-start | bytes 786440 | tf_op jit(solution)/shard_map/ppermute | solution.py:51
  22.9 17.1 %collective-permute-start.2 = (bf16[1024,256]{1,0:T(8,128)(2,1)}, bf16[1024,256]{1,0:T(8,128)(2,1)}, u32[]{:S(2)}, u32[]{:S(2)}) collective-permute-start(bf16[1024,256]{1,0:T(8,128)(2,1)} %dynamic-slice_bitcast_fusion.3), channel_id=1, source_target_pairs={{0,2},{1,3},{2,0},{3,1},{4,6},{5,7},{6,4},{7,5},{8,10},{9,11},{10,... | collective-permute-start | bytes 1572872 | tf_op jit(solution)/shard_map/ppermute | solution.py:51
  24.9 12.2 %collective-permute-start.15 = (bf16[2,128,640]{2,1,0:T(8,128)(2,1)S(1)}, bf16[2,128,640]{2,1,0:T(8,128)(2,1)S(1)}, u32[]{:S(2)}, u32[]{:S(2)}) collective-permute-start(bf16[2,128,640]{2,1,0:T(8,128)(2,1)S(1)} %pad_maximum_fusion.18.refs_0_), channel_id=1, source_target_pairs={{0,8},{4,12},{8,16},{12,20},{16,24},{20,28},{24,0},{28,4},{1,9},{5... | collective-permute-start | bytes 983048 | tf_op jit(solution)/shard_map/ppermute | solution.py:726
  25.3 13.5 %collective-permute-start.14 = (bf16[2,128,640]{2,1,0:T(8,128)(2,1)S(1)}, bf16[2,128,640]{2,1,0:T(8,128)(2,1)S(1)}, u32[]{:S(2)}, u32[]{:S(2)}) collective-permute-start(bf16[2,128,640]{2,1,0:T(8,128)(2,1)S(1)} %pad_maximum_fusion.18.refs_0_), channel_id=1, source_target_pairs={{0,24},{4,28},{8,0},{12,4},{16,8},{20,12},{24,16},{28,20},{1,25},{... | collective-permute-start | bytes 983048 | tf_op jit(solution)/shard_map/ppermute | solution.py:726
  31.7 29.0 %collective-permute-start.12 = (bf16[2,2,1,128,384]{4,3,2,1,0:T(8,128)(2,1)}, bf16[2,2,1,128,384]{4,3,2,1,0:T(8,128)(2,1)}, u32[]{:S(2)}, u32[]{:S(2)}) collective-permute-start(bf16[2,2,1,128,384]{4,3,2,1,0:T(8,128)(2,1)} %bitcast.287), channel_id=1, source_target_pairs={{0,2},{1,3},{2,0},{3,1},{4,6},{5,7},{6,4},{7,5},{8,10},{9,11},{10,... | collective-permute-start | bytes 1179656 | tf_op jit(solution)/shard_map/ppermute | solution.py:51
  33.2 28.7 %collective-permute-start.10 = (bf16[2,2,1,128,384]{4,3,2,1,0:T(8,128)(2,1)}, bf16[2,2,1,128,384]{4,3,2,1,0:T(8,128)(2,1)}, u32[]{:S(2)}, u32[]{:S(2)}) collective-permute-start(bf16[2,2,1,128,384]{4,3,2,1,0:T(8,128)(2,1)} %bitcast.288), channel_id=1, source_target_pairs={{0,4},{4,0},{8,12},{12,8},{16,20},{20,16},{24,28},{28,24},{1,5},{5... | collective-permute-start | bytes 1179656 | tf_op jit(solution)/shard_map/ppermute | solution.py:51
  37.1 19.0 %collective-permute-start.9 = (bf16[2,2,1,128,384]{4,3,2,1,0:T(8,128)(2,1)S(1)}, bf16[2,2,1,128,384]{4,3,2,1,0:T(8,128)(2,1)}, u32[]{:S(2)}, u32[]{:S(2)}) collective-permute-start(bf16[2,2,1,128,384]{4,3,2,1,0:T(8,128)(2,1)S(1)} %bitcast.290), channel_id=1, source_target_pairs={{0,4},{4,0},{8,12},{12,8},{16,20},{20,16},{24,28},{28,24},{1,5},{5... | collective-permute-start | bytes 1179656 | tf_op jit(solution)/shard_map/ppermute | solution.py:51
  49.9 23.3 %collective-permute-start.3 = (bf16[1024,512]{1,0:T(8,128)(2,1)}, bf16[1024,512]{1,0:T(8,128)(2,1)}, u32[]{:S(2)}, u32[]{:S(2)}) collective-permute-start(bf16[1024,512]{1,0:T(8,128)(2,1)} %pad_maximum_fusion.5), channel_id=1, source_target_pairs={{0,1},{1,0},{2,3},{3,2},{4,5},{5,4},{6,7},{7,6},{8,9},{9,8},{10,11... | collective-permute-start | bytes 3145736 | tf_op jit(solution)/shard_map/ppermute | solution.py:51
  55.1 63.0 %collective-permute-start.22 = (bf16[2,2,2,128,512]{4,3,2,1,0:T(8,128)(2,1)}, bf16[2,2,2,128,512]{4,3,2,1,0:T(8,128)(2,1)}, u32[]{:S(2)}, u32[]{:S(2)}) collective-permute-start(bf16[2,2,2,128,512]{4,3,2,1,0:T(8,128)(2,1)} %pad_maximum_fusion.6.refs_0_), channel_id=1, source_target_pairs={{0,8},{4,12},{8,16},{12,20},{16,24},{20,28},{24,0},{28,4},{1,9},{5... | collective-permute-start | bytes 3145736 | tf_op jit(solution)/shard_map/ppermute | solution.py:726
  56.1 62.1 %collective-permute-start.23 = (bf16[2,2,2,128,512]{4,3,2,1,0:T(8,128)(2,1)}, bf16[2,2,2,128,512]{4,3,2,1,0:T(8,128)(2,1)}, u32[]{:S(2)}, u32[]{:S(2)}) collective-permute-start(bf16[2,2,2,128,512]{4,3,2,1,0:T(8,128)(2,1)} %pad_maximum_fusion.6.refs_0_), channel_id=1, source_target_pairs={{0,24},{4,28},{8,0},{12,4},{16,8},{20,12},{24,16},{28,20},{1,25},{... | collective-permute-start | bytes 3145736 | tf_op jit(solution)/shard_map/ppermute | solution.py:726
  60.7 20.5 %collective-permute-start.11 = (bf16[1024,384]{1,0:T(8,128)(2,1)S(1)}, bf16[1024,384]{1,0:T(8,128)(2,1)S(1)}, u32[]{:S(2)}, u32[]{:S(2)}) collective-permute-start(bf16[1024,384]{1,0:T(8,128)(2,1)S(1)} %bitcast.257), channel_id=1, source_target_pairs={{0,2},{1,3},{2,0},{3,1},{4,6},{5,7},{6,4},{7,5},{8,10},{9,11},{10,... | collective-permute-start | bytes 2359304 | tf_op jit(solution)/shard_map/ppermute | solution.py:51
  70.3 35.1 %collective-permute-start.19 = (bf16[2,2,1,128,640]{4,3,2,1,0:T(8,128)(2,1)}, bf16[2,2,1,128,640]{4,3,2,1,0:T(8,128)(2,1)}, u32[]{:S(2)}, u32[]{:S(2)}) collective-permute-start(bf16[2,2,1,128,640]{4,3,2,1,0:T(8,128)(2,1)} %bitcast.38), channel_id=1, source_target_pairs={{0,2},{1,3},{2,0},{3,1},{4,6},{5,7},{6,4},{7,5},{8,10},{9,11},{10,... | collective-permute-start | bytes 1966088 | tf_op jit(solution)/shard_map/ppermute | solution.py:51
  73.2 30.7 %collective-permute-start.24 = (bf16[2,2,1,128,640]{4,3,2,1,0:T(8,128)(2,1)}, bf16[2,2,1,128,640]{4,3,2,1,0:T(8,128)(2,1)}, u32[]{:S(2)}, u32[]{:S(2)}) collective-permute-start(bf16[2,2,1,128,640]{4,3,2,1,0:T(8,128)(2,1)} %bitcast.44), channel_id=1, source_target_pairs={{0,4},{4,0},{8,12},{12,8},{16,20},{20,16},{24,28},{28,24},{1,5},{5... | collective-permute-start | bytes 1966088 | tf_op jit(solution)/shard_map/ppermute | solution.py:51
  81.2 21.3 %collective-permute-start.18 = (bf16[2,2,1,128,640]{4,3,2,1,0:T(8,128)(2,1)S(1)}, bf16[2,2,1,128,640]{4,3,2,1,0:T(8,128)(2,1)S(1)}, u32[]{:S(2)}, u32[]{:S(2)}) collective-permute-start(bf16[2,2,1,128,640]{4,3,2,1,0:T(8,128)(2,1)S(1)} %bitcast.285), channel_id=1, source_target_pairs={{0,4},{4,0},{8,12},{12,8},{16,20},{20,16},{24,28},{28,24},{1,5},{5... | collective-permute-start | bytes 1966088 | tf_op jit(solution)/shard_map/ppermute | solution.py:51
  102.8 23.8 %collective-permute-start.25 = (bf16[1024,640]{1,0:T(8,128)(2,1)S(1)}, bf16[1024,640]{1,0:T(8,128)(2,1)S(1)}, u32[]{:S(2)}, u32[]{:S(2)}) collective-permute-start(bf16[1024,640]{1,0:T(8,128)(2,1)S(1)} %bitcast.235), channel_id=1, source_target_pairs={{0,2},{1,3},{2,0},{3,1},{4,6},{5,7},{6,4},{7,5},{8,10},{9,11},{10,... | collective-permute-start | bytes 3932168 | tf_op jit(solution)/shard_map/ppermute | solution.py:51
  105.4 12.7 %collective-permute-start.26 = (bf16[2,2,1,128,640]{4,3,2,1,0:T(8,128)(2,1)}, bf16[2,2,1,128,640]{4,3,2,1,0:T(8,128)(2,1)S(1)}, u32[]{:S(2)}, u32[]{:S(2)}) collective-permute-start(bf16[2,2,1,128,640]{4,3,2,1,0:T(8,128)(2,1)} %collective-permute-done.19), channel_id=1, source_target_pairs={{0,4},{4,0},{8,12},{12,8},{16,20},{20,16},{24,28},{28,24},{1,5},{5... | collective-permute-start | bytes 1966088 | tf_op jit(solution)/shard_map/ppermute | solution.py:51
  136.2 33.4 %collective-permute-start.33 = (bf16[1024,256]{1,0:T(8,128)(2,1)}, bf16[1024,256]{1,0:T(8,128)(2,1)S(1)}, u32[]{:S(2)}, u32[]{:S(2)}) collective-permute-start(bf16[1024,256]{1,0:T(8,128)(2,1)} %dynamic-slice_bitcast_fusion.2), channel_id=1, source_target_pairs={{0,2},{1,3},{2,0},{3,1},{4,6},{5,7},{6,4},{7,5},{8,10},{9,11},{10,... | collective-permute-start | bytes 1572872 | tf_op jit(solution)/shard_map/ppermute | solution.py:51
  146.8 13.6 %collective-permute-start.29 = (bf16[512,1024]{1,0:T(8,128)(2,1)}, bf16[512,1024]{1,0:T(8,128)(2,1)S(1)}, u32[]{:S(2)}, u32[]{:S(2)}) collective-permute-start(bf16[512,1024]{1,0:T(8,128)(2,1)} %get-tuple-element.145.y_ref.refs_0_), channel_id=1, source_target_pairs={{0,1},{1,0},{2,3},{3,2},{4,5},{5,4},{6,7},{7,6},{8,9},{9,8},{10,11... | collective-permute-start | bytes 3145736 | tf_op jit(solution)/shard_map/ppermute | solution.py:51
  147.9 25.6 %collective-permute-start.31 = (bf16[2,2,128,512]{3,2,1,0:T(8,128)(2,1)S(1)}, bf16[2,2,128,512]{3,2,1,0:T(8,128)(2,1)S(1)}, u32[]{:S(2)}, u32[]{:S(2)}) collective-permute-start(bf16[2,2,128,512]{3,2,1,0:T(8,128)(2,1)S(1)} %slice_bitcast_fusion), channel_id=1, source_target_pairs={{0,24},{4,28},{8,0},{12,4},{16,8},{20,12},{24,16},{28,20},{1,25},{... | collective-permute-start | bytes 1572872 | tf_op jit(solution)/shard_map/ppermute | solution.py:726
  149.8 25.0 %collective-permute-start.30 = (bf16[2,2,128,512]{3,2,1,0:T(8,128)(2,1)}, bf16[2,2,128,512]{3,2,1,0:T(8,128)(2,1)S(1)}, u32[]{:S(2)}, u32[]{:S(2)}) collective-permute-start(bf16[2,2,128,512]{3,2,1,0:T(8,128)(2,1)} %slice_bitcast_fusion.1), channel_id=1, source_target_pairs={{0,8},{4,12},{8,16},{12,20},{16,24},{20,28},{24,0},{28,4},{1,9},{5... | collective-permute-start | bytes 1572872 | tf_op jit(solution)/shard_map/ppermute | solution.py:726
  215.1 27.6 %collective-permute-start.40 = (bf16[2,128,1024]{2,1,0:T(8,128)(2,1)}, bf16[2,128,1024]{2,1,0:T(8,128)(2,1)}, u32[]{:S(2)}, u32[]{:S(2)}) collective-permute-start(bf16[2,128,1024]{2,1,0:T(8,128)(2,1)} %get-tuple-element.175), channel_id=1, source_target_pairs={{0,24},{4,28},{8,0},{12,4},{16,8},{20,12},{24,16},{28,20},{1,25},{... | collective-permute-start | bytes 1572872 | tf_op jit(solution)/shard_map/ppermute | solution.py:726
  215.9 31.7 %collective-permute-start.39 = (bf16[2,128,1024]{2,1,0:T(8,128)(2,1)}, bf16[2,128,1024]{2,1,0:T(8,128)(2,1)S(1)}, u32[]{:S(2)}, u32[]{:S(2)}) collective-permute-start(bf16[2,128,1024]{2,1,0:T(8,128)(2,1)} %get-tuple-element.174), channel_id=1, source_target_pairs={{0,8},{4,12},{8,16},{12,20},{16,24},{20,28},{24,0},{28,4},{1,9},{5... | collective-permute-start | bytes 1572872 | tf_op jit(solution)/shard_map/ppermute | solution.py:726
  239.8 18.6 %collective-permute-start.38 = (bf16[512,1024]{1,0:T(8,128)(2,1)}, bf16[512,1024]{1,0:T(8,128)(2,1)}, u32[]{:S(2)}, u32[]{:S(2)}) collective-permute-start(bf16[512,1024]{1,0:T(8,128)(2,1)} %get-tuple-element.171), channel_id=1, source_target_pairs={{0,1},{1,0},{2,3},{3,2},{4,5},{5,4},{6,7},{7,6},{8,9},{9,8},{10,11... | collective-permute-start | bytes 3145736 | tf_op jit(solution)/shard_map/ppermute | solution.py:51
  241.7 14.2 %collective-permute-start.36 = (bf16[512,512]{1,0:T(8,128)(2,1)}, bf16[512,512]{1,0:T(8,128)(2,1)}, u32[]{:S(2)}, u32[]{:S(2)}) collective-permute-start(bf16[512,512]{1,0:T(8,128)(2,1)} %constant_dynamic-slice_fusion.15), channel_id=1, source_target_pairs={{0,2},{1,3},{2,0},{3,1},{4,6},{5,7},{6,4},{7,5},{8,10},{9,11},{10,... | collective-permute-start | bytes 1572872 | tf_op jit(solution)/shard_map/ppermute | solution.py:51
  245.0 49.0 %collective-permute-start.46 = (bf16[2,2,128,1024]{3,2,1,0:T(8,128)(2,1)}, bf16[2,2,128,1024]{3,2,1,0:T(8,128)(2,1)}, u32[]{:S(2)}, u32[]{:S(2)}) collective-permute-start(bf16[2,2,128,1024]{3,2,1,0:T(8,128)(2,1)} %pad_maximum_fusion.11), channel_id=1, source_target_pairs={{0,24},{4,28},{8,0},{12,4},{16,8},{20,12},{24,16},{28,20},{1,25},{... | collective-permute-start | bytes 3145736 | tf_op jit(solution)/shard_map/ppermute | solution.py:726
  265.6 28.4 %collective-permute-start.45 = (bf16[2,2,128,1024]{3,2,1,0:T(8,128)(2,1)}, bf16[2,2,128,1024]{3,2,1,0:T(8,128)(2,1)}, u32[]{:S(2)}, u32[]{:S(2)}) collective-permute-start(bf16[2,2,128,1024]{3,2,1,0:T(8,128)(2,1)} %pad_maximum_fusion.10), channel_id=1, source_target_pairs={{0,8},{4,12},{8,16},{12,20},{16,24},{20,28},{24,0},{28,4},{1,9},{5... | collective-permute-start | bytes 3145736 | tf_op jit(solution)/shard_map/ppermute | solution.py:726
  266.6 27.4 %collective-permute-start.43 = (bf16[2,2,1,128,512]{4,3,0,2,1:T(8,128)(2,1)}, bf16[2,2,1,128,512]{4,3,0,2,1:T(8,128)(2,1)}, u32[]{:S(2)}, u32[]{:S(2)}) collective-permute-start(bf16[2,2,1,128,512]{4,3,0,2,1:T(8,128)(2,1)} %copy.321), channel_id=1, source_target_pairs={{0,4},{4,0},{8,12},{12,8},{16,20},{20,16},{24,28},{28,24},{1,5},{5... | collective-permute-start | bytes 1572872 | tf_op jit(solution)/shard_map/ppermute | solution.py:51
  269.1 25.4 %collective-permute-start.42 = (bf16[1024,512]{1,0:T(8,128)(2,1)}, bf16[1024,512]{1,0:T(8,128)(2,1)S(1)}, u32[]{:S(2)}, u32[]{:S(2)}) collective-permute-start(bf16[1024,512]{1,0:T(8,128)(2,1)} %get-tuple-element.184), channel_id=1, source_target_pairs={{0,2},{1,3},{2,0},{3,1},{4,6},{5,7},{6,4},{7,5},{8,10},{9,11},{10,... | collective-permute-start | bytes 3145736 | tf_op jit(solution)/shard_map/ppermute | solution.py:51
  272.5 21.5 %collective-permute-start.44 = (bf16[2,2,1,128,512]{4,3,0,2,1:T(8,128)(2,1)}, bf16[2,2,1,128,512]{4,3,0,2,1:T(8,128)(2,1)S(1)}, u32[]{:S(2)}, u32[]{:S(2)}) collective-permute-start(bf16[2,2,1,128,512]{4,3,0,2,1:T(8,128)(2,1)} %copy.322), channel_id=1, source_target_pairs={{0,4},{4,0},{8,12},{12,8},{16,20},{20,16},{24,28},{28,24},{1,5},{5... | collective-permute-start | bytes 1572872 | tf_op jit(solution)/shard_map/ppermute | solution.py:51
  302.1 51.0 %collective-permute-start.49 = (bf16[1024,512]{1,0:T(8,128)(2,1)}, bf16[1024,512]{1,0:T(8,128)(2,1)}, u32[]{:S(2)}, u32[]{:S(2)}) collective-permute-start(bf16[1024,512]{1,0:T(8,128)(2,1)} %get-tuple-element.192), channel_id=1, source_target_pairs={{0,2},{1,3},{2,0},{3,1},{4,6},{5,7},{6,4},{7,5},{8,10},{9,11},{10,... | collective-permute-start | bytes 3145736 | tf_op jit(solution)/shard_map/ppermute | solution.py:51
  306.6 37.7 %collective-permute-start.67 = (bf16[1,2,128,1024]{3,2,1,0:T(8,128)(2,1)}, bf16[1,2,128,1024]{3,2,1,0:T(8,128)(2,1)}, u32[]{:S(2)}, u32[]{:S(2)}) collective-permute-start(bf16[1,2,128,1024]{3,2,1,0:T(8,128)(2,1)} %constant_dynamic-slice_fusion.1), channel_id=1, source_target_pairs={{0,4},{4,0},{8,12},{12,8},{16,20},{20,16},{24,28},{28,24},{1,5},{5... | collective-permute-start | bytes 1572872 | tf_op jit(solution)/shard_map/ppermute | solution.py:51
  308.3 37.3 %collective-permute-start.47 = (bf16[2,2,1,128,512]{4,3,2,1,0:T(8,128)(2,1)}, bf16[2,2,1,128,512]{4,3,2,1,0:T(8,128)(2,1)}, u32[]{:S(2)}, u32[]{:S(2)}) collective-permute-start(bf16[2,2,1,128,512]{4,3,2,1,0:T(8,128)(2,1)} %constant_dynamic-slice_fusion.12), channel_id=1, source_target_pairs={{0,4},{4,0},{8,12},{12,8},{16,20},{20,16},{24,28},{28,24},{1,5},{5... | collective-permute-start | bytes 1572872 | tf_op jit(solution)/shard_map/ppermute | solution.py:51
  310.8 36.5 %collective-permute-start.48 = (bf16[2,2,1,128,512]{4,3,0,2,1:T(8,128)(2,1)}, bf16[2,2,1,128,512]{4,3,0,2,1:T(8,128)(2,1)S(1)}, u32[]{:S(2)}, u32[]{:S(2)}) collective-permute-start(bf16[2,2,1,128,512]{4,3,0,2,1:T(8,128)(2,1)} %add_convert_fusion.12), channel_id=1, source_target_pairs={{0,2},{1,3},{2,0},{3,1},{4,6},{5,7},{6,4},{7,5},{8,10},{9,11},{10,... | collective-permute-start | bytes 1572872 | tf_op jit(solution)/shard_map/ppermute | solution.py:51
  326.7 11.3 %collective-permute-start.50 = (f32[9216]{0:T(1024)S(1)}, f32[9216]{0:T(1024)S(1)}, u32[]{:S(2)}, u32[]{:S(2)}) collective-permute-start(f32[9216]{0:T(1024)S(1)} %constant_dynamic-update-slice_fusion), channel_id=1, source_target_pairs={{0,16},{4,20},{8,24},{12,28},{16,0},{20,4},{24,8},{28,12},{1,17},{... | collective-permute-start | bytes 110600 | tf_op jit(solution)/shard_map/ppermute | solution.py:51
  342.1 19.1 %collective-permute-start.53 = (bf16[2,2,1,128,512]{4,3,2,1,0:T(8,128)(2,1)}, bf16[2,2,1,128,512]{4,3,2,1,0:T(8,128)(2,1)}, u32[]{:S(2)}, u32[]{:S(2)}) collective-permute-start(bf16[2,2,1,128,512]{4,3,2,1,0:T(8,128)(2,1)} %constant_dynamic-slice_fusion.9), channel_id=1, source_target_pairs={{0,4},{4,0},{8,12},{12,8},{16,20},{20,16},{24,28},{28,24},{1,5},{5... | collective-permute-start | bytes 1572872 | tf_op jit(solution)/shard_map/ppermute | solution.py:51
  344.3 23.7 %collective-permute-start.52 = (bf16[2,2,1,128,512]{4,3,2,1,0:T(8,128)(2,1)}, bf16[2,2,1,128,512]{4,3,2,1,0:T(8,128)(2,1)}, u32[]{:S(2)}, u32[]{:S(2)}) collective-permute-start(bf16[2,2,1,128,512]{4,3,2,1,0:T(8,128)(2,1)} %constant_dynamic-slice_fusion.10), channel_id=1, source_target_pairs={{0,4},{4,0},{8,12},{12,8},{16,20},{20,16},{24,28},{28,24},{1,5},{5... | collective-permute-start | bytes 1572872 | tf_op jit(solution)/shard_map/ppermute | solution.py:51
  350.7 14.1 %collective-permute-start.56 = (bf16[2,2,1,1,128,512]{5,4,1,3,2,0:T(8,128)(2,1)}, bf16[2,2,1,1,128,512]{5,4,1,3,2,0:T(8,128)(2,1)}, u32[]{:S(2)}, u32[]{:S(2)}) collective-permute-start(bf16[2,2,1,1,128,512]{5,4,1,3,2,0:T(8,128)(2,1)} %pad_maximum_fusion.15), channel_id=1, source_target_pairs={{0,8},{4,12},{8,0},{12,4},{16,24},{20,28},{24,16},{28,20},{1,9},{5... | collective-permute-start | bytes 1572872 | tf_op jit(solution)/shard_map/ppermute | solution.py:51
  363.2 14.9 %collective-permute-start.55 = (bf16[2,2,1,128,512]{4,3,2,1,0:T(8,128)(2,1)}, bf16[2,2,1,128,512]{4,3,2,1,0:T(8,128)(2,1)S(1)}, u32[]{:S(2)}, u32[]{:S(2)}) collective-permute-start(bf16[2,2,1,128,512]{4,3,2,1,0:T(8,128)(2,1)} %add_convert_fusion.11), channel_id=1, source_target_pairs={{0,2},{1,3},{2,0},{3,1},{4,6},{5,7},{6,4},{7,5},{8,10},{9,11},{10,... | collective-permute-start | bytes 1572872 | tf_op jit(solution)/shard_map/ppermute | solution.py:51
  368.0 23.1 %collective-permute-start.59 = (bf16[512,1024]{1,0:T(8,128)(2,1)}, bf16[512,1024]{1,0:T(8,128)(2,1)}, u32[]{:S(2)}, u32[]{:S(2)}) collective-permute-start(bf16[512,1024]{1,0:T(8,128)(2,1)} %inputs_back.2), channel_id=1, source_target_pairs={{0,1},{1,0},{2,3},{3,2},{4,5},{5,4},{6,7},{7,6},{8,9},{9,8},{10,11... | collective-permute-start | bytes 3145736 | tf_op jit(solution)/shard_map/ppermute | solution.py:51
  368.8 15.0 %collective-permute-start.54 = (bf16[2,2,1,128,512]{4,3,0,2,1:T(8,128)(2,1)}, bf16[2,2,1,128,512]{4,3,0,2,1:T(8,128)(2,1)}, u32[]{:S(2)}, u32[]{:S(2)}) collective-permute-start(bf16[2,2,1,128,512]{4,3,0,2,1:T(8,128)(2,1)} %copy.324), channel_id=1, source_target_pairs={{0,4},{4,0},{8,12},{12,8},{16,20},{20,16},{24,28},{28,24},{1,5},{5... | collective-permute-start | bytes 1572872 | tf_op jit(solution)/shard_map/ppermute | solution.py:51
  370.2 14.8 %collective-permute-start.58 = (f32[9216]{0:T(1024)S(1)}, f32[9216]{0:T(1024)S(1)}, u32[]{:S(2)}, u32[]{:S(2)}) collective-permute-start(f32[9216]{0:T(1024)S(1)} %add.266), channel_id=1, source_target_pairs={{0,4},{4,0},{8,12},{12,8},{16,20},{20,16},{24,28},{28,24},{1,5},{5... | collective-permute-start | bytes 110600 | tf_op jit(solution)/shard_map/ppermute | solution.py:51
  387.3 12.6 %collective-permute-start.62 = (bf16[2,2,1,1,128,512]{5,4,1,3,2,0:T(8,128)(2,1)S(1)}, bf16[2,2,1,1,128,512]{5,4,1,3,2,0:T(8,128)(2,1)S(1)}, u32[]{:S(2)}, u32[]{:S(2)}) collective-permute-start(bf16[2,2,1,1,128,512]{5,4,1,3,2,0:T(8,128)(2,1)S(1)} %pad_maximum_fusion.16), channel_id=1, source_target_pairs={{0,8},{4,12},{8,0},{12,4},{16,24},{20,28},{24,16},{28,20},{1,9},{5... | collective-permute-start | bytes 1572872 | tf_op jit(solution)/shard_map/ppermute | solution.py:51
  391.0 17.4 %collective-permute-start.66 = (f32[6,256]{1,0:T(8,128)S(1)}, f32[6,256]{1,0:T(8,128)S(1)}, u32[]{:S(2)}, u32[]{:S(2)}) collective-permute-start(f32[6,256]{1,0:T(8,128)S(1)} %constant_dynamic-slice_fusion.2), channel_id=1, source_target_pairs={{0,1},{1,0},{2,3},{3,2},{4,5},{5,4},{6,7},{7,6},{8,9},{9,8},{10,11... | collective-permute-start | bytes 18440 | tf_op jit(solution)/shard_map/ppermute | solution.py:51
  393.6 14.4 %collective-permute-start.60 = (bf16[512,512]{1,0:T(8,128)(2,1)S(1)}, bf16[512,512]{1,0:T(8,128)(2,1)S(1)}, u32[]{:S(2)}, u32[]{:S(2)}) collective-permute-start(bf16[512,512]{1,0:T(8,128)(2,1)S(1)} %constant_dynamic-slice_fusion.6), channel_id=1, source_target_pairs={{0,2},{1,3},{2,0},{3,1},{4,6},{5,7},{6,4},{7,5},{8,10},{9,11},{10,... | collective-permute-start | bytes 1572872 | tf_op jit(solution)/shard_map/ppermute | solution.py:51
  401.5 12.9 %collective-permute-start.63 = (bf16[2,1,1,1,128,512]{5,4,3,2,1,0:T(8,128)(2,1)S(1)}, bf16[2,1,1,1,128,512]{5,4,3,2,1,0:T(8,128)(2,1)S(1)}, u32[]{:S(2)}, u32[]{:S(2)}) collective-permute-start(bf16[2,1,1,1,128,512]{5,4,3,2,1,0:T(8,128)(2,1)S(1)} %pad_maximum_fusion.22), channel_id=1, source_target_pairs={{0,16},{4,20},{8,24},{12,28},{16,0},{20,4},{24,8},{28,12},{1,17},{... | collective-permute-start | bytes 786440 | tf_op jit(solution)/shard_map/ppermute | solution.py:51
  (80 other events, 532.8 us)
